TPU v7x, 128 devices: a whole 4x4x4 slice. The times are simulated.
128 devices in a mesh: ctx: 16 (over z, y_lo, core), fsdp: 8 (over x, y_hi).
Axes of the slice: x: 4, y: 4 (y_hi: 2, y_lo: 2; y = y_hi * 2 + y_lo), z: 4, core: 2. Of those that a mesh axis runs over, the one named last changes fastest.
Arguments:
- hidden: bfloat16 [8, 4096, 5376], P('fsdp', 'ctx'), may hold values from -6 to 6
- queries: bfloat16 [8, 4096, 2048], P('fsdp', 'ctx'), may hold values from -23 to 23
- key_heads: bfloat16 [8, 4096, 1024], P('fsdp', 'ctx'), may hold values from -6 to 6
- w_value: bfloat16 [5376, 1024], P('fsdp'), may hold values from -0.078125 to 0.078125
- d_out: bfloat16 [8, 4096, 2048], P('fsdp', 'ctx'), may hold values from -6 to 6
- segments: int32 [8, 4096], P('fsdp', 'ctx'), may hold values from 0 to 3, never falling along the last dimension, each value on 1 to 2048 neighbouring positions
Outputs:
- attn_out: bfloat16 [8, 4096, 2048], P('fsdp', 'ctx')
- d_queries: bfloat16 [8, 4096, 2048], P('fsdp', 'ctx')
- d_keys: bfloat16 [8, 4096, 1024], P('fsdp', 'ctx')
- d_hidden: bfloat16 [8, 4096, 5376], P('fsdp', 'ctx')
- d_w_value: float32 [5376, 1024], P(('ctx', 'fsdp'))
Inputs may be any that keep to these rules, and one draw needn't show every extreme that they name: `segments`: document ids never fall along a sequence; a document holds at most half of the 4096 tokens.
All inputs are finite; a program needn't handle non-finite values.
Results may differ from a plain program's by a relative error of at most 0.024.
Values may be sent and summed in bfloat16 or wider, within the bound.
A program may use at most 256 MiB of HBM per device.

v0:
```python
import math

import jax
import jax.numpy as jnp
from jax import lax
from jax.experimental import pallas as pl
from jax.experimental.pallas import tpu as pltpu
from jax.sharding import PartitionSpec as P

HQ = 16
HK = 8
HD = 128
WINDOW = 1024
GROUP = 2


score_scale = 1.0 / math.sqrt(168.0)


def attention_kernel(q_ref, k_ref, v_ref, do_ref, qtag_ref, ktag_ref, out_ref, dq_ref, dk_ref, dv_ref):
    rows = q_ref.shape[0]
    span = k_ref.shape[0]
    reach = span - rows
    q = jnp.concatenate([q_ref[:, r * HD:(r + 1) * HD] for r in range(GROUP)], axis=0)
    grad = jnp.concatenate([do_ref[:, r * HD:(r + 1) * HD] for r in range(GROUP)], axis=0)
    keys = k_ref[...]
    vals = v_ref[...]
    t_idx = lax.broadcasted_iota(jnp.int32, (rows, span), 0)
    l_idx = lax.broadcasted_iota(jnp.int32, (rows, span), 1)
    allowed = (qtag_ref[...] == ktag_ref[...]) & (l_idx > t_idx) & (l_idx <= t_idx + reach)
    allowed = jnp.concatenate([allowed] * GROUP, axis=0)
    scores = lax.dot_general(q, keys, (((1,), (1,)), ((), ())), preferred_element_type=jnp.float32) * score_scale
    scores = jnp.where(allowed, scores, -jnp.inf)
    highest = jnp.max(scores, axis=-1, keepdims=True)
    raw = jnp.exp(scores - highest)
    probs = raw / jnp.sum(raw, axis=-1, keepdims=True)
    probs_low = probs.astype(jnp.bfloat16)
    out = jnp.dot(probs_low, vals, preferred_element_type=jnp.float32).astype(jnp.bfloat16)
    grad_probs = lax.dot_general(grad, vals, (((1,), (1,)), ((), ())), preferred_element_type=jnp.float32)
    delta = jnp.sum(grad.astype(jnp.float32) * out.astype(jnp.float32), axis=-1, keepdims=True)
    grad_scores = (probs * (grad_probs - delta)).astype(jnp.bfloat16)
    dq = (score_scale * jnp.dot(grad_scores, keys, preferred_element_type=jnp.float32)).astype(jnp.bfloat16)
    dk = score_scale * lax.dot_general(grad_scores, q, (((0,), (0,)), ((), ())), preferred_element_type=jnp.float32)
    dv = lax.dot_general(probs_low, grad, (((0,), (0,)), ((), ())), preferred_element_type=jnp.float32)
    for r in range(GROUP):
        out_ref[:, r * HD:(r + 1) * HD] = out[r * rows:(r + 1) * rows]
        dq_ref[:, r * HD:(r + 1) * HD] = dq[r * rows:(r + 1) * rows]
    dk_ref[...] = dk.astype(jnp.bfloat16)
    dv_ref[...] = dv.astype(jnp.bfloat16)


def fused_attention(queries, keys, values, grads, query_tags, key_tags):
    rows, q_width = queries.shape
    span, kv_width = keys.shape
    heads = kv_width // HD
    group_width = GROUP * HD
    q_spec = pl.BlockSpec((rows, group_width), lambda g: (0, g))
    kv_spec = pl.BlockSpec((span, HD), lambda g: (0, g))
    flops = 12 * rows * GROUP * span * HD * heads
    return pl.pallas_call(
        attention_kernel,
        grid=(heads,),
        in_specs=[
            q_spec,
            kv_spec,
            kv_spec,
            q_spec,
            pl.BlockSpec((rows, 1), lambda g: (0, 0)),
            pl.BlockSpec((1, span), lambda g: (0, 0)),
        ],
        out_specs=[q_spec, q_spec, kv_spec, kv_spec],
        out_shape=[
            jax.ShapeDtypeStruct((rows, q_width), jnp.bfloat16),
            jax.ShapeDtypeStruct((rows, q_width), jnp.bfloat16),
            jax.ShapeDtypeStruct((span, kv_width), jnp.bfloat16),
            jax.ShapeDtypeStruct((span, kv_width), jnp.bfloat16),
        ],
        cost_estimate=pl.CostEstimate(
            flops=flops,
            transcendentals=rows * GROUP * span * heads,
            bytes_accessed=2 * (4 * rows * q_width + 4 * span * kv_width),
        ),
    )(queries, keys, values, grads, query_tags, key_tags)


def shifted(x, axis, by):
    length = lax.axis_size(axis)
    pairs = [(i, i + by) for i in range(length) if 0 <= i + by < length]
    return lax.ppermute(x, axis, pairs)


def shards(hidden, queries, key_heads, w_value, d_out, segments):
    shard_rows = hidden.shape[1]
    kv_width = w_value.shape[1]
    n_hops = WINDOW // shard_rows
    span_rows = (n_hops + 1) * shard_rows
    tokens_in = hidden[0]
    own_keys = key_heads[0]
    own_segments = segments[0]
    n_fsdp = lax.axis_size("fsdp")
    n_ctx = lax.axis_size("ctx")
    model_width = tokens_in.shape[1]
    half_rows = w_value.shape[0] // 2
    core = lax.axis_index("ctx") % 2
    w_mine = lax.all_gather(
        lax.dynamic_slice_in_dim(w_value, core * half_rows, half_rows, 0), "fsdp", axis=0, tiled=False
    )
    w_other = lax.ppermute(w_mine, "ctx", [(i, i ^ 1) for i in range(n_ctx)])
    token_halves = tokens_in.reshape(shard_rows, n_fsdp, 2, half_rows)
    tokens_mine = lax.dynamic_index_in_dim(token_halves, core, axis=2, keepdims=False)
    tokens_other = lax.dynamic_index_in_dim(token_halves, 1 - core, axis=2, keepdims=False)
    values = (
        jnp.einsum("tfr,frn->tn", tokens_mine, w_mine, preferred_element_type=jnp.float32)
        + jnp.einsum("tfr,frn->tn", tokens_other, w_other, preferred_element_type=jnp.float32)
    ).astype(jnp.bfloat16)
    out_rows = model_width // (n_ctx * n_fsdp)
    token_cols = (
        tokens_in.reshape(shard_rows, n_ctx, n_fsdp, out_rows).transpose(2, 0, 1, 3)
    )
    token_cols = lax.all_to_all(token_cols, "fsdp", 0, 0, tiled=True)
    segment_tags = own_segments.astype(jnp.bfloat16)
    arrived = []
    for hop_index in range(1, n_hops + 1):
        arrived.append(shifted((own_keys, values, segment_tags), "ctx", hop_index))
    ordered = arrived[::-1] + [(own_keys, values, segment_tags)]
    window_keys = jnp.concatenate([parcel[0] for parcel in ordered], 0)
    window_values = jnp.concatenate([parcel[1] for parcel in ordered], 0)
    window_tags = jnp.concatenate([parcel[2] for parcel in ordered], 0).astype(jnp.int32)
    first_query = lax.axis_index("ctx") * shard_rows
    key_pos = first_query - WINDOW + jnp.arange(span_rows, dtype=jnp.int32)
    key_tags = jnp.where(key_pos >= 0, window_tags, -1)
    out_rows_attn, d_query_heads, key_terms, value_terms = fused_attention(
        queries[0],
        window_keys,
        window_values,
        d_out[0],
        own_segments.astype(jnp.int32)[:, None],
        key_tags[None, :],
    )
    own_start = n_hops * shard_rows
    key_total = key_terms[own_start:].astype(jnp.float32)
    value_total = value_terms[own_start:].astype(jnp.float32)
    for hop_index in range(1, n_hops + 1):
        low_edge = (n_hops - hop_index) * shard_rows
        back_keys, back_values = shifted(
            (
                key_terms[low_edge : low_edge + shard_rows],
                value_terms[low_edge : low_edge + shard_rows],
            ),
            "ctx",
            -hop_index,
        )
        key_total = key_total + back_keys.astype(jnp.float32)
        value_total = value_total + back_values.astype(jnp.float32)
    d_key_rows = key_total.astype(jnp.bfloat16)
    d_values_low = value_total.astype(jnp.bfloat16)
    d_mine = jnp.einsum("tn,frn->tfr", d_values_low, w_mine, preferred_element_type=jnp.float32).astype(jnp.bfloat16)
    d_other = jnp.einsum("tn,frn->tfr", d_values_low, w_other, preferred_element_type=jnp.float32).astype(jnp.bfloat16)
    d_tokens = jnp.where(
        core == 0, jnp.stack([d_mine, d_other], 2), jnp.stack([d_other, d_mine], 2)
    ).reshape(shard_rows, model_width)
    grads_all = lax.all_gather(d_values_low, "fsdp", axis=0, tiled=False)
    token_cols, grads_all, d_query_heads, d_tokens = lax.optimization_barrier(
        (token_cols, grads_all, d_query_heads, d_tokens)
    )
    weight_part = jnp.einsum(
        "ftcr,ftn->crn", token_cols, grads_all, preferred_element_type=jnp.float32
    ).reshape(n_ctx * out_rows, kv_width)
    d_weight = lax.psum_scatter(weight_part, "ctx", scatter_dimension=0, tiled=True)
    return (
        out_rows_attn[None],
        d_query_heads[None],
        d_key_rows[None],
        d_tokens[None],
        d_weight,
    )


def solution(mesh):
    in_specs = (
        P("fsdp", "ctx", None),
        P("fsdp", "ctx", None),
        P("fsdp", "ctx", None),
        P("fsdp", None),
        P("fsdp", "ctx", None),
        P("fsdp", "ctx"),
    )
    out_specs = (
        P("fsdp", "ctx", None),
        P("fsdp", "ctx", None),
        P("fsdp", "ctx", None),
        P("fsdp", "ctx", None),
        P(("ctx", "fsdp"), None),
    )
    return jax.shard_map(shards, mesh=mesh, in_specs=in_specs, out_specs=out_specs, check_vma=False)
```

profile of v0, /device:TPU:28, one launch (start us, length us, event | category | flops | bytes accessed | tf_op | source)
XLA Modules:
  0.0 447.6 jit_solution(11733677003693572564)
XLA Ops:
  9.5 82.9 %all-gather.5.cloned.1.call-done = bf16[2688,1024]{1,0:T(8,128)(2,1)} async-done(((bf16[336,1024]{1,0:T(8,128)(2,1)}), bf16[2688,1024]{1,0:T(8,128)(2,1)}) %all-gather.5.cloned.1.call-update) | async-done | bytes 5505040 | tf_op jit(solution)/shard_map/all_gather | solution.py:105
  93.0 3.4 collective-permute-start.9
  96.5 2.7 collective-permute-start.10
  99.2 4.0 collective-permute-start.11
  105.1 3.4 copy.19
  109.3 3.2 collective-permute-start
  112.5 3.1 collective-permute-start.1
  120.3 4.4 collective-permute-done
  124.8 4.2 fusion.17
  129.0 4.3 fusion.26
  133.3 4.4 collective-permute-start.5
  137.8 23.8 %collective-permute-start.6 = (bf16[256,1024]{1,0:T(8,128)(2,1)S(1)}, bf16[256,1024]{1,0:T(8,128)(2,1)S(1)}, u32[]{:S(2)}, u32[]{:S(2)}) collective-permute-start(bf16[256,1024]{1,0:T(8,128)(2,1)S(1)} %fusion.26), channel_id=1, source_target_pairs={{0,24},{8,32},{16,40},{24,48},{32,56},{40,64},{48,72},{56,80},{64,... | collective-permute-start | bytes 1572872 | tf_op jit(solution)/shard_map/ppermute | solution.py:89
  166.0 6.3 %collective-permute-done.6 = bf16[256,1024]{1,0:T(8,128)(2,1)S(1)} collective-permute-done((bf16[256,1024]{1,0:T(8,128)(2,1)S(1)}, bf16[256,1024]{1,0:T(8,128)(2,1)S(1)}, u32[]{:S(2)}, u32[]{:S(2)}) %collective-permute-start.6) | collective-permute-done | bytes 524320 | tf_op jit(solution)/shard_map/ppermute | solution.py:89
  172.4 11.7 %collective-permute-done.7 = bf16[256,1024]{1,0:T(8,128)(2,1)S(1)} collective-permute-done((bf16[256,1024]{1,0:T(8,128)(2,1)S(1)}, bf16[256,1024]{1,0:T(8,128)(2,1)S(1)}, u32[]{:S(2)}, u32[]{:S(2)}) %collective-permute-start.7) | collective-permute-done | bytes 524320 | tf_op jit(solution)/shard_map/ppermute | solution.py:89
  187.2 26.8 %shard_map.101 = (bf16[256,2048]{1,0:T(8,128)(2,1)}, bf16[256,2048]{1,0:T(8,128)(2,1)}, bf16[1280,1024]{1,0:T(8,128)(2,1)}, bf16[1280,1024]{1,0:T(8,128)(2,1)}) custom-call(bf16[256,2048]{1,0:T(8,128)(2,1)} %bitcast.76, bf16[1280,1024]{1,0:T(8,128)(2,1)} %copy-done.4, bf16[1280,1024]{1,0:T(8,128)(2,1)} %copy-done.5, bf16[256,2048]{1,0:T(8,128)(2,1)} %bitcast.77, ...), custom_call_target="tpu_custom_call" | custom-call | flops 8053063680 | bytes 14680064 | tf_op jit(solution)/shard_map/pallas_call | solution.py:60
  215.7 16.1 %collective-permute-start.13 = (bf16[256,1024]{1,0:T(8,128)(2,1)S(1)}, bf16[256,1024]{1,0:T(8,128)(2,1)S(1)}, u32[]{:S(2)}, u32[]{:S(2)}) collective-permute-start(bf16[256,1024]{1,0:T(8,128)(2,1)S(1)} %get-tuple-element.35), channel_id=1, source_target_pairs={{8,0},{16,8},{24,16},{32,24},{40,32},{48,40},{56,48},{64,56},{72,6... | collective-permute-start | bytes 1572872 | tf_op jit(solution)/shard_map/ppermute | solution.py:89
  236.4 6.4 %collective-permute-done.13 = bf16[256,1024]{1,0:T(8,128)(2,1)S(1)} collective-permute-done((bf16[256,1024]{1,0:T(8,128)(2,1)S(1)}, bf16[256,1024]{1,0:T(8,128)(2,1)S(1)}, u32[]{:S(2)}, u32[]{:S(2)}) %collective-permute-start.13) | collective-permute-done | bytes 524320 | tf_op jit(solution)/shard_map/ppermute | solution.py:89
  242.7 13.6 %collective-permute-done.14 = bf16[256,1024]{1,0:T(8,128)(2,1)S(1)} collective-permute-done((bf16[256,1024]{1,0:T(8,128)(2,1)S(1)}, bf16[256,1024]{1,0:T(8,128)(2,1)S(1)}, u32[]{:S(2)}, u32[]{:S(2)}) %collective-permute-start.14) | collective-permute-done | bytes 524320 | tf_op jit(solution)/shard_map/ppermute | solution.py:89
  258.1 16.7 %collective-permute-done.16 = bf16[256,1024]{1,0:T(8,128)(2,1)S(1)} collective-permute-done((bf16[256,1024]{1,0:T(8,128)(2,1)S(1)}, bf16[256,1024]{1,0:T(8,128)(2,1)S(1)}, u32[]{:S(2)}, u32[]{:S(2)}) %collective-permute-start.16) | collective-permute-done | bytes 524320 | tf_op jit(solution)/shard_map/ppermute | solution.py:89
  279.7 5.0 %copy.22 = bf16[8,256,16,42]{1,2,3,0:T(8,128)(2,1)} copy(bf16[8,256,16,42]{1,3,0,2:T(8,128)(2,1)} %bitcast.65) | data formatting | bytes 5505024 | tf_op jit(solution)/shard_map/transpose | solution.py:118
  284.7 7.9 %all-to-all-start = ((bf16[8,256,16,42]{1,2,3,0:T(8,128)(2,1)}), bf16[8,256,16,42]{1,2,3,0:T(8,128)(2,1)S(1)}, u32[]{:S(2)}, u32[]{:S(2)}) async-start(bf16[8,256,16,42]{1,2,3,0:T(8,128)(2,1)} %copy.22), calls=%async_computation | async-start | bytes 5505024 | tf_op jit(solution)/shard_map/all_to_all | solution.py:120
  293.8 2.9 fusion.34
  303.3 4.2 fusion.9
  307.5 4.2 fusion.10
  313.9 10.3 %all-to-all-done = bf16[8,256,16,42]{1,2,3,0:T(8,128)(2,1)S(1)} async-done(((bf16[8,256,16,42]{1,2,3,0:T(8,128)(2,1)}), bf16[8,256,16,42]{1,2,3,0:T(8,128)(2,1)S(1)}, u32[]{:S(2)}, u32[]{:S(2)}) %all-to-all-start) | async-done | bytes 2752544 | tf_op jit(solution)/shard_map/all_to_all | solution.py:120
  324.2 54.2 %all-gather.7.cloned.1.call-done = bf16[2048,1024]{1,0:T(8,128)(2,1)} async-done(((bf16[256,1024]{1,0:T(8,128)(2,1)}), bf16[2048,1024]{1,0:T(8,128)(2,1)}) %all-gather.7.cloned.1.call-update) | async-done | bytes 4194320 | tf_op jit(solution)/shard_map/all_gather | solution.py:162
  378.4 7.2 %fusion.4 = f32[16,42,1024]{2,1,0:T(8,128)} fusion(bf16[8,256,1024]{2,1,0:T(8,128)(2,1)} %bitcast.75, bf16[8,256,16,42]{1,2,3,0:T(8,128)(2,1)S(1)} %all-to-all-done), kind=kOutput, calls=%fused_computation.4 | convolution fusion | flops 2818572288 | bytes 9699328 | tf_op jit(solution)/shard_map/ftcr,ftn->crn/dot_general | solution.py:166
  387.7 36.4 %fusion = f32[48,1024]{1,0:T(8,128)S(1)} fusion(f32[672,1024]{1,0:T(8,128)S(1)} %reshape.97), kind=kCustom, calls=%all-reduce-scatter | all-reduce-scatter fusion | flops 786433 | bytes 2949632
  424.1 2.8 collective-permute-start.21
  426.9 5.1 %collective-permute-start.22 = (f32[42,1024]{1,0:T(8,128)S(1)}, f32[42,1024]{1,0:T(8,128)S(1)}, u32[]{:S(2)}, u32[]{:S(2)}) collective-permute-start(f32[42,1024]{1,0:T(8,128)S(1)} %slice.40), channel_id=1, source_target_pairs={{0,16},{8,24},{16,32},{24,40},{32,48},{40,56},{48,64},{56,72},{64,... | collective-permute-start | bytes 516104
  432.0 2.9 fusion.29
  435.0 4.6 %copy.25 = bf16[1,256,5376]{2,1,0:T(8,128)(2,1)} copy(bf16[1,256,5376]{1,2,0:T(8,128)(2,1)} %bitcast.66) | data formatting | bytes 5505024
  (79 shorter events, 43.2 us)
Async XLA Ops:
  7.2 85.2 %all-gather.5.cloned.1.call-start = ((), (), s32[]{:S(2)}) async-start(), calls=%async_computation.1 | async-start | bytes 6193152 | tf_op jit(solution)/shard_map/all_gather | solution.py:105
  9.4 368.9 %all-gather.7.cloned.1.call-start = ((), (), s32[]{:S(2)}) async-start(), calls=%async_computation.2 | async-start | bytes 4718592 | tf_op jit(solution)/shard_map/all_gather | solution.py:162
  92.3 36.7 %collective-permute-start.4 = (bf16[8,336,1024]{2,1,0:T(8,128)(2,1)}, bf16[8,336,1024]{2,1,0:T(8,128)(2,1)}, u32[]{:S(2)}, u32[]{:S(2)}) collective-permute-start(bf16[8,336,1024]{2,1,0:T(8,128)(2,1)} %bitcast.67), channel_id=1, source_target_pairs={{0,8},{8,0},{16,24},{24,16},{32,40},{40,32},{48,56},{56,48},{64,72... | collective-permute-start | bytes 16515080 | tf_op jit(solution)/shard_map/ppermute | solution.py:108
  93.0 16.3 %collective-permute-start.9 = (bf16[256]{0:T(256)(128)(2,1)S(1)}, bf16[256]{0:T(256)(128)(2,1)S(1)}, u32[]{:S(2)}, u32[]{:S(2)}) collective-permute-start(bf16[256]{0:T(256)(128)(2,1)S(1)} %convert_reduce_fusion), channel_id=1, source_target_pairs={{0,32},{8,40},{16,48},{24,56},{32,64},{40,72},{48,80},{56,88},{64,... | collective-permute-start | bytes 1544 | tf_op jit(solution)/shard_map/ppermute | solution.py:89
  96.5 16.0 %collective-permute-start.10 = (bf16[256]{0:T(256)(128)(2,1)S(1)}, bf16[256]{0:T(256)(128)(2,1)S(1)}, u32[]{:S(2)}, u32[]{:S(2)}) collective-permute-start(bf16[256]{0:T(256)(128)(2,1)S(1)} %convert_reduce_fusion), channel_id=1, source_target_pairs={{0,24},{8,32},{16,40},{24,48},{32,56},{40,64},{48,72},{56,80},{64,... | collective-permute-start | bytes 1544 | tf_op jit(solution)/shard_map/ppermute | solution.py:89
  99.2 16.5 %collective-permute-start.11 = (bf16[256]{0:T(256)(128)(2,1)S(1)}, bf16[256]{0:T(256)(128)(2,1)S(1)}, u32[]{:S(2)}, u32[]{:S(2)}) collective-permute-start(bf16[256]{0:T(256)(128)(2,1)S(1)} %convert_reduce_fusion), channel_id=1, source_target_pairs={{0,16},{8,24},{16,32},{24,40},{32,48},{40,56},{48,64},{56,72},{64,... | collective-permute-start | bytes 1544 | tf_op jit(solution)/shard_map/ppermute | solution.py:89
  103.2 14.6 %collective-permute-start.12 = (bf16[256]{0:T(256)(128)(2,1)S(1)}, bf16[256]{0:T(256)(128)(2,1)S(1)}, u32[]{:S(2)}, u32[]{:S(2)}) collective-permute-start(bf16[256]{0:T(256)(128)(2,1)S(1)} %convert_reduce_fusion), channel_id=1, source_target_pairs={{0,8},{8,16},{16,24},{24,32},{32,40},{40,48},{48,56},{56,64},{64,7... | collective-permute-start | bytes 1544 | tf_op jit(solution)/shard_map/ppermute | solution.py:89
  105.1 3.4 copy-start.6
  105.1 4.2 copy-start.3
  109.3 15.4 %collective-permute-start = (bf16[256,1024]{1,0:T(8,128)(2,1)S(1)}, bf16[256,1024]{1,0:T(8,128)(2,1)S(1)}, u32[]{:S(2)}, u32[]{:S(2)}) collective-permute-start(bf16[256,1024]{1,0:T(8,128)(2,1)S(1)} %bitcast.70), channel_id=1, source_target_pairs={{0,32},{8,40},{16,48},{24,56},{32,64},{40,72},{48,80},{56,88},{64,... | collective-permute-start | bytes 1572872 | tf_op jit(solution)/shard_map/ppermute | solution.py:89
  112.5 25.2 %collective-permute-start.1 = (bf16[256,1024]{1,0:T(8,128)(2,1)S(1)}, bf16[256,1024]{1,0:T(8,128)(2,1)S(1)}, u32[]{:S(2)}, u32[]{:S(2)}) collective-permute-start(bf16[256,1024]{1,0:T(8,128)(2,1)S(1)} %bitcast.71), channel_id=1, source_target_pairs={{0,24},{8,32},{16,40},{24,48},{32,56},{40,64},{48,72},{56,80},{64,... | collective-permute-start | bytes 1572872 | tf_op jit(solution)/shard_map/ppermute | solution.py:89
  115.7 46.0 %collective-permute-start.2 = (bf16[256,1024]{1,0:T(8,128)(2,1)S(1)}, bf16[256,1024]{1,0:T(8,128)(2,1)S(1)}, u32[]{:S(2)}, u32[]{:S(2)}) collective-permute-start(bf16[256,1024]{1,0:T(8,128)(2,1)S(1)} %bitcast.72), channel_id=1, source_target_pairs={{0,16},{8,24},{16,32},{24,40},{32,48},{40,56},{48,64},{56,72},{64,... | collective-permute-start | bytes 1572872 | tf_op jit(solution)/shard_map/ppermute | solution.py:89
  117.8 45.9 %collective-permute-start.3 = (bf16[256,1024]{1,0:T(8,128)(2,1)S(1)}, bf16[256,1024]{1,0:T(8,128)(2,1)S(1)}, u32[]{:S(2)}, u32[]{:S(2)}) collective-permute-start(bf16[256,1024]{1,0:T(8,128)(2,1)S(1)} %bitcast.73), channel_id=1, source_target_pairs={{0,8},{8,16},{16,24},{24,32},{32,40},{40,48},{48,56},{56,64},{64,7... | collective-permute-start | bytes 1572872 | tf_op jit(solution)/shard_map/ppermute | solution.py:89
  133.3 32.6 %collective-permute-start.5 = (bf16[256,1024]{1,0:T(8,128)(2,1)S(1)}, bf16[256,1024]{1,0:T(8,128)(2,1)S(1)}, u32[]{:S(2)}, u32[]{:S(2)}) collective-permute-start(bf16[256,1024]{1,0:T(8,128)(2,1)S(1)} %fusion.26), channel_id=1, source_target_pairs={{0,32},{8,40},{16,48},{24,56},{32,64},{40,72},{48,80},{56,88},{64,... | collective-permute-start | bytes 1572872 | tf_op jit(solution)/shard_map/ppermute | solution.py:89
  137.8 34.5 %collective-permute-start.6 = (bf16[256,1024]{1,0:T(8,128)(2,1)S(1)}, bf16[256,1024]{1,0:T(8,128)(2,1)S(1)}, u32[]{:S(2)}, u32[]{:S(2)}) collective-permute-start(bf16[256,1024]{1,0:T(8,128)(2,1)S(1)} %fusion.26), channel_id=1, source_target_pairs={{0,24},{8,32},{16,40},{24,48},{32,56},{40,64},{48,72},{56,80},{64,... | collective-permute-start | bytes 1572872 | tf_op jit(solution)/shard_map/ppermute | solution.py:89
  161.7 22.4 %collective-permute-start.7 = (bf16[256,1024]{1,0:T(8,128)(2,1)S(1)}, bf16[256,1024]{1,0:T(8,128)(2,1)S(1)}, u32[]{:S(2)}, u32[]{:S(2)}) collective-permute-start(bf16[256,1024]{1,0:T(8,128)(2,1)S(1)} %fusion.26), channel_id=1, source_target_pairs={{0,16},{8,24},{16,32},{24,40},{32,48},{40,56},{48,64},{56,72},{64,... | collective-permute-start | bytes 1572872 | tf_op jit(solution)/shard_map/ppermute | solution.py:89
  163.7 21.9 %collective-permute-start.8 = (bf16[256,1024]{1,0:T(8,128)(2,1)S(1)}, bf16[256,1024]{1,0:T(8,128)(2,1)S(1)}, u32[]{:S(2)}, u32[]{:S(2)}) collective-permute-start(bf16[256,1024]{1,0:T(8,128)(2,1)S(1)} %fusion.26), channel_id=1, source_target_pairs={{0,8},{8,16},{16,24},{24,32},{32,40},{40,48},{48,56},{56,64},{64,7... | collective-permute-start | bytes 1572872 | tf_op jit(solution)/shard_map/ppermute | solution.py:89
  165.9 19.8 %copy-start.4 = (bf16[1280,1024]{1,0:T(8,128)(2,1)}, bf16[1280,1024]{1,0:T(8,128)(2,1)S(1)}, u32[]{:S(2)}) copy-start(bf16[1280,1024]{1,0:T(8,128)(2,1)S(1)} %constant_dynamic-update-slice_fusion.k_ref) | copy-start | bytes 7864324
  215.7 27.0 %collective-permute-start.13 = (bf16[256,1024]{1,0:T(8,128)(2,1)S(1)}, bf16[256,1024]{1,0:T(8,128)(2,1)S(1)}, u32[]{:S(2)}, u32[]{:S(2)}) collective-permute-start(bf16[256,1024]{1,0:T(8,128)(2,1)S(1)} %get-tuple-element.35), channel_id=1, source_target_pairs={{8,0},{16,8},{24,16},{32,24},{40,32},{48,40},{56,48},{64,56},{72,6... | collective-permute-start | bytes 1572872 | tf_op jit(solution)/shard_map/ppermute | solution.py:89
  231.8 24.5 %collective-permute-start.14 = (bf16[256,1024]{1,0:T(8,128)(2,1)S(1)}, bf16[256,1024]{1,0:T(8,128)(2,1)S(1)}, u32[]{:S(2)}, u32[]{:S(2)}) collective-permute-start(bf16[256,1024]{1,0:T(8,128)(2,1)S(1)} %get-tuple-element.38), channel_id=1, source_target_pairs={{16,0},{24,8},{32,16},{40,24},{48,32},{56,40},{64,48},{72,56},{80,... | collective-permute-start | bytes 1572872 | tf_op jit(solution)/shard_map/ppermute | solution.py:89
  233.8 24.4 %collective-permute-start.15 = (bf16[256,1024]{1,0:T(8,128)(2,1)S(1)}, bf16[256,1024]{1,0:T(8,128)(2,1)S(1)}, u32[]{:S(2)}, u32[]{:S(2)}) collective-permute-start(bf16[256,1024]{1,0:T(8,128)(2,1)S(1)} %get-tuple-element.37), channel_id=1, source_target_pairs={{24,0},{32,8},{40,16},{48,24},{56,32},{64,40},{72,48},{80,56},{88,... | collective-permute-start | bytes 1572872 | tf_op jit(solution)/shard_map/ppermute | solution.py:89
  235.1 39.8 %collective-permute-start.16 = (bf16[256,1024]{1,0:T(8,128)(2,1)S(1)}, bf16[256,1024]{1,0:T(8,128)(2,1)S(1)}, u32[]{:S(2)}, u32[]{:S(2)}) collective-permute-start(bf16[256,1024]{1,0:T(8,128)(2,1)S(1)} %get-tuple-element.36), channel_id=1, source_target_pairs={{32,0},{40,8},{48,16},{56,24},{64,32},{72,40},{80,48},{88,56},{96,... | collective-permute-start | bytes 1572872 | tf_op jit(solution)/shard_map/ppermute | solution.py:89
  284.7 7.9 %copy-start.7 = (u32[128]{0:T(128)S(1)}, u32[128]{0:T(128)}, u32[]{:S(2)}) copy-start(u32[128]{0:T(128)} %constant.48) | copy-start | bytes 1540
  284.7 39.5 %all-to-all-start = ((bf16[8,256,16,42]{1,2,3,0:T(8,128)(2,1)}), bf16[8,256,16,42]{1,2,3,0:T(8,128)(2,1)S(1)}, u32[]{:S(2)}, u32[]{:S(2)}) async-start(bf16[8,256,16,42]{1,2,3,0:T(8,128)(2,1)} %copy.22), calls=%async_computation | async-start | bytes 5505024 | tf_op jit(solution)/shard_map/all_to_all | solution.py:120
  292.5 10.8 %copy-start.2 = (bf16[256,1024]{1,0:T(8,128)(2,1)S(1)}, bf16[256,1024]{1,0:T(8,128)(2,1)}, u32[]{:S(2)}) copy-start(bf16[256,1024]{1,0:T(8,128)(2,1)} %add_convert_fusion.1) | copy-start | bytes 1572868
  296.7 130.3 %collective-permute-start.17 = (bf16[256,1024]{1,0:T(8,128)(2,1)}, bf16[256,1024]{1,0:T(8,128)(2,1)}, u32[]{:S(2)}, u32[]{:S(2)}) collective-permute-start(bf16[256,1024]{1,0:T(8,128)(2,1)} %get-tuple-element.31), channel_id=1, source_target_pairs={{8,0},{16,8},{24,16},{32,24},{40,32},{48,40},{56,48},{64,56},{72,6... | collective-permute-start | bytes 1572872 | tf_op jit(solution)/shard_map/ppermute | solution.py:89
  298.6 133.4 %collective-permute-start.18 = (bf16[256,1024]{1,0:T(8,128)(2,1)}, bf16[256,1024]{1,0:T(8,128)(2,1)}, u32[]{:S(2)}, u32[]{:S(2)}) collective-permute-start(bf16[256,1024]{1,0:T(8,128)(2,1)} %get-tuple-element.34), channel_id=1, source_target_pairs={{16,0},{24,8},{32,16},{40,24},{48,32},{56,40},{64,48},{72,56},{80,... | collective-permute-start | bytes 1572872 | tf_op jit(solution)/shard_map/ppermute | solution.py:89
  300.7 131.3 %collective-permute-start.19 = (bf16[256,1024]{1,0:T(8,128)(2,1)}, bf16[256,1024]{1,0:T(8,128)(2,1)}, u32[]{:S(2)}, u32[]{:S(2)}) collective-permute-start(bf16[256,1024]{1,0:T(8,128)(2,1)} %get-tuple-element.33), channel_id=1, source_target_pairs={{24,0},{32,8},{40,16},{48,24},{56,32},{64,40},{72,48},{80,56},{88,... | collective-permute-start | bytes 1572872 | tf_op jit(solution)/shard_map/ppermute | solution.py:89
  302.0 130.0 %collective-permute-start.20 = (bf16[256,1024]{1,0:T(8,128)(2,1)}, bf16[256,1024]{1,0:T(8,128)(2,1)}, u32[]{:S(2)}, u32[]{:S(2)}) collective-permute-start(bf16[256,1024]{1,0:T(8,128)(2,1)} %get-tuple-element.32), channel_id=1, source_target_pairs={{32,0},{40,8},{48,16},{56,24},{64,32},{72,40},{80,48},{88,56},{96,... | collective-permute-start | bytes 1572872 | tf_op jit(solution)/shard_map/ppermute | solution.py:89
  424.1 15.5 %collective-permute-start.21 = (f32[48,1024]{1,0:T(8,128)S(1)}, f32[48,1024]{1,0:T(8,128)S(1)}, u32[]{:S(2)}, u32[]{:S(2)}) collective-permute-start(f32[48,1024]{1,0:T(8,128)S(1)} %fusion), channel_id=1, source_target_pairs={{0,8},{8,16},{16,24},{24,32},{32,40},{40,48},{48,56},{56,64},{64,7... | collective-permute-start | bytes 589832
  426.9 12.6 %collective-permute-start.22 = (f32[42,1024]{1,0:T(8,128)S(1)}, f32[42,1024]{1,0:T(8,128)S(1)}, u32[]{:S(2)}, u32[]{:S(2)}) collective-permute-start(f32[42,1024]{1,0:T(8,128)S(1)} %slice.40), channel_id=1, source_target_pairs={{0,16},{8,24},{16,32},{24,40},{32,48},{40,56},{48,64},{56,72},{64,... | collective-permute-start | bytes 516104
  435.0 5.7 %copy-start.1 = (bf16[672,1024]{1,0:T(8,128)(2,1)S(1)}, bf16[672,1024]{1,0:T(8,128)(2,1)}, u32[]{:S(2)}) copy-start(bf16[672,1024]{1,0:T(8,128)(2,1)} %param.9) | copy-start | bytes 4128772
  (2 other events, 2.8 us)
Sparse Core Ops, SparseCore 0:
  10.9 81.3 all-gather.4
  277.4 100.9 all-gather.6
where the time goes:
time: 455 us; the launch traced here: 448 us
  waiting for transfers between devices  210 us (46%)
  starting transfers between devices  97.8 us (21%)
  blocking collectives  36.4 us (8%)
  local copies, waits for them, and re-layouts  30.3 us (7%)
  Pallas kernels  26.8 us (6%)
  matrix products  24.1 us (5%)
  between operations  15.2 us (3%)
  other arithmetic  7.06 us (2%)
    all_gather x1, waiting for transfers between devices, shards(): lax.all_gather(lax.dynamic_slice_in_dim(w_value, core * half_rows, half_r...  82.9 us
    ppermute x20, starting transfers between devices, shifted(): return lax.ppermute(x, axis, pairs)  81.9 us
    ppermute x20, waiting for transfers between devices, shifted(): return lax.ppermute(x, axis, pairs)  62.5 us
    all_gather x1, waiting for transfers between devices, shards(): grads_all = lax.all_gather(d_values_low, 'fsdp', axis=0, tiled=False)  54.2 us
    unnamed x1, blocking collectives  36.4 us
    pallas_call x1, Pallas kernels, fused_attention(): pl.pallas_call(attention_kernel, grid=(heads,), in_specs=[q_spec, kv_spec...  26.8 us
    unnamed x34, local copies, waits for them, and re-layouts  12.8 us
    all_to_all x1, waiting for transfers between devices, shards(): token_cols = lax.all_to_all(token_cols, 'fsdp', 0, 0, tiled=True)  10.3 us
  transfers between devices with their start and end apart: 26, of which 11 were waited for; matrix products, arithmetic and copies ran while one was open for 20% of the time, Pallas kernels for 0%

commit v1 on v0

--- a/solution.py
+++ b/solution.py
@@ -1,3 +1,4 @@
+import functools
 import math
 
 import jax
@@ -83,6 +84,49 @@
     )(queries, keys, values, grads, query_tags, key_tags)
 
 
+def peer_gather_kernel(axis, n, x_ref, o_ref, send_sem, recv_sem, local_sem):
+    me = lax.axis_index(axis)
+    barrier = pltpu.get_barrier_semaphore()
+    for k in range(1, n):
+        pl.semaphore_signal(
+            barrier, inc=1, device_id={axis: lax.rem(me + k, n)}, device_id_type=pl.DeviceIdType.MESH
+        )
+    pl.semaphore_wait(barrier, n - 1)
+    local = pltpu.make_async_copy(x_ref, o_ref.at[me], local_sem)
+    local.start()
+    copies = []
+    for k in range(1, n):
+        copy = pltpu.make_async_remote_copy(
+            src_ref=x_ref,
+            dst_ref=o_ref.at[me],
+            send_sem=send_sem.at[k],
+            recv_sem=recv_sem.at[k],
+            device_id={axis: lax.rem(me + k, n)},
+            device_id_type=pl.DeviceIdType.MESH,
+        )
+        copy.start()
+        copies.append(copy)
+    for copy in copies:
+        copy.wait()
+    local.wait()
+
+
+def peer_gather(x, axis, collective_id):
+    n = lax.axis_size(axis)
+    return pl.pallas_call(
+        functools.partial(peer_gather_kernel, axis, n),
+        out_shape=jax.ShapeDtypeStruct((n,) + x.shape, x.dtype),
+        in_specs=[pl.BlockSpec(memory_space=pl.ANY)],
+        out_specs=pl.BlockSpec(memory_space=pl.ANY),
+        scratch_shapes=[
+            pltpu.SemaphoreType.DMA((n,)),
+            pltpu.SemaphoreType.DMA((n,)),
+            pltpu.SemaphoreType.DMA,
+        ],
+        compiler_params=pltpu.CompilerParams(collective_id=collective_id, has_side_effects=True),
+    )(x)
+
+
 def shifted(x, axis, by):
     length = lax.axis_size(axis)
     pairs = [(i, i + by) for i in range(length) if 0 <= i + by < length]
@@ -102,9 +146,7 @@
     model_width = tokens_in.shape[1]
     half_rows = w_value.shape[0] // 2
     core = lax.axis_index("ctx") % 2
-    w_mine = lax.all_gather(
-        lax.dynamic_slice_in_dim(w_value, core * half_rows, half_rows, 0), "fsdp", axis=0, tiled=False
-    )
+    w_mine = peer_gather(lax.dynamic_slice_in_dim(w_value, core * half_rows, half_rows, 0), "fsdp", 1)
     w_other = lax.ppermute(w_mine, "ctx", [(i, i ^ 1) for i in range(n_ctx)])
     token_halves = tokens_in.reshape(shard_rows, n_fsdp, 2, half_rows)
     tokens_mine = lax.dynamic_index_in_dim(token_halves, core, axis=2, keepdims=False)
@@ -159,7 +201,7 @@
     d_tokens = jnp.where(
         core == 0, jnp.stack([d_mine, d_other], 2), jnp.stack([d_other, d_mine], 2)
     ).reshape(shard_rows, model_width)
-    grads_all = lax.all_gather(d_values_low, "fsdp", axis=0, tiled=False)
+    grads_all = peer_gather(d_values_low, "fsdp", 2)
     token_cols, grads_all, d_query_heads, d_tokens = lax.optimization_barrier(
         (token_cols, grads_all, d_query_heads, d_tokens)
     )

time: 455 us -> 474 us (1.042)
  Pallas kernels: 26.8 us -> 180 us
  waiting for transfers between devices: 210 us -> 100 us
  starting transfers between devices: 97.8 us -> 79.7 us
  between operations: 15.2 us -> 1.8 us
  local copies, waits for them, and re-layouts: 30.3 us -> 37.2 us
    pallas_call x0 -> x2, Pallas kernels: none -> 153 us  [peer_gather(): pl.pallas_call(functools.partial(peer_gather_kernel, axis, n), out_shape=...]
    all_gather x2 -> x0, waiting for transfers between devices: 137 us -> none  [the longest x1 82.9 us: shards(): lax.all_gather(lax.dynamic_slice_in_dim(w_value, core * half_rows, half_r...]
    ppermute x20, waiting for transfers between devices: 62.5 us -> 95.6 us  [shifted(): return lax.ppermute(x, axis, pairs)]
    ppermute x20, starting transfers between devices: 81.9 us -> 67.5 us  [shifted(): return lax.ppermute(x, axis, pairs)]
    all_to_all x1, waiting for transfers between devices: 10.3 us -> 0.01 us  [shards(): token_cols = lax.all_to_all(token_cols, 'fsdp', 0, 0, tiled=True)]
  transfers between devices with their start and end apart: 26 -> 24, of which waited for: 11 -> 10; matrix products, arithmetic and copies ran while one was open for 20% -> 22% of each run, Pallas kernels for 0% -> 17%
where the time goes in v1:
time: 474 us; the launch traced here: 471 us
  Pallas kernels  180 us (38%)
  waiting for transfers between devices  100 us (21%)
  starting transfers between devices  79.7 us (17%)
  blocking collectives  40.3 us (9%)
  local copies, waits for them, and re-layouts  37.2 us (8%)
  matrix products  25.8 us (5%)
  other arithmetic  6.19 us (1%)
    pallas_call x2, Pallas kernels, peer_gather(): pl.pallas_call(functools.partial(peer_gather_kernel, axis, n), out_shape=...  153 us
    ppermute x20, waiting for transfers between devices, shifted(): return lax.ppermute(x, axis, pairs)  95.6 us
    ppermute x20, starting transfers between devices, shifted(): return lax.ppermute(x, axis, pairs)  67.5 us
    unnamed x1, blocking collectives  40.3 us
    pallas_call x1, Pallas kernels, fused_attention(): pl.pallas_call(attention_kernel, grid=(heads,), in_specs=[q_spec, kv_spec...  26.8 us
    unnamed x34, local copies, waits for them, and re-layouts  14.7 us
  transfers between devices with their start and end apart: 24, of which 10 were waited for; matrix products, arithmetic and copies ran while one was open for 22% of the time, Pallas kernels for 17%

profile of v1, /device:TPU:28, one launch (start us, length us, event | category | flops | bytes accessed | tf_op | source)
XLA Modules:
  0.0 471.1 jit_solution(11287340276060587755)
XLA Ops:
  2.9 97.7 %shard_map.101 = bf16[8,336,1024]{2,1,0:T(8,128)(2,1)} custom-call(bf16[336,1024]{1,0:T(8,128)(2,1)} %constant_dynamic-slice_fusion.1.x_ref), custom_call_target="tpu_custom_call" | custom-call | tf_op jit(solution)/shard_map/pallas_call | solution.py:116
  100.7 3.8 collective-permute-start.9
  104.5 3.1 collective-permute-start.10
  107.6 3.9 collective-permute-start.11
  113.4 4.5 copy.19
  117.9 5.3 %reshape_squeeze.7 = bf16[256,16,8,42]{0,3,2,1:T(8,128)(2,1)} reshape(bf16[1,256,5376]{1,2,0:T(8,128)(2,1)} %copy.19) | data formatting | bytes 5505024 | tf_op jit(solution)/shard_map/reshape;squeeze | solution.py:160
  123.2 5.0 %copy.22 = bf16[8,256,16,42]{1,2,3,0:T(8,128)(2,1)} copy(bf16[8,256,16,42]{1,3,0,2:T(8,128)(2,1)} %bitcast.63) | data formatting | bytes 5505024 | tf_op jit(solution)/shard_map/transpose | solution.py:160
  128.2 7.2 %all-to-all-start = ((bf16[8,256,16,42]{1,2,3,0:T(8,128)(2,1)}), bf16[8,256,16,42]{1,2,3,0:T(8,128)(2,1)}, u32[]{:S(2)}, u32[]{:S(2)}) async-start(bf16[8,256,16,42]{1,2,3,0:T(8,128)(2,1)} %copy.22), calls=%async_computation | async-start | bytes 5505024 | tf_op jit(solution)/shard_map/all_to_all | solution.py:162
  135.4 4.7 %fusion.17 = f32[256,1024]{1,0:T(8,128)S(1)} fusion(bf16[8,336,1024]{2,1,0:T(8,128)(2,1)} %shard_map.101, bf16[256,8,2,336]{0,3,2,1:T(8,128)(2,1)} %bitcast.61, s32[]{:T(128)S(6)} %select_n.41), kind=kOutput, calls=%fused_computation.15 | convolution fusion | flops 1409286144 | bytes 7929860 | tf_op jit(solution)/shard_map/tfr,frn->tn/dot_general | solution.py:155
  140.9 3.6 collective-permute-start
  151.7 5.0 %collective-permute-done = bf16[256,1024]{1,0:T(8,128)(2,1)S(1)} collective-permute-done((bf16[256,1024]{1,0:T(8,128)(2,1)S(1)}, bf16[256,1024]{1,0:T(8,128)(2,1)S(1)}, u32[]{:S(2)}, u32[]{:S(2)}) %collective-permute-start) | collective-permute-done | bytes 524320 | tf_op jit(solution)/shard_map/ppermute | solution.py:133
  156.8 4.7 fusion.26
  161.5 4.4 collective-permute-start.5
  165.9 11.5 %collective-permute-done.1 = bf16[256,1024]{1,0:T(8,128)(2,1)S(1)} collective-permute-done((bf16[256,1024]{1,0:T(8,128)(2,1)S(1)}, bf16[256,1024]{1,0:T(8,128)(2,1)S(1)}, u32[]{:S(2)}, u32[]{:S(2)}) %collective-permute-start.1) | collective-permute-done | bytes 524320 | tf_op jit(solution)/shard_map/ppermute | solution.py:133
  177.5 4.8 %collective-permute-start.6 = (bf16[256,1024]{1,0:T(8,128)(2,1)S(1)}, bf16[256,1024]{1,0:T(8,128)(2,1)S(1)}, u32[]{:S(2)}, u32[]{:S(2)}) collective-permute-start(bf16[256,1024]{1,0:T(8,128)(2,1)S(1)} %fusion.26), channel_id=1, source_target_pairs={{0,24},{8,32},{16,40},{24,48},{32,56},{40,64},{48,72},{56,80},{64,... | collective-permute-start | bytes 1572872 | tf_op jit(solution)/shard_map/ppermute | solution.py:133
  182.3 7.4 %collective-permute-done.2 = bf16[256,1024]{1,0:T(8,128)(2,1)S(1)} collective-permute-done((bf16[256,1024]{1,0:T(8,128)(2,1)S(1)}, bf16[256,1024]{1,0:T(8,128)(2,1)S(1)}, u32[]{:S(2)}, u32[]{:S(2)}) %collective-permute-start.2) | collective-permute-done | bytes 524320 | tf_op jit(solution)/shard_map/ppermute | solution.py:133
  189.7 4.4 collective-permute-start.7
  196.1 3.8 collective-permute-done.6
  199.9 12.2 %collective-permute-done.7 = bf16[256,1024]{1,0:T(8,128)(2,1)S(1)} collective-permute-done((bf16[256,1024]{1,0:T(8,128)(2,1)S(1)}, bf16[256,1024]{1,0:T(8,128)(2,1)S(1)}, u32[]{:S(2)}, u32[]{:S(2)}) %collective-permute-start.7) | collective-permute-done | bytes 524320 | tf_op jit(solution)/shard_map/ppermute | solution.py:133
  213.8 26.8 %shard_map.102 = (bf16[256,2048]{1,0:T(8,128)(2,1)}, bf16[256,2048]{1,0:T(8,128)(2,1)}, bf16[1280,1024]{1,0:T(8,128)(2,1)}, bf16[1280,1024]{1,0:T(8,128)(2,1)}) custom-call(bf16[256,2048]{1,0:T(8,128)(2,1)} %bitcast.70, bf16[1280,1024]{1,0:T(8,128)(2,1)} %copy-done.4, bf16[1280,1024]{1,0:T(8,128)(2,1)} %copy-done.5, bf16[256,2048]{1,0:T(8,128)(2,1)} %bitcast.71, ...), custom_call_target="tpu_custom_call" | custom-call | flops 8053063680 | bytes 14680064 | tf_op jit(solution)/shard_map/pallas_call | solution.py:61
  243.4 18.1 %collective-permute-start.13 = (bf16[256,1024]{1,0:T(8,128)(2,1)S(1)}, bf16[256,1024]{1,0:T(8,128)(2,1)S(1)}, u32[]{:S(2)}, u32[]{:S(2)}) collective-permute-start(bf16[256,1024]{1,0:T(8,128)(2,1)S(1)} %get-tuple-element.35), channel_id=1, source_target_pairs={{8,0},{16,8},{24,16},{32,24},{40,32},{48,40},{56,48},{64,56},{72,6... | collective-permute-start | bytes 1572872 | tf_op jit(solution)/shard_map/ppermute | solution.py:133
  274.3 11.7 %collective-permute-done.14 = bf16[256,1024]{1,0:T(8,128)(2,1)S(1)} collective-permute-done((bf16[256,1024]{1,0:T(8,128)(2,1)S(1)}, bf16[256,1024]{1,0:T(8,128)(2,1)S(1)}, u32[]{:S(2)}, u32[]{:S(2)}) %collective-permute-start.14) | collective-permute-done | bytes 524320 | tf_op jit(solution)/shard_map/ppermute | solution.py:133
  291.2 41.4 %collective-permute-done.16 = bf16[256,1024]{1,0:T(8,128)(2,1)} collective-permute-done((bf16[256,1024]{1,0:T(8,128)(2,1)}, bf16[256,1024]{1,0:T(8,128)(2,1)}, u32[]{:S(2)}, u32[]{:S(2)}) %collective-permute-start.16) | collective-permute-done | bytes 524320 | tf_op jit(solution)/shard_map/ppermute | solution.py:133
  335.2 55.3 %shard_map.103 = bf16[8,256,1024]{2,1,0:T(8,128)(2,1)} custom-call(bf16[256,1024]{1,0:T(8,128)(2,1)} %add_convert_fusion.1.x_ref), custom_call_target="tpu_custom_call" | custom-call | tf_op jit(solution)/shard_map/pallas_call | solution.py:116
  390.5 4.2 fusion.9
  394.7 4.2 fusion.10
  401.1 8.1 %fusion.4 = f32[16,42,1024]{2,1,0:T(8,128)} fusion(bf16[8,256,1024]{2,1,0:T(8,128)(2,1)} %shard_map.103, bf16[8,256,16,42]{1,2,3,0:T(8,128)(2,1)} %all-to-all-done), kind=kOutput, calls=%fused_computation.4 | convolution fusion | flops 2818572288 | bytes 9699328 | tf_op jit(solution)/shard_map/ftcr,ftn->crn/dot_general | solution.py:208
  409.2 3.1 reshape.97
  412.3 40.3 %fusion = f32[48,1024]{1,0:T(8,128)S(1)} fusion(f32[672,1024]{1,0:T(8,128)} %reshape.97), kind=kCustom, calls=%all-reduce-scatter | all-reduce-scatter fusion | flops 786433 | bytes 2949632
  455.2 4.6 copy.25
  459.8 3.0 collective-permute-start.22
  465.3 4.6 collective-permute-done.22
  (75 shorter events, 47.1 us)
Async XLA Ops:
  0.6 1.3 copy-start
  2.9 97.8 %copy-start.6 = (s32[1,256]{1,0:T(1,128)S(1)}, s32[1,256]{1,0:T(1,128)}, u32[]{:S(2)}) copy-start(s32[1,256]{1,0:T(1,128)} %param.11) | copy-start | bytes 3076
  100.5 56.3 %collective-permute-start.4 = (bf16[8,336,1024]{2,1,0:T(8,128)(2,1)}, bf16[8,336,1024]{2,1,0:T(8,128)(2,1)}, u32[]{:S(2)}, u32[]{:S(2)}) collective-permute-start(bf16[8,336,1024]{2,1,0:T(8,128)(2,1)} %shard_map.101), channel_id=1, source_target_pairs={{0,8},{8,0},{16,24},{24,16},{32,40},{40,32},{48,56},{56,48},{64,72... | collective-permute-start | bytes 16515080 | tf_op jit(solution)/shard_map/ppermute | solution.py:150
  100.7 40.3 %collective-permute-start.9 = (bf16[256]{0:T(256)(128)(2,1)S(1)}, bf16[256]{0:T(256)(128)(2,1)S(1)}, u32[]{:S(2)}, u32[]{:S(2)}) collective-permute-start(bf16[256]{0:T(256)(128)(2,1)S(1)} %convert_reduce_fusion), channel_id=1, source_target_pairs={{0,32},{8,40},{16,48},{24,56},{32,64},{40,72},{48,80},{56,88},{64,... | collective-permute-start | bytes 1544 | tf_op jit(solution)/shard_map/ppermute | solution.py:133
  104.5 40.0 %collective-permute-start.10 = (bf16[256]{0:T(256)(128)(2,1)S(1)}, bf16[256]{0:T(256)(128)(2,1)S(1)}, u32[]{:S(2)}, u32[]{:S(2)}) collective-permute-start(bf16[256]{0:T(256)(128)(2,1)S(1)} %convert_reduce_fusion), channel_id=1, source_target_pairs={{0,24},{8,32},{16,40},{24,48},{32,56},{40,64},{48,72},{56,80},{64,... | collective-permute-start | bytes 1544 | tf_op jit(solution)/shard_map/ppermute | solution.py:133
  107.6 39.4 %collective-permute-start.11 = (bf16[256]{0:T(256)(128)(2,1)S(1)}, bf16[256]{0:T(256)(128)(2,1)S(1)}, u32[]{:S(2)}, u32[]{:S(2)}) collective-permute-start(bf16[256]{0:T(256)(128)(2,1)S(1)} %convert_reduce_fusion), channel_id=1, source_target_pairs={{0,16},{8,24},{16,32},{24,40},{32,48},{40,56},{48,64},{56,72},{64,... | collective-permute-start | bytes 1544 | tf_op jit(solution)/shard_map/ppermute | solution.py:133
  111.5 37.7 %collective-permute-start.12 = (bf16[256]{0:T(256)(128)(2,1)S(1)}, bf16[256]{0:T(256)(128)(2,1)S(1)}, u32[]{:S(2)}, u32[]{:S(2)}) collective-permute-start(bf16[256]{0:T(256)(128)(2,1)S(1)} %convert_reduce_fusion), channel_id=1, source_target_pairs={{0,8},{8,16},{16,24},{24,32},{32,40},{40,48},{48,56},{56,64},{64,7... | collective-permute-start | bytes 1544 | tf_op jit(solution)/shard_map/ppermute | solution.py:133
  128.2 273.0 %all-to-all-start = ((bf16[8,256,16,42]{1,2,3,0:T(8,128)(2,1)}), bf16[8,256,16,42]{1,2,3,0:T(8,128)(2,1)}, u32[]{:S(2)}, u32[]{:S(2)}) async-start(bf16[8,256,16,42]{1,2,3,0:T(8,128)(2,1)} %copy.22), calls=%async_computation | async-start | bytes 5505024 | tf_op jit(solution)/shard_map/all_to_all | solution.py:162
  135.4 5.5 %copy-start.3 = (bf16[1,256,1024]{2,1,0:T(8,128)(2,1)S(1)}, bf16[1,256,1024]{2,1,0:T(8,128)(2,1)}, u32[]{:S(2)}) copy-start(bf16[1,256,1024]{2,1,0:T(8,128)(2,1)} %param.8) | copy-start | bytes 1572868
  140.9 15.8 %collective-permute-start = (bf16[256,1024]{1,0:T(8,128)(2,1)S(1)}, bf16[256,1024]{1,0:T(8,128)(2,1)S(1)}, u32[]{:S(2)}, u32[]{:S(2)}) collective-permute-start(bf16[256,1024]{1,0:T(8,128)(2,1)S(1)} %bitcast.65), channel_id=1, source_target_pairs={{0,32},{8,40},{16,48},{24,56},{32,64},{40,72},{48,80},{56,88},{64,... | collective-permute-start | bytes 1572872 | tf_op jit(solution)/shard_map/ppermute | solution.py:133
  144.5 32.9 %collective-permute-start.1 = (bf16[256,1024]{1,0:T(8,128)(2,1)S(1)}, bf16[256,1024]{1,0:T(8,128)(2,1)S(1)}, u32[]{:S(2)}, u32[]{:S(2)}) collective-permute-start(bf16[256,1024]{1,0:T(8,128)(2,1)S(1)} %bitcast.66), channel_id=1, source_target_pairs={{0,24},{8,32},{16,40},{24,48},{32,56},{40,64},{48,72},{56,80},{64,... | collective-permute-start | bytes 1572872 | tf_op jit(solution)/shard_map/ppermute | solution.py:133
  147.1 42.6 %collective-permute-start.2 = (bf16[256,1024]{1,0:T(8,128)(2,1)S(1)}, bf16[256,1024]{1,0:T(8,128)(2,1)S(1)}, u32[]{:S(2)}, u32[]{:S(2)}) collective-permute-start(bf16[256,1024]{1,0:T(8,128)(2,1)S(1)} %bitcast.67), channel_id=1, source_target_pairs={{0,16},{8,24},{16,32},{24,40},{32,48},{40,56},{48,64},{56,72},{64,... | collective-permute-start | bytes 1572872 | tf_op jit(solution)/shard_map/ppermute | solution.py:133
  149.2 44.9 %collective-permute-start.3 = (bf16[256,1024]{1,0:T(8,128)(2,1)S(1)}, bf16[256,1024]{1,0:T(8,128)(2,1)S(1)}, u32[]{:S(2)}, u32[]{:S(2)}) collective-permute-start(bf16[256,1024]{1,0:T(8,128)(2,1)S(1)} %bitcast.68), channel_id=1, source_target_pairs={{0,8},{8,16},{16,24},{24,32},{32,40},{40,48},{48,56},{56,64},{64,7... | collective-permute-start | bytes 1572872 | tf_op jit(solution)/shard_map/ppermute | solution.py:133
  161.5 34.6 %collective-permute-start.5 = (bf16[256,1024]{1,0:T(8,128)(2,1)S(1)}, bf16[256,1024]{1,0:T(8,128)(2,1)S(1)}, u32[]{:S(2)}, u32[]{:S(2)}) collective-permute-start(bf16[256,1024]{1,0:T(8,128)(2,1)S(1)} %fusion.26), channel_id=1, source_target_pairs={{0,32},{8,40},{16,48},{24,56},{32,64},{40,72},{48,80},{56,88},{64,... | collective-permute-start | bytes 1572872 | tf_op jit(solution)/shard_map/ppermute | solution.py:133
  177.5 22.4 %collective-permute-start.6 = (bf16[256,1024]{1,0:T(8,128)(2,1)S(1)}, bf16[256,1024]{1,0:T(8,128)(2,1)S(1)}, u32[]{:S(2)}, u32[]{:S(2)}) collective-permute-start(bf16[256,1024]{1,0:T(8,128)(2,1)S(1)} %fusion.26), channel_id=1, source_target_pairs={{0,24},{8,32},{16,40},{24,48},{32,56},{40,64},{48,72},{56,80},{64,... | collective-permute-start | bytes 1572872 | tf_op jit(solution)/shard_map/ppermute | solution.py:133
  189.7 22.4 %collective-permute-start.7 = (bf16[256,1024]{1,0:T(8,128)(2,1)S(1)}, bf16[256,1024]{1,0:T(8,128)(2,1)S(1)}, u32[]{:S(2)}, u32[]{:S(2)}) collective-permute-start(bf16[256,1024]{1,0:T(8,128)(2,1)S(1)} %fusion.26), channel_id=1, source_target_pairs={{0,16},{8,24},{16,32},{24,40},{32,48},{40,56},{48,64},{56,72},{64,... | collective-permute-start | bytes 1572872 | tf_op jit(solution)/shard_map/ppermute | solution.py:133
  194.1 18.0 %collective-permute-start.8 = (bf16[256,1024]{1,0:T(8,128)(2,1)S(1)}, bf16[256,1024]{1,0:T(8,128)(2,1)S(1)}, u32[]{:S(2)}, u32[]{:S(2)}) collective-permute-start(bf16[256,1024]{1,0:T(8,128)(2,1)S(1)} %fusion.26), channel_id=1, source_target_pairs={{0,8},{8,16},{16,24},{24,32},{32,40},{40,48},{48,56},{56,64},{64,7... | collective-permute-start | bytes 1572872 | tf_op jit(solution)/shard_map/ppermute | solution.py:133
  196.1 16.2 %copy-start.4 = (bf16[1280,1024]{1,0:T(8,128)(2,1)}, bf16[1280,1024]{1,0:T(8,128)(2,1)S(1)}, u32[]{:S(2)}) copy-start(bf16[1280,1024]{1,0:T(8,128)(2,1)S(1)} %constant_dynamic-update-slice_fusion.k_ref) | copy-start | bytes 7864324
  212.2 1.6 copy-start.5
  240.6 25.4 %copy-start.7 = (u32[128]{0:T(128)S(1)}, u32[128]{0:T(128)}, u32[]{:S(2)}) copy-start(u32[128]{0:T(128)} %constant.48) | copy-start | bytes 1540
  243.4 29.0 %collective-permute-start.13 = (bf16[256,1024]{1,0:T(8,128)(2,1)S(1)}, bf16[256,1024]{1,0:T(8,128)(2,1)S(1)}, u32[]{:S(2)}, u32[]{:S(2)}) collective-permute-start(bf16[256,1024]{1,0:T(8,128)(2,1)S(1)} %get-tuple-element.35), channel_id=1, source_target_pairs={{8,0},{16,8},{24,16},{32,24},{40,32},{48,40},{56,48},{64,56},{72,6... | collective-permute-start | bytes 1572872 | tf_op jit(solution)/shard_map/ppermute | solution.py:133
  261.5 24.5 %collective-permute-start.14 = (bf16[256,1024]{1,0:T(8,128)(2,1)S(1)}, bf16[256,1024]{1,0:T(8,128)(2,1)S(1)}, u32[]{:S(2)}, u32[]{:S(2)}) collective-permute-start(bf16[256,1024]{1,0:T(8,128)(2,1)S(1)} %get-tuple-element.38), channel_id=1, source_target_pairs={{16,0},{24,8},{32,16},{40,24},{48,32},{56,40},{64,48},{72,56},{80,... | collective-permute-start | bytes 1572872 | tf_op jit(solution)/shard_map/ppermute | solution.py:133
  263.5 26.3 %collective-permute-start.15 = (bf16[256,1024]{1,0:T(8,128)(2,1)}, bf16[256,1024]{1,0:T(8,128)(2,1)}, u32[]{:S(2)}, u32[]{:S(2)}) collective-permute-start(bf16[256,1024]{1,0:T(8,128)(2,1)} %get-tuple-element.37), channel_id=1, source_target_pairs={{24,0},{32,8},{40,16},{48,24},{56,32},{64,40},{72,48},{80,56},{88,... | collective-permute-start | bytes 1572872 | tf_op jit(solution)/shard_map/ppermute | solution.py:133
  264.8 67.8 %collective-permute-start.16 = (bf16[256,1024]{1,0:T(8,128)(2,1)}, bf16[256,1024]{1,0:T(8,128)(2,1)}, u32[]{:S(2)}, u32[]{:S(2)}) collective-permute-start(bf16[256,1024]{1,0:T(8,128)(2,1)} %get-tuple-element.36), channel_id=1, source_target_pairs={{32,0},{40,8},{48,16},{56,24},{64,32},{72,40},{80,48},{88,56},{96,... | collective-permute-start | bytes 1572872 | tf_op jit(solution)/shard_map/ppermute | solution.py:133
  270.2 189.6 %collective-permute-start.17 = (bf16[256,1024]{1,0:T(8,128)(2,1)}, bf16[256,1024]{1,0:T(8,128)(2,1)S(1)}, u32[]{:S(2)}, u32[]{:S(2)}) collective-permute-start(bf16[256,1024]{1,0:T(8,128)(2,1)} %get-tuple-element.31), channel_id=1, source_target_pairs={{8,0},{16,8},{24,16},{32,24},{40,32},{48,40},{56,48},{64,56},{72,6... | collective-permute-start | bytes 1572872 | tf_op jit(solution)/shard_map/ppermute | solution.py:133
  272.4 190.4 %collective-permute-start.18 = (bf16[256,1024]{1,0:T(8,128)(2,1)}, bf16[256,1024]{1,0:T(8,128)(2,1)S(1)}, u32[]{:S(2)}, u32[]{:S(2)}) collective-permute-start(bf16[256,1024]{1,0:T(8,128)(2,1)} %get-tuple-element.34), channel_id=1, source_target_pairs={{16,0},{24,8},{32,16},{40,24},{48,32},{56,40},{64,48},{72,56},{80,... | collective-permute-start | bytes 1572872 | tf_op jit(solution)/shard_map/ppermute | solution.py:133
  286.0 176.8 %collective-permute-start.19 = (bf16[256,1024]{1,0:T(8,128)(2,1)}, bf16[256,1024]{1,0:T(8,128)(2,1)S(1)}, u32[]{:S(2)}, u32[]{:S(2)}) collective-permute-start(bf16[256,1024]{1,0:T(8,128)(2,1)} %get-tuple-element.33), channel_id=1, source_target_pairs={{24,0},{32,8},{40,16},{48,24},{56,32},{64,40},{72,48},{80,56},{88,... | collective-permute-start | bytes 1572872 | tf_op jit(solution)/shard_map/ppermute | solution.py:133
  289.7 173.1 %collective-permute-start.20 = (bf16[256,1024]{1,0:T(8,128)(2,1)}, bf16[256,1024]{1,0:T(8,128)(2,1)}, u32[]{:S(2)}, u32[]{:S(2)}) collective-permute-start(bf16[256,1024]{1,0:T(8,128)(2,1)} %get-tuple-element.32), channel_id=1, source_target_pairs={{32,0},{40,8},{48,16},{56,24},{64,32},{72,40},{80,48},{88,56},{96,... | collective-permute-start | bytes 1572872 | tf_op jit(solution)/shard_map/ppermute | solution.py:133
  335.2 55.3 %copy-start.2 = (bf16[256,1024]{1,0:T(8,128)(2,1)S(1)}, bf16[256,1024]{1,0:T(8,128)(2,1)}, u32[]{:S(2)}) copy-start(bf16[256,1024]{1,0:T(8,128)(2,1)} %add_convert_fusion.1.x_ref) | copy-start | bytes 1572868
  453.3 16.6 %collective-permute-start.21 = (f32[48,1024]{1,0:T(8,128)S(1)}, f32[48,1024]{1,0:T(8,128)S(1)}, u32[]{:S(2)}, u32[]{:S(2)}) collective-permute-start(f32[48,1024]{1,0:T(8,128)S(1)} %fusion), channel_id=1, source_target_pairs={{0,8},{8,16},{16,24},{24,32},{32,40},{40,48},{48,56},{56,64},{64,7... | collective-permute-start | bytes 589832
  455.2 15.9 %copy-start.1 = (bf16[672,1024]{1,0:T(8,128)(2,1)S(1)}, bf16[672,1024]{1,0:T(8,128)(2,1)}, u32[]{:S(2)}) copy-start(bf16[672,1024]{1,0:T(8,128)(2,1)} %param.9) | copy-start | bytes 4128772
  459.8 10.1 %collective-permute-start.22 = (f32[42,1024]{1,0:T(8,128)}, f32[42,1024]{1,0:T(8,128)S(1)}, u32[]{:S(2)}, u32[]{:S(2)}) collective-permute-start(f32[42,1024]{1,0:T(8,128)} %slice.40), channel_id=1, source_target_pairs={{0,16},{8,24},{16,32},{24,40},{32,48},{40,56},{48,64},{56,72},{64,... | collective-permute-start | bytes 516104

commit v2 on v1

--- a/solution.py
+++ b/solution.py
@@ -127,6 +127,54 @@
     )(x)
 
 
+def peer_sum_kernel(axis, n, x_ref, o_ref, landed, send_sem, recv_sem, local_sem):
+    me = lax.axis_index(axis)
+    barrier = pltpu.get_barrier_semaphore()
+    for k in range(1, n):
+        pl.semaphore_signal(
+            barrier, inc=1, device_id={axis: lax.rem(me + k, n)}, device_id_type=pl.DeviceIdType.MESH
+        )
+    pl.semaphore_wait(barrier, n - 1)
+    local = pltpu.make_async_copy(x_ref.at[me], landed.at[0], local_sem)
+    local.start()
+    copies = []
+    for k in range(1, n):
+        peer = lax.rem(me + k, n)
+        copy = pltpu.make_async_remote_copy(
+            src_ref=x_ref.at[peer],
+            dst_ref=landed.at[k],
+            send_sem=send_sem.at[k],
+            recv_sem=recv_sem.at[k],
+            device_id={axis: peer},
+            device_id_type=pl.DeviceIdType.MESH,
+        )
+        copy.start()
+        copies.append(copy)
+    local.wait()
+    total = landed[0]
+    for k in range(1, n):
+        copies[k - 1].wait()
+        total = total + landed[k]
+    o_ref[...] = total
+
+
+def peer_sum_scatter(x, axis, collective_id):
+    n = lax.axis_size(axis)
+    return pl.pallas_call(
+        functools.partial(peer_sum_kernel, axis, n),
+        out_shape=jax.ShapeDtypeStruct(x.shape[1:], x.dtype),
+        in_specs=[pl.BlockSpec(memory_space=pl.ANY)],
+        out_specs=pl.BlockSpec(memory_space=pltpu.VMEM),
+        scratch_shapes=[
+            pltpu.VMEM(x.shape, x.dtype),
+            pltpu.SemaphoreType.DMA((n,)),
+            pltpu.SemaphoreType.DMA((n,)),
+            pltpu.SemaphoreType.DMA,
+        ],
+        compiler_params=pltpu.CompilerParams(collective_id=collective_id, has_side_effects=True),
+    )(x)
+
+
 def shifted(x, axis, by):
     length = lax.axis_size(axis)
     pairs = [(i, i + by) for i in range(length) if 0 <= i + by < length]
@@ -207,8 +255,8 @@
     )
     weight_part = jnp.einsum(
         "ftcr,ftn->crn", token_cols, grads_all, preferred_element_type=jnp.float32
-    ).reshape(n_ctx * out_rows, kv_width)
-    d_weight = lax.psum_scatter(weight_part, "ctx", scatter_dimension=0, tiled=True)
+    )
+    d_weight = peer_sum_scatter(weight_part, "ctx", 3)
     return (
         out_rows_attn[None],
         d_query_heads[None],

time: 474 us -> 466 us (0.983)
  Pallas kernels: 180 us -> 244 us
  blocking collectives: 40.3 us -> 0 us
  waiting for transfers between devices: 100 us -> 76.4 us
    pallas_call x0 -> x1, Pallas kernels: none -> 45.4 us  [peer_sum_scatter(): pl.pallas_call(functools.partial(peer_sum_kernel, axis, n), out_shape=jax...]
    unnamed x1 -> x0, blocking collectives: 40.3 us -> none
    ppermute x20, waiting for transfers between devices: 95.6 us -> 76.4 us  [shifted(): return lax.ppermute(x, axis, pairs)]
    pallas_call x2, Pallas kernels: 153 us -> 172 us  [peer_gather(): pl.pallas_call(functools.partial(peer_gather_kernel, axis, n), out_shape=...]
    unnamed x2 -> x0, starting transfers between devices: 4.9 us -> none
    unnamed x34 -> x33, local copies, waits for them, and re-layouts: 14.7 us -> 13.7 us
  transfers between devices with their start and end apart: 24 -> 22, of which waited for: 10 -> 5; matrix products, arithmetic and copies ran while one was open for 22% -> 12% of each run, Pallas kernels for 17% -> 32%
where the time goes in v2:
time: 466 us; the launch traced here: 463 us
  Pallas kernels  244 us (52%)
  starting transfers between devices  76.6 us (16%)
  waiting for transfers between devices  76.4 us (16%)
  local copies, waits for them, and re-layouts  33 us (7%)
  matrix products  25.9 us (6%)
  other arithmetic  6.08 us (1%)
    pallas_call x2, Pallas kernels, peer_gather(): pl.pallas_call(functools.partial(peer_gather_kernel, axis, n), out_shape=...  172 us
    ppermute x20, waiting for transfers between devices, shifted(): return lax.ppermute(x, axis, pairs)  76.4 us
    ppermute x20, starting transfers between devices, shifted(): return lax.ppermute(x, axis, pairs)  69.3 us
    pallas_call x1, Pallas kernels, peer_sum_scatter(): pl.pallas_call(functools.partial(peer_sum_kernel, axis, n), out_shape=jax...  45.4 us
    pallas_call x1, Pallas kernels, fused_attention(): pl.pallas_call(attention_kernel, grid=(heads,), in_specs=[q_spec, kv_spec...  26.8 us
    unnamed x33, local copies, waits for them, and re-layouts  13.7 us
  transfers between devices with their start and end apart: 22, of which 5 were waited for; matrix products, arithmetic and copies ran while one was open for 12% of the time, Pallas kernels for 32%

profile of v2, /device:TPU:28, one launch (start us, length us, event | category | flops | bytes accessed | tf_op | source)
XLA Modules:
  0.0 463.0 jit_solution(15134270767594529597)
XLA Ops:
  2.9 97.7 %shard_map.101 = bf16[8,336,1024]{2,1,0:T(8,128)(2,1)} custom-call(bf16[336,1024]{1,0:T(8,128)(2,1)} %constant_dynamic-slice_fusion.x_ref), custom_call_target="tpu_custom_call" | custom-call | tf_op jit(solution)/shard_map/pallas_call | solution.py:116
  100.7 2.4 collective-permute-start.12
  103.1 3.3 collective-permute-start.11
  106.4 4.2 collective-permute-start.10
  110.6 3.5 collective-permute-start.9
  114.2 4.5 copy.19
  118.7 5.3 %reshape_squeeze.7 = bf16[256,16,8,42]{0,3,2,1:T(8,128)(2,1)} reshape(bf16[1,256,5376]{1,2,0:T(8,128)(2,1)} %copy.19) | data formatting | bytes 5505024 | tf_op jit(solution)/shard_map/reshape;squeeze | solution.py:208
  124.0 5.0 %copy.22 = bf16[8,256,16,42]{1,2,3,0:T(8,128)(2,1)} copy(bf16[8,256,16,42]{1,3,0,2:T(8,128)(2,1)} %bitcast.60) | data formatting | bytes 5505024 | tf_op jit(solution)/shard_map/transpose | solution.py:208
  128.9 7.2 %all-to-all-start = ((bf16[8,256,16,42]{1,2,3,0:T(8,128)(2,1)}), bf16[8,256,16,42]{1,2,3,0:T(8,128)(2,1)}, u32[]{:S(2)}, u32[]{:S(2)}) async-start(bf16[8,256,16,42]{1,2,3,0:T(8,128)(2,1)} %copy.22), calls=%async_computation | async-start | bytes 5505024 | tf_op jit(solution)/shard_map/all_to_all | solution.py:210
  136.1 4.7 %fusion.16 = f32[256,1024]{1,0:T(8,128)S(1)} fusion(bf16[8,336,1024]{2,1,0:T(8,128)(2,1)} %shard_map.101, bf16[256,8,2,336]{0,3,2,1:T(8,128)(2,1)} %bitcast.58, s32[]{:T(128)S(6)} %select_n.41), kind=kOutput, calls=%fused_computation.15 | convolution fusion | flops 1409286144 | bytes 7929860 | tf_op jit(solution)/shard_map/tfr,frn->tn/dot_general | solution.py:203
  143.6 3.9 collective-permute-start.2
  147.5 2.8 collective-permute-start.1
  152.4 11.7 %collective-permute-done = bf16[256,1024]{1,0:T(8,128)(2,1)S(1)} collective-permute-done((bf16[256,1024]{1,0:T(8,128)(2,1)S(1)}, bf16[256,1024]{1,0:T(8,128)(2,1)S(1)}, u32[]{:S(2)}, u32[]{:S(2)}) %collective-permute-start) | collective-permute-done | bytes 524320 | tf_op jit(solution)/shard_map/ppermute | solution.py:181
  164.1 4.7 %fusion.25 = bf16[256,1024]{1,0:T(8,128)(2,1)S(1)} fusion(f32[256,1024]{1,0:T(8,128)S(1)} %fusion.16, bf16[8,336,1024]{2,1,0:T(8,128)(2,1)} %collective-permute-done.4, bf16[256,8,2,336]{0,3,2,1:T(8,128)(2,1)} %bitcast.59, s32[]{:T(128)S(6)} %select_n.43), kind=kOutput, calls=%fused_computation.18 | convolution fusion | flops 1409810432 | bytes 8454148 | tf_op jit(solution)/shard_map/tfr,frn->tn/dot_general | solution.py:204
  168.8 4.4 collective-permute-start.5
  173.2 14.4 %collective-permute-done.1 = bf16[256,1024]{1,0:T(8,128)(2,1)S(1)} collective-permute-done((bf16[256,1024]{1,0:T(8,128)(2,1)S(1)}, bf16[256,1024]{1,0:T(8,128)(2,1)S(1)}, u32[]{:S(2)}, u32[]{:S(2)}) %collective-permute-start.1) | collective-permute-done | bytes 524320 | tf_op jit(solution)/shard_map/ppermute | solution.py:181
  187.7 14.2 %collective-permute-start.6 = (bf16[256,1024]{1,0:T(8,128)(2,1)S(1)}, bf16[256,1024]{1,0:T(8,128)(2,1)S(1)}, u32[]{:S(2)}, u32[]{:S(2)}) collective-permute-start(bf16[256,1024]{1,0:T(8,128)(2,1)S(1)} %fusion.25), channel_id=1, source_target_pairs={{0,24},{8,32},{16,40},{24,48},{32,56},{40,64},{48,72},{56,80},{64,... | collective-permute-start | bytes 1572872 | tf_op jit(solution)/shard_map/ppermute | solution.py:181
  206.0 6.7 %collective-permute-done.6 = bf16[256,1024]{1,0:T(8,128)(2,1)S(1)} collective-permute-done((bf16[256,1024]{1,0:T(8,128)(2,1)S(1)}, bf16[256,1024]{1,0:T(8,128)(2,1)S(1)}, u32[]{:S(2)}, u32[]{:S(2)}) %collective-permute-start.6) | collective-permute-done | bytes 524320 | tf_op jit(solution)/shard_map/ppermute | solution.py:181
  212.8 11.2 %collective-permute-done.7 = bf16[256,1024]{1,0:T(8,128)(2,1)S(1)} collective-permute-done((bf16[256,1024]{1,0:T(8,128)(2,1)S(1)}, bf16[256,1024]{1,0:T(8,128)(2,1)S(1)}, u32[]{:S(2)}, u32[]{:S(2)}) %collective-permute-start.7) | collective-permute-done | bytes 524320 | tf_op jit(solution)/shard_map/ppermute | solution.py:181
  225.7 26.8 %shard_map.102 = (bf16[256,2048]{1,0:T(8,128)(2,1)}, bf16[256,2048]{1,0:T(8,128)(2,1)}, bf16[1280,1024]{1,0:T(8,128)(2,1)}, bf16[1280,1024]{1,0:T(8,128)(2,1)}) custom-call(bf16[256,2048]{1,0:T(8,128)(2,1)} %bitcast.67, bf16[1280,1024]{1,0:T(8,128)(2,1)} %copy-done.6, bf16[1280,1024]{1,0:T(8,128)(2,1)} %copy-done.7, bf16[256,2048]{1,0:T(8,128)(2,1)} %bitcast.68, ...), custom_call_target="tpu_custom_call" | custom-call | flops 8053063680 | bytes 14680064 | tf_op jit(solution)/shard_map/pallas_call | solution.py:61
  252.5 2.7 fusion.34
  255.2 12.3 %collective-permute-start.13 = (bf16[256,1024]{1,0:T(8,128)(2,1)S(1)}, bf16[256,1024]{1,0:T(8,128)(2,1)S(1)}, u32[]{:S(2)}, u32[]{:S(2)}) collective-permute-start(bf16[256,1024]{1,0:T(8,128)(2,1)S(1)} %get-tuple-element.35), channel_id=1, source_target_pairs={{8,0},{16,8},{24,16},{32,24},{40,32},{48,40},{56,48},{64,56},{72,6... | collective-permute-start | bytes 1572872 | tf_op jit(solution)/shard_map/ppermute | solution.py:181
  272.0 2.9 fusion.33
  278.2 32.3 %collective-permute-done.16 = bf16[256,1024]{1,0:T(8,128)(2,1)S(1)} collective-permute-done((bf16[256,1024]{1,0:T(8,128)(2,1)S(1)}, bf16[256,1024]{1,0:T(8,128)(2,1)S(1)}, u32[]{:S(2)}, u32[]{:S(2)}) %collective-permute-start.16) | collective-permute-done | bytes 524320 | tf_op jit(solution)/shard_map/ppermute | solution.py:181
  314.7 2.6 add_convert_fusion.1.x_ref
  317.3 73.9 %shard_map.103 = bf16[8,256,1024]{2,1,0:T(8,128)(2,1)} custom-call(bf16[256,1024]{1,0:T(8,128)(2,1)} %add_convert_fusion.1.x_ref), custom_call_target="tpu_custom_call" | custom-call | tf_op jit(solution)/shard_map/pallas_call | solution.py:116
  391.2 4.2 fusion.8
  395.4 4.2 fusion.9
  401.8 4.5 copy.25
  406.3 8.2 %fusion.3.x_ref = f32[16,42,1024]{2,1,0:T(8,128)} fusion(bf16[8,256,1024]{2,1,0:T(8,128)(2,1)} %shard_map.103, bf16[8,256,16,42]{1,2,3,0:T(8,128)(2,1)} %all-to-all-done), kind=kOutput, calls=%fused_computation.4 | convolution fusion | flops 2818572288 | bytes 9699328 | tf_op jit(solution)/shard_map/ftcr,ftn->crn/dot_general | solution.py:256
  414.5 45.4 %shard_map.104 = f32[42,1024]{1,0:T(8,128)} custom-call(f32[16,42,1024]{2,1,0:T(8,128)} %fusion.3.x_ref), custom_call_target="tpu_custom_call" | custom-call | tf_op jit(solution)/shard_map/pallas_call | solution.py:163
  460.0 2.3 fusion.28
  (69 shorter events, 27.6 us)
Async XLA Ops:
  0.6 1.3 copy-start
  2.9 97.8 %copy-start.8 = (s32[1,256]{1,0:T(1,128)S(1)}, s32[1,256]{1,0:T(1,128)}, u32[]{:S(2)}) copy-start(s32[1,256]{1,0:T(1,128)} %param.11) | copy-start | bytes 3076
  100.5 63.6 %collective-permute-start.4 = (bf16[8,336,1024]{2,1,0:T(8,128)(2,1)}, bf16[8,336,1024]{2,1,0:T(8,128)(2,1)}, u32[]{:S(2)}, u32[]{:S(2)}) collective-permute-start(bf16[8,336,1024]{2,1,0:T(8,128)(2,1)} %shard_map.101), channel_id=1, source_target_pairs={{0,8},{8,0},{16,24},{24,16},{32,40},{40,32},{48,56},{56,48},{64,72... | collective-permute-start | bytes 16515080 | tf_op jit(solution)/shard_map/ppermute | solution.py:198
  100.7 49.7 %collective-permute-start.12 = (bf16[256]{0:T(256)(128)(2,1)S(1)}, bf16[256]{0:T(256)(128)(2,1)S(1)}, u32[]{:S(2)}, u32[]{:S(2)}) collective-permute-start(bf16[256]{0:T(256)(128)(2,1)S(1)} %convert_reduce_fusion), channel_id=1, source_target_pairs={{0,8},{8,16},{16,24},{24,32},{32,40},{40,48},{48,56},{56,64},{64,7... | collective-permute-start | bytes 1544 | tf_op jit(solution)/shard_map/ppermute | solution.py:181
  103.1 44.5 %collective-permute-start.11 = (bf16[256]{0:T(256)(128)(2,1)S(1)}, bf16[256]{0:T(256)(128)(2,1)S(1)}, u32[]{:S(2)}, u32[]{:S(2)}) collective-permute-start(bf16[256]{0:T(256)(128)(2,1)S(1)} %convert_reduce_fusion), channel_id=1, source_target_pairs={{0,16},{8,24},{16,32},{24,40},{32,48},{40,56},{48,64},{56,72},{64,... | collective-permute-start | bytes 1544 | tf_op jit(solution)/shard_map/ppermute | solution.py:181
  106.4 37.2 %collective-permute-start.10 = (bf16[256]{0:T(256)(128)(2,1)S(1)}, bf16[256]{0:T(256)(128)(2,1)S(1)}, u32[]{:S(2)}, u32[]{:S(2)}) collective-permute-start(bf16[256]{0:T(256)(128)(2,1)S(1)} %convert_reduce_fusion), channel_id=1, source_target_pairs={{0,24},{8,32},{16,40},{24,48},{32,56},{40,64},{48,72},{56,80},{64,... | collective-permute-start | bytes 1544 | tf_op jit(solution)/shard_map/ppermute | solution.py:181
  110.6 31.0 %collective-permute-start.9 = (bf16[256]{0:T(256)(128)(2,1)S(1)}, bf16[256]{0:T(256)(128)(2,1)S(1)}, u32[]{:S(2)}, u32[]{:S(2)}) collective-permute-start(bf16[256]{0:T(256)(128)(2,1)S(1)} %convert_reduce_fusion), channel_id=1, source_target_pairs={{0,32},{8,40},{16,48},{24,56},{32,64},{40,72},{48,80},{56,88},{64,... | collective-permute-start | bytes 1544 | tf_op jit(solution)/shard_map/ppermute | solution.py:181
  128.9 272.9 %all-to-all-start = ((bf16[8,256,16,42]{1,2,3,0:T(8,128)(2,1)}), bf16[8,256,16,42]{1,2,3,0:T(8,128)(2,1)}, u32[]{:S(2)}, u32[]{:S(2)}) async-start(bf16[8,256,16,42]{1,2,3,0:T(8,128)(2,1)} %copy.22), calls=%async_computation | async-start | bytes 5505024 | tf_op jit(solution)/shard_map/all_to_all | solution.py:210
  136.1 5.5 %copy-start.4 = (bf16[1,256,1024]{2,1,0:T(8,128)(2,1)S(1)}, bf16[1,256,1024]{2,1,0:T(8,128)(2,1)}, u32[]{:S(2)}) copy-start(bf16[1,256,1024]{2,1,0:T(8,128)(2,1)} %param.8) | copy-start | bytes 1572868
  141.7 62.2 %collective-permute-start.3 = (bf16[256,1024]{1,0:T(8,128)(2,1)S(1)}, bf16[256,1024]{1,0:T(8,128)(2,1)S(1)}, u32[]{:S(2)}, u32[]{:S(2)}) collective-permute-start(bf16[256,1024]{1,0:T(8,128)(2,1)S(1)} %bitcast.62), channel_id=1, source_target_pairs={{0,8},{8,16},{16,24},{24,32},{32,40},{40,48},{48,56},{56,64},{64,7... | collective-permute-start | bytes 1572872 | tf_op jit(solution)/shard_map/ppermute | solution.py:181
  143.6 58.2 %collective-permute-start.2 = (bf16[256,1024]{1,0:T(8,128)(2,1)S(1)}, bf16[256,1024]{1,0:T(8,128)(2,1)S(1)}, u32[]{:S(2)}, u32[]{:S(2)}) collective-permute-start(bf16[256,1024]{1,0:T(8,128)(2,1)S(1)} %bitcast.63), channel_id=1, source_target_pairs={{0,16},{8,24},{16,32},{24,40},{32,48},{40,56},{48,64},{56,72},{64,... | collective-permute-start | bytes 1572872 | tf_op jit(solution)/shard_map/ppermute | solution.py:181
  147.5 40.1 %collective-permute-start.1 = (bf16[256,1024]{1,0:T(8,128)(2,1)S(1)}, bf16[256,1024]{1,0:T(8,128)(2,1)S(1)}, u32[]{:S(2)}, u32[]{:S(2)}) collective-permute-start(bf16[256,1024]{1,0:T(8,128)(2,1)S(1)} %bitcast.64), channel_id=1, source_target_pairs={{0,24},{8,32},{16,40},{24,48},{32,56},{40,64},{48,72},{56,80},{64,... | collective-permute-start | bytes 1572872 | tf_op jit(solution)/shard_map/ppermute | solution.py:181
  150.4 13.7 %collective-permute-start = (bf16[256,1024]{1,0:T(8,128)(2,1)S(1)}, bf16[256,1024]{1,0:T(8,128)(2,1)S(1)}, u32[]{:S(2)}, u32[]{:S(2)}) collective-permute-start(bf16[256,1024]{1,0:T(8,128)(2,1)S(1)} %bitcast.65), channel_id=1, source_target_pairs={{0,32},{8,40},{16,48},{24,56},{32,64},{40,72},{48,80},{56,88},{64,... | collective-permute-start | bytes 1572872 | tf_op jit(solution)/shard_map/ppermute | solution.py:181
  168.8 37.2 %collective-permute-start.5 = (bf16[256,1024]{1,0:T(8,128)(2,1)S(1)}, bf16[256,1024]{1,0:T(8,128)(2,1)S(1)}, u32[]{:S(2)}, u32[]{:S(2)}) collective-permute-start(bf16[256,1024]{1,0:T(8,128)(2,1)S(1)} %fusion.25), channel_id=1, source_target_pairs={{0,32},{8,40},{16,48},{24,56},{32,64},{40,72},{48,80},{56,88},{64,... | collective-permute-start | bytes 1572872 | tf_op jit(solution)/shard_map/ppermute | solution.py:181
  187.7 25.1 %collective-permute-start.6 = (bf16[256,1024]{1,0:T(8,128)(2,1)S(1)}, bf16[256,1024]{1,0:T(8,128)(2,1)S(1)}, u32[]{:S(2)}, u32[]{:S(2)}) collective-permute-start(bf16[256,1024]{1,0:T(8,128)(2,1)S(1)} %fusion.25), channel_id=1, source_target_pairs={{0,24},{8,32},{16,40},{24,48},{32,56},{40,64},{48,72},{56,80},{64,... | collective-permute-start | bytes 1572872 | tf_op jit(solution)/shard_map/ppermute | solution.py:181
  201.9 22.1 %collective-permute-start.7 = (bf16[256,1024]{1,0:T(8,128)(2,1)S(1)}, bf16[256,1024]{1,0:T(8,128)(2,1)S(1)}, u32[]{:S(2)}, u32[]{:S(2)}) collective-permute-start(bf16[256,1024]{1,0:T(8,128)(2,1)S(1)} %fusion.25), channel_id=1, source_target_pairs={{0,16},{8,24},{16,32},{24,40},{32,48},{40,56},{48,64},{56,72},{64,... | collective-permute-start | bytes 1572872 | tf_op jit(solution)/shard_map/ppermute | solution.py:181
  203.9 20.1 %collective-permute-start.8 = (bf16[256,1024]{1,0:T(8,128)(2,1)S(1)}, bf16[256,1024]{1,0:T(8,128)(2,1)S(1)}, u32[]{:S(2)}, u32[]{:S(2)}) collective-permute-start(bf16[256,1024]{1,0:T(8,128)(2,1)S(1)} %fusion.25), channel_id=1, source_target_pairs={{0,8},{8,16},{16,24},{24,32},{32,40},{40,48},{48,56},{56,64},{64,7... | collective-permute-start | bytes 1572872 | tf_op jit(solution)/shard_map/ppermute | solution.py:181
  206.0 18.2 %copy-start.6 = (bf16[1280,1024]{1,0:T(8,128)(2,1)}, bf16[1280,1024]{1,0:T(8,128)(2,1)S(1)}, u32[]{:S(2)}) copy-start(bf16[1280,1024]{1,0:T(8,128)(2,1)S(1)} %constant_dynamic-update-slice_fusion.k_ref) | copy-start | bytes 7864324
  224.1 1.6 copy-start.7
  255.2 21.7 %collective-permute-start.13 = (bf16[256,1024]{1,0:T(8,128)(2,1)S(1)}, bf16[256,1024]{1,0:T(8,128)(2,1)S(1)}, u32[]{:S(2)}, u32[]{:S(2)}) collective-permute-start(bf16[256,1024]{1,0:T(8,128)(2,1)S(1)} %get-tuple-element.35), channel_id=1, source_target_pairs={{8,0},{16,8},{24,16},{32,24},{40,32},{48,40},{56,48},{64,56},{72,6... | collective-permute-start | bytes 1572872 | tf_op jit(solution)/shard_map/ppermute | solution.py:181
  267.5 42.9 %collective-permute-start.16 = (bf16[256,1024]{1,0:T(8,128)(2,1)S(1)}, bf16[256,1024]{1,0:T(8,128)(2,1)S(1)}, u32[]{:S(2)}, u32[]{:S(2)}) collective-permute-start(bf16[256,1024]{1,0:T(8,128)(2,1)S(1)} %get-tuple-element.36), channel_id=1, source_target_pairs={{32,0},{40,8},{48,16},{56,24},{64,32},{72,40},{80,48},{88,56},{96,... | collective-permute-start | bytes 1572872 | tf_op jit(solution)/shard_map/ppermute | solution.py:181
  268.8 42.9 %collective-permute-start.15 = (bf16[256,1024]{1,0:T(8,128)(2,1)}, bf16[256,1024]{1,0:T(8,128)(2,1)S(1)}, u32[]{:S(2)}, u32[]{:S(2)}) collective-permute-start(bf16[256,1024]{1,0:T(8,128)(2,1)} %get-tuple-element.37), channel_id=1, source_target_pairs={{24,0},{32,8},{40,16},{48,24},{56,32},{64,40},{72,48},{80,56},{88,... | collective-permute-start | bytes 1572872 | tf_op jit(solution)/shard_map/ppermute | solution.py:181
  270.1 44.5 %collective-permute-start.14 = (bf16[256,1024]{1,0:T(8,128)(2,1)}, bf16[256,1024]{1,0:T(8,128)(2,1)}, u32[]{:S(2)}, u32[]{:S(2)}) collective-permute-start(bf16[256,1024]{1,0:T(8,128)(2,1)} %get-tuple-element.38), channel_id=1, source_target_pairs={{16,0},{24,8},{32,16},{40,24},{48,32},{56,40},{64,48},{72,56},{80,... | collective-permute-start | bytes 1572872 | tf_op jit(solution)/shard_map/ppermute | solution.py:181
  275.0 185.0 %collective-permute-start.17 = (bf16[256,1024]{1,0:T(8,128)(2,1)}, bf16[256,1024]{1,0:T(8,128)(2,1)S(1)}, u32[]{:S(2)}, u32[]{:S(2)}) collective-permute-start(bf16[256,1024]{1,0:T(8,128)(2,1)} %get-tuple-element.31), channel_id=1, source_target_pairs={{8,0},{16,8},{24,16},{32,24},{40,32},{48,40},{56,48},{64,56},{72,6... | collective-permute-start | bytes 1572872 | tf_op jit(solution)/shard_map/ppermute | solution.py:181
  276.9 183.0 %collective-permute-start.20 = (bf16[256,1024]{1,0:T(8,128)(2,1)}, bf16[256,1024]{1,0:T(8,128)(2,1)S(1)}, u32[]{:S(2)}, u32[]{:S(2)}) collective-permute-start(bf16[256,1024]{1,0:T(8,128)(2,1)} %get-tuple-element.32), channel_id=1, source_target_pairs={{32,0},{40,8},{48,16},{56,24},{64,32},{72,40},{80,48},{88,56},{96,... | collective-permute-start | bytes 1572872 | tf_op jit(solution)/shard_map/ppermute | solution.py:181
  310.5 149.5 %collective-permute-start.19 = (bf16[256,1024]{1,0:T(8,128)(2,1)}, bf16[256,1024]{1,0:T(8,128)(2,1)S(1)}, u32[]{:S(2)}, u32[]{:S(2)}) collective-permute-start(bf16[256,1024]{1,0:T(8,128)(2,1)} %get-tuple-element.33), channel_id=1, source_target_pairs={{24,0},{32,8},{40,16},{48,24},{56,32},{64,40},{72,48},{80,56},{88,... | collective-permute-start | bytes 1572872 | tf_op jit(solution)/shard_map/ppermute | solution.py:181
  311.8 0.8 copy-start.5
  312.6 147.4 %collective-permute-start.18 = (bf16[256,1024]{1,0:T(8,128)(2,1)}, bf16[256,1024]{1,0:T(8,128)(2,1)S(1)}, u32[]{:S(2)}, u32[]{:S(2)}) collective-permute-start(bf16[256,1024]{1,0:T(8,128)(2,1)} %get-tuple-element.34), channel_id=1, source_target_pairs={{16,0},{24,8},{32,16},{40,24},{48,32},{56,40},{64,48},{72,56},{80,... | collective-permute-start | bytes 1572872 | tf_op jit(solution)/shard_map/ppermute | solution.py:181
  317.3 73.9 %copy-start.2 = (bf16[256,1024]{1,0:T(8,128)(2,1)S(1)}, bf16[256,1024]{1,0:T(8,128)(2,1)}, u32[]{:S(2)}) copy-start(bf16[256,1024]{1,0:T(8,128)(2,1)} %add_convert_fusion.1.x_ref) | copy-start | bytes 1572868
  406.3 56.7 %copy-start.1 = (bf16[672,1024]{1,0:T(8,128)(2,1)S(1)}, bf16[672,1024]{1,0:T(8,128)(2,1)}, u32[]{:S(2)}) copy-start(bf16[672,1024]{1,0:T(8,128)(2,1)} %param.9) | copy-start | bytes 4128772
  459.9 2.4 copy-start.3

commit v3 on v2

--- a/solution.py
+++ b/solution.py
@@ -18,14 +18,10 @@
 score_scale = 1.0 / math.sqrt(168.0)
 
 
-def attention_kernel(q_ref, k_ref, v_ref, do_ref, qtag_ref, ktag_ref, out_ref, dq_ref, dk_ref, dv_ref):
-    rows = q_ref.shape[0]
-    span = k_ref.shape[0]
+def window_probs(q, keys, qtag_ref, ktag_ref):
+    rows = qtag_ref.shape[0]
+    span = keys.shape[0]
     reach = span - rows
-    q = jnp.concatenate([q_ref[:, r * HD:(r + 1) * HD] for r in range(GROUP)], axis=0)
-    grad = jnp.concatenate([do_ref[:, r * HD:(r + 1) * HD] for r in range(GROUP)], axis=0)
-    keys = k_ref[...]
-    vals = v_ref[...]
     t_idx = lax.broadcasted_iota(jnp.int32, (rows, span), 0)
     l_idx = lax.broadcasted_iota(jnp.int32, (rows, span), 1)
     allowed = (qtag_ref[...] == ktag_ref[...]) & (l_idx > t_idx) & (l_idx <= t_idx + reach)
@@ -34,7 +30,27 @@
     scores = jnp.where(allowed, scores, -jnp.inf)
     highest = jnp.max(scores, axis=-1, keepdims=True)
     raw = jnp.exp(scores - highest)
-    probs = raw / jnp.sum(raw, axis=-1, keepdims=True)
+    return raw / jnp.sum(raw, axis=-1, keepdims=True)
+
+
+def stacked_heads(ref):
+    return jnp.concatenate([ref[:, r * HD:(r + 1) * HD] for r in range(GROUP)], axis=0)
+
+
+def value_grad_kernel(q_ref, k_ref, do_ref, qtag_ref, ktag_ref, dv_ref):
+    probs_low = window_probs(stacked_heads(q_ref), k_ref[...], qtag_ref, ktag_ref).astype(jnp.bfloat16)
+    grad = stacked_heads(do_ref)
+    dv = lax.dot_general(probs_low, grad, (((0,), (0,)), ((), ())), preferred_element_type=jnp.float32)
+    dv_ref[...] = dv.astype(jnp.bfloat16)
+
+
+def attention_kernel(q_ref, k_ref, v_ref, do_ref, qtag_ref, ktag_ref, out_ref, dq_ref, dk_ref):
+    rows = q_ref.shape[0]
+    q = stacked_heads(q_ref)
+    grad = stacked_heads(do_ref)
+    keys = k_ref[...]
+    vals = v_ref[...]
+    probs = window_probs(q, keys, qtag_ref, ktag_ref)
     probs_low = probs.astype(jnp.bfloat16)
     out = jnp.dot(probs_low, vals, preferred_element_type=jnp.float32).astype(jnp.bfloat16)
     grad_probs = lax.dot_general(grad, vals, (((1,), (1,)), ((), ())), preferred_element_type=jnp.float32)
@@ -42,44 +58,57 @@
     grad_scores = (probs * (grad_probs - delta)).astype(jnp.bfloat16)
     dq = (score_scale * jnp.dot(grad_scores, keys, preferred_element_type=jnp.float32)).astype(jnp.bfloat16)
     dk = score_scale * lax.dot_general(grad_scores, q, (((0,), (0,)), ((), ())), preferred_element_type=jnp.float32)
-    dv = lax.dot_general(probs_low, grad, (((0,), (0,)), ((), ())), preferred_element_type=jnp.float32)
     for r in range(GROUP):
         out_ref[:, r * HD:(r + 1) * HD] = out[r * rows:(r + 1) * rows]
         dq_ref[:, r * HD:(r + 1) * HD] = dq[r * rows:(r + 1) * rows]
     dk_ref[...] = dk.astype(jnp.bfloat16)
-    dv_ref[...] = dv.astype(jnp.bfloat16)
+
+
+def head_specs(rows, span):
+    q_spec = pl.BlockSpec((rows, GROUP * HD), lambda g: (0, g))
+    kv_spec = pl.BlockSpec((span, HD), lambda g: (0, g))
+    tag_specs = [pl.BlockSpec((rows, 1), lambda g: (0, 0)), pl.BlockSpec((1, span), lambda g: (0, 0))]
+    return q_spec, kv_spec, tag_specs
+
+
+def value_grads(queries, keys, grads, query_tags, key_tags):
+    rows, q_width = queries.shape
+    span, kv_width = keys.shape
+    heads = kv_width // HD
+    q_spec, kv_spec, tag_specs = head_specs(rows, span)
+    return pl.pallas_call(
+        value_grad_kernel,
+        grid=(heads,),
+        in_specs=[q_spec, kv_spec, q_spec] + tag_specs,
+        out_specs=kv_spec,
+        out_shape=jax.ShapeDtypeStruct((span, kv_width), jnp.bfloat16),
+        cost_estimate=pl.CostEstimate(
+            flops=4 * rows * GROUP * span * HD * heads,
+            transcendentals=rows * GROUP * span * heads,
+            bytes_accessed=2 * (2 * rows * q_width + 2 * span * kv_width),
+        ),
+    )(queries, keys, grads, query_tags, key_tags)
 
 
 def fused_attention(queries, keys, values, grads, query_tags, key_tags):
     rows, q_width = queries.shape
     span, kv_width = keys.shape
     heads = kv_width // HD
-    group_width = GROUP * HD
-    q_spec = pl.BlockSpec((rows, group_width), lambda g: (0, g))
-    kv_spec = pl.BlockSpec((span, HD), lambda g: (0, g))
-    flops = 12 * rows * GROUP * span * HD * heads
+    q_spec, kv_spec, tag_specs = head_specs(rows, span)
     return pl.pallas_call(
         attention_kernel,
         grid=(heads,),
-        in_specs=[
-            q_spec,
-            kv_spec,
-            kv_spec,
-            q_spec,
-            pl.BlockSpec((rows, 1), lambda g: (0, 0)),
-            pl.BlockSpec((1, span), lambda g: (0, 0)),
-        ],
-        out_specs=[q_spec, q_spec, kv_spec, kv_spec],
+        in_specs=[q_spec, kv_spec, kv_spec, q_spec] + tag_specs,
+        out_specs=[q_spec, q_spec, kv_spec],
         out_shape=[
             jax.ShapeDtypeStruct((rows, q_width), jnp.bfloat16),
             jax.ShapeDtypeStruct((rows, q_width), jnp.bfloat16),
             jax.ShapeDtypeStruct((span, kv_width), jnp.bfloat16),
-            jax.ShapeDtypeStruct((span, kv_width), jnp.bfloat16),
         ],
         cost_estimate=pl.CostEstimate(
-            flops=flops,
+            flops=10 * rows * GROUP * span * HD * heads,
             transcendentals=rows * GROUP * span * heads,
-            bytes_accessed=2 * (4 * rows * q_width + 4 * span * kv_width),
+            bytes_accessed=2 * (4 * rows * q_width + 3 * span * kv_width),
         ),
     )(queries, keys, values, grads, query_tags, key_tags)
 
@@ -194,69 +223,60 @@
     model_width = tokens_in.shape[1]
     half_rows = w_value.shape[0] // 2
     core = lax.axis_index("ctx") % 2
-    w_mine = peer_gather(lax.dynamic_slice_in_dim(w_value, core * half_rows, half_rows, 0), "fsdp", 1)
-    w_other = lax.ppermute(w_mine, "ctx", [(i, i ^ 1) for i in range(n_ctx)])
+    w_mine = lax.all_gather(
+        lax.dynamic_slice_in_dim(w_value, core * half_rows, half_rows, 0), "fsdp", axis=0, tiled=False
+    )
     token_halves = tokens_in.reshape(shard_rows, n_fsdp, 2, half_rows)
     tokens_mine = lax.dynamic_index_in_dim(token_halves, core, axis=2, keepdims=False)
     tokens_other = lax.dynamic_index_in_dim(token_halves, 1 - core, axis=2, keepdims=False)
+    out_rows = model_width // (n_ctx * n_fsdp)
+    token_cols = (
+        tokens_in.reshape(shard_rows, n_ctx, n_fsdp, out_rows).transpose(2, 0, 1, 3)
+    )
+    token_cols = lax.all_to_all(token_cols, "fsdp", 0, 0, tiled=True)
+    segment_tags = own_segments.astype(jnp.bfloat16)
+    arrived = [shifted((own_keys, segment_tags), "ctx", hop) for hop in range(1, n_hops + 1)]
+    ordered = arrived[::-1] + [(own_keys, segment_tags)]
+    window_keys = jnp.concatenate([parcel[0] for parcel in ordered], 0)
+    window_tags = jnp.concatenate([parcel[1] for parcel in ordered], 0).astype(jnp.int32)
+    first_query = lax.axis_index("ctx") * shard_rows
+    key_pos = first_query - WINDOW + jnp.arange(span_rows, dtype=jnp.int32)
+    key_tags = jnp.where(key_pos >= 0, window_tags, -1)
+    query_tags = own_segments.astype(jnp.int32)[:, None]
+    own_start = n_hops * shard_rows
+
+    def returned_sum(terms):
+        total = terms[own_start:].astype(jnp.float32)
+        for hop in range(1, n_hops + 1):
+            low_edge = (n_hops - hop) * shard_rows
+            total = total + shifted(terms[low_edge : low_edge + shard_rows], "ctx", -hop).astype(jnp.float32)
+        return total.astype(jnp.bfloat16)
+
+    value_terms = value_grads(queries[0], window_keys, d_out[0], query_tags, key_tags[None, :])
+    w_mine, value_terms = lax.optimization_barrier((w_mine, value_terms))
+    w_other = lax.ppermute(w_mine, "ctx", [(i, i ^ 1) for i in range(n_ctx)])
+    d_values_low = returned_sum(value_terms)
+    grads_all = peer_gather(d_values_low, "fsdp", 2)
+    weight_part = jnp.einsum(
+        "ftcr,ftn->crn", token_cols, grads_all, preferred_element_type=jnp.float32
+    )
+    d_weight = peer_sum_scatter(weight_part, "ctx", 3)
+
     values = (
         jnp.einsum("tfr,frn->tn", tokens_mine, w_mine, preferred_element_type=jnp.float32)
         + jnp.einsum("tfr,frn->tn", tokens_other, w_other, preferred_element_type=jnp.float32)
     ).astype(jnp.bfloat16)
-    out_rows = model_width // (n_ctx * n_fsdp)
-    token_cols = (
-        tokens_in.reshape(shard_rows, n_ctx, n_fsdp, out_rows).transpose(2, 0, 1, 3)
-    )
-    token_cols = lax.all_to_all(token_cols, "fsdp", 0, 0, tiled=True)
-    segment_tags = own_segments.astype(jnp.bfloat16)
-    arrived = []
-    for hop_index in range(1, n_hops + 1):
-        arrived.append(shifted((own_keys, values, segment_tags), "ctx", hop_index))
-    ordered = arrived[::-1] + [(own_keys, values, segment_tags)]
-    window_keys = jnp.concatenate([parcel[0] for parcel in ordered], 0)
-    window_values = jnp.concatenate([parcel[1] for parcel in ordered], 0)
-    window_tags = jnp.concatenate([parcel[2] for parcel in ordered], 0).astype(jnp.int32)
-    first_query = lax.axis_index("ctx") * shard_rows
-    key_pos = first_query - WINDOW + jnp.arange(span_rows, dtype=jnp.int32)
-    key_tags = jnp.where(key_pos >= 0, window_tags, -1)
-    out_rows_attn, d_query_heads, key_terms, value_terms = fused_attention(
-        queries[0],
-        window_keys,
-        window_values,
-        d_out[0],
-        own_segments.astype(jnp.int32)[:, None],
-        key_tags[None, :],
-    )
-    own_start = n_hops * shard_rows
-    key_total = key_terms[own_start:].astype(jnp.float32)
-    value_total = value_terms[own_start:].astype(jnp.float32)
-    for hop_index in range(1, n_hops + 1):
-        low_edge = (n_hops - hop_index) * shard_rows
-        back_keys, back_values = shifted(
-            (
-                key_terms[low_edge : low_edge + shard_rows],
-                value_terms[low_edge : low_edge + shard_rows],
-            ),
-            "ctx",
-            -hop_index,
-        )
-        key_total = key_total + back_keys.astype(jnp.float32)
-        value_total = value_total + back_values.astype(jnp.float32)
-    d_key_rows = key_total.astype(jnp.bfloat16)
-    d_values_low = value_total.astype(jnp.bfloat16)
+    arrived_values = [shifted(values, "ctx", hop) for hop in range(1, n_hops + 1)]
+    window_values = jnp.concatenate(arrived_values[::-1] + [values], 0)
+    out_rows_attn, d_query_heads, key_terms = fused_attention(
+        queries[0], window_keys, window_values, d_out[0], query_tags, key_tags[None, :]
+    )
+    d_key_rows = returned_sum(key_terms)
     d_mine = jnp.einsum("tn,frn->tfr", d_values_low, w_mine, preferred_element_type=jnp.float32).astype(jnp.bfloat16)
     d_other = jnp.einsum("tn,frn->tfr", d_values_low, w_other, preferred_element_type=jnp.float32).astype(jnp.bfloat16)
     d_tokens = jnp.where(
         core == 0, jnp.stack([d_mine, d_other], 2), jnp.stack([d_other, d_mine], 2)
     ).reshape(shard_rows, model_width)
-    grads_all = peer_gather(d_values_low, "fsdp", 2)
-    token_cols, grads_all, d_query_heads, d_tokens = lax.optimization_barrier(
-        (token_cols, grads_all, d_query_heads, d_tokens)
-    )
-    weight_part = jnp.einsum(
-        "ftcr,ftn->crn", token_cols, grads_all, preferred_element_type=jnp.float32
-    )
-    d_weight = peer_sum_scatter(weight_part, "ctx", 3)
     return (
         out_rows_attn[None],
         d_query_heads[None],

time: 466 us -> 416 us (0.89)
  Pallas kernels: 244 us -> 157 us
  waiting for transfers between devices: 76.4 us -> 108 us
  between operations: 1.16 us -> 14.4 us
  starting transfers between devices: 76.6 us -> 65.7 us
    pallas_call x2 -> x1, Pallas kernels: 172 us -> 69.9 us  [peer_gather(): pl.pallas_call(functools.partial(peer_gather_kernel, axis, n), out_shape=...]
    all_gather x0 -> x1, waiting for transfers between devices: none -> 25.8 us  [shards(): lax.all_gather(lax.dynamic_slice_in_dim(w_value, core * half_rows, half_r...]
    pallas_call x0 -> x1, Pallas kernels: none -> 15.2 us  [value_grads(): pl.pallas_call(value_grad_kernel, grid=(heads,), in_specs=[q_spec, kv_spe...]
    ppermute x20, starting transfers between devices: 69.3 us -> 57.8 us  [shifted(): return lax.ppermute(x, axis, pairs)]
    ppermute x20, waiting for transfers between devices: 76.4 us -> 82.4 us  [shifted(): return lax.ppermute(x, axis, pairs)]
    unnamed x33 -> x27, local copies, waits for them, and re-layouts: 13.7 us -> 18 us
  transfers between devices with their start and end apart: 22 -> 23, of which waited for: 5 -> 9; matrix products, arithmetic and copies ran while one was open for 12% -> 14% of each run, Pallas kernels for 32% -> 32%
where the time goes in v3:
time: 416 us; the launch traced here: 413 us
  Pallas kernels  157 us (38%)
  waiting for transfers between devices  108 us (26%)
  starting transfers between devices  65.7 us (16%)
  local copies, waits for them, and re-layouts  34.9 us (8%)
  matrix products  26.3 us (6%)
  between operations  14.4 us (3%)
  other arithmetic  7.29 us (2%)
    ppermute x20, waiting for transfers between devices, shifted(): return lax.ppermute(x, axis, pairs)  82.4 us
    pallas_call x1, Pallas kernels, peer_gather(): pl.pallas_call(functools.partial(peer_gather_kernel, axis, n), out_shape=...  69.9 us
    ppermute x20, starting transfers between devices, shifted(): return lax.ppermute(x, axis, pairs)  57.8 us
    pallas_call x1, Pallas kernels, peer_sum_scatter(): pl.pallas_call(functools.partial(peer_sum_kernel, axis, n), out_shape=jax...  47.5 us
    all_gather x1, waiting for transfers between devices, shards(): lax.all_gather(lax.dynamic_slice_in_dim(w_value, core * half_rows, half_r...  25.8 us
    pallas_call x1, Pallas kernels, fused_attention(): pl.pallas_call(attention_kernel, grid=(heads,), in_specs=[q_spec, kv_spec...  24 us
    unnamed x27, local copies, waits for them, and re-layouts  18 us
    pallas_call x1, Pallas kernels, value_grads(): pl.pallas_call(value_grad_kernel, grid=(heads,), in_specs=[q_spec, kv_spe...  15.2 us
  transfers between devices with their start and end apart: 23, of which 9 were waited for; matrix products, arithmetic and copies ran while one was open for 14% of the time, Pallas kernels for 32%

profile of v3, /device:TPU:28, one launch (start us, length us, event | category | flops | bytes accessed | tf_op | source)
XLA Modules:
  0.0 413.4 jit_solution(7159174801441889580)
XLA Ops:
  10.2 3.8 collective-permute-start.4
  14.0 3.2 collective-permute-start.5
  17.2 3.2 collective-permute-start.6
  20.4 2.9 collective-permute-start.7
  27.4 3.1 collective-permute-start.1
  30.5 2.7 collective-permute-start.2
  38.5 3.2 collective-permute-done.1
  41.7 12.6 %collective-permute-done.2 = bf16[256,1024]{1,0:T(8,128)(2,1)S(1)} collective-permute-done((bf16[256,1024]{1,0:T(8,128)(2,1)}, bf16[256,1024]{1,0:T(8,128)(2,1)S(1)}, u32[]{:S(2)}, u32[]{:S(2)}) %collective-permute-start.2) | collective-permute-done | bytes 524320 | tf_op jit(solution)/shard_map/ppermute | solution.py:210
  57.4 15.2 %shard_map.101 = bf16[1280,1024]{1,0:T(8,128)(2,1)} custom-call(bf16[256,2048]{1,0:T(8,128)(2,1)} %bitcast.72, bf16[1280,1024]{1,0:T(8,128)(2,1)} %copy-done.5, bf16[256,2048]{1,0:T(8,128)(2,1)} %bitcast.74, s32[256,1]{1,0:T(8,128)} %copy.21.qtag_ref, s32[1,1280]{1,0:T(1,128)} %compare_select_fusion.ktag_ref), custom_call_target="tpu_custom_call" | custom-call | flops 2684354560 | bytes 7340032 | tf_op jit(solution)/shard_map/pallas_call | solution.py:79
  72.6 25.8 %all-gather.3.cloned.1.call-done = bf16[2688,1024]{1,0:T(8,128)(2,1)} async-done(((bf16[336,1024]{1,0:T(8,128)(2,1)}), bf16[2688,1024]{1,0:T(8,128)(2,1)}) %all-gather.3.cloned.1.call-update) | async-done | bytes 5505040 | tf_op jit(solution)/shard_map/all_gather | solution.py:226
  98.3 3.3 copy.20
  104.1 5.0 %copy.25 = bf16[8,256,16,42]{1,2,3,0:T(8,128)(2,1)} copy(bf16[8,256,16,42]{1,3,0,2:T(8,128)(2,1)} %bitcast.62) | data formatting | bytes 5505024 | tf_op jit(solution)/shard_map/transpose | solution.py:234
  109.1 7.9 %all-to-all-start = ((bf16[8,256,16,42]{1,2,3,0:T(8,128)(2,1)}), bf16[8,256,16,42]{1,2,3,0:T(8,128)(2,1)}, u32[]{:S(2)}, u32[]{:S(2)}) async-start(bf16[8,256,16,42]{1,2,3,0:T(8,128)(2,1)} %copy.25), calls=%async_computation | async-start | bytes 5505024 | tf_op jit(solution)/shard_map/all_to_all | solution.py:236
  125.8 5.2 %fusion.16 = f32[256,1024]{1,0:T(8,128)} fusion(bf16[8,336,1024]{2,1,0:T(8,128)(2,1)} %bitcast.65, bf16[256,8,2,336]{0,3,2,1:T(8,128)(2,1)S(1)} %bitcast.60, s32[]{:T(128)S(6)} %select_n.47), kind=kOutput, calls=%fused_computation.15 | convolution fusion | flops 1409286144 | bytes 7929860 | tf_op jit(solution)/shard_map/tfr,frn->tn/dot_general | solution.py:266
  131.0 27.5 %collective-permute-done.17 = bf16[256,1024]{1,0:T(8,128)(2,1)S(1)} collective-permute-done((bf16[256,1024]{1,0:T(8,128)(2,1)S(1)}, bf16[256,1024]{1,0:T(8,128)(2,1)S(1)}, u32[]{:S(2)}, u32[]{:S(2)}) %collective-permute-start.17) | collective-permute-done | bytes 524320 | tf_op jit(solution)/shard_map/ppermute | solution.py:210
  158.5 13.5 %collective-permute-done.18 = bf16[256,1024]{1,0:T(8,128)(2,1)S(1)} collective-permute-done((bf16[256,1024]{1,0:T(8,128)(2,1)S(1)}, bf16[256,1024]{1,0:T(8,128)(2,1)S(1)}, u32[]{:S(2)}, u32[]{:S(2)}) %collective-permute-start.18) | collective-permute-done | bytes 524320 | tf_op jit(solution)/shard_map/ppermute | solution.py:210
  174.3 69.9 %shard_map.103 = bf16[8,256,1024]{2,1,0:T(8,128)(2,1)} custom-call(bf16[256,1024]{1,0:T(8,128)(2,1)} %add_convert_fusion.x_ref), custom_call_target="tpu_custom_call" | custom-call | tf_op jit(solution)/shard_map/pallas_call | solution.py:145
  244.2 4.5 %fusion.25 = bf16[256,1024]{1,0:T(8,128)(2,1)S(1)} fusion(f32[256,1024]{1,0:T(8,128)} %fusion.16, bf16[8,336,1024]{2,1,0:T(8,128)(2,1)} %collective-permute-done.8, bf16[256,8,2,336]{0,3,2,1:T(8,128)(2,1)S(1)} %bitcast.61, s32[]{:T(128)S(6)} %select_n.50), kind=kOutput, calls=%fused_computation.18 | convolution fusion | flops 1409810432 | bytes 8454148 | tf_op jit(solution)/shard_map/tfr,frn->tn/dot_general | solution.py:267
  248.8 3.8 collective-permute-start.9
  252.6 8.2 %fusion.3.x_ref = f32[16,42,1024]{2,1,0:T(8,128)} fusion(bf16[8,256,16,42]{1,2,3,0:T(8,128)(2,1)} %all-to-all-done, bf16[8,256,1024]{2,1,0:T(8,128)(2,1)} %shard_map.103), kind=kOutput, calls=%fused_computation.4 | convolution fusion | flops 2818572288 | bytes 9699328 | tf_op jit(solution)/shard_map/ftcr,ftn->crn/dot_general | solution.py:260
  260.8 2.7 collective-permute-start.10
  263.5 3.5 collective-permute-start.11
  267.0 3.0 collective-permute-start.12
  270.0 4.2 %fusion.8 = bf16[256,8,1,336]{0,3,1,2:T(8,128)(2,1)S(1)} fusion(bf16[8,336,1024]{2,1,0:T(8,128)(2,1)} %bitcast.66, bf16[256,1024]{1,0:T(8,128)(2,1)S(1)} %copy-done.2), kind=kOutput, calls=%fused_computation.7 | convolution fusion | flops 1409974272 | bytes 7405568 | tf_op jit(solution)/shard_map/tn,frn->tfr/dot_general | solution.py:275
  274.2 47.5 %shard_map.104 = f32[42,1024]{1,0:T(8,128)} custom-call(f32[16,42,1024]{2,1,0:T(8,128)} %fusion.3.x_ref), custom_call_target="tpu_custom_call" | custom-call | tf_op jit(solution)/shard_map/pallas_call | solution.py:192
  329.0 24.0 %shard_map.102 = (bf16[256,2048]{1,0:T(8,128)(2,1)}, bf16[256,2048]{1,0:T(8,128)(2,1)}, bf16[1280,1024]{1,0:T(8,128)(2,1)}) custom-call(bf16[256,2048]{1,0:T(8,128)(2,1)} %bitcast.73, bf16[1280,1024]{1,0:T(8,128)(2,1)} %copy-done.5, bf16[1280,1024]{1,0:T(8,128)(2,1)} %constant_dynamic-update-slice_fusion.10.v_ref, bf16[256,2048]{1,0:T(8,128)(2,1)} %bitcast.75, ...), custom_call_target="tpu_custom_call" | custom-call | flops 6710886400 | bytes 12058624 | tf_op jit(solution)/shard_map/pallas_call | solution.py:98
  353.0 2.9 fusion.34
  355.9 9.8 %collective-permute-start.13 = (bf16[256,1024]{1,0:T(8,128)(2,1)}, bf16[256,1024]{1,0:T(8,128)(2,1)S(1)}, u32[]{:S(2)}, u32[]{:S(2)}) collective-permute-start(bf16[256,1024]{1,0:T(8,128)(2,1)} %get-tuple-element.29), channel_id=1, source_target_pairs={{8,0},{16,8},{24,16},{32,24},{40,32},{48,40},{56,48},{64,56},{72,6... | collective-permute-start | bytes 1572872 | tf_op jit(solution)/shard_map/ppermute | solution.py:210
  370.2 4.2 %fusion.9 = bf16[256,8,1,336]{0,3,1,2:T(8,128)(2,1)S(1)} fusion(bf16[8,336,1024]{2,1,0:T(8,128)(2,1)} %collective-permute-done.8, bf16[256,1024]{1,0:T(8,128)(2,1)S(1)} %copy-done.2), kind=kOutput, calls=%fused_computation.8 | convolution fusion | flops 1409974272 | bytes 7405568 | tf_op jit(solution)/shard_map/tn,frn->tfr/dot_general | solution.py:276
  376.6 4.6 %copy.27 = bf16[1,256,5376]{2,1,0:T(8,128)(2,1)} copy(bf16[1,256,5376]{1,2,0:T(8,128)(2,1)} %bitcast.63) | data formatting | bytes 5505024
  381.2 6.9 %collective-permute-done.14 = bf16[256,1024]{1,0:T(8,128)(2,1)S(1)} collective-permute-done((bf16[256,1024]{1,0:T(8,128)(2,1)}, bf16[256,1024]{1,0:T(8,128)(2,1)S(1)}, u32[]{:S(2)}, u32[]{:S(2)}) %collective-permute-start.14) | collective-permute-done | bytes 524320 | tf_op jit(solution)/shard_map/ppermute | solution.py:210
  388.1 15.3 %collective-permute-done.16 = bf16[256,1024]{1,0:T(8,128)(2,1)} collective-permute-done((bf16[256,1024]{1,0:T(8,128)(2,1)}, bf16[256,1024]{1,0:T(8,128)(2,1)}, u32[]{:S(2)}, u32[]{:S(2)}) %collective-permute-start.16) | collective-permute-done | bytes 524320 | tf_op jit(solution)/shard_map/ppermute | solution.py:210
  (66 shorter events, 46.0 us)
Async XLA Ops:
  7.2 1.3 copy-start
  7.2 91.1 %all-gather.3.cloned.1.call-start = ((), (), s32[]{:S(2)}) async-start(), calls=%async_computation.1 | async-start | bytes 6193152 | tf_op jit(solution)/shard_map/all_gather | solution.py:226
  9.4 46.4 %copy-start.4 = (bf16[1,256,1024]{2,1,0:T(8,128)(2,1)S(1)}, bf16[1,256,1024]{2,1,0:T(8,128)(2,1)}, u32[]{:S(2)}) copy-start(bf16[1,256,1024]{2,1,0:T(8,128)(2,1)} %param.8) | copy-start | bytes 1572868
  10.2 17.2 %collective-permute-start.4 = (bf16[256]{0:T(256)(128)(2,1)S(1)}, bf16[256]{0:T(256)(128)(2,1)S(1)}, u32[]{:S(2)}, u32[]{:S(2)}) collective-permute-start(bf16[256]{0:T(256)(128)(2,1)S(1)} %convert_reduce_fusion), channel_id=1, source_target_pairs={{0,32},{8,40},{16,48},{24,56},{32,64},{40,72},{48,80},{56,88},{64,... | collective-permute-start | bytes 1544 | tf_op jit(solution)/shard_map/ppermute | solution.py:210
  14.0 16.5 %collective-permute-start.5 = (bf16[256]{0:T(256)(128)(2,1)S(1)}, bf16[256]{0:T(256)(128)(2,1)S(1)}, u32[]{:S(2)}, u32[]{:S(2)}) collective-permute-start(bf16[256]{0:T(256)(128)(2,1)S(1)} %convert_reduce_fusion), channel_id=1, source_target_pairs={{0,24},{8,32},{16,40},{24,48},{32,56},{40,64},{48,72},{56,80},{64,... | collective-permute-start | bytes 1544 | tf_op jit(solution)/shard_map/ppermute | solution.py:210
  17.2 16.1 %collective-permute-start.6 = (bf16[256]{0:T(256)(128)(2,1)S(1)}, bf16[256]{0:T(256)(128)(2,1)S(1)}, u32[]{:S(2)}, u32[]{:S(2)}) collective-permute-start(bf16[256]{0:T(256)(128)(2,1)S(1)} %convert_reduce_fusion), channel_id=1, source_target_pairs={{0,16},{8,24},{16,32},{24,40},{32,48},{40,56},{48,64},{56,72},{64,... | collective-permute-start | bytes 1544 | tf_op jit(solution)/shard_map/ppermute | solution.py:210
  20.4 14.8 %collective-permute-start.7 = (bf16[256]{0:T(256)(128)(2,1)S(1)}, bf16[256]{0:T(256)(128)(2,1)S(1)}, u32[]{:S(2)}, u32[]{:S(2)}) collective-permute-start(bf16[256]{0:T(256)(128)(2,1)S(1)} %convert_reduce_fusion), channel_id=1, source_target_pairs={{0,8},{8,16},{16,24},{24,32},{32,40},{40,48},{48,56},{56,64},{64,7... | collective-permute-start | bytes 1544 | tf_op jit(solution)/shard_map/ppermute | solution.py:210
  23.3 15.1 %collective-permute-start = (bf16[256,1024]{1,0:T(8,128)(2,1)}, bf16[256,1024]{1,0:T(8,128)(2,1)S(1)}, u32[]{:S(2)}, u32[]{:S(2)}) collective-permute-start(bf16[256,1024]{1,0:T(8,128)(2,1)} %bitcast.67), channel_id=1, source_target_pairs={{0,32},{8,40},{16,48},{24,56},{32,64},{40,72},{48,80},{56,88},{64,... | collective-permute-start | bytes 1572872 | tf_op jit(solution)/shard_map/ppermute | solution.py:210
  27.4 14.3 %collective-permute-start.1 = (bf16[256,1024]{1,0:T(8,128)(2,1)}, bf16[256,1024]{1,0:T(8,128)(2,1)S(1)}, u32[]{:S(2)}, u32[]{:S(2)}) collective-permute-start(bf16[256,1024]{1,0:T(8,128)(2,1)} %bitcast.68), channel_id=1, source_target_pairs={{0,24},{8,32},{16,40},{24,48},{32,56},{40,64},{48,72},{56,80},{64,... | collective-permute-start | bytes 1572872 | tf_op jit(solution)/shard_map/ppermute | solution.py:210
  30.5 23.9 %collective-permute-start.2 = (bf16[256,1024]{1,0:T(8,128)(2,1)}, bf16[256,1024]{1,0:T(8,128)(2,1)S(1)}, u32[]{:S(2)}, u32[]{:S(2)}) collective-permute-start(bf16[256,1024]{1,0:T(8,128)(2,1)} %bitcast.69), channel_id=1, source_target_pairs={{0,16},{8,24},{16,32},{24,40},{32,48},{40,56},{48,64},{56,72},{64,... | collective-permute-start | bytes 1572872 | tf_op jit(solution)/shard_map/ppermute | solution.py:210
  33.2 22.5 %collective-permute-start.3 = (bf16[256,1024]{1,0:T(8,128)(2,1)}, bf16[256,1024]{1,0:T(8,128)(2,1)S(1)}, u32[]{:S(2)}, u32[]{:S(2)}) collective-permute-start(bf16[256,1024]{1,0:T(8,128)(2,1)} %bitcast.70), channel_id=1, source_target_pairs={{0,8},{8,16},{16,24},{24,32},{32,40},{40,48},{48,56},{56,64},{64,7... | collective-permute-start | bytes 1572872 | tf_op jit(solution)/shard_map/ppermute | solution.py:210
  55.9 1.5 copy-start.5
  98.3 145.9 %collective-permute-start.8 = (bf16[8,336,1024]{2,1,0:T(8,128)(2,1)}, bf16[8,336,1024]{2,1,0:T(8,128)(2,1)}, u32[]{:S(2)}, u32[]{:S(2)}) collective-permute-start(bf16[8,336,1024]{2,1,0:T(8,128)(2,1)} %bitcast.64), channel_id=1, source_target_pairs={{0,8},{8,0},{16,24},{24,16},{32,40},{40,32},{48,56},{56,48},{64,72... | collective-permute-start | bytes 16515080 | tf_op jit(solution)/shard_map/ppermute | solution.py:257
  109.1 143.6 %all-to-all-start = ((bf16[8,256,16,42]{1,2,3,0:T(8,128)(2,1)}), bf16[8,256,16,42]{1,2,3,0:T(8,128)(2,1)}, u32[]{:S(2)}, u32[]{:S(2)}) async-start(bf16[8,256,16,42]{1,2,3,0:T(8,128)(2,1)} %copy.25), calls=%async_computation | async-start | bytes 5505024 | tf_op jit(solution)/shard_map/all_to_all | solution.py:236
  118.6 39.9 %collective-permute-start.17 = (bf16[256,1024]{1,0:T(8,128)(2,1)S(1)}, bf16[256,1024]{1,0:T(8,128)(2,1)S(1)}, u32[]{:S(2)}, u32[]{:S(2)}) collective-permute-start(bf16[256,1024]{1,0:T(8,128)(2,1)S(1)} %get-tuple-element.25), channel_id=1, source_target_pairs={{8,0},{16,8},{24,16},{32,24},{40,32},{48,40},{56,48},{64,56},{72,6... | collective-permute-start | bytes 1572872 | tf_op jit(solution)/shard_map/ppermute | solution.py:210
  121.2 50.8 %collective-permute-start.18 = (bf16[256,1024]{1,0:T(8,128)(2,1)S(1)}, bf16[256,1024]{1,0:T(8,128)(2,1)S(1)}, u32[]{:S(2)}, u32[]{:S(2)}) collective-permute-start(bf16[256,1024]{1,0:T(8,128)(2,1)S(1)} %get-tuple-element.28), channel_id=1, source_target_pairs={{16,0},{24,8},{32,16},{40,24},{48,32},{56,40},{64,48},{72,56},{80,... | collective-permute-start | bytes 1572872 | tf_op jit(solution)/shard_map/ppermute | solution.py:210
  123.2 48.8 %collective-permute-start.19 = (bf16[256,1024]{1,0:T(8,128)(2,1)S(1)}, bf16[256,1024]{1,0:T(8,128)(2,1)S(1)}, u32[]{:S(2)}, u32[]{:S(2)}) collective-permute-start(bf16[256,1024]{1,0:T(8,128)(2,1)S(1)} %get-tuple-element.27), channel_id=1, source_target_pairs={{24,0},{32,8},{40,16},{48,24},{56,32},{64,40},{72,48},{80,56},{88,... | collective-permute-start | bytes 1572872 | tf_op jit(solution)/shard_map/ppermute | solution.py:210
  124.5 47.5 %collective-permute-start.20 = (bf16[256,1024]{1,0:T(8,128)(2,1)S(1)}, bf16[256,1024]{1,0:T(8,128)(2,1)S(1)}, u32[]{:S(2)}, u32[]{:S(2)}) collective-permute-start(bf16[256,1024]{1,0:T(8,128)(2,1)S(1)} %get-tuple-element.26), channel_id=1, source_target_pairs={{32,0},{40,8},{48,16},{56,24},{64,32},{72,40},{80,48},{88,56},{96,... | collective-permute-start | bytes 1572872 | tf_op jit(solution)/shard_map/ppermute | solution.py:210
  248.8 21.3 %copy-start.2 = (bf16[256,1024]{1,0:T(8,128)(2,1)S(1)}, bf16[256,1024]{1,0:T(8,128)(2,1)}, u32[]{:S(2)}) copy-start(bf16[256,1024]{1,0:T(8,128)(2,1)} %add_convert_fusion.x_ref) | copy-start | bytes 1572868
  248.8 72.9 %collective-permute-start.9 = (bf16[256,1024]{1,0:T(8,128)(2,1)S(1)}, bf16[256,1024]{1,0:T(8,128)(2,1)S(1)}, u32[]{:S(2)}, u32[]{:S(2)}) collective-permute-start(bf16[256,1024]{1,0:T(8,128)(2,1)S(1)} %fusion.25), channel_id=1, source_target_pairs={{0,32},{8,40},{16,48},{24,56},{32,64},{40,72},{48,80},{56,88},{64,... | collective-permute-start | bytes 1572872 | tf_op jit(solution)/shard_map/ppermute | solution.py:210
  260.8 61.8 %collective-permute-start.10 = (bf16[256,1024]{1,0:T(8,128)(2,1)S(1)}, bf16[256,1024]{1,0:T(8,128)(2,1)}, u32[]{:S(2)}, u32[]{:S(2)}) collective-permute-start(bf16[256,1024]{1,0:T(8,128)(2,1)S(1)} %fusion.25), channel_id=1, source_target_pairs={{0,24},{8,32},{16,40},{24,48},{32,56},{40,64},{48,72},{56,80},{64,... | collective-permute-start | bytes 1572872 | tf_op jit(solution)/shard_map/ppermute | solution.py:210
  263.5 60.9 %collective-permute-start.11 = (bf16[256,1024]{1,0:T(8,128)(2,1)S(1)}, bf16[256,1024]{1,0:T(8,128)(2,1)}, u32[]{:S(2)}, u32[]{:S(2)}) collective-permute-start(bf16[256,1024]{1,0:T(8,128)(2,1)S(1)} %fusion.25), channel_id=1, source_target_pairs={{0,16},{8,24},{16,32},{24,40},{32,48},{40,56},{48,64},{56,72},{64,... | collective-permute-start | bytes 1572872 | tf_op jit(solution)/shard_map/ppermute | solution.py:210
  267.0 59.3 %collective-permute-start.12 = (bf16[256,1024]{1,0:T(8,128)(2,1)S(1)}, bf16[256,1024]{1,0:T(8,128)(2,1)}, u32[]{:S(2)}, u32[]{:S(2)}) collective-permute-start(bf16[256,1024]{1,0:T(8,128)(2,1)S(1)} %fusion.25), channel_id=1, source_target_pairs={{0,8},{8,16},{16,24},{24,32},{32,40},{40,48},{48,56},{56,64},{64,7... | collective-permute-start | bytes 1572872 | tf_op jit(solution)/shard_map/ppermute | solution.py:210
  355.9 25.3 %collective-permute-start.13 = (bf16[256,1024]{1,0:T(8,128)(2,1)}, bf16[256,1024]{1,0:T(8,128)(2,1)S(1)}, u32[]{:S(2)}, u32[]{:S(2)}) collective-permute-start(bf16[256,1024]{1,0:T(8,128)(2,1)} %get-tuple-element.29), channel_id=1, source_target_pairs={{8,0},{16,8},{24,16},{32,24},{40,32},{48,40},{56,48},{64,56},{72,6... | collective-permute-start | bytes 1572872 | tf_op jit(solution)/shard_map/ppermute | solution.py:210
  365.7 22.4 %collective-permute-start.14 = (bf16[256,1024]{1,0:T(8,128)(2,1)}, bf16[256,1024]{1,0:T(8,128)(2,1)S(1)}, u32[]{:S(2)}, u32[]{:S(2)}) collective-permute-start(bf16[256,1024]{1,0:T(8,128)(2,1)} %get-tuple-element.32), channel_id=1, source_target_pairs={{16,0},{24,8},{32,16},{40,24},{48,32},{56,40},{64,48},{72,56},{80,... | collective-permute-start | bytes 1572872 | tf_op jit(solution)/shard_map/ppermute | solution.py:210
  367.6 20.5 %collective-permute-start.15 = (bf16[256,1024]{1,0:T(8,128)(2,1)}, bf16[256,1024]{1,0:T(8,128)(2,1)S(1)}, u32[]{:S(2)}, u32[]{:S(2)}) collective-permute-start(bf16[256,1024]{1,0:T(8,128)(2,1)} %get-tuple-element.31), channel_id=1, source_target_pairs={{24,0},{32,8},{40,16},{48,24},{56,32},{64,40},{72,48},{80,56},{88,... | collective-permute-start | bytes 1572872 | tf_op jit(solution)/shard_map/ppermute | solution.py:210
  368.9 34.5 %collective-permute-start.16 = (bf16[256,1024]{1,0:T(8,128)(2,1)}, bf16[256,1024]{1,0:T(8,128)(2,1)}, u32[]{:S(2)}, u32[]{:S(2)}) collective-permute-start(bf16[256,1024]{1,0:T(8,128)(2,1)} %get-tuple-element.30), channel_id=1, source_target_pairs={{32,0},{40,8},{48,16},{56,24},{64,32},{72,40},{80,48},{88,56},{96,... | collective-permute-start | bytes 1572872 | tf_op jit(solution)/shard_map/ppermute | solution.py:210
  376.6 29.9 %copy-start.1 = (bf16[672,1024]{1,0:T(8,128)(2,1)S(1)}, bf16[672,1024]{1,0:T(8,128)(2,1)}, u32[]{:S(2)}) copy-start(bf16[672,1024]{1,0:T(8,128)(2,1)} %param.9) | copy-start | bytes 4128772
  381.2 24.7 %copy-start.3 = (f32[42,1024]{1,0:T(8,128)S(1)}, f32[42,1024]{1,0:T(8,128)}, u32[]{:S(2)}) copy-start(f32[42,1024]{1,0:T(8,128)} %shard_map.104) | copy-start | bytes 516100
Sparse Core Ops, SparseCore 0:
  10.9 87.3 all-gather.2

commit v4 on v3

--- a/solution.py
+++ b/solution.py
@@ -180,10 +180,10 @@
         copy.start()
         copies.append(copy)
     local.wait()
-    total = landed[0]
+    total = landed[0].astype(jnp.float32)
     for k in range(1, n):
         copies[k - 1].wait()
-        total = total + landed[k]
+        total = total + landed[k].astype(jnp.float32)
     o_ref[...] = total
 
 
@@ -191,7 +191,7 @@
     n = lax.axis_size(axis)
     return pl.pallas_call(
         functools.partial(peer_sum_kernel, axis, n),
-        out_shape=jax.ShapeDtypeStruct(x.shape[1:], x.dtype),
+        out_shape=jax.ShapeDtypeStruct(x.shape[1:], jnp.float32),
         in_specs=[pl.BlockSpec(memory_space=pl.ANY)],
         out_specs=pl.BlockSpec(memory_space=pltpu.VMEM),
         scratch_shapes=[
@@ -234,11 +234,12 @@
         tokens_in.reshape(shard_rows, n_ctx, n_fsdp, out_rows).transpose(2, 0, 1, 3)
     )
     token_cols = lax.all_to_all(token_cols, "fsdp", 0, 0, tiled=True)
-    segment_tags = own_segments.astype(jnp.bfloat16)
-    arrived = [shifted((own_keys, segment_tags), "ctx", hop) for hop in range(1, n_hops + 1)]
-    ordered = arrived[::-1] + [(own_keys, segment_tags)]
-    window_keys = jnp.concatenate([parcel[0] for parcel in ordered], 0)
-    window_tags = jnp.concatenate([parcel[1] for parcel in ordered], 0).astype(jnp.int32)
+    tag_columns = jnp.broadcast_to(own_segments.astype(jnp.bfloat16)[:, None], (shard_rows, HD))
+    parcel = jnp.concatenate([own_keys, tag_columns], 1)
+    arrived = [shifted(parcel, "ctx", hop) for hop in range(1, n_hops + 1)]
+    window_parcel = jnp.concatenate(arrived[::-1] + [parcel], 0)
+    window_keys = window_parcel[:, :kv_width]
+    window_tags = window_parcel[:, kv_width].astype(jnp.int32)
     first_query = lax.axis_index("ctx") * shard_rows
     key_pos = first_query - WINDOW + jnp.arange(span_rows, dtype=jnp.int32)
     key_tags = jnp.where(key_pos >= 0, window_tags, -1)
@@ -260,7 +261,7 @@
     weight_part = jnp.einsum(
         "ftcr,ftn->crn", token_cols, grads_all, preferred_element_type=jnp.float32
     )
-    d_weight = peer_sum_scatter(weight_part, "ctx", 3)
+    d_weight = peer_sum_scatter(weight_part.astype(jnp.bfloat16), "ctx", 3)
 
     values = (
         jnp.einsum("tfr,frn->tn", tokens_mine, w_mine, preferred_element_type=jnp.float32)

time: 416 us -> 401 us (0.964)
  Pallas kernels: 157 us -> 141 us
  waiting for transfers between devices: 108 us -> 121 us
  starting transfers between devices: 65.7 us -> 53.6 us
    pallas_call x1, Pallas kernels: 47.5 us -> 32.3 us  [peer_sum_scatter(): pl.pallas_call(functools.partial(peer_sum_kernel, axis, n), out_shape=jax...]
    ppermute x20 -> x16, starting transfers between devices: 57.8 us -> 45.7 us  [shifted(): return lax.ppermute(x, axis, pairs)]
    ppermute x20 -> x16, waiting for transfers between devices: 82.4 us -> 91.2 us  [shifted(): return lax.ppermute(x, axis, pairs)]
    unnamed x27 -> x23, local copies, waits for them, and re-layouts: 18 us -> 16.5 us
  transfers between devices with their start and end apart: 23 -> 19, of which waited for: 9 -> 9; matrix products, arithmetic and copies ran while one was open for 14% -> 14% of each run, Pallas kernels for 32% -> 29%
where the time goes in v4:
time: 401 us; the launch traced here: 399 us
  Pallas kernels  141 us (35%)
  waiting for transfers between devices  121 us (30%)
  starting transfers between devices  53.6 us (13%)
  local copies, waits for them, and re-layouts  34.7 us (9%)
  matrix products  25.8 us (6%)
  between operations  14.4 us (4%)
  other arithmetic  8.02 us (2%)
    ppermute x16, waiting for transfers between devices, shifted(): return lax.ppermute(x, axis, pairs)  91.2 us
    pallas_call x1, Pallas kernels, peer_gather(): pl.pallas_call(functools.partial(peer_gather_kernel, axis, n), out_shape=...  69.9 us
    ppermute x16, starting transfers between devices, shifted(): return lax.ppermute(x, axis, pairs)  45.7 us
    pallas_call x1, Pallas kernels, peer_sum_scatter(): pl.pallas_call(functools.partial(peer_sum_kernel, axis, n), out_shape=jax...  32.3 us
    all_gather x1, waiting for transfers between devices, shards(): lax.all_gather(lax.dynamic_slice_in_dim(w_value, core * half_rows, half_r...  29.5 us
    pallas_call x1, Pallas kernels, fused_attention(): pl.pallas_call(attention_kernel, grid=(heads,), in_specs=[q_spec, kv_spec...  24 us
    unnamed x23, local copies, waits for them, and re-layouts  16.5 us
    pallas_call x1, Pallas kernels, value_grads(): pl.pallas_call(value_grad_kernel, grid=(heads,), in_specs=[q_spec, kv_spe...  15.2 us
  transfers between devices with their start and end apart: 19, of which 9 were waited for; matrix products, arithmetic and copies ran while one was open for 14% of the time, Pallas kernels for 29%

profile of v4, /device:TPU:28, one launch (start us, length us, event | category | flops | bytes accessed | tf_op | source)
XLA Modules:
  0.0 398.5 jit_solution(6486457754203876704)
XLA Ops:
  11.4 3.9 collective-permute-start
  15.3 3.2 collective-permute-start.1
  18.4 3.2 collective-permute-start.2
  21.6 2.9 collective-permute-start.3
  25.4 3.6 collective-permute-done
  29.0 3.9 collective-permute-done.1
  33.0 15.7 %collective-permute-done.2 = bf16[256,1152]{1,0:T(8,128)(2,1)S(1)} collective-permute-done((bf16[256,1152]{1,0:T(8,128)(2,1)S(1)}, bf16[256,1152]{1,0:T(8,128)(2,1)S(1)}, u32[]{:S(2)}, u32[]{:S(2)}) %collective-permute-start.2) | collective-permute-done | bytes 589856 | tf_op jit(solution)/shard_map/ppermute | solution.py:210
  48.8 3.8 collective-permute-done.3
  55.4 15.2 %shard_map.101 = bf16[1280,1024]{1,0:T(8,128)(2,1)} custom-call(bf16[256,2048]{1,0:T(8,128)(2,1)} %bitcast.73, bf16[1280,1024]{1,0:T(8,128)(2,1)} %slice.48.k_ref, bf16[256,2048]{1,0:T(8,128)(2,1)} %bitcast.75, s32[256,1]{1,0:T(8,128)} %copy.21.qtag_ref, s32[1,1280]{1,0:T(1,128)} %compare_select_fusion.ktag_ref), custom_call_target="tpu_custom_call" | custom-call | flops 2684354560 | bytes 7340032 | tf_op jit(solution)/shard_map/pallas_call | solution.py:79
  70.6 29.5 %all-gather.3.cloned.1.call-done = bf16[2688,1024]{1,0:T(8,128)(2,1)} async-done(((bf16[336,1024]{1,0:T(8,128)(2,1)}), bf16[2688,1024]{1,0:T(8,128)(2,1)}) %all-gather.3.cloned.1.call-update) | async-done | bytes 5505040 | tf_op jit(solution)/shard_map/all_gather | solution.py:226
  100.1 3.3 copy.20
  105.8 5.0 %copy.25 = bf16[8,256,16,42]{1,2,3,0:T(8,128)(2,1)} copy(bf16[8,256,16,42]{1,3,0,2:T(8,128)(2,1)} %bitcast.65) | data formatting | bytes 5505024 | tf_op jit(solution)/shard_map/transpose | solution.py:234
  110.8 7.9 %all-to-all-start = ((bf16[8,256,16,42]{1,2,3,0:T(8,128)(2,1)}), bf16[8,256,16,42]{1,2,3,0:T(8,128)(2,1)}, u32[]{:S(2)}, u32[]{:S(2)}) async-start(bf16[8,256,16,42]{1,2,3,0:T(8,128)(2,1)} %copy.25), calls=%async_computation | async-start | bytes 5505024 | tf_op jit(solution)/shard_map/all_to_all | solution.py:236
  127.5 5.2 %fusion.20 = f32[256,1024]{1,0:T(8,128)} fusion(bf16[8,336,1024]{2,1,0:T(8,128)(2,1)} %bitcast.68, bf16[256,8,2,336]{0,3,2,1:T(8,128)(2,1)S(1)} %bitcast.63, s32[]{:T(128)S(6)} %select_n.47), kind=kOutput, calls=%fused_computation.16 | convolution fusion | flops 1409286144 | bytes 7929860 | tf_op jit(solution)/shard_map/tfr,frn->tn/dot_general | solution.py:267
  132.7 27.5 %collective-permute-done.13 = bf16[256,1024]{1,0:T(8,128)(2,1)S(1)} collective-permute-done((bf16[256,1024]{1,0:T(8,128)(2,1)S(1)}, bf16[256,1024]{1,0:T(8,128)(2,1)S(1)}, u32[]{:S(2)}, u32[]{:S(2)}) %collective-permute-start.13) | collective-permute-done | bytes 524320 | tf_op jit(solution)/shard_map/ppermute | solution.py:210
  160.2 13.5 %collective-permute-done.14 = bf16[256,1024]{1,0:T(8,128)(2,1)S(1)} collective-permute-done((bf16[256,1024]{1,0:T(8,128)(2,1)S(1)}, bf16[256,1024]{1,0:T(8,128)(2,1)S(1)}, u32[]{:S(2)}, u32[]{:S(2)}) %collective-permute-start.14) | collective-permute-done | bytes 524320 | tf_op jit(solution)/shard_map/ppermute | solution.py:210
  176.0 69.9 %shard_map.103 = bf16[8,256,1024]{2,1,0:T(8,128)(2,1)} custom-call(bf16[256,1024]{1,0:T(8,128)(2,1)} %add_convert_fusion.x_ref), custom_call_target="tpu_custom_call" | custom-call | tf_op jit(solution)/shard_map/pallas_call | solution.py:145
  246.0 4.5 %fusion.29 = bf16[256,1024]{1,0:T(8,128)(2,1)S(1)} fusion(f32[256,1024]{1,0:T(8,128)} %fusion.20, bf16[8,336,1024]{2,1,0:T(8,128)(2,1)} %collective-permute-done.4, bf16[256,8,2,336]{0,3,2,1:T(8,128)(2,1)S(1)} %bitcast.64, s32[]{:T(128)S(6)} %select_n.50), kind=kOutput, calls=%fused_computation.19 | convolution fusion | flops 1409810432 | bytes 8454148 | tf_op jit(solution)/shard_map/tfr,frn->tn/dot_general | solution.py:268
  250.5 3.8 collective-permute-start.5
  254.3 7.7 %fusion.7.x_ref = bf16[16,42,1024]{2,1,0:T(8,128)(2,1)} fusion(bf16[8,256,16,42]{1,2,3,0:T(8,128)(2,1)} %all-to-all-done, bf16[8,256,1024]{2,1,0:T(8,128)(2,1)} %shard_map.103), kind=kOutput, calls=%fused_computation.7 | convolution fusion | flops 2819260416 | bytes 8323072 | tf_op jit(solution)/shard_map/ftcr,ftn->crn/dot_general | solution.py:261
  262.0 2.7 collective-permute-start.6
  264.8 3.5 collective-permute-start.7
  268.3 3.0 collective-permute-start.8
  271.3 4.2 %fusion.12 = bf16[256,8,1,336]{0,3,1,2:T(8,128)(2,1)S(1)} fusion(bf16[8,336,1024]{2,1,0:T(8,128)(2,1)} %bitcast.69, bf16[256,1024]{1,0:T(8,128)(2,1)S(1)} %copy-done.3), kind=kOutput, calls=%fused_computation.8 | convolution fusion | flops 1409974272 | bytes 7405568 | tf_op jit(solution)/shard_map/tn,frn->tfr/dot_general | solution.py:276
  275.5 32.3 %shard_map.104 = f32[42,1024]{1,0:T(8,128)} custom-call(bf16[16,42,1024]{2,1,0:T(8,128)(2,1)} %fusion.7.x_ref), custom_call_target="tpu_custom_call" | custom-call | tf_op jit(solution)/shard_map/pallas_call | solution.py:192
  315.0 24.0 %shard_map.102 = (bf16[256,2048]{1,0:T(8,128)(2,1)}, bf16[256,2048]{1,0:T(8,128)(2,1)}, bf16[1280,1024]{1,0:T(8,128)(2,1)}) custom-call(bf16[256,2048]{1,0:T(8,128)(2,1)} %bitcast.74, bf16[1280,1024]{1,0:T(8,128)(2,1)} %slice.48.k_ref, bf16[1280,1024]{1,0:T(8,128)(2,1)} %constant_dynamic-update-slice_fusion.5.v_ref, bf16[256,2048]{1,0:T(8,128)(2,1)} %bitcast.76, ...), custom_call_target="tpu_custom_call" | custom-call | flops 6710886400 | bytes 12058624 | tf_op jit(solution)/shard_map/pallas_call | solution.py:98
  339.0 2.9 fusion.38
  341.9 7.7 %collective-permute-start.10 = (bf16[256,1024]{1,0:T(8,128)(2,1)}, bf16[256,1024]{1,0:T(8,128)(2,1)S(1)}, u32[]{:S(2)}, u32[]{:S(2)}) collective-permute-start(bf16[256,1024]{1,0:T(8,128)(2,1)} %get-tuple-element.32), channel_id=1, source_target_pairs={{16,0},{24,8},{32,16},{40,24},{48,32},{56,40},{64,48},{72,56},{80,... | collective-permute-start | bytes 1572872 | tf_op jit(solution)/shard_map/ppermute | solution.py:210
  354.4 4.2 %fusion.13 = bf16[256,8,1,336]{0,3,1,2:T(8,128)(2,1)S(1)} fusion(bf16[8,336,1024]{2,1,0:T(8,128)(2,1)} %collective-permute-done.4, bf16[256,1024]{1,0:T(8,128)(2,1)S(1)} %copy-done.3), kind=kOutput, calls=%fused_computation.9 | convolution fusion | flops 1409974272 | bytes 7405568 | tf_op jit(solution)/shard_map/tn,frn->tfr/dot_general | solution.py:277
  360.8 4.6 %copy.27 = bf16[1,256,5376]{2,1,0:T(8,128)(2,1)} copy(bf16[1,256,5376]{1,2,0:T(8,128)(2,1)} %bitcast.66) | data formatting | bytes 5505024
  365.4 6.4 %collective-permute-done.11 = bf16[256,1024]{1,0:T(8,128)(2,1)S(1)} collective-permute-done((bf16[256,1024]{1,0:T(8,128)(2,1)}, bf16[256,1024]{1,0:T(8,128)(2,1)S(1)}, u32[]{:S(2)}, u32[]{:S(2)}) %collective-permute-start.11) | collective-permute-done | bytes 524320 | tf_op jit(solution)/shard_map/ppermute | solution.py:210
  371.8 16.7 %collective-permute-done.12 = bf16[256,1024]{1,0:T(8,128)(2,1)S(1)} collective-permute-done((bf16[256,1024]{1,0:T(8,128)(2,1)}, bf16[256,1024]{1,0:T(8,128)(2,1)S(1)}, u32[]{:S(2)}, u32[]{:S(2)}) %collective-permute-start.12) | collective-permute-done | bytes 524320 | tf_op jit(solution)/shard_map/ppermute | solution.py:210
  (57 shorter events, 38.9 us)
Async XLA Ops:
  7.2 1.3 copy-start
  7.2 17.4 %copy-start.5 = (s32[1,256]{1,0:T(1,128)S(1)}, s32[1,256]{1,0:T(1,128)}, u32[]{:S(2)}) copy-start(s32[1,256]{1,0:T(1,128)} %param.11) | copy-start | bytes 3076
  7.2 92.9 %all-gather.3.cloned.1.call-start = ((), (), s32[]{:S(2)}) async-start(), calls=%async_computation.1 | async-start | bytes 6193152 | tf_op jit(solution)/shard_map/all_gather | solution.py:226
  10.2 42.4 %copy-start.2 = (bf16[1,256,1024]{2,1,0:T(8,128)(2,1)S(1)}, bf16[1,256,1024]{2,1,0:T(8,128)(2,1)}, u32[]{:S(2)}) copy-start(bf16[1,256,1024]{2,1,0:T(8,128)(2,1)} %param.8) | copy-start | bytes 1572868
  11.4 17.5 %collective-permute-start = (bf16[256,1152]{1,0:T(8,128)(2,1)S(1)}, bf16[256,1152]{1,0:T(8,128)(2,1)S(1)}, u32[]{:S(2)}, u32[]{:S(2)}) collective-permute-start(bf16[256,1152]{1,0:T(8,128)(2,1)S(1)} %pad_maximum_fusion), channel_id=1, source_target_pairs={{0,32},{8,40},{16,48},{24,56},{32,64},{40,72},{48,80},{56,88},{64,... | collective-permute-start | bytes 1769480 | tf_op jit(solution)/shard_map/ppermute | solution.py:210
  15.3 17.6 %collective-permute-start.1 = (bf16[256,1152]{1,0:T(8,128)(2,1)S(1)}, bf16[256,1152]{1,0:T(8,128)(2,1)S(1)}, u32[]{:S(2)}, u32[]{:S(2)}) collective-permute-start(bf16[256,1152]{1,0:T(8,128)(2,1)S(1)} %pad_maximum_fusion), channel_id=1, source_target_pairs={{0,24},{8,32},{16,40},{24,48},{32,56},{40,64},{48,72},{56,80},{64,... | collective-permute-start | bytes 1769480 | tf_op jit(solution)/shard_map/ppermute | solution.py:210
  18.4 30.2 %collective-permute-start.2 = (bf16[256,1152]{1,0:T(8,128)(2,1)S(1)}, bf16[256,1152]{1,0:T(8,128)(2,1)S(1)}, u32[]{:S(2)}, u32[]{:S(2)}) collective-permute-start(bf16[256,1152]{1,0:T(8,128)(2,1)S(1)} %pad_maximum_fusion), channel_id=1, source_target_pairs={{0,16},{8,24},{16,32},{24,40},{32,48},{40,56},{48,64},{56,72},{64,... | collective-permute-start | bytes 1769480 | tf_op jit(solution)/shard_map/ppermute | solution.py:210
  21.6 30.9 %collective-permute-start.3 = (bf16[256,1152]{1,0:T(8,128)(2,1)S(1)}, bf16[256,1152]{1,0:T(8,128)(2,1)S(1)}, u32[]{:S(2)}, u32[]{:S(2)}) collective-permute-start(bf16[256,1152]{1,0:T(8,128)(2,1)S(1)} %pad_maximum_fusion), channel_id=1, source_target_pairs={{0,8},{8,16},{16,24},{24,32},{32,40},{40,48},{48,56},{56,64},{64,7... | collective-permute-start | bytes 1769480 | tf_op jit(solution)/shard_map/ppermute | solution.py:210
  100.1 145.9 %collective-permute-start.4 = (bf16[8,336,1024]{2,1,0:T(8,128)(2,1)}, bf16[8,336,1024]{2,1,0:T(8,128)(2,1)}, u32[]{:S(2)}, u32[]{:S(2)}) collective-permute-start(bf16[8,336,1024]{2,1,0:T(8,128)(2,1)} %bitcast.67), channel_id=1, source_target_pairs={{0,8},{8,0},{16,24},{24,16},{32,40},{40,32},{48,56},{56,48},{64,72... | collective-permute-start | bytes 16515080 | tf_op jit(solution)/shard_map/ppermute | solution.py:258
  110.8 143.5 %all-to-all-start = ((bf16[8,256,16,42]{1,2,3,0:T(8,128)(2,1)}), bf16[8,256,16,42]{1,2,3,0:T(8,128)(2,1)}, u32[]{:S(2)}, u32[]{:S(2)}) async-start(bf16[8,256,16,42]{1,2,3,0:T(8,128)(2,1)} %copy.25), calls=%async_computation | async-start | bytes 5505024 | tf_op jit(solution)/shard_map/all_to_all | solution.py:236
  120.4 39.9 %collective-permute-start.13 = (bf16[256,1024]{1,0:T(8,128)(2,1)S(1)}, bf16[256,1024]{1,0:T(8,128)(2,1)S(1)}, u32[]{:S(2)}, u32[]{:S(2)}) collective-permute-start(bf16[256,1024]{1,0:T(8,128)(2,1)S(1)} %get-tuple-element.25), channel_id=1, source_target_pairs={{8,0},{16,8},{24,16},{32,24},{40,32},{48,40},{56,48},{64,56},{72,6... | collective-permute-start | bytes 1572872 | tf_op jit(solution)/shard_map/ppermute | solution.py:210
  123.0 50.8 %collective-permute-start.14 = (bf16[256,1024]{1,0:T(8,128)(2,1)S(1)}, bf16[256,1024]{1,0:T(8,128)(2,1)S(1)}, u32[]{:S(2)}, u32[]{:S(2)}) collective-permute-start(bf16[256,1024]{1,0:T(8,128)(2,1)S(1)} %get-tuple-element.28), channel_id=1, source_target_pairs={{16,0},{24,8},{32,16},{40,24},{48,32},{56,40},{64,48},{72,56},{80,... | collective-permute-start | bytes 1572872 | tf_op jit(solution)/shard_map/ppermute | solution.py:210
  124.9 48.8 %collective-permute-start.15 = (bf16[256,1024]{1,0:T(8,128)(2,1)S(1)}, bf16[256,1024]{1,0:T(8,128)(2,1)S(1)}, u32[]{:S(2)}, u32[]{:S(2)}) collective-permute-start(bf16[256,1024]{1,0:T(8,128)(2,1)S(1)} %get-tuple-element.27), channel_id=1, source_target_pairs={{24,0},{32,8},{40,16},{48,24},{56,32},{64,40},{72,48},{80,56},{88,... | collective-permute-start | bytes 1572872 | tf_op jit(solution)/shard_map/ppermute | solution.py:210
  126.2 47.5 %collective-permute-start.16 = (bf16[256,1024]{1,0:T(8,128)(2,1)S(1)}, bf16[256,1024]{1,0:T(8,128)(2,1)S(1)}, u32[]{:S(2)}, u32[]{:S(2)}) collective-permute-start(bf16[256,1024]{1,0:T(8,128)(2,1)S(1)} %get-tuple-element.26), channel_id=1, source_target_pairs={{32,0},{40,8},{48,16},{56,24},{64,32},{72,40},{80,48},{88,56},{96,... | collective-permute-start | bytes 1572872 | tf_op jit(solution)/shard_map/ppermute | solution.py:210
  250.5 20.8 %copy-start.3 = (bf16[256,1024]{1,0:T(8,128)(2,1)S(1)}, bf16[256,1024]{1,0:T(8,128)(2,1)}, u32[]{:S(2)}) copy-start(bf16[256,1024]{1,0:T(8,128)(2,1)} %add_convert_fusion.x_ref) | copy-start | bytes 1572868
  250.5 57.2 %collective-permute-start.5 = (bf16[256,1024]{1,0:T(8,128)(2,1)S(1)}, bf16[256,1024]{1,0:T(8,128)(2,1)S(1)}, u32[]{:S(2)}, u32[]{:S(2)}) collective-permute-start(bf16[256,1024]{1,0:T(8,128)(2,1)S(1)} %fusion.29), channel_id=1, source_target_pairs={{0,32},{8,40},{16,48},{24,56},{32,64},{40,72},{48,80},{56,88},{64,... | collective-permute-start | bytes 1572872 | tf_op jit(solution)/shard_map/ppermute | solution.py:210
  262.0 46.6 %collective-permute-start.6 = (bf16[256,1024]{1,0:T(8,128)(2,1)S(1)}, bf16[256,1024]{1,0:T(8,128)(2,1)}, u32[]{:S(2)}, u32[]{:S(2)}) collective-permute-start(bf16[256,1024]{1,0:T(8,128)(2,1)S(1)} %fusion.29), channel_id=1, source_target_pairs={{0,24},{8,32},{16,40},{24,48},{32,56},{40,64},{48,72},{56,80},{64,... | collective-permute-start | bytes 1572872 | tf_op jit(solution)/shard_map/ppermute | solution.py:210
  264.8 45.7 %collective-permute-start.7 = (bf16[256,1024]{1,0:T(8,128)(2,1)S(1)}, bf16[256,1024]{1,0:T(8,128)(2,1)}, u32[]{:S(2)}, u32[]{:S(2)}) collective-permute-start(bf16[256,1024]{1,0:T(8,128)(2,1)S(1)} %fusion.29), channel_id=1, source_target_pairs={{0,16},{8,24},{16,32},{24,40},{32,48},{40,56},{48,64},{56,72},{64,... | collective-permute-start | bytes 1572872 | tf_op jit(solution)/shard_map/ppermute | solution.py:210
  268.3 44.1 %collective-permute-start.8 = (bf16[256,1024]{1,0:T(8,128)(2,1)S(1)}, bf16[256,1024]{1,0:T(8,128)(2,1)}, u32[]{:S(2)}, u32[]{:S(2)}) collective-permute-start(bf16[256,1024]{1,0:T(8,128)(2,1)S(1)} %fusion.29), channel_id=1, source_target_pairs={{0,8},{8,16},{16,24},{24,32},{32,40},{40,48},{48,56},{56,64},{64,7... | collective-permute-start | bytes 1572872 | tf_op jit(solution)/shard_map/ppermute | solution.py:210
  341.9 23.5 %collective-permute-start.10 = (bf16[256,1024]{1,0:T(8,128)(2,1)}, bf16[256,1024]{1,0:T(8,128)(2,1)S(1)}, u32[]{:S(2)}, u32[]{:S(2)}) collective-permute-start(bf16[256,1024]{1,0:T(8,128)(2,1)} %get-tuple-element.32), channel_id=1, source_target_pairs={{16,0},{24,8},{32,16},{40,24},{48,32},{56,40},{64,48},{72,56},{80,... | collective-permute-start | bytes 1572872 | tf_op jit(solution)/shard_map/ppermute | solution.py:210
  349.6 22.2 %collective-permute-start.11 = (bf16[256,1024]{1,0:T(8,128)(2,1)}, bf16[256,1024]{1,0:T(8,128)(2,1)S(1)}, u32[]{:S(2)}, u32[]{:S(2)}) collective-permute-start(bf16[256,1024]{1,0:T(8,128)(2,1)} %get-tuple-element.31), channel_id=1, source_target_pairs={{24,0},{32,8},{40,16},{48,24},{56,32},{64,40},{72,48},{80,56},{88,... | collective-permute-start | bytes 1572872 | tf_op jit(solution)/shard_map/ppermute | solution.py:210
  350.9 37.6 %collective-permute-start.12 = (bf16[256,1024]{1,0:T(8,128)(2,1)}, bf16[256,1024]{1,0:T(8,128)(2,1)S(1)}, u32[]{:S(2)}, u32[]{:S(2)}) collective-permute-start(bf16[256,1024]{1,0:T(8,128)(2,1)} %get-tuple-element.30), channel_id=1, source_target_pairs={{32,0},{40,8},{48,16},{56,24},{64,32},{72,40},{80,48},{88,56},{96,... | collective-permute-start | bytes 1572872 | tf_op jit(solution)/shard_map/ppermute | solution.py:210
  352.2 36.3 %collective-permute-start.9 = (bf16[256,1024]{1,0:T(8,128)(2,1)}, bf16[256,1024]{1,0:T(8,128)(2,1)}, u32[]{:S(2)}, u32[]{:S(2)}) collective-permute-start(bf16[256,1024]{1,0:T(8,128)(2,1)} %get-tuple-element.29), channel_id=1, source_target_pairs={{8,0},{16,8},{24,16},{32,24},{40,32},{48,40},{56,48},{64,56},{72,6... | collective-permute-start | bytes 1572872 | tf_op jit(solution)/shard_map/ppermute | solution.py:210
  360.8 30.9 %copy-start.1 = (bf16[672,1024]{1,0:T(8,128)(2,1)S(1)}, bf16[672,1024]{1,0:T(8,128)(2,1)}, u32[]{:S(2)}) copy-start(bf16[672,1024]{1,0:T(8,128)(2,1)} %param.9) | copy-start | bytes 4128772
  365.4 25.6 %copy-start.4 = (f32[42,1024]{1,0:T(8,128)S(1)}, f32[42,1024]{1,0:T(8,128)}, u32[]{:S(2)}) copy-start(f32[42,1024]{1,0:T(8,128)} %shard_map.104) | copy-start | bytes 516100
Sparse Core Ops, SparseCore 0:
  10.9 89.1 all-gather.2

commit v5 on v4

--- a/solution.py
+++ b/solution.py
@@ -254,9 +254,9 @@
         return total.astype(jnp.bfloat16)
 
     value_terms = value_grads(queries[0], window_keys, d_out[0], query_tags, key_tags[None, :])
-    w_mine, value_terms = lax.optimization_barrier((w_mine, value_terms))
+    d_values_low = returned_sum(value_terms)
+    w_mine, _ = lax.optimization_barrier((w_mine, d_values_low))
     w_other = lax.ppermute(w_mine, "ctx", [(i, i ^ 1) for i in range(n_ctx)])
-    d_values_low = returned_sum(value_terms)
     grads_all = peer_gather(d_values_low, "fsdp", 2)
     weight_part = jnp.einsum(
         "ftcr,ftn->crn", token_cols, grads_all, preferred_element_type=jnp.float32

time: 401 us -> 415 us (1.035)
  Pallas kernels: 141 us -> 167 us
  waiting for transfers between devices: 121 us -> 108 us
  starting transfers between devices: 53.6 us -> 59.9 us
    pallas_call x1, Pallas kernels: 69.9 us -> 106 us  [peer_gather(): pl.pallas_call(functools.partial(peer_gather_kernel, axis, n), out_shape=...]
    all_gather x1, waiting for transfers between devices: 29.5 us -> 0.01 us  [shards(): lax.all_gather(lax.dynamic_slice_in_dim(w_value, core * half_rows, half_r...]
    ppermute x16, waiting for transfers between devices: 91.2 us -> 108 us  [shifted(): return lax.ppermute(x, axis, pairs)]
    pallas_call x1, Pallas kernels: 32.3 us -> 21.6 us  [peer_sum_scatter(): pl.pallas_call(functools.partial(peer_sum_kernel, axis, n), out_shape=jax...]
    ppermute x16, starting transfers between devices: 45.7 us -> 52.7 us  [shifted(): return lax.ppermute(x, axis, pairs)]
  transfers between devices with their start and end apart: 19 -> 19, of which waited for: 9 -> 13; matrix products, arithmetic and copies ran while one was open for 14% -> 13% of each run, Pallas kernels for 29% -> 35%
where the time goes in v5:
time: 415 us; the launch traced here: 414 us
  Pallas kernels  167 us (40%)
  waiting for transfers between devices  108 us (26%)
  starting transfers between devices  59.9 us (14%)
  local copies, waits for them, and re-layouts  31.6 us (8%)
  matrix products  24.6 us (6%)
  between operations  14.4 us (3%)
  other arithmetic  8.02 us (2%)
    ppermute x16, waiting for transfers between devices, shifted(): return lax.ppermute(x, axis, pairs)  108 us
    pallas_call x1, Pallas kernels, peer_gather(): pl.pallas_call(functools.partial(peer_gather_kernel, axis, n), out_shape=...  106 us
    ppermute x16, starting transfers between devices, shifted(): return lax.ppermute(x, axis, pairs)  52.7 us
    pallas_call x1, Pallas kernels, fused_attention(): pl.pallas_call(attention_kernel, grid=(heads,), in_specs=[q_spec, kv_spec...  24 us
    pallas_call x1, Pallas kernels, peer_sum_scatter(): pl.pallas_call(functools.partial(peer_sum_kernel, axis, n), out_shape=jax...  21.6 us
    pallas_call x1, Pallas kernels, value_grads(): pl.pallas_call(value_grad_kernel, grid=(heads,), in_specs=[q_spec, kv_spe...  15.1 us
    unnamed x23, local copies, waits for them, and re-layouts  13.4 us
  transfers between devices with their start and end apart: 19, of which 13 were waited for; matrix products, arithmetic and copies ran while one was open for 13% of the time, Pallas kernels for 35%

profile of v5, /device:TPU:28, one launch (start us, length us, event | category | flops | bytes accessed | tf_op | source)
XLA Modules:
  0.0 413.6 jit_solution(3250297839766875179)
XLA Ops:
  11.4 3.9 collective-permute-start
  15.3 3.2 collective-permute-start.1
  18.4 3.2 collective-permute-start.2
  21.6 2.9 collective-permute-start.3
  25.4 3.6 collective-permute-done
  29.0 3.9 collective-permute-done.1
  33.0 15.7 %collective-permute-done.2 = bf16[256,1152]{1,0:T(8,128)(2,1)S(1)} collective-permute-done((bf16[256,1152]{1,0:T(8,128)(2,1)S(1)}, bf16[256,1152]{1,0:T(8,128)(2,1)S(1)}, u32[]{:S(2)}, u32[]{:S(2)}) %collective-permute-start.2) | collective-permute-done | bytes 589856 | tf_op jit(solution)/shard_map/ppermute | solution.py:210
  48.8 3.8 collective-permute-done.3
  55.4 15.1 %shard_map.101 = bf16[1280,1024]{1,0:T(8,128)(2,1)} custom-call(bf16[256,2048]{1,0:T(8,128)(2,1)} %bitcast.73, bf16[1280,1024]{1,0:T(8,128)(2,1)} %slice.48.k_ref, bf16[256,2048]{1,0:T(8,128)(2,1)} %bitcast.75, s32[256,1]{1,0:T(8,128)} %copy.21.qtag_ref, s32[1,1280]{1,0:T(1,128)} %compare_select_fusion.ktag_ref), custom_call_target="tpu_custom_call" | custom-call | flops 2684354560 | bytes 7340032 | tf_op jit(solution)/shard_map/pallas_call | solution.py:79
  72.2 9.4 %collective-permute-start.4 = (bf16[256,1024]{1,0:T(8,128)(2,1)S(1)}, bf16[256,1024]{1,0:T(8,128)(2,1)S(1)}, u32[]{:S(2)}, u32[]{:S(2)}) collective-permute-start(bf16[256,1024]{1,0:T(8,128)(2,1)S(1)} %get-tuple-element.27), channel_id=1, source_target_pairs={{8,0},{16,8},{24,16},{32,24},{40,32},{48,40},{56,48},{64,56},{72,6... | collective-permute-start | bytes 1572872 | tf_op jit(solution)/shard_map/ppermute | solution.py:210
  86.2 10.7 %collective-permute-done.4 = bf16[256,1024]{1,0:T(8,128)(2,1)S(1)} collective-permute-done((bf16[256,1024]{1,0:T(8,128)(2,1)S(1)}, bf16[256,1024]{1,0:T(8,128)(2,1)S(1)}, u32[]{:S(2)}, u32[]{:S(2)}) %collective-permute-start.4) | collective-permute-done | bytes 524320 | tf_op jit(solution)/shard_map/ppermute | solution.py:210
  96.9 13.4 %collective-permute-done.5 = bf16[256,1024]{1,0:T(8,128)(2,1)S(1)} collective-permute-done((bf16[256,1024]{1,0:T(8,128)(2,1)S(1)}, bf16[256,1024]{1,0:T(8,128)(2,1)S(1)}, u32[]{:S(2)}, u32[]{:S(2)}) %collective-permute-start.5) | collective-permute-done | bytes 524320 | tf_op jit(solution)/shard_map/ppermute | solution.py:210
  110.9 16.2 %collective-permute-done.7 = bf16[256,1024]{1,0:T(8,128)(2,1)S(1)} collective-permute-done((bf16[256,1024]{1,0:T(8,128)(2,1)S(1)}, bf16[256,1024]{1,0:T(8,128)(2,1)S(1)}, u32[]{:S(2)}, u32[]{:S(2)}) %collective-permute-start.7) | collective-permute-done | bytes 524320 | tf_op jit(solution)/shard_map/ppermute | solution.py:210
  129.5 3.3 copy.20
  135.3 5.0 %copy.25 = bf16[8,256,16,42]{1,2,3,0:T(8,128)(2,1)} copy(bf16[8,256,16,42]{1,3,0,2:T(8,128)(2,1)} %bitcast.65) | data formatting | bytes 5505024 | tf_op jit(solution)/shard_map/transpose | solution.py:234
  140.2 7.2 %all-to-all-start = ((bf16[8,256,16,42]{1,2,3,0:T(8,128)(2,1)}), bf16[8,256,16,42]{1,2,3,0:T(8,128)(2,1)}, u32[]{:S(2)}, u32[]{:S(2)}) async-start(bf16[8,256,16,42]{1,2,3,0:T(8,128)(2,1)} %copy.25), calls=%async_computation | async-start | bytes 5505024 | tf_op jit(solution)/shard_map/all_to_all | solution.py:236
  147.4 106.2 %shard_map.103 = bf16[8,256,1024]{2,1,0:T(8,128)(2,1)} custom-call(bf16[256,1024]{1,0:T(8,128)(2,1)} %add_convert_fusion.1.x_ref), custom_call_target="tpu_custom_call" | custom-call | tf_op jit(solution)/shard_map/pallas_call | solution.py:145
  253.6 4.2 %fusion.20 = f32[256,1024]{1,0:T(8,128)S(1)} fusion(bf16[8,336,1024]{2,1,0:T(8,128)(2,1)} %bitcast.68, bf16[256,8,2,336]{0,3,2,1:T(8,128)(2,1)S(1)} %bitcast.63, s32[]{:T(128)S(6)} %select_n.47), kind=kOutput, calls=%fused_computation.16 | convolution fusion | flops 1409286144 | bytes 7929860 | tf_op jit(solution)/shard_map/tfr,frn->tn/dot_general | solution.py:267
  257.9 4.3 %fusion.29 = bf16[256,1024]{1,0:T(8,128)(2,1)S(1)} fusion(f32[256,1024]{1,0:T(8,128)S(1)} %fusion.20, bf16[8,336,1024]{2,1,0:T(8,128)(2,1)} %collective-permute-done.8, bf16[256,8,2,336]{0,3,2,1:T(8,128)(2,1)S(1)} %bitcast.64, s32[]{:T(128)S(6)} %select_n.50), kind=kOutput, calls=%fused_computation.19 | convolution fusion | flops 1409810432 | bytes 8454148 | tf_op jit(solution)/shard_map/tfr,frn->tn/dot_general | solution.py:268
  262.2 4.2 %collective-permute-start.9 = (bf16[256,1024]{1,0:T(8,128)(2,1)S(1)}, bf16[256,1024]{1,0:T(8,128)(2,1)S(1)}, u32[]{:S(2)}, u32[]{:S(2)}) collective-permute-start(bf16[256,1024]{1,0:T(8,128)(2,1)S(1)} %fusion.29), channel_id=1, source_target_pairs={{0,32},{8,40},{16,48},{24,56},{32,64},{40,72},{48,80},{56,88},{64,... | collective-permute-start | bytes 1572872 | tf_op jit(solution)/shard_map/ppermute | solution.py:210
  266.4 7.7 %fusion.7.x_ref = bf16[16,42,1024]{2,1,0:T(8,128)(2,1)} fusion(bf16[8,256,16,42]{1,2,3,0:T(8,128)(2,1)} %all-to-all-done, bf16[8,256,1024]{2,1,0:T(8,128)(2,1)} %shard_map.103), kind=kOutput, calls=%fused_computation.7 | convolution fusion | flops 2819260416 | bytes 8323072 | tf_op jit(solution)/shard_map/ftcr,ftn->crn/dot_general | solution.py:261
  274.1 21.6 %shard_map.104 = f32[42,1024]{1,0:T(8,128)} custom-call(bf16[16,42,1024]{2,1,0:T(8,128)(2,1)} %fusion.7.x_ref), custom_call_target="tpu_custom_call" | custom-call | tf_op jit(solution)/shard_map/pallas_call | solution.py:192
  295.7 3.2 collective-permute-start.10
  298.9 4.8 %collective-permute-start.11 = (bf16[256,1024]{1,0:T(8,128)(2,1)S(1)}, bf16[256,1024]{1,0:T(8,128)(2,1)S(1)}, u32[]{:S(2)}, u32[]{:S(2)}) collective-permute-start(bf16[256,1024]{1,0:T(8,128)(2,1)S(1)} %fusion.29), channel_id=1, source_target_pairs={{0,16},{8,24},{16,32},{24,40},{32,48},{40,56},{48,64},{56,72},{64,... | collective-permute-start | bytes 1572872 | tf_op jit(solution)/shard_map/ppermute | solution.py:210
  305.6 4.2 %fusion.12 = bf16[256,8,1,336]{0,3,1,2:T(8,128)(2,1)S(1)} fusion(bf16[8,336,1024]{2,1,0:T(8,128)(2,1)} %bitcast.69, bf16[256,1024]{1,0:T(8,128)(2,1)S(1)} %copy-done.3), kind=kOutput, calls=%fused_computation.8 | convolution fusion | flops 1409974272 | bytes 7405568 | tf_op jit(solution)/shard_map/tn,frn->tfr/dot_general | solution.py:276
  311.5 11.8 %collective-permute-done.11 = bf16[256,1024]{1,0:T(8,128)(2,1)S(1)} collective-permute-done((bf16[256,1024]{1,0:T(8,128)(2,1)S(1)}, bf16[256,1024]{1,0:T(8,128)(2,1)S(1)}, u32[]{:S(2)}, u32[]{:S(2)}) %collective-permute-start.11) | collective-permute-done | bytes 524320 | tf_op jit(solution)/shard_map/ppermute | solution.py:210
  326.5 24.0 %shard_map.102 = (bf16[256,2048]{1,0:T(8,128)(2,1)}, bf16[256,2048]{1,0:T(8,128)(2,1)}, bf16[1280,1024]{1,0:T(8,128)(2,1)}) custom-call(bf16[256,2048]{1,0:T(8,128)(2,1)} %bitcast.74, bf16[1280,1024]{1,0:T(8,128)(2,1)} %slice.48.k_ref, bf16[1280,1024]{1,0:T(8,128)(2,1)} %constant_dynamic-update-slice_fusion.5.v_ref, bf16[256,2048]{1,0:T(8,128)(2,1)} %bitcast.76, ...), custom_call_target="tpu_custom_call" | custom-call | flops 6710886400 | bytes 12058624 | tf_op jit(solution)/shard_map/pallas_call | solution.py:98
  353.3 6.9 %collective-permute-start.13 = (bf16[256,1024]{1,0:T(8,128)(2,1)}, bf16[256,1024]{1,0:T(8,128)(2,1)S(1)}, u32[]{:S(2)}, u32[]{:S(2)}) collective-permute-start(bf16[256,1024]{1,0:T(8,128)(2,1)} %get-tuple-element.23), channel_id=1, source_target_pairs={{8,0},{16,8},{24,16},{32,24},{40,32},{48,40},{56,48},{64,56},{72,6... | collective-permute-start | bytes 1572872 | tf_op jit(solution)/shard_map/ppermute | solution.py:210
  365.0 4.2 %fusion.13 = bf16[256,8,1,336]{0,3,1,2:T(8,128)(2,1)S(1)} fusion(bf16[8,336,1024]{2,1,0:T(8,128)(2,1)} %collective-permute-done.8, bf16[256,1024]{1,0:T(8,128)(2,1)S(1)} %copy-done.3), kind=kOutput, calls=%fused_computation.9 | convolution fusion | flops 1409974272 | bytes 7405568 | tf_op jit(solution)/shard_map/tn,frn->tfr/dot_general | solution.py:277
  371.4 4.6 %copy.27 = bf16[1,256,5376]{2,1,0:T(8,128)(2,1)} copy(bf16[1,256,5376]{1,2,0:T(8,128)(2,1)} %bitcast.66) | data formatting | bytes 5505024
  376.0 8.9 %collective-permute-done.14 = bf16[256,1024]{1,0:T(8,128)(2,1)S(1)} collective-permute-done((bf16[256,1024]{1,0:T(8,128)(2,1)}, bf16[256,1024]{1,0:T(8,128)(2,1)S(1)}, u32[]{:S(2)}, u32[]{:S(2)}) %collective-permute-start.14) | collective-permute-done | bytes 524320 | tf_op jit(solution)/shard_map/ppermute | solution.py:210
  386.8 16.9 %collective-permute-done.16 = bf16[256,1024]{1,0:T(8,128)(2,1)} collective-permute-done((bf16[256,1024]{1,0:T(8,128)(2,1)}, bf16[256,1024]{1,0:T(8,128)(2,1)}, u32[]{:S(2)}, u32[]{:S(2)}) %collective-permute-start.16) | collective-permute-done | bytes 524320 | tf_op jit(solution)/shard_map/ppermute | solution.py:210
  (57 shorter events, 41.1 us)
Async XLA Ops:
  7.2 1.3 copy-start
  7.2 17.4 %copy-start.5 = (s32[1,256]{1,0:T(1,128)S(1)}, s32[1,256]{1,0:T(1,128)}, u32[]{:S(2)}) copy-start(s32[1,256]{1,0:T(1,128)} %param.11) | copy-start | bytes 3076
  7.2 122.3 %all-gather.3.cloned.1.call-start = ((), (), s32[]{:S(2)}) async-start(), calls=%async_computation.1 | async-start | bytes 6193152 | tf_op jit(solution)/shard_map/all_gather | solution.py:226
  10.2 42.4 %copy-start.2 = (bf16[1,256,1024]{2,1,0:T(8,128)(2,1)S(1)}, bf16[1,256,1024]{2,1,0:T(8,128)(2,1)}, u32[]{:S(2)}) copy-start(bf16[1,256,1024]{2,1,0:T(8,128)(2,1)} %param.8) | copy-start | bytes 1572868
  11.4 17.5 %collective-permute-start = (bf16[256,1152]{1,0:T(8,128)(2,1)S(1)}, bf16[256,1152]{1,0:T(8,128)(2,1)S(1)}, u32[]{:S(2)}, u32[]{:S(2)}) collective-permute-start(bf16[256,1152]{1,0:T(8,128)(2,1)S(1)} %pad_maximum_fusion), channel_id=1, source_target_pairs={{0,32},{8,40},{16,48},{24,56},{32,64},{40,72},{48,80},{56,88},{64,... | collective-permute-start | bytes 1769480 | tf_op jit(solution)/shard_map/ppermute | solution.py:210
  15.3 17.6 %collective-permute-start.1 = (bf16[256,1152]{1,0:T(8,128)(2,1)S(1)}, bf16[256,1152]{1,0:T(8,128)(2,1)S(1)}, u32[]{:S(2)}, u32[]{:S(2)}) collective-permute-start(bf16[256,1152]{1,0:T(8,128)(2,1)S(1)} %pad_maximum_fusion), channel_id=1, source_target_pairs={{0,24},{8,32},{16,40},{24,48},{32,56},{40,64},{48,72},{56,80},{64,... | collective-permute-start | bytes 1769480 | tf_op jit(solution)/shard_map/ppermute | solution.py:210
  18.4 30.2 %collective-permute-start.2 = (bf16[256,1152]{1,0:T(8,128)(2,1)S(1)}, bf16[256,1152]{1,0:T(8,128)(2,1)S(1)}, u32[]{:S(2)}, u32[]{:S(2)}) collective-permute-start(bf16[256,1152]{1,0:T(8,128)(2,1)S(1)} %pad_maximum_fusion), channel_id=1, source_target_pairs={{0,16},{8,24},{16,32},{24,40},{32,48},{40,56},{48,64},{56,72},{64,... | collective-permute-start | bytes 1769480 | tf_op jit(solution)/shard_map/ppermute | solution.py:210
  21.6 30.9 %collective-permute-start.3 = (bf16[256,1152]{1,0:T(8,128)(2,1)S(1)}, bf16[256,1152]{1,0:T(8,128)(2,1)S(1)}, u32[]{:S(2)}, u32[]{:S(2)}) collective-permute-start(bf16[256,1152]{1,0:T(8,128)(2,1)S(1)} %pad_maximum_fusion), channel_id=1, source_target_pairs={{0,8},{8,16},{16,24},{24,32},{32,40},{40,48},{48,56},{56,64},{64,7... | collective-permute-start | bytes 1769480 | tf_op jit(solution)/shard_map/ppermute | solution.py:210
  72.2 24.7 %collective-permute-start.4 = (bf16[256,1024]{1,0:T(8,128)(2,1)S(1)}, bf16[256,1024]{1,0:T(8,128)(2,1)S(1)}, u32[]{:S(2)}, u32[]{:S(2)}) collective-permute-start(bf16[256,1024]{1,0:T(8,128)(2,1)S(1)} %get-tuple-element.27), channel_id=1, source_target_pairs={{8,0},{16,8},{24,16},{32,24},{40,32},{48,40},{56,48},{64,56},{72,6... | collective-permute-start | bytes 1572872 | tf_op jit(solution)/shard_map/ppermute | solution.py:210
  81.6 28.7 %collective-permute-start.5 = (bf16[256,1024]{1,0:T(8,128)(2,1)S(1)}, bf16[256,1024]{1,0:T(8,128)(2,1)S(1)}, u32[]{:S(2)}, u32[]{:S(2)}) collective-permute-start(bf16[256,1024]{1,0:T(8,128)(2,1)S(1)} %get-tuple-element.30), channel_id=1, source_target_pairs={{16,0},{24,8},{32,16},{40,24},{48,32},{56,40},{64,48},{72,56},{80,... | collective-permute-start | bytes 1572872 | tf_op jit(solution)/shard_map/ppermute | solution.py:210
  83.6 27.4 %collective-permute-start.6 = (bf16[256,1024]{1,0:T(8,128)(2,1)S(1)}, bf16[256,1024]{1,0:T(8,128)(2,1)S(1)}, u32[]{:S(2)}, u32[]{:S(2)}) collective-permute-start(bf16[256,1024]{1,0:T(8,128)(2,1)S(1)} %get-tuple-element.29), channel_id=1, source_target_pairs={{24,0},{32,8},{40,16},{48,24},{56,32},{64,40},{72,48},{80,56},{88,... | collective-permute-start | bytes 1572872 | tf_op jit(solution)/shard_map/ppermute | solution.py:210
  84.9 42.3 %collective-permute-start.7 = (bf16[256,1024]{1,0:T(8,128)(2,1)S(1)}, bf16[256,1024]{1,0:T(8,128)(2,1)S(1)}, u32[]{:S(2)}, u32[]{:S(2)}) collective-permute-start(bf16[256,1024]{1,0:T(8,128)(2,1)S(1)} %get-tuple-element.28), channel_id=1, source_target_pairs={{32,0},{40,8},{48,16},{56,24},{64,32},{72,40},{80,48},{88,56},{96,... | collective-permute-start | bytes 1572872 | tf_op jit(solution)/shard_map/ppermute | solution.py:210
  129.5 128.4 %collective-permute-start.8 = (bf16[8,336,1024]{2,1,0:T(8,128)(2,1)}, bf16[8,336,1024]{2,1,0:T(8,128)(2,1)}, u32[]{:S(2)}, u32[]{:S(2)}) collective-permute-start(bf16[8,336,1024]{2,1,0:T(8,128)(2,1)} %bitcast.67), channel_id=1, source_target_pairs={{0,8},{8,0},{16,24},{24,16},{32,40},{40,32},{48,56},{56,48},{64,72... | collective-permute-start | bytes 16515080 | tf_op jit(solution)/shard_map/ppermute | solution.py:259
  140.2 126.1 %all-to-all-start = ((bf16[8,256,16,42]{1,2,3,0:T(8,128)(2,1)}), bf16[8,256,16,42]{1,2,3,0:T(8,128)(2,1)}, u32[]{:S(2)}, u32[]{:S(2)}) async-start(bf16[8,256,16,42]{1,2,3,0:T(8,128)(2,1)} %copy.25), calls=%async_computation | async-start | bytes 5505024 | tf_op jit(solution)/shard_map/all_to_all | solution.py:236
  262.2 43.4 %copy-start.3 = (bf16[256,1024]{1,0:T(8,128)(2,1)S(1)}, bf16[256,1024]{1,0:T(8,128)(2,1)}, u32[]{:S(2)}) copy-start(bf16[256,1024]{1,0:T(8,128)(2,1)} %add_convert_fusion.1.x_ref) | copy-start | bytes 1572868
  262.2 47.6 %collective-permute-start.9 = (bf16[256,1024]{1,0:T(8,128)(2,1)S(1)}, bf16[256,1024]{1,0:T(8,128)(2,1)S(1)}, u32[]{:S(2)}, u32[]{:S(2)}) collective-permute-start(bf16[256,1024]{1,0:T(8,128)(2,1)S(1)} %fusion.29), channel_id=1, source_target_pairs={{0,32},{8,40},{16,48},{24,56},{32,64},{40,72},{48,80},{56,88},{64,... | collective-permute-start | bytes 1572872 | tf_op jit(solution)/shard_map/ppermute | solution.py:210
  295.7 15.0 %collective-permute-start.10 = (bf16[256,1024]{1,0:T(8,128)(2,1)S(1)}, bf16[256,1024]{1,0:T(8,128)(2,1)S(1)}, u32[]{:S(2)}, u32[]{:S(2)}) collective-permute-start(bf16[256,1024]{1,0:T(8,128)(2,1)S(1)} %fusion.29), channel_id=1, source_target_pairs={{0,24},{8,32},{16,40},{24,48},{32,56},{40,64},{48,72},{56,80},{64,... | collective-permute-start | bytes 1572872 | tf_op jit(solution)/shard_map/ppermute | solution.py:210
  298.9 24.4 %collective-permute-start.11 = (bf16[256,1024]{1,0:T(8,128)(2,1)S(1)}, bf16[256,1024]{1,0:T(8,128)(2,1)S(1)}, u32[]{:S(2)}, u32[]{:S(2)}) collective-permute-start(bf16[256,1024]{1,0:T(8,128)(2,1)S(1)} %fusion.29), channel_id=1, source_target_pairs={{0,16},{8,24},{16,32},{24,40},{32,48},{40,56},{48,64},{56,72},{64,... | collective-permute-start | bytes 1572872 | tf_op jit(solution)/shard_map/ppermute | solution.py:210
  303.7 21.2 %collective-permute-start.12 = (bf16[256,1024]{1,0:T(8,128)(2,1)S(1)}, bf16[256,1024]{1,0:T(8,128)(2,1)S(1)}, u32[]{:S(2)}, u32[]{:S(2)}) collective-permute-start(bf16[256,1024]{1,0:T(8,128)(2,1)S(1)} %fusion.29), channel_id=1, source_target_pairs={{0,8},{8,16},{16,24},{24,32},{32,40},{40,48},{48,56},{56,64},{64,7... | collective-permute-start | bytes 1572872 | tf_op jit(solution)/shard_map/ppermute | solution.py:210
  353.3 22.7 %collective-permute-start.13 = (bf16[256,1024]{1,0:T(8,128)(2,1)}, bf16[256,1024]{1,0:T(8,128)(2,1)S(1)}, u32[]{:S(2)}, u32[]{:S(2)}) collective-permute-start(bf16[256,1024]{1,0:T(8,128)(2,1)} %get-tuple-element.23), channel_id=1, source_target_pairs={{8,0},{16,8},{24,16},{32,24},{40,32},{48,40},{56,48},{64,56},{72,6... | collective-permute-start | bytes 1572872 | tf_op jit(solution)/shard_map/ppermute | solution.py:210
  360.3 24.7 %collective-permute-start.14 = (bf16[256,1024]{1,0:T(8,128)(2,1)}, bf16[256,1024]{1,0:T(8,128)(2,1)S(1)}, u32[]{:S(2)}, u32[]{:S(2)}) collective-permute-start(bf16[256,1024]{1,0:T(8,128)(2,1)} %get-tuple-element.26), channel_id=1, source_target_pairs={{16,0},{24,8},{32,16},{40,24},{48,32},{56,40},{64,48},{72,56},{80,... | collective-permute-start | bytes 1572872 | tf_op jit(solution)/shard_map/ppermute | solution.py:210
  362.2 24.6 %collective-permute-start.15 = (bf16[256,1024]{1,0:T(8,128)(2,1)}, bf16[256,1024]{1,0:T(8,128)(2,1)S(1)}, u32[]{:S(2)}, u32[]{:S(2)}) collective-permute-start(bf16[256,1024]{1,0:T(8,128)(2,1)} %get-tuple-element.25), channel_id=1, source_target_pairs={{24,0},{32,8},{40,16},{48,24},{56,32},{64,40},{72,48},{80,56},{88,... | collective-permute-start | bytes 1572872 | tf_op jit(solution)/shard_map/ppermute | solution.py:210
  363.5 40.1 %collective-permute-start.16 = (bf16[256,1024]{1,0:T(8,128)(2,1)}, bf16[256,1024]{1,0:T(8,128)(2,1)}, u32[]{:S(2)}, u32[]{:S(2)}) collective-permute-start(bf16[256,1024]{1,0:T(8,128)(2,1)} %get-tuple-element.24), channel_id=1, source_target_pairs={{32,0},{40,8},{48,16},{56,24},{64,32},{72,40},{80,48},{88,56},{96,... | collective-permute-start | bytes 1572872 | tf_op jit(solution)/shard_map/ppermute | solution.py:210
  371.4 35.4 %copy-start.1 = (bf16[672,1024]{1,0:T(8,128)(2,1)S(1)}, bf16[672,1024]{1,0:T(8,128)(2,1)}, u32[]{:S(2)}) copy-start(bf16[672,1024]{1,0:T(8,128)(2,1)} %param.9) | copy-start | bytes 4128772
  376.0 30.1 %copy-start.4 = (f32[42,1024]{1,0:T(8,128)S(1)}, f32[42,1024]{1,0:T(8,128)}, u32[]{:S(2)}) copy-start(f32[42,1024]{1,0:T(8,128)} %shard_map.104) | copy-start | bytes 516100
Sparse Core Ops, SparseCore 0:
  10.9 92.3 all-gather.2

commit v6 on v5

--- a/solution.py
+++ b/solution.py
@@ -226,9 +226,12 @@
     w_mine = lax.all_gather(
         lax.dynamic_slice_in_dim(w_value, core * half_rows, half_rows, 0), "fsdp", axis=0, tiled=False
     )
+    partner = [(i, i ^ 1) for i in range(n_ctx)]
     token_halves = tokens_in.reshape(shard_rows, n_fsdp, 2, half_rows)
     tokens_mine = lax.dynamic_index_in_dim(token_halves, core, axis=2, keepdims=False)
-    tokens_other = lax.dynamic_index_in_dim(token_halves, 1 - core, axis=2, keepdims=False)
+    partner_tokens = lax.ppermute(
+        lax.dynamic_index_in_dim(token_halves, 1 - core, axis=2, keepdims=False), "ctx", partner
+    )
     out_rows = model_width // (n_ctx * n_fsdp)
     token_cols = (
         tokens_in.reshape(shard_rows, n_ctx, n_fsdp, out_rows).transpose(2, 0, 1, 3)
@@ -256,16 +259,16 @@
     value_terms = value_grads(queries[0], window_keys, d_out[0], query_tags, key_tags[None, :])
     d_values_low = returned_sum(value_terms)
     w_mine, _ = lax.optimization_barrier((w_mine, d_values_low))
-    w_other = lax.ppermute(w_mine, "ctx", [(i, i ^ 1) for i in range(n_ctx)])
     grads_all = peer_gather(d_values_low, "fsdp", 2)
     weight_part = jnp.einsum(
         "ftcr,ftn->crn", token_cols, grads_all, preferred_element_type=jnp.float32
     )
     d_weight = peer_sum_scatter(weight_part.astype(jnp.bfloat16), "ctx", 3)
 
+    partner_part = jnp.einsum("tfr,frn->tn", partner_tokens, w_mine, preferred_element_type=jnp.float32)
     values = (
         jnp.einsum("tfr,frn->tn", tokens_mine, w_mine, preferred_element_type=jnp.float32)
-        + jnp.einsum("tfr,frn->tn", tokens_other, w_other, preferred_element_type=jnp.float32)
+        + lax.ppermute(partner_part, "ctx", partner)
     ).astype(jnp.bfloat16)
     arrived_values = [shifted(values, "ctx", hop) for hop in range(1, n_hops + 1)]
     window_values = jnp.concatenate(arrived_values[::-1] + [values], 0)
@@ -274,7 +277,12 @@
     )
     d_key_rows = returned_sum(key_terms)
     d_mine = jnp.einsum("tn,frn->tfr", d_values_low, w_mine, preferred_element_type=jnp.float32).astype(jnp.bfloat16)
-    d_other = jnp.einsum("tn,frn->tfr", d_values_low, w_other, preferred_element_type=jnp.float32).astype(jnp.bfloat16)
+    partner_grads = lax.ppermute(d_values_low, "ctx", partner)
+    d_other = lax.ppermute(
+        jnp.einsum("tn,frn->tfr", partner_grads, w_mine, preferred_element_type=jnp.float32).astype(jnp.bfloat16),
+        "ctx",
+        partner,
+    )
     d_tokens = jnp.where(
         core == 0, jnp.stack([d_mine, d_other], 2), jnp.stack([d_other, d_mine], 2)
     ).reshape(shard_rows, model_width)

time: 415 us -> 376 us (0.906); the launches traced: 414 us -> 369 us
  waiting for transfers between devices: 108 us -> 54.3 us
  Pallas kernels: 167 us -> 147 us
  starting transfers between devices: 59.9 us -> 74 us
  local copies, waits for them, and re-layouts: 31.6 us -> 42.6 us
    ppermute x16, waiting for transfers between devices: 108 us -> 54.2 us  [shifted(): return lax.ppermute(x, axis, pairs)]
    pallas_call x1, Pallas kernels: 106 us -> 80.4 us  [peer_gather(): pl.pallas_call(functools.partial(peer_gather_kernel, axis, n), out_shape=...]
    ppermute x16, starting transfers between devices: 52.7 us -> 60.1 us  [shifted(): return lax.ppermute(x, axis, pairs)]
    ppermute x1 -> x4, starting transfers between devices: 0.01 us -> 6.64 us  [the longest x1 5.73 us: shards(): lax.ppermute(partner_part, 'ctx', partner)]
    unnamed x23 -> x27, local copies, waits for them, and re-layouts: 13.4 us -> 18.9 us
    pallas_call x1, Pallas kernels: 21.6 us -> 27.1 us  [peer_sum_scatter(): pl.pallas_call(functools.partial(peer_sum_kernel, axis, n), out_shape=jax...]
  transfers between devices with their start and end apart: 19 -> 22, of which waited for: 13 -> 5; matrix products, arithmetic and copies ran while one was open for 13% -> 20% of each run, Pallas kernels for 35% -> 40%
where the time goes in v6:
time: 376 us; the launch traced here: 369 us
  Pallas kernels  147 us (39%)
  starting transfers between devices  74 us (20%)
  waiting for transfers between devices  54.3 us (14%)
  local copies, waits for them, and re-layouts  42.6 us (11%)
  matrix products  27.5 us (7%)
  between operations  14.4 us (4%)
  other arithmetic  8.91 us (2%)
    pallas_call x1, Pallas kernels, peer_gather(): pl.pallas_call(functools.partial(peer_gather_kernel, axis, n), out_shape=...  80.4 us
    ppermute x16, starting transfers between devices, shifted(): return lax.ppermute(x, axis, pairs)  60.1 us
    ppermute x16, waiting for transfers between devices, shifted(): return lax.ppermute(x, axis, pairs)  54.2 us
    pallas_call x1, Pallas kernels, peer_sum_scatter(): pl.pallas_call(functools.partial(peer_sum_kernel, axis, n), out_shape=jax...  27.1 us
    pallas_call x1, Pallas kernels, fused_attention(): pl.pallas_call(attention_kernel, grid=(heads,), in_specs=[q_spec, kv_spec...  24 us
    unnamed x27, local copies, waits for them, and re-layouts  18.9 us
    pallas_call x1, Pallas kernels, value_grads(): pl.pallas_call(value_grad_kernel, grid=(heads,), in_specs=[q_spec, kv_spe...  15.4 us
    dot_general x1, matrix products, shards(): jnp.einsum('ftcr,ftn->crn', token_cols, grads_all, preferred_element_type...  7.69 us
  transfers between devices with their start and end apart: 22, of which 5 were waited for; matrix products, arithmetic and copies ran while one was open for 20% of the time, Pallas kernels for 40%

profile of v6, /device:TPU:28, one launch (start us, length us, event | category | flops | bytes accessed | tf_op | source)
XLA Modules:
  0.0 368.6 jit_solution(14212594482083556881)
XLA Ops:
  12.1 4.6 %collective-permute-start = (bf16[256,1152]{1,0:T(8,128)(2,1)}, bf16[256,1152]{1,0:T(8,128)(2,1)}, u32[]{:S(2)}, u32[]{:S(2)}) collective-permute-start(bf16[256,1152]{1,0:T(8,128)(2,1)} %pad_maximum_fusion), channel_id=1, source_target_pairs={{0,32},{8,40},{16,48},{24,56},{32,64},{40,72},{48,80},{56,88},{64,... | collective-permute-start | bytes 1769480 | tf_op jit(solution)/shard_map/ppermute | solution.py:210
  16.8 3.2 collective-permute-start.1
  21.9 3.7 collective-permute-start.2
  25.6 4.5 %copy.20 = bf16[1,256,5376]{1,2,0:T(8,128)(2,1)} copy(bf16[1,256,5376]{2,1,0:T(8,128)(2,1)} %param.6) | data formatting | bytes 5505024 | tf_op args[0]
  33.9 2.8 collective-permute-done.1
  37.9 13.0 %collective-permute-done.2 = bf16[256,1152]{1,0:T(8,128)(2,1)} collective-permute-done((bf16[256,1152]{1,0:T(8,128)(2,1)}, bf16[256,1152]{1,0:T(8,128)(2,1)}, u32[]{:S(2)}, u32[]{:S(2)}) %collective-permute-start.2) | collective-permute-done | bytes 589856 | tf_op jit(solution)/shard_map/ppermute | solution.py:210
  55.9 15.4 %shard_map.101 = bf16[1280,1024]{1,0:T(8,128)(2,1)} custom-call(bf16[256,2048]{1,0:T(8,128)(2,1)} %bitcast.69, bf16[1280,1024]{1,0:T(8,128)(2,1)} %slice.48.k_ref, bf16[256,2048]{1,0:T(8,128)(2,1)} %bitcast.71, s32[256,1]{1,0:T(8,128)} %copy.21.qtag_ref, s32[1,1280]{1,0:T(1,128)} %compare_select_fusion.ktag_ref), custom_call_target="tpu_custom_call" | custom-call | flops 2684354560 | bytes 7340032 | tf_op jit(solution)/shard_map/pallas_call | solution.py:79
  71.4 2.9 fusion.26
  74.2 12.9 %collective-permute-start.4 = (bf16[256,1024]{1,0:T(8,128)(2,1)}, bf16[256,1024]{1,0:T(8,128)(2,1)S(1)}, u32[]{:S(2)}, u32[]{:S(2)}) collective-permute-start(bf16[256,1024]{1,0:T(8,128)(2,1)} %get-tuple-element.27), channel_id=1, source_target_pairs={{8,0},{16,8},{24,16},{32,24},{40,32},{48,40},{56,48},{64,56},{72,6... | collective-permute-start | bytes 1572872 | tf_op jit(solution)/shard_map/ppermute | solution.py:210
  91.6 5.3 %reshape_squeeze.7 = bf16[256,16,8,42]{0,3,2,1:T(8,128)(2,1)} reshape(bf16[1,256,5376]{1,2,0:T(8,128)(2,1)} %copy.20) | data formatting | bytes 5505024 | tf_op jit(solution)/shard_map/reshape;squeeze | solution.py:237
  96.9 5.0 %copy.25 = bf16[8,256,16,42]{1,2,3,0:T(8,128)(2,1)} copy(bf16[8,256,16,42]{1,3,0,2:T(8,128)(2,1)} %bitcast.63) | data formatting | bytes 5505024 | tf_op jit(solution)/shard_map/transpose | solution.py:237
  101.9 7.2 %all-to-all-start = ((bf16[8,256,16,42]{1,2,3,0:T(8,128)(2,1)}), bf16[8,256,16,42]{1,2,3,0:T(8,128)(2,1)}, u32[]{:S(2)}, u32[]{:S(2)}) async-start(bf16[8,256,16,42]{1,2,3,0:T(8,128)(2,1)} %copy.25), calls=%async_computation | async-start | bytes 5505024 | tf_op jit(solution)/shard_map/all_to_all | solution.py:239
  109.1 10.1 %collective-permute-done.7 = bf16[256,1024]{1,0:T(8,128)(2,1)} collective-permute-done((bf16[256,1024]{1,0:T(8,128)(2,1)}, bf16[256,1024]{1,0:T(8,128)(2,1)}, u32[]{:S(2)}, u32[]{:S(2)}) %collective-permute-start.7) | collective-permute-done | bytes 524320 | tf_op jit(solution)/shard_map/ppermute | solution.py:210
  121.4 5.4 %convolution_bitcast_fusion = f32[256,1024]{1,0:T(8,128)} fusion(bf16[256,8,336]{0,2,1:T(8,128)(2,1)S(1)} %collective-permute-done.8, bf16[8,336,1024]{2,1,0:T(8,128)(2,1)} %bitcast.57), kind=kOutput, calls=%fused_computation.14 | convolution fusion | flops 1409286144 | bytes 7929856 | tf_op jit(solution)/shard_map/tfr,frn->tn/dot_general | solution.py:268
  126.8 5.7 %collective-permute-start.9 = (f32[256,1024]{1,0:T(8,128)}, f32[256,1024]{1,0:T(8,128)S(1)}, u32[]{:S(2)}, u32[]{:S(2)}) collective-permute-start(f32[256,1024]{1,0:T(8,128)} %convolution_bitcast_fusion), channel_id=1, source_target_pairs={{0,8},{8,0},{16,24},{24,16},{32,40},{40,32},{48,56},{56,48},{64,72... | collective-permute-start | bytes 3145736 | tf_op jit(solution)/shard_map/ppermute | solution.py:271
  132.6 80.4 %shard_map.103 = bf16[8,256,1024]{2,1,0:T(8,128)(2,1)} custom-call(bf16[256,1024]{1,0:T(8,128)(2,1)} %copy-done.3), custom_call_target="tpu_custom_call" | custom-call | tf_op jit(solution)/shard_map/pallas_call | solution.py:145
  212.9 4.7 %add_convert_fusion.1 = bf16[256,1024]{1,0:T(8,128)(2,1)S(1)} fusion(f32[256,1024]{1,0:T(8,128)S(1)} %collective-permute-done.9, bf16[8,336,1024]{2,1,0:T(8,128)(2,1)} %bitcast.58, bf16[256,8,2,336]{0,3,2,1:T(8,128)(2,1)} %bitcast.62, s32[]{:T(128)S(6)} %select_n.47), kind=kOutput, calls=%fused_computation.16 | convolution fusion | flops 1409810432 | bytes 8454148 | tf_op jit(solution)/shard_map/tfr,frn->tn/dot_general | solution.py:270
  217.6 7.0 %collective-permute-start.10 = (bf16[256,1024]{1,0:T(8,128)(2,1)S(1)}, bf16[256,1024]{1,0:T(8,128)(2,1)S(1)}, u32[]{:S(2)}, u32[]{:S(2)}) collective-permute-start(bf16[256,1024]{1,0:T(8,128)(2,1)S(1)} %add_convert_fusion.1), channel_id=1, source_target_pairs={{0,32},{8,40},{16,48},{24,56},{32,64},{40,72},{48,80},{56,88},{64,... | collective-permute-start | bytes 1572872 | tf_op jit(solution)/shard_map/ppermute | solution.py:210
  224.6 7.7 %fusion.7.x_ref = bf16[16,42,1024]{2,1,0:T(8,128)(2,1)} fusion(bf16[8,256,16,42]{1,2,3,0:T(8,128)(2,1)} %all-to-all-done, bf16[8,256,1024]{2,1,0:T(8,128)(2,1)} %shard_map.103), kind=kOutput, calls=%fused_computation.7 | convolution fusion | flops 2819260416 | bytes 8323072 | tf_op jit(solution)/shard_map/ftcr,ftn->crn/dot_general | solution.py:263
  232.3 27.1 %shard_map.104 = f32[42,1024]{1,0:T(8,128)} custom-call(bf16[16,42,1024]{2,1,0:T(8,128)(2,1)} %fusion.7.x_ref), custom_call_target="tpu_custom_call" | custom-call | tf_op jit(solution)/shard_map/pallas_call | solution.py:192
  259.4 3.0 collective-permute-start.13
  262.4 2.3 collective-permute-start.12
  264.8 3.7 collective-permute-start.11
  268.4 5.5 %convolution_convert_fusion = bf16[256,8,336]{0,2,1:T(8,128)(2,1)} fusion(bf16[8,336,1024]{2,1,0:T(8,128)(2,1)} %bitcast.59, bf16[256,1024]{1,0:T(8,128)(2,1)} %collective-permute-done.18), kind=kOutput, calls=%fused_computation.5 | convolution fusion | flops 1409974272 | bytes 7405568 | tf_op jit(solution)/shard_map/tn,frn->tfr/dot_general | solution.py:282
  275.3 10.0 %collective-permute-done.11 = bf16[256,1024]{1,0:T(8,128)(2,1)S(1)} collective-permute-done((bf16[256,1024]{1,0:T(8,128)(2,1)S(1)}, bf16[256,1024]{1,0:T(8,128)(2,1)S(1)}, u32[]{:S(2)}, u32[]{:S(2)}) %collective-permute-start.11) | collective-permute-done | bytes 524320 | tf_op jit(solution)/shard_map/ppermute | solution.py:210
  288.6 24.0 %shard_map.102 = (bf16[256,2048]{1,0:T(8,128)(2,1)}, bf16[256,2048]{1,0:T(8,128)(2,1)}, bf16[1280,1024]{1,0:T(8,128)(2,1)}) custom-call(bf16[256,2048]{1,0:T(8,128)(2,1)} %bitcast.70, bf16[1280,1024]{1,0:T(8,128)(2,1)} %slice.48.k_ref, bf16[1280,1024]{1,0:T(8,128)(2,1)} %constant_dynamic-update-slice_fusion.5.v_ref, bf16[256,2048]{1,0:T(8,128)(2,1)} %bitcast.72, ...), custom_call_target="tpu_custom_call" | custom-call | flops 6710886400 | bytes 12058624 | tf_op jit(solution)/shard_map/pallas_call | solution.py:98
  312.6 2.9 fusion.25
  315.6 8.6 %collective-permute-start.14 = (bf16[256,1024]{1,0:T(8,128)(2,1)}, bf16[256,1024]{1,0:T(8,128)(2,1)S(1)}, u32[]{:S(2)}, u32[]{:S(2)}) collective-permute-start(bf16[256,1024]{1,0:T(8,128)(2,1)} %get-tuple-element.23), channel_id=1, source_target_pairs={{8,0},{16,8},{24,16},{32,24},{40,32},{48,40},{56,48},{64,56},{72,6... | collective-permute-start | bytes 1572872 | tf_op jit(solution)/shard_map/ppermute | solution.py:210
  329.0 4.2 %fusion.12 = bf16[256,8,1,336]{0,3,1,2:T(8,128)(2,1)S(1)} fusion(bf16[8,336,1024]{2,1,0:T(8,128)(2,1)} %bitcast.60, bf16[256,1024]{1,0:T(8,128)(2,1)S(1)} %copy-done.4), kind=kOutput, calls=%fused_computation.8 | convolution fusion | flops 1409974272 | bytes 7405568 | tf_op jit(solution)/shard_map/tn,frn->tfr/dot_general | solution.py:279
  335.4 4.6 %copy.27 = bf16[1,256,5376]{2,1,0:T(8,128)(2,1)} copy(bf16[1,256,5376]{1,2,0:T(8,128)(2,1)} %bitcast.64) | data formatting | bytes 5505024
  340.0 18.2 %collective-permute-done.17 = bf16[256,1024]{1,0:T(8,128)(2,1)} collective-permute-done((bf16[256,1024]{1,0:T(8,128)(2,1)}, bf16[256,1024]{1,0:T(8,128)(2,1)}, u32[]{:S(2)}, u32[]{:S(2)}) %collective-permute-start.17) | collective-permute-done | bytes 524320 | tf_op jit(solution)/shard_map/ppermute | solution.py:210
  358.3 2.8 fusion.19
  (68 shorter events, 35.7 us)
Async XLA Ops:
  7.2 1.3 copy-start
  7.2 114.2 %all-gather.3.cloned.1.call-start = ((), (), s32[]{:S(2)}) async-start(), calls=%async_computation.1 | async-start | bytes 6193152 | tf_op jit(solution)/shard_map/all_gather | solution.py:226
  12.1 20.6 %collective-permute-start = (bf16[256,1152]{1,0:T(8,128)(2,1)}, bf16[256,1152]{1,0:T(8,128)(2,1)}, u32[]{:S(2)}, u32[]{:S(2)}) collective-permute-start(bf16[256,1152]{1,0:T(8,128)(2,1)} %pad_maximum_fusion), channel_id=1, source_target_pairs={{0,32},{8,40},{16,48},{24,56},{32,64},{40,72},{48,80},{56,88},{64,... | collective-permute-start | bytes 1769480 | tf_op jit(solution)/shard_map/ppermute | solution.py:210
  16.8 19.9 %collective-permute-start.1 = (bf16[256,1152]{1,0:T(8,128)(2,1)}, bf16[256,1152]{1,0:T(8,128)(2,1)}, u32[]{:S(2)}, u32[]{:S(2)}) collective-permute-start(bf16[256,1152]{1,0:T(8,128)(2,1)} %pad_maximum_fusion), channel_id=1, source_target_pairs={{0,24},{8,32},{16,40},{24,48},{32,56},{40,64},{48,72},{56,80},{64,... | collective-permute-start | bytes 1769480 | tf_op jit(solution)/shard_map/ppermute | solution.py:210
  19.9 32.0 %collective-permute-start.3 = (bf16[256,1152]{1,0:T(8,128)(2,1)}, bf16[256,1152]{1,0:T(8,128)(2,1)}, u32[]{:S(2)}, u32[]{:S(2)}) collective-permute-start(bf16[256,1152]{1,0:T(8,128)(2,1)} %pad_maximum_fusion), channel_id=1, source_target_pairs={{0,8},{8,16},{16,24},{24,32},{32,40},{40,48},{48,56},{56,64},{64,7... | collective-permute-start | bytes 1769480 | tf_op jit(solution)/shard_map/ppermute | solution.py:210
  21.9 29.0 %collective-permute-start.2 = (bf16[256,1152]{1,0:T(8,128)(2,1)}, bf16[256,1152]{1,0:T(8,128)(2,1)}, u32[]{:S(2)}, u32[]{:S(2)}) collective-permute-start(bf16[256,1152]{1,0:T(8,128)(2,1)} %pad_maximum_fusion), channel_id=1, source_target_pairs={{0,16},{8,24},{16,32},{24,40},{32,48},{40,56},{48,64},{56,72},{64,... | collective-permute-start | bytes 1769480 | tf_op jit(solution)/shard_map/ppermute | solution.py:210
  30.1 1.9 copy-start.7
  31.5 21.6 %copy-start.2 = (bf16[1,256,1024]{2,1,0:T(8,128)(2,1)S(1)}, bf16[1,256,1024]{2,1,0:T(8,128)(2,1)}, u32[]{:S(2)}) copy-start(bf16[1,256,1024]{2,1,0:T(8,128)(2,1)} %param.8) | copy-start | bytes 1572868
  31.5 89.9 %collective-permute-start.8 = (bf16[256,8,336]{0,2,1:T(8,128)(2,1)S(1)}, bf16[256,8,336]{0,2,1:T(8,128)(2,1)S(1)}, u32[]{:S(2)}, u32[]{:S(2)}) collective-permute-start(bf16[256,8,336]{0,2,1:T(8,128)(2,1)S(1)} %dynamic-slice_bitcast_fusion), channel_id=1, source_target_pairs={{0,8},{8,0},{16,24},{24,16},{32,40},{40,32},{48,56},{56,48},{64,72... | collective-permute-start | bytes 4128776 | tf_op jit(solution)/shard_map/ppermute | solution.py:232
  74.2 34.9 %collective-permute-start.4 = (bf16[256,1024]{1,0:T(8,128)(2,1)}, bf16[256,1024]{1,0:T(8,128)(2,1)S(1)}, u32[]{:S(2)}, u32[]{:S(2)}) collective-permute-start(bf16[256,1024]{1,0:T(8,128)(2,1)} %get-tuple-element.27), channel_id=1, source_target_pairs={{8,0},{16,8},{24,16},{32,24},{40,32},{48,40},{56,48},{64,56},{72,6... | collective-permute-start | bytes 1572872 | tf_op jit(solution)/shard_map/ppermute | solution.py:210
  87.1 32.1 %collective-permute-start.7 = (bf16[256,1024]{1,0:T(8,128)(2,1)}, bf16[256,1024]{1,0:T(8,128)(2,1)}, u32[]{:S(2)}, u32[]{:S(2)}) collective-permute-start(bf16[256,1024]{1,0:T(8,128)(2,1)} %get-tuple-element.28), channel_id=1, source_target_pairs={{32,0},{40,8},{48,16},{56,24},{64,32},{72,40},{80,48},{88,56},{96,... | collective-permute-start | bytes 1572872 | tf_op jit(solution)/shard_map/ppermute | solution.py:210
  88.4 30.8 %collective-permute-start.6 = (bf16[256,1024]{1,0:T(8,128)(2,1)}, bf16[256,1024]{1,0:T(8,128)(2,1)}, u32[]{:S(2)}, u32[]{:S(2)}) collective-permute-start(bf16[256,1024]{1,0:T(8,128)(2,1)} %get-tuple-element.29), channel_id=1, source_target_pairs={{24,0},{32,8},{40,16},{48,24},{56,32},{64,40},{72,48},{80,56},{88,... | collective-permute-start | bytes 1572872 | tf_op jit(solution)/shard_map/ppermute | solution.py:210
  89.7 29.5 %collective-permute-start.5 = (bf16[256,1024]{1,0:T(8,128)(2,1)}, bf16[256,1024]{1,0:T(8,128)(2,1)}, u32[]{:S(2)}, u32[]{:S(2)}) collective-permute-start(bf16[256,1024]{1,0:T(8,128)(2,1)} %get-tuple-element.30), channel_id=1, source_target_pairs={{16,0},{24,8},{32,16},{40,24},{48,32},{56,40},{64,48},{72,56},{80,... | collective-permute-start | bytes 1572872 | tf_op jit(solution)/shard_map/ppermute | solution.py:210
  101.9 122.7 %all-to-all-start = ((bf16[8,256,16,42]{1,2,3,0:T(8,128)(2,1)}), bf16[8,256,16,42]{1,2,3,0:T(8,128)(2,1)}, u32[]{:S(2)}, u32[]{:S(2)}) async-start(bf16[8,256,16,42]{1,2,3,0:T(8,128)(2,1)} %copy.25), calls=%async_computation | async-start | bytes 5505024 | tf_op jit(solution)/shard_map/all_to_all | solution.py:239
  109.1 10.1 %copy-start.6 = (bf16[256,1024]{1,0:T(8,128)(2,1)}, bf16[256,1024]{1,0:T(8,128)(2,1)S(1)}, u32[]{:S(2)}) copy-start(bf16[256,1024]{1,0:T(8,128)(2,1)S(1)} %collective-permute-done.4) | copy-start | bytes 1572868
  121.4 11.2 %copy-start.3 = (bf16[256,1024]{1,0:T(8,128)(2,1)}, bf16[256,1024]{1,0:T(8,128)(2,1)S(1)}, u32[]{:S(2)}) copy-start(bf16[256,1024]{1,0:T(8,128)(2,1)S(1)} %add_convert_fusion.2.x_ref) | copy-start | bytes 1572868
  126.8 86.1 %collective-permute-start.9 = (f32[256,1024]{1,0:T(8,128)}, f32[256,1024]{1,0:T(8,128)S(1)}, u32[]{:S(2)}, u32[]{:S(2)}) collective-permute-start(f32[256,1024]{1,0:T(8,128)} %convolution_bitcast_fusion), channel_id=1, source_target_pairs={{0,8},{8,0},{16,24},{24,16},{32,40},{40,32},{48,56},{56,48},{64,72... | collective-permute-start | bytes 3145736 | tf_op jit(solution)/shard_map/ppermute | solution.py:271
  132.5 135.9 %collective-permute-start.18 = (bf16[256,1024]{1,0:T(8,128)(2,1)S(1)}, bf16[256,1024]{1,0:T(8,128)(2,1)}, u32[]{:S(2)}, u32[]{:S(2)}) collective-permute-start(bf16[256,1024]{1,0:T(8,128)(2,1)S(1)} %add_convert_fusion.2.x_ref), channel_id=1, source_target_pairs={{0,8},{8,0},{16,24},{24,16},{32,40},{40,32},{48,56},{56,48},{64,72... | collective-permute-start | bytes 1572872 | tf_op jit(solution)/shard_map/ppermute | solution.py:280
  217.6 56.8 %collective-permute-start.10 = (bf16[256,1024]{1,0:T(8,128)(2,1)S(1)}, bf16[256,1024]{1,0:T(8,128)(2,1)S(1)}, u32[]{:S(2)}, u32[]{:S(2)}) collective-permute-start(bf16[256,1024]{1,0:T(8,128)(2,1)S(1)} %add_convert_fusion.1), channel_id=1, source_target_pairs={{0,32},{8,40},{16,48},{24,56},{32,64},{40,72},{48,80},{56,88},{64,... | collective-permute-start | bytes 1572872 | tf_op jit(solution)/shard_map/ppermute | solution.py:210
  259.4 27.6 %collective-permute-start.13 = (bf16[256,1024]{1,0:T(8,128)(2,1)S(1)}, bf16[256,1024]{1,0:T(8,128)(2,1)S(1)}, u32[]{:S(2)}, u32[]{:S(2)}) collective-permute-start(bf16[256,1024]{1,0:T(8,128)(2,1)S(1)} %add_convert_fusion.1), channel_id=1, source_target_pairs={{0,8},{8,16},{16,24},{24,32},{32,40},{40,48},{48,56},{56,64},{64,7... | collective-permute-start | bytes 1572872 | tf_op jit(solution)/shard_map/ppermute | solution.py:210
  262.4 23.7 %collective-permute-start.12 = (bf16[256,1024]{1,0:T(8,128)(2,1)S(1)}, bf16[256,1024]{1,0:T(8,128)(2,1)S(1)}, u32[]{:S(2)}, u32[]{:S(2)}) collective-permute-start(bf16[256,1024]{1,0:T(8,128)(2,1)S(1)} %add_convert_fusion.1), channel_id=1, source_target_pairs={{0,16},{8,24},{16,32},{24,40},{32,48},{40,56},{48,64},{56,72},{64,... | collective-permute-start | bytes 1572872 | tf_op jit(solution)/shard_map/ppermute | solution.py:210
  264.8 20.5 %collective-permute-start.11 = (bf16[256,1024]{1,0:T(8,128)(2,1)S(1)}, bf16[256,1024]{1,0:T(8,128)(2,1)S(1)}, u32[]{:S(2)}, u32[]{:S(2)}) collective-permute-start(bf16[256,1024]{1,0:T(8,128)(2,1)S(1)} %add_convert_fusion.1), channel_id=1, source_target_pairs={{0,24},{8,32},{16,40},{24,48},{32,56},{40,64},{48,72},{56,80},{64,... | collective-permute-start | bytes 1572872 | tf_op jit(solution)/shard_map/ppermute | solution.py:210
  274.0 59.2 %collective-permute-start.19 = (bf16[256,8,336]{0,2,1:T(8,128)(2,1)}, bf16[256,8,336]{0,2,1:T(8,128)(2,1)S(1)}, u32[]{:S(2)}, u32[]{:S(2)}) collective-permute-start(bf16[256,8,336]{0,2,1:T(8,128)(2,1)} %convolution_convert_fusion), channel_id=1, source_target_pairs={{0,8},{8,0},{16,24},{24,16},{32,40},{40,32},{48,56},{56,48},{64,72... | collective-permute-start | bytes 4128776 | tf_op jit(solution)/shard_map/ppermute | solution.py:281
  312.6 16.4 %copy-start.4 = (bf16[256,1024]{1,0:T(8,128)(2,1)S(1)}, bf16[256,1024]{1,0:T(8,128)(2,1)}, u32[]{:S(2)}) copy-start(bf16[256,1024]{1,0:T(8,128)(2,1)} %copy-done.3) | copy-start | bytes 1572868
  315.6 24.4 %collective-permute-start.14 = (bf16[256,1024]{1,0:T(8,128)(2,1)}, bf16[256,1024]{1,0:T(8,128)(2,1)S(1)}, u32[]{:S(2)}, u32[]{:S(2)}) collective-permute-start(bf16[256,1024]{1,0:T(8,128)(2,1)} %get-tuple-element.23), channel_id=1, source_target_pairs={{8,0},{16,8},{24,16},{32,24},{40,32},{48,40},{56,48},{64,56},{72,6... | collective-permute-start | bytes 1572872 | tf_op jit(solution)/shard_map/ppermute | solution.py:210
  324.2 34.0 %collective-permute-start.17 = (bf16[256,1024]{1,0:T(8,128)(2,1)}, bf16[256,1024]{1,0:T(8,128)(2,1)}, u32[]{:S(2)}, u32[]{:S(2)}) collective-permute-start(bf16[256,1024]{1,0:T(8,128)(2,1)} %get-tuple-element.24), channel_id=1, source_target_pairs={{32,0},{40,8},{48,16},{56,24},{64,32},{72,40},{80,48},{88,56},{96,... | collective-permute-start | bytes 1572872 | tf_op jit(solution)/shard_map/ppermute | solution.py:210
  325.5 32.7 %collective-permute-start.16 = (bf16[256,1024]{1,0:T(8,128)(2,1)}, bf16[256,1024]{1,0:T(8,128)(2,1)}, u32[]{:S(2)}, u32[]{:S(2)}) collective-permute-start(bf16[256,1024]{1,0:T(8,128)(2,1)} %get-tuple-element.25), channel_id=1, source_target_pairs={{24,0},{32,8},{40,16},{48,24},{56,32},{64,40},{72,48},{80,56},{88,... | collective-permute-start | bytes 1572872 | tf_op jit(solution)/shard_map/ppermute | solution.py:210
  326.8 31.4 %collective-permute-start.15 = (bf16[256,1024]{1,0:T(8,128)(2,1)}, bf16[256,1024]{1,0:T(8,128)(2,1)}, u32[]{:S(2)}, u32[]{:S(2)}) collective-permute-start(bf16[256,1024]{1,0:T(8,128)(2,1)} %get-tuple-element.26), channel_id=1, source_target_pairs={{16,0},{24,8},{32,16},{40,24},{48,32},{56,40},{64,48},{72,56},{80,... | collective-permute-start | bytes 1572872 | tf_op jit(solution)/shard_map/ppermute | solution.py:210
  335.4 26.3 %copy-start.1 = (bf16[672,1024]{1,0:T(8,128)(2,1)S(1)}, bf16[672,1024]{1,0:T(8,128)(2,1)}, u32[]{:S(2)}) copy-start(bf16[672,1024]{1,0:T(8,128)(2,1)} %param.9) | copy-start | bytes 4128772
  340.0 21.0 %copy-start.5 = (f32[42,1024]{1,0:T(8,128)S(1)}, f32[42,1024]{1,0:T(8,128)}, u32[]{:S(2)}) copy-start(f32[42,1024]{1,0:T(8,128)} %shard_map.104) | copy-start | bytes 516100
Sparse Core Ops, SparseCore 0:
  10.9 89.0 all-gather.2

commit v7 on v6

--- a/solution.py
+++ b/solution.py
@@ -259,11 +259,6 @@
     value_terms = value_grads(queries[0], window_keys, d_out[0], query_tags, key_tags[None, :])
     d_values_low = returned_sum(value_terms)
     w_mine, _ = lax.optimization_barrier((w_mine, d_values_low))
-    grads_all = peer_gather(d_values_low, "fsdp", 2)
-    weight_part = jnp.einsum(
-        "ftcr,ftn->crn", token_cols, grads_all, preferred_element_type=jnp.float32
-    )
-    d_weight = peer_sum_scatter(weight_part.astype(jnp.bfloat16), "ctx", 3)
 
     partner_part = jnp.einsum("tfr,frn->tn", partner_tokens, w_mine, preferred_element_type=jnp.float32)
     values = (
@@ -276,6 +271,12 @@
         queries[0], window_keys, window_values, d_out[0], query_tags, key_tags[None, :]
     )
     d_key_rows = returned_sum(key_terms)
+    grads_for_weight, _ = lax.optimization_barrier((d_values_low, key_terms))
+    grads_all = peer_gather(grads_for_weight, "fsdp", 2)
+    weight_part = jnp.einsum(
+        "ftcr,ftn->crn", token_cols, grads_all, preferred_element_type=jnp.float32
+    )
+    d_weight = peer_sum_scatter(weight_part.astype(jnp.bfloat16), "ctx", 3)
     d_mine = jnp.einsum("tn,frn->tfr", d_values_low, w_mine, preferred_element_type=jnp.float32).astype(jnp.bfloat16)
     partner_grads = lax.ppermute(d_values_low, "ctx", partner)
     d_other = lax.ppermute(

time: 376 us -> 362 us (0.963); the launches traced: 369 us -> 359 us
  starting transfers between devices: 74 us -> 62.3 us
  waiting for transfers between devices: 54.3 us -> 64.6 us
  Pallas kernels: 147 us -> 142 us
  matrix products: 27.5 us -> 22.7 us
    ppermute x16, starting transfers between devices: 60.1 us -> 48.7 us  [shifted(): return lax.ppermute(x, axis, pairs)]
    ppermute x16, waiting for transfers between devices: 54.2 us -> 64.6 us  [shifted(): return lax.ppermute(x, axis, pairs)]
    ppermute x1, starting transfers between devices: 5.73 us -> 0.06 us  [shards(): lax.ppermute(partner_part, 'ctx', partner)]
    ppermute x1, starting transfers between devices: 0.01 us -> 5.51 us  [shards(): partner_grads = lax.ppermute(d_values_low, 'ctx', partner)]
    pallas_call x1, Pallas kernels: 80.4 us -> 76.2 us  [peer_gather(): pl.pallas_call(functools.partial(peer_gather_kernel, axis, n), out_shape=...]
    unnamed x27 -> x31, local copies, waits for them, and re-layouts: 18.9 us -> 19.8 us
  transfers between devices with their start and end apart: 22 -> 22, of which waited for: 5 -> 6; matrix products, arithmetic and copies ran while one was open for 20% -> 19% of each run, Pallas kernels for 40% -> 40%
where the time goes in v7:
time: 362 us; the launch traced here: 359 us
  Pallas kernels  142 us (39%)
  waiting for transfers between devices  64.6 us (18%)
  starting transfers between devices  62.3 us (17%)
  local copies, waits for them, and re-layouts  43.5 us (12%)
  matrix products  22.7 us (6%)
  between operations  14.4 us (4%)
  other arithmetic  8.87 us (2%)
    pallas_call x1, Pallas kernels, peer_gather(): pl.pallas_call(functools.partial(peer_gather_kernel, axis, n), out_shape=...  76.2 us
    ppermute x16, waiting for transfers between devices, shifted(): return lax.ppermute(x, axis, pairs)  64.6 us
    ppermute x16, starting transfers between devices, shifted(): return lax.ppermute(x, axis, pairs)  48.7 us
    pallas_call x1, Pallas kernels, peer_sum_scatter(): pl.pallas_call(functools.partial(peer_sum_kernel, axis, n), out_shape=jax...  27 us
    pallas_call x1, Pallas kernels, fused_attention(): pl.pallas_call(attention_kernel, grid=(heads,), in_specs=[q_spec, kv_spec...  24 us
    unnamed x31, local copies, waits for them, and re-layouts  19.8 us
    pallas_call x1, Pallas kernels, value_grads(): pl.pallas_call(value_grad_kernel, grid=(heads,), in_specs=[q_spec, kv_spe...  15.2 us
    dot_general x1, matrix products, shards(): jnp.einsum('ftcr,ftn->crn', token_cols, grads_all, preferred_element_type...  7.84 us
  transfers between devices with their start and end apart: 22, of which 6 were waited for; matrix products, arithmetic and copies ran while one was open for 19% of the time, Pallas kernels for 40%

profile of v7, /device:TPU:28, one launch (start us, length us, event | category | flops | bytes accessed | tf_op | source)
XLA Modules:
  0.0 358.7 jit_solution(15041911455170091026)
XLA Ops:
  11.3 4.7 %collective-permute-start = (bf16[256,1152]{1,0:T(8,128)(2,1)S(1)}, bf16[256,1152]{1,0:T(8,128)(2,1)}, u32[]{:S(2)}, u32[]{:S(2)}) collective-permute-start(bf16[256,1152]{1,0:T(8,128)(2,1)S(1)} %pad_maximum_fusion), channel_id=1, source_target_pairs={{0,32},{8,40},{16,48},{24,56},{32,64},{40,72},{48,80},{56,88},{64,... | collective-permute-start | bytes 1769480 | tf_op jit(solution)/shard_map/ppermute | solution.py:210
  16.0 3.2 collective-permute-start.1
  21.1 3.7 %collective-permute-start.2 = (bf16[256,1152]{1,0:T(8,128)(2,1)S(1)}, bf16[256,1152]{1,0:T(8,128)(2,1)}, u32[]{:S(2)}, u32[]{:S(2)}) collective-permute-start(bf16[256,1152]{1,0:T(8,128)(2,1)S(1)} %pad_maximum_fusion), channel_id=1, source_target_pairs={{0,16},{8,24},{16,32},{24,40},{32,48},{40,56},{48,64},{56,72},{64,... | collective-permute-start | bytes 1769480 | tf_op jit(solution)/shard_map/ppermute | solution.py:210
  24.8 4.5 %copy.20 = bf16[1,256,5376]{1,2,0:T(8,128)(2,1)} copy(bf16[1,256,5376]{2,1,0:T(8,128)(2,1)} %param.6) | data formatting | bytes 5505024 | tf_op args[0]
  29.3 2.6 dynamic-slice_bitcast_fusion
  35.6 14.2 %collective-permute-done.2 = bf16[256,1152]{1,0:T(8,128)(2,1)} collective-permute-done((bf16[256,1152]{1,0:T(8,128)(2,1)S(1)}, bf16[256,1152]{1,0:T(8,128)(2,1)}, u32[]{:S(2)}, u32[]{:S(2)}) %collective-permute-start.2) | collective-permute-done | bytes 589856 | tf_op jit(solution)/shard_map/ppermute | solution.py:210
  53.9 15.2 %shard_map.101 = bf16[1280,1024]{1,0:T(8,128)(2,1)} custom-call(bf16[256,2048]{1,0:T(8,128)(2,1)} %bitcast.72, bf16[1280,1024]{1,0:T(8,128)(2,1)} %slice.48.k_ref, bf16[256,2048]{1,0:T(8,128)(2,1)} %bitcast.74, s32[256,1]{1,0:T(8,128)} %copy.21.qtag_ref, s32[1,1280]{1,0:T(1,128)} %compare_select_fusion.ktag_ref), custom_call_target="tpu_custom_call" | custom-call | flops 2684354560 | bytes 7340032 | tf_op jit(solution)/shard_map/pallas_call | solution.py:79
  70.8 13.0 %collective-permute-start.4 = (bf16[256,1024]{1,0:T(8,128)(2,1)S(1)}, bf16[256,1024]{1,0:T(8,128)(2,1)S(1)}, u32[]{:S(2)}, u32[]{:S(2)}) collective-permute-start(bf16[256,1024]{1,0:T(8,128)(2,1)S(1)} %get-tuple-element.29), channel_id=1, source_target_pairs={{8,0},{16,8},{24,16},{32,24},{40,32},{48,40},{56,48},{64,56},{72,6... | collective-permute-start | bytes 1572872 | tf_op jit(solution)/shard_map/ppermute | solution.py:210
  88.4 9.5 %collective-permute-done.4 = bf16[256,1024]{1,0:T(8,128)(2,1)S(1)} collective-permute-done((bf16[256,1024]{1,0:T(8,128)(2,1)S(1)}, bf16[256,1024]{1,0:T(8,128)(2,1)S(1)}, u32[]{:S(2)}, u32[]{:S(2)}) %collective-permute-start.4) | collective-permute-done | bytes 524320 | tf_op jit(solution)/shard_map/ppermute | solution.py:210
  97.9 18.6 %collective-permute-done.7 = bf16[256,1024]{1,0:T(8,128)(2,1)S(1)} collective-permute-done((bf16[256,1024]{1,0:T(8,128)(2,1)S(1)}, bf16[256,1024]{1,0:T(8,128)(2,1)S(1)}, u32[]{:S(2)}, u32[]{:S(2)}) %collective-permute-start.7) | collective-permute-done | bytes 524320 | tf_op jit(solution)/shard_map/ppermute | solution.py:210
  118.0 5.5 %collective-permute-start.18 = (bf16[256,1024]{1,0:T(8,128)(2,1)S(1)}, bf16[256,1024]{1,0:T(8,128)(2,1)S(1)}, u32[]{:S(2)}, u32[]{:S(2)}) collective-permute-start(bf16[256,1024]{1,0:T(8,128)(2,1)S(1)} %add_convert_fusion.2.x_ref), channel_id=1, source_target_pairs={{0,8},{8,0},{16,24},{24,16},{32,40},{40,32},{48,56},{56,48},{64,72... | collective-permute-start | bytes 1572872 | tf_op jit(solution)/shard_map/ppermute | solution.py:281
  123.5 5.4 %convolution_bitcast_fusion = f32[256,1024]{1,0:T(8,128)} fusion(bf16[256,8,336]{0,2,1:T(8,128)(2,1)S(1)} %collective-permute-done.8, bf16[8,336,1024]{2,1,0:T(8,128)(2,1)} %bitcast.57), kind=kOutput, calls=%fused_computation.14 | convolution fusion | flops 1409286144 | bytes 7929856 | tf_op jit(solution)/shard_map/tfr,frn->tn/dot_general | solution.py:263
  129.0 2.8 convolution_convert_fusion
  132.3 5.3 %reshape_squeeze.7 = bf16[256,16,8,42]{0,3,2,1:T(8,128)(2,1)} reshape(bf16[1,256,5376]{1,2,0:T(8,128)(2,1)} %copy.20) | data formatting | bytes 5505024 | tf_op jit(solution)/shard_map/reshape;squeeze | solution.py:237
  137.6 5.0 %copy.25 = bf16[8,256,16,42]{1,2,3,0:T(8,128)(2,1)} copy(bf16[8,256,16,42]{1,3,0,2:T(8,128)(2,1)} %bitcast.67) | data formatting | bytes 5505024 | tf_op jit(solution)/shard_map/transpose | solution.py:237
  142.5 7.2 %all-to-all-start = ((bf16[8,256,16,42]{1,2,3,0:T(8,128)(2,1)}), bf16[8,256,16,42]{1,2,3,0:T(8,128)(2,1)}, u32[]{:S(2)}, u32[]{:S(2)}) async-start(bf16[8,256,16,42]{1,2,3,0:T(8,128)(2,1)} %copy.25), calls=%async_computation | async-start | bytes 5505024 | tf_op jit(solution)/shard_map/all_to_all | solution.py:239
  149.7 5.0 %add_convert_fusion.1 = bf16[256,1024]{1,0:T(8,128)(2,1)S(1)} fusion(f32[256,1024]{1,0:T(8,128)} %collective-permute-done.9, bf16[8,336,1024]{2,1,0:T(8,128)(2,1)} %bitcast.58, bf16[256,8,2,336]{0,3,2,1:T(8,128)(2,1)} %bitcast.66, s32[]{:T(128)S(6)} %select_n.47), kind=kOutput, calls=%fused_computation.16 | convolution fusion | flops 1409810432 | bytes 8454148 | tf_op jit(solution)/shard_map/tfr,frn->tn/dot_general | solution.py:265
  154.8 2.1 collective-permute-start.11
  156.9 4.1 %collective-permute-start.10 = (bf16[256,1024]{1,0:T(8,128)(2,1)S(1)}, bf16[256,1024]{1,0:T(8,128)(2,1)}, u32[]{:S(2)}, u32[]{:S(2)}) collective-permute-start(bf16[256,1024]{1,0:T(8,128)(2,1)S(1)} %add_convert_fusion.1), channel_id=1, source_target_pairs={{0,32},{8,40},{16,48},{24,56},{32,64},{40,72},{48,80},{56,88},{64,... | collective-permute-start | bytes 1572872 | tf_op jit(solution)/shard_map/ppermute | solution.py:210
  162.6 3.0 collective-permute-start.13
  165.7 1.9 collective-permute-start.12
  167.6 2.3 maximum_select_fusion
  171.6 4.5 %copy.27 = bf16[1,256,5376]{2,1,0:T(8,128)(2,1)} copy(bf16[1,256,5376]{1,2,0:T(8,128)(2,1)} %bitcast.68) | data formatting | bytes 5505024
  178.0 12.7 %collective-permute-done.11 = bf16[256,1024]{1,0:T(8,128)(2,1)} collective-permute-done((bf16[256,1024]{1,0:T(8,128)(2,1)S(1)}, bf16[256,1024]{1,0:T(8,128)(2,1)}, u32[]{:S(2)}, u32[]{:S(2)}) %collective-permute-start.11) | collective-permute-done | bytes 524320 | tf_op jit(solution)/shard_map/ppermute | solution.py:210
  192.5 9.3 %collective-permute-done.12 = bf16[256,1024]{1,0:T(8,128)(2,1)S(1)} collective-permute-done((bf16[256,1024]{1,0:T(8,128)(2,1)S(1)}, bf16[256,1024]{1,0:T(8,128)(2,1)S(1)}, u32[]{:S(2)}, u32[]{:S(2)}) %collective-permute-start.12) | collective-permute-done | bytes 524320 | tf_op jit(solution)/shard_map/ppermute | solution.py:210
  204.3 24.0 %shard_map.102 = (bf16[256,2048]{1,0:T(8,128)(2,1)}, bf16[256,2048]{1,0:T(8,128)(2,1)}, bf16[1280,1024]{1,0:T(8,128)(2,1)}) custom-call(bf16[256,2048]{1,0:T(8,128)(2,1)} %bitcast.73, bf16[1280,1024]{1,0:T(8,128)(2,1)} %slice.48.k_ref, bf16[1280,1024]{1,0:T(8,128)(2,1)} %constant_dynamic-update-slice_fusion.5.v_ref, bf16[256,2048]{1,0:T(8,128)(2,1)} %bitcast.75, ...), custom_call_target="tpu_custom_call" | custom-call | flops 6710886400 | bytes 12058624 | tf_op jit(solution)/shard_map/pallas_call | solution.py:98
  228.2 2.9 fusion.25
  235.6 2.1 collective-permute-start.15
  237.8 76.2 %shard_map.103 = bf16[8,256,1024]{2,1,0:T(8,128)(2,1)} custom-call(bf16[256,1024]{1,0:T(8,128)(2,1)} %copy-done.3), custom_call_target="tpu_custom_call" | custom-call | tf_op jit(solution)/shard_map/pallas_call | solution.py:145
  314.0 7.8 %fusion.7.x_ref = bf16[16,42,1024]{2,1,0:T(8,128)(2,1)} fusion(bf16[8,256,16,42]{1,2,3,0:T(8,128)(2,1)} %all-to-all-done, bf16[8,256,1024]{2,1,0:T(8,128)(2,1)} %shard_map.103), kind=kOutput, calls=%fused_computation.7 | convolution fusion | flops 2819260416 | bytes 8323072 | tf_op jit(solution)/shard_map/ftcr,ftn->crn/dot_general | solution.py:276
  321.8 27.0 %shard_map.104 = f32[42,1024]{1,0:T(8,128)} custom-call(bf16[16,42,1024]{2,1,0:T(8,128)(2,1)} %fusion.7.x_ref), custom_call_target="tpu_custom_call" | custom-call | tf_op jit(solution)/shard_map/pallas_call | solution.py:192
  348.8 2.3 fusion.19
  (74 shorter events, 36.9 us)
Async XLA Ops:
  7.2 1.3 copy-start
  7.2 116.3 %all-gather.3.cloned.1.call-start = ((), (), s32[]{:S(2)}) async-start(), calls=%async_computation.1 | async-start | bytes 6193152 | tf_op jit(solution)/shard_map/all_gather | solution.py:226
  11.3 21.7 %collective-permute-start = (bf16[256,1152]{1,0:T(8,128)(2,1)S(1)}, bf16[256,1152]{1,0:T(8,128)(2,1)}, u32[]{:S(2)}, u32[]{:S(2)}) collective-permute-start(bf16[256,1152]{1,0:T(8,128)(2,1)S(1)} %pad_maximum_fusion), channel_id=1, source_target_pairs={{0,32},{8,40},{16,48},{24,56},{32,64},{40,72},{48,80},{56,88},{64,... | collective-permute-start | bytes 1769480 | tf_op jit(solution)/shard_map/ppermute | solution.py:210
  16.0 18.5 %collective-permute-start.1 = (bf16[256,1152]{1,0:T(8,128)(2,1)S(1)}, bf16[256,1152]{1,0:T(8,128)(2,1)}, u32[]{:S(2)}, u32[]{:S(2)}) collective-permute-start(bf16[256,1152]{1,0:T(8,128)(2,1)S(1)} %pad_maximum_fusion), channel_id=1, source_target_pairs={{0,24},{8,32},{16,40},{24,48},{32,56},{40,64},{48,72},{56,80},{64,... | collective-permute-start | bytes 1769480 | tf_op jit(solution)/shard_map/ppermute | solution.py:210
  19.2 31.8 %collective-permute-start.3 = (bf16[256,1152]{1,0:T(8,128)(2,1)S(1)}, bf16[256,1152]{1,0:T(8,128)(2,1)S(1)}, u32[]{:S(2)}, u32[]{:S(2)}) collective-permute-start(bf16[256,1152]{1,0:T(8,128)(2,1)S(1)} %pad_maximum_fusion), channel_id=1, source_target_pairs={{0,8},{8,16},{16,24},{24,32},{32,40},{40,48},{48,56},{56,64},{64,7... | collective-permute-start | bytes 1769480 | tf_op jit(solution)/shard_map/ppermute | solution.py:210
  21.1 28.7 %collective-permute-start.2 = (bf16[256,1152]{1,0:T(8,128)(2,1)S(1)}, bf16[256,1152]{1,0:T(8,128)(2,1)}, u32[]{:S(2)}, u32[]{:S(2)}) collective-permute-start(bf16[256,1152]{1,0:T(8,128)(2,1)S(1)} %pad_maximum_fusion), channel_id=1, source_target_pairs={{0,16},{8,24},{16,32},{24,40},{32,48},{40,56},{48,64},{56,72},{64,... | collective-permute-start | bytes 1769480 | tf_op jit(solution)/shard_map/ppermute | solution.py:210
  29.2 2.9 copy-start.5
  31.8 19.2 %copy-start.2 = (bf16[1,256,1024]{2,1,0:T(8,128)(2,1)S(1)}, bf16[1,256,1024]{2,1,0:T(8,128)(2,1)}, u32[]{:S(2)}) copy-start(bf16[1,256,1024]{2,1,0:T(8,128)(2,1)} %param.8) | copy-start | bytes 1572868
  31.8 91.7 %collective-permute-start.8 = (bf16[256,8,336]{0,2,1:T(8,128)(2,1)}, bf16[256,8,336]{0,2,1:T(8,128)(2,1)S(1)}, u32[]{:S(2)}, u32[]{:S(2)}) collective-permute-start(bf16[256,8,336]{0,2,1:T(8,128)(2,1)} %dynamic-slice_bitcast_fusion), channel_id=1, source_target_pairs={{0,8},{8,0},{16,24},{24,16},{32,40},{40,32},{48,56},{56,48},{64,72... | collective-permute-start | bytes 4128776 | tf_op jit(solution)/shard_map/ppermute | solution.py:232
  70.8 27.0 %collective-permute-start.4 = (bf16[256,1024]{1,0:T(8,128)(2,1)S(1)}, bf16[256,1024]{1,0:T(8,128)(2,1)S(1)}, u32[]{:S(2)}, u32[]{:S(2)}) collective-permute-start(bf16[256,1024]{1,0:T(8,128)(2,1)S(1)} %get-tuple-element.29), channel_id=1, source_target_pairs={{8,0},{16,8},{24,16},{32,24},{40,32},{48,40},{56,48},{64,56},{72,6... | collective-permute-start | bytes 1572872 | tf_op jit(solution)/shard_map/ppermute | solution.py:210
  83.9 32.6 %collective-permute-start.7 = (bf16[256,1024]{1,0:T(8,128)(2,1)S(1)}, bf16[256,1024]{1,0:T(8,128)(2,1)S(1)}, u32[]{:S(2)}, u32[]{:S(2)}) collective-permute-start(bf16[256,1024]{1,0:T(8,128)(2,1)S(1)} %get-tuple-element.30), channel_id=1, source_target_pairs={{32,0},{40,8},{48,16},{56,24},{64,32},{72,40},{80,48},{88,56},{96,... | collective-permute-start | bytes 1572872 | tf_op jit(solution)/shard_map/ppermute | solution.py:210
  85.2 31.3 %collective-permute-start.6 = (bf16[256,1024]{1,0:T(8,128)(2,1)S(1)}, bf16[256,1024]{1,0:T(8,128)(2,1)S(1)}, u32[]{:S(2)}, u32[]{:S(2)}) collective-permute-start(bf16[256,1024]{1,0:T(8,128)(2,1)S(1)} %get-tuple-element.31), channel_id=1, source_target_pairs={{24,0},{32,8},{40,16},{48,24},{56,32},{64,40},{72,48},{80,56},{88,... | collective-permute-start | bytes 1572872 | tf_op jit(solution)/shard_map/ppermute | solution.py:210
  86.5 30.0 %collective-permute-start.5 = (bf16[256,1024]{1,0:T(8,128)(2,1)S(1)}, bf16[256,1024]{1,0:T(8,128)(2,1)S(1)}, u32[]{:S(2)}, u32[]{:S(2)}) collective-permute-start(bf16[256,1024]{1,0:T(8,128)(2,1)S(1)} %get-tuple-element.32), channel_id=1, source_target_pairs={{16,0},{24,8},{32,16},{40,24},{48,32},{56,40},{64,48},{72,56},{80,... | collective-permute-start | bytes 1572872 | tf_op jit(solution)/shard_map/ppermute | solution.py:210
  118.0 43.0 %copy-start.3 = (bf16[256,1024]{1,0:T(8,128)(2,1)}, bf16[256,1024]{1,0:T(8,128)(2,1)S(1)}, u32[]{:S(2)}) copy-start(bf16[256,1024]{1,0:T(8,128)(2,1)S(1)} %add_convert_fusion.2.x_ref) | copy-start | bytes 1572868
  118.0 11.0 %collective-permute-start.18 = (bf16[256,1024]{1,0:T(8,128)(2,1)S(1)}, bf16[256,1024]{1,0:T(8,128)(2,1)S(1)}, u32[]{:S(2)}, u32[]{:S(2)}) collective-permute-start(bf16[256,1024]{1,0:T(8,128)(2,1)S(1)} %add_convert_fusion.2.x_ref), channel_id=1, source_target_pairs={{0,8},{8,0},{16,24},{24,16},{32,40},{40,32},{48,56},{56,48},{64,72... | collective-permute-start | bytes 1572872 | tf_op jit(solution)/shard_map/ppermute | solution.py:281
  123.5 5.4 %slice-start = ((s8[5505024]{0:T(1024)(128)(4,1)}), s8[4194304]{0:T(1024)(128)(4,1)S(1)}, s32[]{:S(2)}) async-start(s8[5505024]{0:T(1024)(128)(4,1)} %bitcast.59), calls=%async_computation.2 | async-start | bytes 8388608
  123.5 5.4 %slice-start.1 = ((s8[5505024]{0:T(1024)(128)(4,1)}), s8[1310720]{0:T(1024)(128)(4,1)S(1)}, s32[]{:S(2)}) async-start(s8[5505024]{0:T(1024)(128)(4,1)} %bitcast.59), calls=%async_computation.3 | async-start | bytes 2621440
  128.9 20.8 %collective-permute-start.9 = (f32[256,1024]{1,0:T(8,128)}, f32[256,1024]{1,0:T(8,128)}, u32[]{:S(2)}, u32[]{:S(2)}) collective-permute-start(f32[256,1024]{1,0:T(8,128)} %convolution_bitcast_fusion), channel_id=1, source_target_pairs={{0,8},{8,0},{16,24},{24,16},{32,40},{40,32},{48,56},{56,48},{64,72... | collective-permute-start | bytes 3145736 | tf_op jit(solution)/shard_map/ppermute | solution.py:266
  131.8 35.8 %collective-permute-start.19 = (bf16[256,8,336]{0,2,1:T(8,128)(2,1)}, bf16[256,8,336]{0,2,1:T(8,128)(2,1)}, u32[]{:S(2)}, u32[]{:S(2)}) collective-permute-start(bf16[256,8,336]{0,2,1:T(8,128)(2,1)} %convolution_convert_fusion), channel_id=1, source_target_pairs={{0,8},{8,0},{16,24},{24,16},{32,40},{40,32},{48,56},{56,48},{64,72... | collective-permute-start | bytes 4128776 | tf_op jit(solution)/shard_map/ppermute | solution.py:282
  142.5 171.4 %all-to-all-start = ((bf16[8,256,16,42]{1,2,3,0:T(8,128)(2,1)}), bf16[8,256,16,42]{1,2,3,0:T(8,128)(2,1)}, u32[]{:S(2)}, u32[]{:S(2)}) async-start(bf16[8,256,16,42]{1,2,3,0:T(8,128)(2,1)} %copy.25), calls=%async_computation | async-start | bytes 5505024 | tf_op jit(solution)/shard_map/all_to_all | solution.py:239
  149.7 11.3 %slice-start.2 = ((s8[5505024]{0:T(1024)(128)(4,1)}), s8[1310720]{0:T(1024)(128)(4,1)S(1)}, s32[]{:S(2)}) async-start(s8[5505024]{0:T(1024)(128)(4,1)} %bitcast.62), calls=%async_computation.4 | async-start | bytes 2621440
  149.7 11.3 %slice-start.3 = ((s8[5505024]{0:T(1024)(128)(4,1)}), s8[4194304]{0:T(1024)(128)(4,1)S(1)}, s32[]{:S(2)}) async-start(s8[5505024]{0:T(1024)(128)(4,1)} %bitcast.62), calls=%async_computation.5 | async-start | bytes 8388608
  154.8 35.9 %collective-permute-start.11 = (bf16[256,1024]{1,0:T(8,128)(2,1)S(1)}, bf16[256,1024]{1,0:T(8,128)(2,1)}, u32[]{:S(2)}, u32[]{:S(2)}) collective-permute-start(bf16[256,1024]{1,0:T(8,128)(2,1)S(1)} %add_convert_fusion.1), channel_id=1, source_target_pairs={{0,24},{8,32},{16,40},{24,48},{32,56},{40,64},{48,72},{56,80},{64,... | collective-permute-start | bytes 1572872 | tf_op jit(solution)/shard_map/ppermute | solution.py:210
  156.9 19.2 %collective-permute-start.10 = (bf16[256,1024]{1,0:T(8,128)(2,1)S(1)}, bf16[256,1024]{1,0:T(8,128)(2,1)}, u32[]{:S(2)}, u32[]{:S(2)}) collective-permute-start(bf16[256,1024]{1,0:T(8,128)(2,1)S(1)} %add_convert_fusion.1), channel_id=1, source_target_pairs={{0,32},{8,40},{16,48},{24,56},{32,64},{40,72},{48,80},{56,88},{64,... | collective-permute-start | bytes 1572872 | tf_op jit(solution)/shard_map/ppermute | solution.py:210
  162.6 40.0 %collective-permute-start.13 = (bf16[256,1024]{1,0:T(8,128)(2,1)S(1)}, bf16[256,1024]{1,0:T(8,128)(2,1)S(1)}, u32[]{:S(2)}, u32[]{:S(2)}) collective-permute-start(bf16[256,1024]{1,0:T(8,128)(2,1)S(1)} %add_convert_fusion.1), channel_id=1, source_target_pairs={{0,8},{8,16},{16,24},{24,32},{32,40},{40,48},{48,56},{56,64},{64,7... | collective-permute-start | bytes 1572872 | tf_op jit(solution)/shard_map/ppermute | solution.py:210
  165.7 36.1 %collective-permute-start.12 = (bf16[256,1024]{1,0:T(8,128)(2,1)S(1)}, bf16[256,1024]{1,0:T(8,128)(2,1)S(1)}, u32[]{:S(2)}, u32[]{:S(2)}) collective-permute-start(bf16[256,1024]{1,0:T(8,128)(2,1)S(1)} %add_convert_fusion.1), channel_id=1, source_target_pairs={{0,16},{8,24},{16,32},{24,40},{32,48},{40,56},{48,64},{56,72},{64,... | collective-permute-start | bytes 1572872 | tf_op jit(solution)/shard_map/ppermute | solution.py:210
  231.1 117.7 %collective-permute-start.14 = (bf16[256,1024]{1,0:T(8,128)(2,1)}, bf16[256,1024]{1,0:T(8,128)(2,1)S(1)}, u32[]{:S(2)}, u32[]{:S(2)}) collective-permute-start(bf16[256,1024]{1,0:T(8,128)(2,1)} %get-tuple-element.25), channel_id=1, source_target_pairs={{8,0},{16,8},{24,16},{32,24},{40,32},{48,40},{56,48},{64,56},{72,6... | collective-permute-start | bytes 1572872 | tf_op jit(solution)/shard_map/ppermute | solution.py:210
  233.0 115.8 %collective-permute-start.17 = (bf16[256,1024]{1,0:T(8,128)(2,1)}, bf16[256,1024]{1,0:T(8,128)(2,1)S(1)}, u32[]{:S(2)}, u32[]{:S(2)}) collective-permute-start(bf16[256,1024]{1,0:T(8,128)(2,1)} %get-tuple-element.26), channel_id=1, source_target_pairs={{32,0},{40,8},{48,16},{56,24},{64,32},{72,40},{80,48},{88,56},{96,... | collective-permute-start | bytes 1572872 | tf_op jit(solution)/shard_map/ppermute | solution.py:210
  234.3 114.5 %collective-permute-start.16 = (bf16[256,1024]{1,0:T(8,128)(2,1)}, bf16[256,1024]{1,0:T(8,128)(2,1)S(1)}, u32[]{:S(2)}, u32[]{:S(2)}) collective-permute-start(bf16[256,1024]{1,0:T(8,128)(2,1)} %get-tuple-element.27), channel_id=1, source_target_pairs={{24,0},{32,8},{40,16},{48,24},{56,32},{64,40},{72,48},{80,56},{88,... | collective-permute-start | bytes 1572872 | tf_op jit(solution)/shard_map/ppermute | solution.py:210
  235.6 113.2 %collective-permute-start.15 = (bf16[256,1024]{1,0:T(8,128)(2,1)}, bf16[256,1024]{1,0:T(8,128)(2,1)S(1)}, u32[]{:S(2)}, u32[]{:S(2)}) collective-permute-start(bf16[256,1024]{1,0:T(8,128)(2,1)} %get-tuple-element.28), channel_id=1, source_target_pairs={{16,0},{24,8},{32,16},{40,24},{48,32},{56,40},{64,48},{72,56},{80,... | collective-permute-start | bytes 1572872 | tf_op jit(solution)/shard_map/ppermute | solution.py:210
  314.0 37.9 %copy-start.1 = (bf16[672,1024]{1,0:T(8,128)(2,1)S(1)}, bf16[672,1024]{1,0:T(8,128)(2,1)}, u32[]{:S(2)}) copy-start(bf16[672,1024]{1,0:T(8,128)(2,1)} %param.9) | copy-start | bytes 4128772
  348.8 2.4 copy-start.4
Sparse Core Ops, SparseCore 0:
  10.9 91.5 all-gather.2

commit v8 on v7

--- a/solution.py
+++ b/solution.py
@@ -259,6 +259,7 @@
     value_terms = value_grads(queries[0], window_keys, d_out[0], query_tags, key_tags[None, :])
     d_values_low = returned_sum(value_terms)
     w_mine, _ = lax.optimization_barrier((w_mine, d_values_low))
+    grads_all = lax.all_gather(d_values_low, "fsdp", axis=0, tiled=False)
 
     partner_part = jnp.einsum("tfr,frn->tn", partner_tokens, w_mine, preferred_element_type=jnp.float32)
     values = (
@@ -271,8 +272,7 @@
         queries[0], window_keys, window_values, d_out[0], query_tags, key_tags[None, :]
     )
     d_key_rows = returned_sum(key_terms)
-    grads_for_weight, _ = lax.optimization_barrier((d_values_low, key_terms))
-    grads_all = peer_gather(grads_for_weight, "fsdp", 2)
+    grads_all, _ = lax.optimization_barrier((grads_all, key_terms))
     weight_part = jnp.einsum(
         "ftcr,ftn->crn", token_cols, grads_all, preferred_element_type=jnp.float32
     )

time: 362 us -> 330 us (0.912)
  Pallas kernels: 142 us -> 86.1 us
  waiting for transfers between devices: 64.6 us -> 95.6 us
  starting transfers between devices: 62.3 us -> 57.3 us
    pallas_call x1 -> x0, Pallas kernels: 76.2 us -> none  [peer_gather(): pl.pallas_call(functools.partial(peer_gather_kernel, axis, n), out_shape=...]
    ppermute x16, waiting for transfers between devices: 64.6 us -> 91.8 us  [shifted(): return lax.ppermute(x, axis, pairs)]
    pallas_call x1, Pallas kernels: 27 us -> 46.6 us  [peer_sum_scatter(): pl.pallas_call(functools.partial(peer_sum_kernel, axis, n), out_shape=jax...]
    ppermute x1, starting transfers between devices: 0.34 us -> 7.18 us  [shards(): lax.ppermute(lax.dynamic_index_in_dim(token_halves, 1 - core, axis=2, kee...]
    ppermute x16, starting transfers between devices: 48.7 us -> 42.3 us  [shifted(): return lax.ppermute(x, axis, pairs)]
    ppermute x1, starting transfers between devices: 5.51 us -> 0.01 us  [shards(): partner_grads = lax.ppermute(d_values_low, 'ctx', partner)]
    ppermute x1, waiting for transfers between devices: 0.01 us -> 3.69 us  [shards(): lax.ppermute(lax.dynamic_index_in_dim(token_halves, 1 - core, axis=2, kee...]
  transfers between devices with their start and end apart: 22 -> 23, of which waited for: 6 -> 11; matrix products, arithmetic and copies ran while one was open for 19% -> 21% of each run, Pallas kernels for 40% -> 26%
where the time goes in v8:
time: 330 us; the launch traced here: 327 us
  waiting for transfers between devices  95.6 us (29%)
  Pallas kernels  86.1 us (26%)
  starting transfers between devices  57.3 us (17%)
  local copies, waits for them, and re-layouts  41.3 us (13%)
  matrix products  22.6 us (7%)
  between operations  14.4 us (4%)
  other arithmetic  9.62 us (3%)
    ppermute x16, waiting for transfers between devices, shifted(): return lax.ppermute(x, axis, pairs)  91.8 us
    pallas_call x1, Pallas kernels, peer_sum_scatter(): pl.pallas_call(functools.partial(peer_sum_kernel, axis, n), out_shape=jax...  46.6 us
    ppermute x16, starting transfers between devices, shifted(): return lax.ppermute(x, axis, pairs)  42.3 us
    pallas_call x1, Pallas kernels, fused_attention(): pl.pallas_call(attention_kernel, grid=(heads,), in_specs=[q_spec, kv_spec...  24 us
    unnamed x31, local copies, waits for them, and re-layouts  17.7 us
    pallas_call x1, Pallas kernels, value_grads(): pl.pallas_call(value_grad_kernel, grid=(heads,), in_specs=[q_spec, kv_spe...  15.5 us
    dot_general x1, matrix products, shards(): jnp.einsum('ftcr,ftn->crn', token_cols, grads_all, preferred_element_type...  7.79 us
    all_to_all x1, starting transfers between devices, shards(): token_cols = lax.all_to_all(token_cols, 'fsdp', 0, 0, tiled=True)  7.21 us
  transfers between devices with their start and end apart: 23, of which 11 were waited for; matrix products, arithmetic and copies ran while one was open for 21% of the time, Pallas kernels for 26%

profile of v8, /device:TPU:28, one launch (start us, length us, event | category | flops | bytes accessed | tf_op | source)
XLA Modules:
  0.0 326.9 jit_solution(8009082227433142881)
XLA Ops:
  11.4 4.6 %collective-permute-start = (bf16[256,1152]{1,0:T(8,128)(2,1)S(1)}, bf16[256,1152]{1,0:T(8,128)(2,1)}, u32[]{:S(2)}, u32[]{:S(2)}) collective-permute-start(bf16[256,1152]{1,0:T(8,128)(2,1)S(1)} %pad_maximum_fusion), channel_id=1, source_target_pairs={{0,32},{8,40},{16,48},{24,56},{32,64},{40,72},{48,80},{56,88},{64,... | collective-permute-start | bytes 1769480 | tf_op jit(solution)/shard_map/ppermute | solution.py:210
  16.1 2.4 collective-permute-start.1
  18.5 3.2 collective-permute-start.2
  21.7 2.9 collective-permute-start.3
  25.4 3.6 %collective-permute-done = bf16[256,1152]{1,0:T(8,128)(2,1)} collective-permute-done((bf16[256,1152]{1,0:T(8,128)(2,1)S(1)}, bf16[256,1152]{1,0:T(8,128)(2,1)}, u32[]{:S(2)}, u32[]{:S(2)}) %collective-permute-start) | collective-permute-done | bytes 589856 | tf_op jit(solution)/shard_map/ppermute | solution.py:210
  30.1 2.9 collective-permute-done.1
  33.1 17.2 %collective-permute-done.2 = bf16[256,1152]{1,0:T(8,128)(2,1)S(1)} collective-permute-done((bf16[256,1152]{1,0:T(8,128)(2,1)S(1)}, bf16[256,1152]{1,0:T(8,128)(2,1)S(1)}, u32[]{:S(2)}, u32[]{:S(2)}) %collective-permute-start.2) | collective-permute-done | bytes 589856 | tf_op jit(solution)/shard_map/ppermute | solution.py:210
  50.3 3.0 collective-permute-done.3
  56.3 15.5 %shard_map.101 = bf16[1280,1024]{1,0:T(8,128)(2,1)} custom-call(bf16[256,2048]{1,0:T(8,128)(2,1)} %bitcast.74, bf16[1280,1024]{1,0:T(8,128)(2,1)} %slice.48.k_ref, bf16[256,2048]{1,0:T(8,128)(2,1)} %bitcast.76, s32[256,1]{1,0:T(8,128)} %copy.21.qtag_ref, s32[1,1280]{1,0:T(1,128)} %compare_select_fusion.ktag_ref), custom_call_target="tpu_custom_call" | custom-call | flops 2684354560 | bytes 7340032 | tf_op jit(solution)/shard_map/pallas_call | solution.py:79
  76.1 4.5 %collective-permute-start.5 = (bf16[256,1024]{1,0:T(8,128)(2,1)S(1)}, bf16[256,1024]{1,0:T(8,128)(2,1)S(1)}, u32[]{:S(2)}, u32[]{:S(2)}) collective-permute-start(bf16[256,1024]{1,0:T(8,128)(2,1)S(1)} %get-tuple-element.32), channel_id=1, source_target_pairs={{16,0},{24,8},{32,16},{40,24},{48,32},{56,40},{64,48},{72,56},{80,... | collective-permute-start | bytes 1572872 | tf_op jit(solution)/shard_map/ppermute | solution.py:210
  80.7 5.0 %collective-permute-start.4 = (bf16[256,1024]{1,0:T(8,128)(2,1)S(1)}, bf16[256,1024]{1,0:T(8,128)(2,1)S(1)}, u32[]{:S(2)}, u32[]{:S(2)}) collective-permute-start(bf16[256,1024]{1,0:T(8,128)(2,1)S(1)} %get-tuple-element.29), channel_id=1, source_target_pairs={{8,0},{16,8},{24,16},{32,24},{40,32},{48,40},{56,48},{64,56},{72,6... | collective-permute-start | bytes 1572872 | tf_op jit(solution)/shard_map/ppermute | solution.py:210
  85.7 2.9 collective-permute-done.7
  88.6 10.0 %collective-permute-done.6 = bf16[256,1024]{1,0:T(8,128)(2,1)S(1)} collective-permute-done((bf16[256,1024]{1,0:T(8,128)(2,1)S(1)}, bf16[256,1024]{1,0:T(8,128)(2,1)S(1)}, u32[]{:S(2)}, u32[]{:S(2)}) %collective-permute-start.6) | collective-permute-done | bytes 524320 | tf_op jit(solution)/shard_map/ppermute | solution.py:210
  100.7 7.8 %collective-permute-done.4 = bf16[256,1024]{1,0:T(8,128)(2,1)S(1)} collective-permute-done((bf16[256,1024]{1,0:T(8,128)(2,1)S(1)}, bf16[256,1024]{1,0:T(8,128)(2,1)S(1)}, u32[]{:S(2)}, u32[]{:S(2)}) %collective-permute-start.4) | collective-permute-done | bytes 524320 | tf_op jit(solution)/shard_map/ppermute | solution.py:210
  110.9 4.5 %copy.20 = bf16[1,256,5376]{1,2,0:T(8,128)(2,1)} copy(bf16[1,256,5376]{2,1,0:T(8,128)(2,1)} %param.6) | data formatting | bytes 5505024 | tf_op args[0]
  115.4 2.6 dynamic-slice_bitcast_fusion
  118.0 7.2 %collective-permute-start.8 = (bf16[256,8,336]{0,2,1:T(8,128)(2,1)}, bf16[256,8,336]{0,2,1:T(8,128)(2,1)S(1)}, u32[]{:S(2)}, u32[]{:S(2)}) collective-permute-start(bf16[256,8,336]{0,2,1:T(8,128)(2,1)} %dynamic-slice_bitcast_fusion), channel_id=1, source_target_pairs={{0,8},{8,0},{16,24},{24,16},{32,40},{40,32},{48,56},{56,48},{64,72... | collective-permute-start | bytes 4128776 | tf_op jit(solution)/shard_map/ppermute | solution.py:232
  125.2 3.7 %collective-permute-done.8 = bf16[256,8,336]{0,2,1:T(8,128)(2,1)S(1)} collective-permute-done((bf16[256,8,336]{0,2,1:T(8,128)(2,1)}, bf16[256,8,336]{0,2,1:T(8,128)(2,1)S(1)}, u32[]{:S(2)}, u32[]{:S(2)}) %collective-permute-start.8) | collective-permute-done | bytes 1376288 | tf_op jit(solution)/shard_map/ppermute | solution.py:232
  128.9 5.3 %convolution_bitcast_fusion = f32[256,1024]{1,0:T(8,128)} fusion(bf16[256,8,336]{0,2,1:T(8,128)(2,1)S(1)} %collective-permute-done.8, bf16[8,336,1024]{2,1,0:T(8,128)(2,1)} %bitcast.58), kind=kOutput, calls=%fused_computation.14 | convolution fusion | flops 1409286144 | bytes 7929856 | tf_op jit(solution)/shard_map/tfr,frn->tn/dot_general | solution.py:264
  134.5 2.8 convolution_convert_fusion
  137.5 5.3 %reshape_squeeze.7 = bf16[256,16,8,42]{0,3,2,1:T(8,128)(2,1)} reshape(bf16[1,256,5376]{1,2,0:T(8,128)(2,1)} %copy.20) | data formatting | bytes 5505024 | tf_op jit(solution)/shard_map/reshape;squeeze | solution.py:237
  142.8 5.0 %copy.25 = bf16[8,256,16,42]{1,2,3,0:T(8,128)(2,1)} copy(bf16[8,256,16,42]{1,3,0,2:T(8,128)(2,1)} %bitcast.68) | data formatting | bytes 5505024 | tf_op jit(solution)/shard_map/transpose | solution.py:237
  147.8 7.2 %all-to-all-start = ((bf16[8,256,16,42]{1,2,3,0:T(8,128)(2,1)}), bf16[8,256,16,42]{1,2,3,0:T(8,128)(2,1)}, u32[]{:S(2)}, u32[]{:S(2)}) async-start(bf16[8,256,16,42]{1,2,3,0:T(8,128)(2,1)} %copy.25), calls=%async_computation | async-start | bytes 5505024 | tf_op jit(solution)/shard_map/all_to_all | solution.py:239
  155.0 5.0 %add_convert_fusion.1 = bf16[256,1024]{1,0:T(8,128)(2,1)S(1)} fusion(f32[256,1024]{1,0:T(8,128)} %collective-permute-done.9, bf16[8,336,1024]{2,1,0:T(8,128)(2,1)} %bitcast.59, bf16[256,8,2,336]{0,3,2,1:T(8,128)(2,1)} %bitcast.67, s32[]{:T(128)S(6)} %select_n.47), kind=kOutput, calls=%fused_computation.16 | convolution fusion | flops 1409810432 | bytes 8454148 | tf_op jit(solution)/shard_map/tfr,frn->tn/dot_general | solution.py:266
  160.1 4.3 %collective-permute-start.10 = (bf16[256,1024]{1,0:T(8,128)(2,1)S(1)}, bf16[256,1024]{1,0:T(8,128)(2,1)}, u32[]{:S(2)}, u32[]{:S(2)}) collective-permute-start(bf16[256,1024]{1,0:T(8,128)(2,1)S(1)} %add_convert_fusion.1), channel_id=1, source_target_pairs={{0,32},{8,40},{16,48},{24,56},{32,64},{40,72},{48,80},{56,88},{64,... | collective-permute-start | bytes 1572872 | tf_op jit(solution)/shard_map/ppermute | solution.py:210
  176.3 4.5 %copy.27 = bf16[1,256,5376]{2,1,0:T(8,128)(2,1)} copy(bf16[1,256,5376]{1,2,0:T(8,128)(2,1)} %bitcast.69) | data formatting | bytes 5505024
  182.7 32.6 %collective-permute-done.11 = bf16[256,1024]{1,0:T(8,128)(2,1)} collective-permute-done((bf16[256,1024]{1,0:T(8,128)(2,1)S(1)}, bf16[256,1024]{1,0:T(8,128)(2,1)}, u32[]{:S(2)}, u32[]{:S(2)}) %collective-permute-start.11) | collective-permute-done | bytes 524320 | tf_op jit(solution)/shard_map/ppermute | solution.py:210
  217.1 9.6 %collective-permute-done.12 = bf16[256,1024]{1,0:T(8,128)(2,1)S(1)} collective-permute-done((bf16[256,1024]{1,0:T(8,128)(2,1)S(1)}, bf16[256,1024]{1,0:T(8,128)(2,1)S(1)}, u32[]{:S(2)}, u32[]{:S(2)}) %collective-permute-start.12) | collective-permute-done | bytes 524320 | tf_op jit(solution)/shard_map/ppermute | solution.py:210
  229.3 24.0 %shard_map.102 = (bf16[256,2048]{1,0:T(8,128)(2,1)}, bf16[256,2048]{1,0:T(8,128)(2,1)}, bf16[1280,1024]{1,0:T(8,128)(2,1)}) custom-call(bf16[256,2048]{1,0:T(8,128)(2,1)} %bitcast.75, bf16[1280,1024]{1,0:T(8,128)(2,1)} %slice.48.k_ref, bf16[1280,1024]{1,0:T(8,128)(2,1)} %constant_dynamic-update-slice_fusion.5.v_ref, bf16[256,2048]{1,0:T(8,128)(2,1)} %bitcast.77, ...), custom_call_target="tpu_custom_call" | custom-call | flops 6710886400 | bytes 12058624 | tf_op jit(solution)/shard_map/pallas_call | solution.py:98
  253.3 2.9 fusion.25
  262.6 7.8 %fusion.7.x_ref = bf16[16,42,1024]{2,1,0:T(8,128)(2,1)} fusion(bf16[8,256,16,42]{1,2,3,0:T(8,128)(2,1)} %all-to-all-done, bf16[8,256,1024]{2,1,0:T(8,128)(2,1)} %bitcast.73), kind=kOutput, calls=%fused_computation.7 | convolution fusion | flops 2819260416 | bytes 8323072 | tf_op jit(solution)/shard_map/ftcr,ftn->crn/dot_general | solution.py:276
  270.4 46.6 %shard_map.103 = f32[42,1024]{1,0:T(8,128)} custom-call(bf16[16,42,1024]{2,1,0:T(8,128)(2,1)} %fusion.7.x_ref), custom_call_target="tpu_custom_call" | custom-call | tf_op jit(solution)/shard_map/pallas_call | solution.py:192
  (76 shorter events, 46.0 us)
Async XLA Ops:
  7.2 17.4 %copy-start.5 = (s32[1,256]{1,0:T(1,128)S(1)}, s32[1,256]{1,0:T(1,128)}, u32[]{:S(2)}) copy-start(s32[1,256]{1,0:T(1,128)} %param.11) | copy-start | bytes 3076
  7.2 118.0 %all-gather.5.cloned.1.call-start = ((), (), s32[]{:S(2)}) async-start(), calls=%async_computation.1 | async-start | bytes 6193152 | tf_op jit(solution)/shard_map/all_gather | solution.py:226
  9.4 253.2 %all-gather.7.cloned.1.call-start = ((), (), s32[]{:S(2)}) async-start(), calls=%async_computation.2 | async-start | bytes 4718592 | tf_op jit(solution)/shard_map/all_gather | solution.py:262
  10.3 43.1 %copy-start.2 = (bf16[1,256,1024]{2,1,0:T(8,128)(2,1)S(1)}, bf16[1,256,1024]{2,1,0:T(8,128)(2,1)}, u32[]{:S(2)}) copy-start(bf16[1,256,1024]{2,1,0:T(8,128)(2,1)} %param.8) | copy-start | bytes 1572868
  11.4 17.5 %collective-permute-start = (bf16[256,1152]{1,0:T(8,128)(2,1)S(1)}, bf16[256,1152]{1,0:T(8,128)(2,1)}, u32[]{:S(2)}, u32[]{:S(2)}) collective-permute-start(bf16[256,1152]{1,0:T(8,128)(2,1)S(1)} %pad_maximum_fusion), channel_id=1, source_target_pairs={{0,32},{8,40},{16,48},{24,56},{32,64},{40,72},{48,80},{56,88},{64,... | collective-permute-start | bytes 1769480 | tf_op jit(solution)/shard_map/ppermute | solution.py:210
  16.1 16.9 %collective-permute-start.1 = (bf16[256,1152]{1,0:T(8,128)(2,1)S(1)}, bf16[256,1152]{1,0:T(8,128)(2,1)S(1)}, u32[]{:S(2)}, u32[]{:S(2)}) collective-permute-start(bf16[256,1152]{1,0:T(8,128)(2,1)S(1)} %pad_maximum_fusion), channel_id=1, source_target_pairs={{0,24},{8,32},{16,40},{24,48},{32,56},{40,64},{48,72},{56,80},{64,... | collective-permute-start | bytes 1769480 | tf_op jit(solution)/shard_map/ppermute | solution.py:210
  18.5 31.8 %collective-permute-start.2 = (bf16[256,1152]{1,0:T(8,128)(2,1)S(1)}, bf16[256,1152]{1,0:T(8,128)(2,1)S(1)}, u32[]{:S(2)}, u32[]{:S(2)}) collective-permute-start(bf16[256,1152]{1,0:T(8,128)(2,1)S(1)} %pad_maximum_fusion), channel_id=1, source_target_pairs={{0,16},{8,24},{16,32},{24,40},{32,48},{40,56},{48,64},{56,72},{64,... | collective-permute-start | bytes 1769480 | tf_op jit(solution)/shard_map/ppermute | solution.py:210
  21.7 31.7 %collective-permute-start.3 = (bf16[256,1152]{1,0:T(8,128)(2,1)S(1)}, bf16[256,1152]{1,0:T(8,128)(2,1)S(1)}, u32[]{:S(2)}, u32[]{:S(2)}) collective-permute-start(bf16[256,1152]{1,0:T(8,128)(2,1)S(1)} %pad_maximum_fusion), channel_id=1, source_target_pairs={{0,8},{8,16},{16,24},{24,32},{32,40},{40,48},{48,56},{56,64},{64,7... | collective-permute-start | bytes 1769480 | tf_op jit(solution)/shard_map/ppermute | solution.py:210
  73.5 15.1 %collective-permute-start.7 = (bf16[256,1024]{1,0:T(8,128)(2,1)S(1)}, bf16[256,1024]{1,0:T(8,128)(2,1)S(1)}, u32[]{:S(2)}, u32[]{:S(2)}) collective-permute-start(bf16[256,1024]{1,0:T(8,128)(2,1)S(1)} %get-tuple-element.30), channel_id=1, source_target_pairs={{32,0},{40,8},{48,16},{56,24},{64,32},{72,40},{80,48},{88,56},{96,... | collective-permute-start | bytes 1572872 | tf_op jit(solution)/shard_map/ppermute | solution.py:210
  74.8 23.8 %collective-permute-start.6 = (bf16[256,1024]{1,0:T(8,128)(2,1)S(1)}, bf16[256,1024]{1,0:T(8,128)(2,1)S(1)}, u32[]{:S(2)}, u32[]{:S(2)}) collective-permute-start(bf16[256,1024]{1,0:T(8,128)(2,1)S(1)} %get-tuple-element.31), channel_id=1, source_target_pairs={{24,0},{32,8},{40,16},{48,24},{56,32},{64,40},{72,48},{80,56},{88,... | collective-permute-start | bytes 1572872 | tf_op jit(solution)/shard_map/ppermute | solution.py:210
  76.1 24.6 %collective-permute-start.5 = (bf16[256,1024]{1,0:T(8,128)(2,1)S(1)}, bf16[256,1024]{1,0:T(8,128)(2,1)S(1)}, u32[]{:S(2)}, u32[]{:S(2)}) collective-permute-start(bf16[256,1024]{1,0:T(8,128)(2,1)S(1)} %get-tuple-element.32), channel_id=1, source_target_pairs={{16,0},{24,8},{32,16},{40,24},{48,32},{56,40},{64,48},{72,56},{80,... | collective-permute-start | bytes 1572872 | tf_op jit(solution)/shard_map/ppermute | solution.py:210
  80.7 27.9 %collective-permute-start.4 = (bf16[256,1024]{1,0:T(8,128)(2,1)S(1)}, bf16[256,1024]{1,0:T(8,128)(2,1)S(1)}, u32[]{:S(2)}, u32[]{:S(2)}) collective-permute-start(bf16[256,1024]{1,0:T(8,128)(2,1)S(1)} %get-tuple-element.29), channel_id=1, source_target_pairs={{8,0},{16,8},{24,16},{32,24},{40,32},{48,40},{56,48},{64,56},{72,6... | collective-permute-start | bytes 1572872 | tf_op jit(solution)/shard_map/ppermute | solution.py:210
  115.4 9.7 %copy-start.3 = (bf16[256,1024]{1,0:T(8,128)(2,1)S(1)}, bf16[256,1024]{1,0:T(8,128)(2,1)}, u32[]{:S(2)}) copy-start(bf16[256,1024]{1,0:T(8,128)(2,1)} %add_convert_fusion.2) | copy-start | bytes 1572868
  118.0 10.9 %collective-permute-start.8 = (bf16[256,8,336]{0,2,1:T(8,128)(2,1)}, bf16[256,8,336]{0,2,1:T(8,128)(2,1)S(1)}, u32[]{:S(2)}, u32[]{:S(2)}) collective-permute-start(bf16[256,8,336]{0,2,1:T(8,128)(2,1)} %dynamic-slice_bitcast_fusion), channel_id=1, source_target_pairs={{0,8},{8,0},{16,24},{24,16},{32,40},{40,32},{48,56},{56,48},{64,72... | collective-permute-start | bytes 4128776 | tf_op jit(solution)/shard_map/ppermute | solution.py:232
  125.1 9.4 %collective-permute-start.18 = (bf16[256,1024]{1,0:T(8,128)(2,1)S(1)}, bf16[256,1024]{1,0:T(8,128)(2,1)S(1)}, u32[]{:S(2)}, u32[]{:S(2)}) collective-permute-start(bf16[256,1024]{1,0:T(8,128)(2,1)S(1)} %copy-done.3), channel_id=1, source_target_pairs={{0,8},{8,0},{16,24},{24,16},{32,40},{40,32},{48,56},{56,48},{64,72... | collective-permute-start | bytes 1572872 | tf_op jit(solution)/shard_map/ppermute | solution.py:281
  125.2 9.4 %slice-start = ((s8[5505024]{0:T(1024)(128)(4,1)}), s8[4194304]{0:T(1024)(128)(4,1)S(1)}, s32[]{:S(2)}) async-start(s8[5505024]{0:T(1024)(128)(4,1)} %bitcast.60), calls=%async_computation.3 | async-start | bytes 8388608
  125.2 9.4 %slice-start.1 = ((s8[5505024]{0:T(1024)(128)(4,1)}), s8[1310720]{0:T(1024)(128)(4,1)S(1)}, s32[]{:S(2)}) async-start(s8[5505024]{0:T(1024)(128)(4,1)} %bitcast.60), calls=%async_computation.4 | async-start | bytes 2621440
  134.2 20.8 %collective-permute-start.9 = (f32[256,1024]{1,0:T(8,128)}, f32[256,1024]{1,0:T(8,128)}, u32[]{:S(2)}, u32[]{:S(2)}) collective-permute-start(f32[256,1024]{1,0:T(8,128)} %convolution_bitcast_fusion), channel_id=1, source_target_pairs={{0,8},{8,0},{16,24},{24,16},{32,40},{40,32},{48,56},{56,48},{64,72... | collective-permute-start | bytes 3145736 | tf_op jit(solution)/shard_map/ppermute | solution.py:267
  137.3 35.0 %collective-permute-start.19 = (bf16[256,8,336]{0,2,1:T(8,128)(2,1)}, bf16[256,8,336]{0,2,1:T(8,128)(2,1)}, u32[]{:S(2)}, u32[]{:S(2)}) collective-permute-start(bf16[256,8,336]{0,2,1:T(8,128)(2,1)} %convolution_convert_fusion), channel_id=1, source_target_pairs={{0,8},{8,0},{16,24},{24,16},{32,40},{40,32},{48,56},{56,48},{64,72... | collective-permute-start | bytes 4128776 | tf_op jit(solution)/shard_map/ppermute | solution.py:282
  147.8 114.8 %all-to-all-start = ((bf16[8,256,16,42]{1,2,3,0:T(8,128)(2,1)}), bf16[8,256,16,42]{1,2,3,0:T(8,128)(2,1)}, u32[]{:S(2)}, u32[]{:S(2)}) async-start(bf16[8,256,16,42]{1,2,3,0:T(8,128)(2,1)} %copy.25), calls=%async_computation | async-start | bytes 5505024 | tf_op jit(solution)/shard_map/all_to_all | solution.py:239
  155.0 11.5 %slice-start.2 = ((s8[5505024]{0:T(1024)(128)(4,1)}), s8[1310720]{0:T(1024)(128)(4,1)S(1)}, s32[]{:S(2)}) async-start(s8[5505024]{0:T(1024)(128)(4,1)} %bitcast.63), calls=%async_computation.5 | async-start | bytes 2621440
  155.0 11.5 %slice-start.3 = ((s8[5505024]{0:T(1024)(128)(4,1)}), s8[4194304]{0:T(1024)(128)(4,1)S(1)}, s32[]{:S(2)}) async-start(s8[5505024]{0:T(1024)(128)(4,1)} %bitcast.63), calls=%async_computation.6 | async-start | bytes 8388608
  160.1 20.8 %collective-permute-start.10 = (bf16[256,1024]{1,0:T(8,128)(2,1)S(1)}, bf16[256,1024]{1,0:T(8,128)(2,1)}, u32[]{:S(2)}, u32[]{:S(2)}) collective-permute-start(bf16[256,1024]{1,0:T(8,128)(2,1)S(1)} %add_convert_fusion.1), channel_id=1, source_target_pairs={{0,32},{8,40},{16,48},{24,56},{32,64},{40,72},{48,80},{56,88},{64,... | collective-permute-start | bytes 1572872 | tf_op jit(solution)/shard_map/ppermute | solution.py:210
  164.4 50.9 %collective-permute-start.11 = (bf16[256,1024]{1,0:T(8,128)(2,1)S(1)}, bf16[256,1024]{1,0:T(8,128)(2,1)}, u32[]{:S(2)}, u32[]{:S(2)}) collective-permute-start(bf16[256,1024]{1,0:T(8,128)(2,1)S(1)} %add_convert_fusion.1), channel_id=1, source_target_pairs={{0,24},{8,32},{16,40},{24,48},{32,56},{40,64},{48,72},{56,80},{64,... | collective-permute-start | bytes 1572872 | tf_op jit(solution)/shard_map/ppermute | solution.py:210
  168.1 58.6 %collective-permute-start.12 = (bf16[256,1024]{1,0:T(8,128)(2,1)S(1)}, bf16[256,1024]{1,0:T(8,128)(2,1)S(1)}, u32[]{:S(2)}, u32[]{:S(2)}) collective-permute-start(bf16[256,1024]{1,0:T(8,128)(2,1)S(1)} %add_convert_fusion.1), channel_id=1, source_target_pairs={{0,16},{8,24},{16,32},{24,40},{32,48},{40,56},{48,64},{56,72},{64,... | collective-permute-start | bytes 1572872 | tf_op jit(solution)/shard_map/ppermute | solution.py:210
  170.4 57.1 %collective-permute-start.13 = (bf16[256,1024]{1,0:T(8,128)(2,1)S(1)}, bf16[256,1024]{1,0:T(8,128)(2,1)S(1)}, u32[]{:S(2)}, u32[]{:S(2)}) collective-permute-start(bf16[256,1024]{1,0:T(8,128)(2,1)S(1)} %add_convert_fusion.1), channel_id=1, source_target_pairs={{0,8},{8,16},{16,24},{24,32},{32,40},{40,48},{48,56},{56,64},{64,7... | collective-permute-start | bytes 1572872 | tf_op jit(solution)/shard_map/ppermute | solution.py:210
  256.1 60.9 %collective-permute-start.17 = (bf16[256,1024]{1,0:T(8,128)(2,1)}, bf16[256,1024]{1,0:T(8,128)(2,1)S(1)}, u32[]{:S(2)}, u32[]{:S(2)}) collective-permute-start(bf16[256,1024]{1,0:T(8,128)(2,1)} %get-tuple-element.26), channel_id=1, source_target_pairs={{32,0},{40,8},{48,16},{56,24},{64,32},{72,40},{80,48},{88,56},{96,... | collective-permute-start | bytes 1572872 | tf_op jit(solution)/shard_map/ppermute | solution.py:210
  257.4 59.6 %collective-permute-start.16 = (bf16[256,1024]{1,0:T(8,128)(2,1)}, bf16[256,1024]{1,0:T(8,128)(2,1)S(1)}, u32[]{:S(2)}, u32[]{:S(2)}) collective-permute-start(bf16[256,1024]{1,0:T(8,128)(2,1)} %get-tuple-element.27), channel_id=1, source_target_pairs={{24,0},{32,8},{40,16},{48,24},{56,32},{64,40},{72,48},{80,56},{88,... | collective-permute-start | bytes 1572872 | tf_op jit(solution)/shard_map/ppermute | solution.py:210
  258.7 58.3 %collective-permute-start.15 = (bf16[256,1024]{1,0:T(8,128)(2,1)}, bf16[256,1024]{1,0:T(8,128)(2,1)S(1)}, u32[]{:S(2)}, u32[]{:S(2)}) collective-permute-start(bf16[256,1024]{1,0:T(8,128)(2,1)} %get-tuple-element.28), channel_id=1, source_target_pairs={{16,0},{24,8},{32,16},{40,24},{48,32},{56,40},{64,48},{72,56},{80,... | collective-permute-start | bytes 1572872 | tf_op jit(solution)/shard_map/ppermute | solution.py:210
  260.7 56.4 %collective-permute-start.14 = (bf16[256,1024]{1,0:T(8,128)(2,1)}, bf16[256,1024]{1,0:T(8,128)(2,1)S(1)}, u32[]{:S(2)}, u32[]{:S(2)}) collective-permute-start(bf16[256,1024]{1,0:T(8,128)(2,1)} %get-tuple-element.25), channel_id=1, source_target_pairs={{8,0},{16,8},{24,16},{32,24},{40,32},{48,40},{56,48},{64,56},{72,6... | collective-permute-start | bytes 1572872 | tf_op jit(solution)/shard_map/ppermute | solution.py:210
  262.6 57.5 %copy-start.1 = (bf16[672,1024]{1,0:T(8,128)(2,1)S(1)}, bf16[672,1024]{1,0:T(8,128)(2,1)}, u32[]{:S(2)}) copy-start(bf16[672,1024]{1,0:T(8,128)(2,1)} %param.9) | copy-start | bytes 4128772
  317.0 2.4 copy-start.4
  (1 other events, 1.3 us)
Sparse Core Ops, SparseCore 0:
  10.9 95.0 all-gather.4
  111.0 117.6 all-gather.6

commit v9 on v8

--- a/solution.py
+++ b/solution.py
@@ -241,6 +241,7 @@
     parcel = jnp.concatenate([own_keys, tag_columns], 1)
     arrived = [shifted(parcel, "ctx", hop) for hop in range(1, n_hops + 1)]
     window_parcel = jnp.concatenate(arrived[::-1] + [parcel], 0)
+    window_parcel, token_cols = lax.optimization_barrier((window_parcel, token_cols))
     window_keys = window_parcel[:, :kv_width]
     window_tags = window_parcel[:, kv_width].astype(jnp.int32)
     first_query = lax.axis_index("ctx") * shard_rows

time: 330 us -> 351 us (1.064)
  waiting for transfers between devices: 95.6 us -> 123 us
  starting transfers between devices: 57.3 us -> 47.1 us
  local copies, waits for them, and re-layouts: 41.3 us -> 46.1 us
    ppermute x16, waiting for transfers between devices: 91.8 us -> 119 us  [shifted(): return lax.ppermute(x, axis, pairs)]
    ppermute x1, starting transfers between devices: 7.18 us -> 0.01 us  [shards(): lax.ppermute(lax.dynamic_index_in_dim(token_halves, 1 - core, axis=2, kee...]
    ppermute x16, starting transfers between devices: 42.3 us -> 38.7 us  [shifted(): return lax.ppermute(x, axis, pairs)]
  transfers between devices with their start and end apart: 23 -> 23, of which waited for: 11 -> 10; matrix products, arithmetic and copies ran while one was open for 21% -> 21% of each run, Pallas kernels for 26% -> 24%
where the time goes in v9:
time: 351 us; the launch traced here: 347 us
  waiting for transfers between devices  123 us (35%)
  Pallas kernels  84.4 us (24%)
  starting transfers between devices  47.1 us (13%)
  local copies, waits for them, and re-layouts  46.1 us (13%)
  matrix products  22.4 us (6%)
  between operations  14.3 us (4%)
  other arithmetic  9.59 us (3%)
    ppermute x16, waiting for transfers between devices, shifted(): return lax.ppermute(x, axis, pairs)  119 us
    pallas_call x1, Pallas kernels, peer_sum_scatter(): pl.pallas_call(functools.partial(peer_sum_kernel, axis, n), out_shape=jax...  45.2 us
    ppermute x16, starting transfers between devices, shifted(): return lax.ppermute(x, axis, pairs)  38.7 us
    pallas_call x1, Pallas kernels, fused_attention(): pl.pallas_call(attention_kernel, grid=(heads,), in_specs=[q_spec, kv_spec...  24 us
    unnamed x31, local copies, waits for them, and re-layouts  20.9 us
    pallas_call x1, Pallas kernels, value_grads(): pl.pallas_call(value_grad_kernel, grid=(heads,), in_specs=[q_spec, kv_spe...  15.2 us
    dot_general x1, matrix products, shards(): jnp.einsum('ftcr,ftn->crn', token_cols, grads_all, preferred_element_type...  7.69 us
    all_to_all x1, starting transfers between devices, shards(): token_cols = lax.all_to_all(token_cols, 'fsdp', 0, 0, tiled=True)  7.34 us
  transfers between devices with their start and end apart: 23, of which 10 were waited for; matrix products, arithmetic and copies ran while one was open for 21% of the time, Pallas kernels for 24%

profile of v9, /device:TPU:28, one launch (start us, length us, event | category | flops | bytes accessed | tf_op | source)
XLA Modules:
  0.0 347.0 jit_solution(11225505065365190882)
XLA Ops:
  9.4 4.5 %copy.20 = bf16[1,256,5376]{1,2,0:T(8,128)(2,1)} copy(bf16[1,256,5376]{2,1,0:T(8,128)(2,1)} %param.6) | data formatting | bytes 5505024 | tf_op args[0]
  13.9 5.3 %reshape_squeeze.6 = bf16[256,16,8,42]{0,3,2,1:T(8,128)(2,1)} reshape(bf16[1,256,5376]{1,2,0:T(8,128)(2,1)} %copy.20) | data formatting | bytes 5505024 | tf_op jit(solution)/shard_map/reshape;squeeze | solution.py:237
  19.2 4.9 %copy.21 = bf16[8,256,16,42]{1,2,3,0:T(8,128)(2,1)} copy(bf16[8,256,16,42]{1,3,0,2:T(8,128)(2,1)} %bitcast.62) | data formatting | bytes 5505024 | tf_op jit(solution)/shard_map/transpose | solution.py:237
  24.1 7.3 %all-to-all-start = ((bf16[8,256,16,42]{1,2,3,0:T(8,128)(2,1)}), bf16[8,256,16,42]{1,2,3,0:T(8,128)(2,1)}, u32[]{:S(2)}, u32[]{:S(2)}) async-start(bf16[8,256,16,42]{1,2,3,0:T(8,128)(2,1)} %copy.21), calls=%async_computation | async-start | bytes 5505024 | tf_op jit(solution)/shard_map/all_to_all | solution.py:239
  31.7 4.7 %collective-permute-start = (bf16[256,1152]{1,0:T(8,128)(2,1)S(1)}, bf16[256,1152]{1,0:T(8,128)(2,1)}, u32[]{:S(2)}, u32[]{:S(2)}) collective-permute-start(bf16[256,1152]{1,0:T(8,128)(2,1)S(1)} %pad_maximum_fusion), channel_id=1, source_target_pairs={{0,32},{8,40},{16,48},{24,56},{32,64},{40,72},{48,80},{56,88},{64,... | collective-permute-start | bytes 1769480 | tf_op jit(solution)/shard_map/ppermute | solution.py:210
  38.1 3.3 collective-permute-start.2
  41.4 3.4 collective-permute-start.3
  45.6 3.7 %collective-permute-done = bf16[256,1152]{1,0:T(8,128)(2,1)} collective-permute-done((bf16[256,1152]{1,0:T(8,128)(2,1)S(1)}, bf16[256,1152]{1,0:T(8,128)(2,1)}, u32[]{:S(2)}, u32[]{:S(2)}) %collective-permute-start) | collective-permute-done | bytes 589856 | tf_op jit(solution)/shard_map/ppermute | solution.py:210
  51.2 28.6 %collective-permute-done.1 = bf16[256,1152]{1,0:T(8,128)(2,1)S(1)} collective-permute-done((bf16[256,1152]{1,0:T(8,128)(2,1)S(1)}, bf16[256,1152]{1,0:T(8,128)(2,1)S(1)}, u32[]{:S(2)}, u32[]{:S(2)}) %collective-permute-start.1) | collective-permute-done | bytes 589856 | tf_op jit(solution)/shard_map/ppermute | solution.py:210
  80.6 25.3 %collective-permute-done.2 = bf16[256,1152]{1,0:T(8,128)(2,1)S(1)} collective-permute-done((bf16[256,1152]{1,0:T(8,128)(2,1)S(1)}, bf16[256,1152]{1,0:T(8,128)(2,1)S(1)}, u32[]{:S(2)}, u32[]{:S(2)}) %collective-permute-start.2) | collective-permute-done | bytes 589856 | tf_op jit(solution)/shard_map/ppermute | solution.py:210
  108.6 3.4 slice.36.k_ref
  113.8 15.2 %shard_map.101 = bf16[1280,1024]{1,0:T(8,128)(2,1)} custom-call(bf16[256,2048]{1,0:T(8,128)(2,1)} %bitcast.68, bf16[1280,1024]{1,0:T(8,128)(2,1)} %slice.36.k_ref, bf16[256,2048]{1,0:T(8,128)(2,1)} %bitcast.70, s32[256,1]{1,0:T(8,128)} %copy.23.qtag_ref, s32[1,1280]{1,0:T(1,128)} %compare_select_fusion.ktag_ref), custom_call_target="tpu_custom_call" | custom-call | flops 2684354560 | bytes 7340032 | tf_op jit(solution)/shard_map/pallas_call | solution.py:79
  137.2 6.0 %collective-permute-done.4 = bf16[256,1024]{1,0:T(8,128)(2,1)S(1)} collective-permute-done((bf16[256,1024]{1,0:T(8,128)(2,1)S(1)}, bf16[256,1024]{1,0:T(8,128)(2,1)S(1)}, u32[]{:S(2)}, u32[]{:S(2)}) %collective-permute-start.4) | collective-permute-done | bytes 524320 | tf_op jit(solution)/shard_map/ppermute | solution.py:210
  143.2 13.2 %collective-permute-done.5 = bf16[256,1024]{1,0:T(8,128)(2,1)S(1)} collective-permute-done((bf16[256,1024]{1,0:T(8,128)(2,1)S(1)}, bf16[256,1024]{1,0:T(8,128)(2,1)S(1)}, u32[]{:S(2)}, u32[]{:S(2)}) %collective-permute-start.5) | collective-permute-done | bytes 524320 | tf_op jit(solution)/shard_map/ppermute | solution.py:210
  156.4 2.4 collective-permute-done.6
  158.8 16.7 %collective-permute-done.7 = bf16[256,1024]{1,0:T(8,128)(2,1)S(1)} collective-permute-done((bf16[256,1024]{1,0:T(8,128)(2,1)S(1)}, bf16[256,1024]{1,0:T(8,128)(2,1)S(1)}, u32[]{:S(2)}, u32[]{:S(2)}) %collective-permute-start.7) | collective-permute-done | bytes 524320 | tf_op jit(solution)/shard_map/ppermute | solution.py:210
  175.6 2.3 add_convert_fusion.2
  177.9 2.6 dynamic-slice_bitcast_fusion
  181.0 3.6 %collective-permute-done.8 = bf16[256,8,336]{0,2,1:T(8,128)(2,1)S(1)} collective-permute-done((bf16[256,8,336]{0,2,1:T(8,128)(2,1)}, bf16[256,8,336]{0,2,1:T(8,128)(2,1)S(1)}, u32[]{:S(2)}, u32[]{:S(2)}) %collective-permute-start.8) | collective-permute-done | bytes 1376288 | tf_op jit(solution)/shard_map/ppermute | solution.py:232
  184.6 5.2 %convolution_bitcast_fusion = f32[256,1024]{1,0:T(8,128)} fusion(bf16[256,8,336]{0,2,1:T(8,128)(2,1)S(1)} %collective-permute-done.8, bf16[8,336,1024]{2,1,0:T(8,128)(2,1)} %bitcast.52), kind=kOutput, calls=%fused_computation.13 | convolution fusion | flops 1409286144 | bytes 7929856 | tf_op jit(solution)/shard_map/tfr,frn->tn/dot_general | solution.py:265
  189.9 2.8 convolution_convert_fusion
  193.1 5.1 %add_convert_fusion.1 = bf16[256,1024]{1,0:T(8,128)(2,1)S(1)} fusion(f32[256,1024]{1,0:T(8,128)} %collective-permute-done.9, bf16[8,336,1024]{2,1,0:T(8,128)(2,1)} %bitcast.53, bf16[256,8,2,336]{0,3,2,1:T(8,128)(2,1)} %bitcast.61, s32[]{:T(128)S(6)} %select_n.47), kind=kOutput, calls=%fused_computation.15 | convolution fusion | flops 1409810432 | bytes 8454148 | tf_op jit(solution)/shard_map/tfr,frn->tn/dot_general | solution.py:267
  198.2 4.7 %collective-permute-start.10 = (bf16[256,1024]{1,0:T(8,128)(2,1)S(1)}, bf16[256,1024]{1,0:T(8,128)(2,1)}, u32[]{:S(2)}, u32[]{:S(2)}) collective-permute-start(bf16[256,1024]{1,0:T(8,128)(2,1)S(1)} %add_convert_fusion.1), channel_id=1, source_target_pairs={{0,32},{8,40},{16,48},{24,56},{32,64},{40,72},{48,80},{56,88},{64,... | collective-permute-start | bytes 1572872 | tf_op jit(solution)/shard_map/ppermute | solution.py:210
  206.6 4.1 %collective-permute-start.12 = (bf16[256,1024]{1,0:T(8,128)(2,1)S(1)}, bf16[256,1024]{1,0:T(8,128)(2,1)S(1)}, u32[]{:S(2)}, u32[]{:S(2)}) collective-permute-start(bf16[256,1024]{1,0:T(8,128)(2,1)S(1)} %add_convert_fusion.1), channel_id=1, source_target_pairs={{0,16},{8,24},{16,32},{24,40},{32,48},{40,56},{48,64},{56,72},{64,... | collective-permute-start | bytes 1572872 | tf_op jit(solution)/shard_map/ppermute | solution.py:210
  216.5 4.5 %copy.27 = bf16[1,256,5376]{2,1,0:T(8,128)(2,1)} copy(bf16[1,256,5376]{1,2,0:T(8,128)(2,1)} %bitcast.63) | data formatting | bytes 5505024
  224.7 10.2 %collective-permute-done.12 = bf16[256,1024]{1,0:T(8,128)(2,1)S(1)} collective-permute-done((bf16[256,1024]{1,0:T(8,128)(2,1)S(1)}, bf16[256,1024]{1,0:T(8,128)(2,1)S(1)}, u32[]{:S(2)}, u32[]{:S(2)}) %collective-permute-start.12) | collective-permute-done | bytes 524320 | tf_op jit(solution)/shard_map/ppermute | solution.py:210
  235.8 13.4 %collective-permute-done.13 = bf16[256,1024]{1,0:T(8,128)(2,1)S(1)} collective-permute-done((bf16[256,1024]{1,0:T(8,128)(2,1)S(1)}, bf16[256,1024]{1,0:T(8,128)(2,1)S(1)}, u32[]{:S(2)}, u32[]{:S(2)}) %collective-permute-start.13) | collective-permute-done | bytes 524320 | tf_op jit(solution)/shard_map/ppermute | solution.py:210
  250.9 24.0 %shard_map.102 = (bf16[256,2048]{1,0:T(8,128)(2,1)}, bf16[256,2048]{1,0:T(8,128)(2,1)}, bf16[1280,1024]{1,0:T(8,128)(2,1)}) custom-call(bf16[256,2048]{1,0:T(8,128)(2,1)} %bitcast.69, bf16[1280,1024]{1,0:T(8,128)(2,1)} %slice.36.k_ref, bf16[1280,1024]{1,0:T(8,128)(2,1)} %constant_dynamic-update-slice_fusion.5.v_ref, bf16[256,2048]{1,0:T(8,128)(2,1)} %bitcast.71, ...), custom_call_target="tpu_custom_call" | custom-call | flops 6710886400 | bytes 12058624 | tf_op jit(solution)/shard_map/pallas_call | solution.py:98
  274.9 2.9 fusion.20
  284.2 7.7 %bitcast_convert_fusion.x_ref = bf16[16,42,1024]{2,1,0:T(8,128)(2,1)} fusion(bf16[8,256,1024]{2,1,0:T(8,128)(2,1)} %bitcast.67, bf16[8,256,16,42]{1,2,3,0:T(8,128)(2,1)} %all-to-all-done), kind=kOutput, calls=%fused_computation.2 | convolution fusion | flops 2819260416 | bytes 8323072 | tf_op jit(solution)/shard_map/ftcr,ftn->crn/dot_general | solution.py:277
  291.9 45.2 %shard_map.103 = f32[42,1024]{1,0:T(8,128)} custom-call(bf16[16,42,1024]{2,1,0:T(8,128)(2,1)} %bitcast_convert_fusion.x_ref), custom_call_target="tpu_custom_call" | custom-call | tf_op jit(solution)/shard_map/pallas_call | solution.py:192
  337.2 2.3 fusion.14
  (76 shorter events, 44.3 us)
Async XLA Ops:
  7.2 173.8 %all-gather.5.cloned.1.call-start = ((), (), s32[]{:S(2)}) async-start(), calls=%async_computation.1 | async-start | bytes 6193152 | tf_op jit(solution)/shard_map/all_gather | solution.py:226
  24.1 7.3 %copy-start.5 = (s32[1,256]{1,0:T(1,128)S(1)}, s32[1,256]{1,0:T(1,128)}, u32[]{:S(2)}) copy-start(s32[1,256]{1,0:T(1,128)} %param.11) | copy-start | bytes 3076
  24.1 7.5 %copy-start.2 = (bf16[1,256,1024]{2,1,0:T(8,128)(2,1)S(1)}, bf16[1,256,1024]{2,1,0:T(8,128)(2,1)}, u32[]{:S(2)}) copy-start(bf16[1,256,1024]{2,1,0:T(8,128)(2,1)} %param.8) | copy-start | bytes 1572868
  24.1 84.4 %all-to-all-start = ((bf16[8,256,16,42]{1,2,3,0:T(8,128)(2,1)}), bf16[8,256,16,42]{1,2,3,0:T(8,128)(2,1)}, u32[]{:S(2)}, u32[]{:S(2)}) async-start(bf16[8,256,16,42]{1,2,3,0:T(8,128)(2,1)} %copy.21), calls=%async_computation | async-start | bytes 5505024 | tf_op jit(solution)/shard_map/all_to_all | solution.py:239
  31.5 246.3 %all-gather.7.cloned.1.call-start = ((), (), s32[]{:S(2)}) async-start(), calls=%async_computation.2 | async-start | bytes 4718592 | tf_op jit(solution)/shard_map/all_gather | solution.py:263
  31.7 17.6 %collective-permute-start = (bf16[256,1152]{1,0:T(8,128)(2,1)S(1)}, bf16[256,1152]{1,0:T(8,128)(2,1)}, u32[]{:S(2)}, u32[]{:S(2)}) collective-permute-start(bf16[256,1152]{1,0:T(8,128)(2,1)S(1)} %pad_maximum_fusion), channel_id=1, source_target_pairs={{0,32},{8,40},{16,48},{24,56},{32,64},{40,72},{48,80},{56,88},{64,... | collective-permute-start | bytes 1769480 | tf_op jit(solution)/shard_map/ppermute | solution.py:210
  36.3 43.4 %collective-permute-start.1 = (bf16[256,1152]{1,0:T(8,128)(2,1)S(1)}, bf16[256,1152]{1,0:T(8,128)(2,1)S(1)}, u32[]{:S(2)}, u32[]{:S(2)}) collective-permute-start(bf16[256,1152]{1,0:T(8,128)(2,1)S(1)} %pad_maximum_fusion), channel_id=1, source_target_pairs={{0,24},{8,32},{16,40},{24,48},{32,56},{40,64},{48,72},{56,80},{64,... | collective-permute-start | bytes 1769480 | tf_op jit(solution)/shard_map/ppermute | solution.py:210
  38.1 67.7 %collective-permute-start.2 = (bf16[256,1152]{1,0:T(8,128)(2,1)S(1)}, bf16[256,1152]{1,0:T(8,128)(2,1)S(1)}, u32[]{:S(2)}, u32[]{:S(2)}) collective-permute-start(bf16[256,1152]{1,0:T(8,128)(2,1)S(1)} %pad_maximum_fusion), channel_id=1, source_target_pairs={{0,16},{8,24},{16,32},{24,40},{32,48},{40,56},{48,64},{56,72},{64,... | collective-permute-start | bytes 1769480 | tf_op jit(solution)/shard_map/ppermute | solution.py:210
  41.4 65.3 %collective-permute-start.3 = (bf16[256,1152]{1,0:T(8,128)(2,1)S(1)}, bf16[256,1152]{1,0:T(8,128)(2,1)S(1)}, u32[]{:S(2)}, u32[]{:S(2)}) collective-permute-start(bf16[256,1152]{1,0:T(8,128)(2,1)S(1)} %pad_maximum_fusion), channel_id=1, source_target_pairs={{0,8},{8,16},{16,24},{24,32},{32,40},{40,48},{48,56},{56,64},{64,7... | collective-permute-start | bytes 1769480 | tf_op jit(solution)/shard_map/ppermute | solution.py:210
  130.8 12.4 %collective-permute-start.4 = (bf16[256,1024]{1,0:T(8,128)(2,1)S(1)}, bf16[256,1024]{1,0:T(8,128)(2,1)S(1)}, u32[]{:S(2)}, u32[]{:S(2)}) collective-permute-start(bf16[256,1024]{1,0:T(8,128)(2,1)S(1)} %get-tuple-element.33), channel_id=1, source_target_pairs={{8,0},{16,8},{24,16},{32,24},{40,32},{48,40},{56,48},{64,56},{72,6... | collective-permute-start | bytes 1572872 | tf_op jit(solution)/shard_map/ppermute | solution.py:210
  132.7 23.7 %collective-permute-start.5 = (bf16[256,1024]{1,0:T(8,128)(2,1)S(1)}, bf16[256,1024]{1,0:T(8,128)(2,1)S(1)}, u32[]{:S(2)}, u32[]{:S(2)}) collective-permute-start(bf16[256,1024]{1,0:T(8,128)(2,1)S(1)} %get-tuple-element.36), channel_id=1, source_target_pairs={{16,0},{24,8},{32,16},{40,24},{48,32},{56,40},{64,48},{72,56},{80,... | collective-permute-start | bytes 1572872 | tf_op jit(solution)/shard_map/ppermute | solution.py:210
  134.6 24.2 %collective-permute-start.6 = (bf16[256,1024]{1,0:T(8,128)(2,1)S(1)}, bf16[256,1024]{1,0:T(8,128)(2,1)S(1)}, u32[]{:S(2)}, u32[]{:S(2)}) collective-permute-start(bf16[256,1024]{1,0:T(8,128)(2,1)S(1)} %get-tuple-element.35), channel_id=1, source_target_pairs={{24,0},{32,8},{40,16},{48,24},{56,32},{64,40},{72,48},{80,56},{88,... | collective-permute-start | bytes 1572872 | tf_op jit(solution)/shard_map/ppermute | solution.py:210
  135.9 39.6 %collective-permute-start.7 = (bf16[256,1024]{1,0:T(8,128)(2,1)S(1)}, bf16[256,1024]{1,0:T(8,128)(2,1)S(1)}, u32[]{:S(2)}, u32[]{:S(2)}) collective-permute-start(bf16[256,1024]{1,0:T(8,128)(2,1)S(1)} %get-tuple-element.34), channel_id=1, source_target_pairs={{32,0},{40,8},{48,16},{56,24},{64,32},{72,40},{80,48},{88,56},{96,... | collective-permute-start | bytes 1572872 | tf_op jit(solution)/shard_map/ppermute | solution.py:210
  177.9 2.6 copy-start.3
  180.5 4.1 %collective-permute-start.8 = (bf16[256,8,336]{0,2,1:T(8,128)(2,1)}, bf16[256,8,336]{0,2,1:T(8,128)(2,1)S(1)}, u32[]{:S(2)}, u32[]{:S(2)}) collective-permute-start(bf16[256,8,336]{0,2,1:T(8,128)(2,1)} %dynamic-slice_bitcast_fusion), channel_id=1, source_target_pairs={{0,8},{8,0},{16,24},{24,16},{32,40},{40,32},{48,56},{56,48},{64,72... | collective-permute-start | bytes 4128776 | tf_op jit(solution)/shard_map/ppermute | solution.py:232
  180.5 9.4 %collective-permute-start.18 = (bf16[256,1024]{1,0:T(8,128)(2,1)S(1)}, bf16[256,1024]{1,0:T(8,128)(2,1)S(1)}, u32[]{:S(2)}, u32[]{:S(2)}) collective-permute-start(bf16[256,1024]{1,0:T(8,128)(2,1)S(1)} %copy-done.3), channel_id=1, source_target_pairs={{0,8},{8,0},{16,24},{24,16},{32,40},{40,32},{48,56},{56,48},{64,72... | collective-permute-start | bytes 1572872 | tf_op jit(solution)/shard_map/ppermute | solution.py:282
  181.0 8.9 %slice-start = ((s8[5505024]{0:T(1024)(128)(4,1)}), s8[4194304]{0:T(1024)(128)(4,1)S(1)}, s32[]{:S(2)}) async-start(s8[5505024]{0:T(1024)(128)(4,1)} %bitcast.54), calls=%async_computation.3 | async-start | bytes 8388608
  181.0 8.9 %slice-start.1 = ((s8[5505024]{0:T(1024)(128)(4,1)}), s8[1310720]{0:T(1024)(128)(4,1)S(1)}, s32[]{:S(2)}) async-start(s8[5505024]{0:T(1024)(128)(4,1)} %bitcast.54), calls=%async_computation.4 | async-start | bytes 2621440
  189.8 3.4 collective-permute-start.9
  192.8 19.9 %collective-permute-start.19 = (bf16[256,8,336]{0,2,1:T(8,128)(2,1)}, bf16[256,8,336]{0,2,1:T(8,128)(2,1)}, u32[]{:S(2)}, u32[]{:S(2)}) collective-permute-start(bf16[256,8,336]{0,2,1:T(8,128)(2,1)} %convolution_convert_fusion), channel_id=1, source_target_pairs={{0,8},{8,0},{16,24},{24,16},{32,40},{40,32},{48,56},{56,48},{64,72... | collective-permute-start | bytes 4128776 | tf_op jit(solution)/shard_map/ppermute | solution.py:283
  193.1 11.8 %slice-start.2 = ((s8[5505024]{0:T(1024)(128)(4,1)}), s8[1310720]{0:T(1024)(128)(4,1)S(1)}, s32[]{:S(2)}) async-start(s8[5505024]{0:T(1024)(128)(4,1)} %bitcast.57), calls=%async_computation.5 | async-start | bytes 2621440
  193.1 11.8 %slice-start.3 = ((s8[5505024]{0:T(1024)(128)(4,1)}), s8[4194304]{0:T(1024)(128)(4,1)S(1)}, s32[]{:S(2)}) async-start(s8[5505024]{0:T(1024)(128)(4,1)} %bitcast.57), calls=%async_computation.6 | async-start | bytes 8388608
  198.2 22.8 %collective-permute-start.10 = (bf16[256,1024]{1,0:T(8,128)(2,1)S(1)}, bf16[256,1024]{1,0:T(8,128)(2,1)}, u32[]{:S(2)}, u32[]{:S(2)}) collective-permute-start(bf16[256,1024]{1,0:T(8,128)(2,1)S(1)} %add_convert_fusion.1), channel_id=1, source_target_pairs={{0,32},{8,40},{16,48},{24,56},{32,64},{40,72},{48,80},{56,88},{64,... | collective-permute-start | bytes 1572872 | tf_op jit(solution)/shard_map/ppermute | solution.py:210
  202.9 20.0 %collective-permute-start.11 = (bf16[256,1024]{1,0:T(8,128)(2,1)S(1)}, bf16[256,1024]{1,0:T(8,128)(2,1)}, u32[]{:S(2)}, u32[]{:S(2)}) collective-permute-start(bf16[256,1024]{1,0:T(8,128)(2,1)S(1)} %add_convert_fusion.1), channel_id=1, source_target_pairs={{0,24},{8,32},{16,40},{24,48},{32,56},{40,64},{48,72},{56,80},{64,... | collective-permute-start | bytes 1572872 | tf_op jit(solution)/shard_map/ppermute | solution.py:210
  206.6 28.3 %collective-permute-start.12 = (bf16[256,1024]{1,0:T(8,128)(2,1)S(1)}, bf16[256,1024]{1,0:T(8,128)(2,1)S(1)}, u32[]{:S(2)}, u32[]{:S(2)}) collective-permute-start(bf16[256,1024]{1,0:T(8,128)(2,1)S(1)} %add_convert_fusion.1), channel_id=1, source_target_pairs={{0,16},{8,24},{16,32},{24,40},{32,48},{40,56},{48,64},{56,72},{64,... | collective-permute-start | bytes 1572872 | tf_op jit(solution)/shard_map/ppermute | solution.py:210
  210.7 38.5 %collective-permute-start.13 = (bf16[256,1024]{1,0:T(8,128)(2,1)S(1)}, bf16[256,1024]{1,0:T(8,128)(2,1)S(1)}, u32[]{:S(2)}, u32[]{:S(2)}) collective-permute-start(bf16[256,1024]{1,0:T(8,128)(2,1)S(1)} %add_convert_fusion.1), channel_id=1, source_target_pairs={{0,8},{8,16},{16,24},{24,32},{32,40},{40,48},{48,56},{56,64},{64,7... | collective-permute-start | bytes 1572872 | tf_op jit(solution)/shard_map/ppermute | solution.py:210
  277.8 59.3 %collective-permute-start.14 = (bf16[256,1024]{1,0:T(8,128)(2,1)}, bf16[256,1024]{1,0:T(8,128)(2,1)S(1)}, u32[]{:S(2)}, u32[]{:S(2)}) collective-permute-start(bf16[256,1024]{1,0:T(8,128)(2,1)} %get-tuple-element.29), channel_id=1, source_target_pairs={{8,0},{16,8},{24,16},{32,24},{40,32},{48,40},{56,48},{64,56},{72,6... | collective-permute-start | bytes 1572872 | tf_op jit(solution)/shard_map/ppermute | solution.py:210
  279.7 57.4 %collective-permute-start.15 = (bf16[256,1024]{1,0:T(8,128)(2,1)}, bf16[256,1024]{1,0:T(8,128)(2,1)S(1)}, u32[]{:S(2)}, u32[]{:S(2)}) collective-permute-start(bf16[256,1024]{1,0:T(8,128)(2,1)} %get-tuple-element.32), channel_id=1, source_target_pairs={{16,0},{24,8},{32,16},{40,24},{48,32},{56,40},{64,48},{72,56},{80,... | collective-permute-start | bytes 1572872 | tf_op jit(solution)/shard_map/ppermute | solution.py:210
  281.6 55.5 %collective-permute-start.16 = (bf16[256,1024]{1,0:T(8,128)(2,1)}, bf16[256,1024]{1,0:T(8,128)(2,1)S(1)}, u32[]{:S(2)}, u32[]{:S(2)}) collective-permute-start(bf16[256,1024]{1,0:T(8,128)(2,1)} %get-tuple-element.31), channel_id=1, source_target_pairs={{24,0},{32,8},{40,16},{48,24},{56,32},{64,40},{72,48},{80,56},{88,... | collective-permute-start | bytes 1572872 | tf_op jit(solution)/shard_map/ppermute | solution.py:210
  282.9 54.2 %collective-permute-start.17 = (bf16[256,1024]{1,0:T(8,128)(2,1)}, bf16[256,1024]{1,0:T(8,128)(2,1)S(1)}, u32[]{:S(2)}, u32[]{:S(2)}) collective-permute-start(bf16[256,1024]{1,0:T(8,128)(2,1)} %get-tuple-element.30), channel_id=1, source_target_pairs={{32,0},{40,8},{48,16},{56,24},{64,32},{72,40},{80,48},{88,56},{96,... | collective-permute-start | bytes 1572872 | tf_op jit(solution)/shard_map/ppermute | solution.py:210
  284.2 55.9 %copy-start.1 = (bf16[672,1024]{1,0:T(8,128)(2,1)S(1)}, bf16[672,1024]{1,0:T(8,128)(2,1)}, u32[]{:S(2)}) copy-start(bf16[672,1024]{1,0:T(8,128)(2,1)} %param.9) | copy-start | bytes 4128772
  337.1 2.4 copy-start.4
  (1 other events, 1.3 us)
Sparse Core Ops, SparseCore 0:
  10.9 119.0 all-gather.4
  178.0 83.1 all-gather.6

commit v10 on v8

--- a/solution.py
+++ b/solution.py
@@ -241,6 +241,7 @@
     parcel = jnp.concatenate([own_keys, tag_columns], 1)
     arrived = [shifted(parcel, "ctx", hop) for hop in range(1, n_hops + 1)]
     window_parcel = jnp.concatenate(arrived[::-1] + [parcel], 0)
+    window_parcel, partner_tokens = lax.optimization_barrier((window_parcel, partner_tokens))
     window_keys = window_parcel[:, :kv_width]
     window_tags = window_parcel[:, kv_width].astype(jnp.int32)
     first_query = lax.axis_index("ctx") * shard_rows

time: 330 us -> 324 us (0.982)
  waiting for transfers between devices: 95.6 us -> 82.5 us
  starting transfers between devices: 57.3 us -> 63.3 us
    ppermute x1, starting transfers between devices: 0.01 us -> 10.5 us  [shards(): partner_grads = lax.ppermute(d_values_low, 'ctx', partner)]
    ppermute x16, waiting for transfers between devices: 91.8 us -> 82.4 us  [shifted(): return lax.ppermute(x, axis, pairs)]
    ppermute x1, starting transfers between devices: 7.18 us -> 0.09 us  [shards(): lax.ppermute(lax.dynamic_index_in_dim(token_halves, 1 - core, axis=2, kee...]
    ppermute x1, waiting for transfers between devices: 3.69 us -> 0.01 us  [shards(): lax.ppermute(lax.dynamic_index_in_dim(token_halves, 1 - core, axis=2, kee...]
    unnamed x31 -> x29, local copies, waits for them, and re-layouts: 17.7 us -> 19.9 us
  transfers between devices with their start and end apart: 23 -> 23, of which waited for: 11 -> 8; matrix products, arithmetic and copies ran while one was open for 21% -> 22% of each run, Pallas kernels for 26% -> 27%
where the time goes in v10:
time: 324 us; the launch traced here: 321 us
  Pallas kernels  85.7 us (26%)
  waiting for transfers between devices  82.5 us (25%)
  starting transfers between devices  63.3 us (20%)
  local copies, waits for them, and re-layouts  42.5 us (13%)
  matrix products  22.7 us (7%)
  between operations  14.4 us (4%)
  other arithmetic  10.4 us (3%)
    ppermute x16, waiting for transfers between devices, shifted(): return lax.ppermute(x, axis, pairs)  82.4 us
    pallas_call x1, Pallas kernels, peer_sum_scatter(): pl.pallas_call(functools.partial(peer_sum_kernel, axis, n), out_shape=jax...  46.4 us
    ppermute x16, starting transfers between devices, shifted(): return lax.ppermute(x, axis, pairs)  45 us
    pallas_call x1, Pallas kernels, fused_attention(): pl.pallas_call(attention_kernel, grid=(heads,), in_specs=[q_spec, kv_spec...  24 us
    unnamed x29, local copies, waits for them, and re-layouts  19.9 us
    pallas_call x1, Pallas kernels, value_grads(): pl.pallas_call(value_grad_kernel, grid=(heads,), in_specs=[q_spec, kv_spe...  15.2 us
    ppermute x1, starting transfers between devices, shards(): partner_grads = lax.ppermute(d_values_low, 'ctx', partner)  10.5 us
    dot_general x1, matrix products, shards(): jnp.einsum('ftcr,ftn->crn', token_cols, grads_all, preferred_element_type...  7.79 us
  transfers between devices with their start and end apart: 23, of which 8 were waited for; matrix products, arithmetic and copies ran while one was open for 22% of the time, Pallas kernels for 27%

profile of v10, /device:TPU:28, one launch (start us, length us, event | category | flops | bytes accessed | tf_op | source)
XLA Modules:
  0.0 321.4 jit_solution(1810103555123205519)
XLA Ops:
  12.2 4.7 %collective-permute-start = (bf16[256,1152]{1,0:T(8,128)(2,1)}, bf16[256,1152]{1,0:T(8,128)(2,1)}, u32[]{:S(2)}, u32[]{:S(2)}) collective-permute-start(bf16[256,1152]{1,0:T(8,128)(2,1)} %pad_maximum_fusion), channel_id=1, source_target_pairs={{0,32},{8,40},{16,48},{24,56},{32,64},{40,72},{48,80},{56,88},{64,... | collective-permute-start | bytes 1769480 | tf_op jit(solution)/shard_map/ppermute | solution.py:210
  16.8 3.2 collective-permute-start.1
  20.0 4.5 %copy.20 = bf16[1,256,5376]{1,2,0:T(8,128)(2,1)} copy(bf16[1,256,5376]{2,1,0:T(8,128)(2,1)} %param.6) | data formatting | bytes 5505024 | tf_op args[0]
  26.1 3.7 %collective-permute-start.2 = (bf16[256,1152]{1,0:T(8,128)(2,1)}, bf16[256,1152]{1,0:T(8,128)(2,1)}, u32[]{:S(2)}, u32[]{:S(2)}) collective-permute-start(bf16[256,1152]{1,0:T(8,128)(2,1)} %pad_maximum_fusion), channel_id=1, source_target_pairs={{0,16},{8,24},{16,32},{24,40},{32,48},{40,56},{48,64},{56,72},{64,... | collective-permute-start | bytes 1769480 | tf_op jit(solution)/shard_map/ppermute | solution.py:210
  34.8 13.8 %collective-permute-done.2 = bf16[256,1152]{1,0:T(8,128)(2,1)} collective-permute-done((bf16[256,1152]{1,0:T(8,128)(2,1)}, bf16[256,1152]{1,0:T(8,128)(2,1)}, u32[]{:S(2)}, u32[]{:S(2)}) %collective-permute-start.2) | collective-permute-done | bytes 589856 | tf_op jit(solution)/shard_map/ppermute | solution.py:210
  49.7 4.7 %collective-permute-done.3 = bf16[256,1152]{1,0:T(8,128)(2,1)} collective-permute-done((bf16[256,1152]{1,0:T(8,128)(2,1)}, bf16[256,1152]{1,0:T(8,128)(2,1)}, u32[]{:S(2)}, u32[]{:S(2)}) %collective-permute-start.3) | collective-permute-done | bytes 589856 | tf_op jit(solution)/shard_map/ppermute | solution.py:210
  58.4 15.2 %shard_map.101 = bf16[1280,1024]{1,0:T(8,128)(2,1)} custom-call(bf16[256,2048]{1,0:T(8,128)(2,1)} %bitcast.72, bf16[1280,1024]{1,0:T(8,128)(2,1)} %slice.36.k_ref, bf16[256,2048]{1,0:T(8,128)(2,1)} %bitcast.74, s32[256,1]{1,0:T(8,128)} %copy.21.qtag_ref, s32[1,1280]{1,0:T(1,128)} %compare_select_fusion.ktag_ref), custom_call_target="tpu_custom_call" | custom-call | flops 2684354560 | bytes 7340032 | tf_op jit(solution)/shard_map/pallas_call | solution.py:79
  77.9 7.2 %collective-permute-start.6 = (bf16[256,1024]{1,0:T(8,128)(2,1)S(1)}, bf16[256,1024]{1,0:T(8,128)(2,1)S(1)}, u32[]{:S(2)}, u32[]{:S(2)}) collective-permute-start(bf16[256,1024]{1,0:T(8,128)(2,1)S(1)} %get-tuple-element.36), channel_id=1, source_target_pairs={{16,0},{24,8},{32,16},{40,24},{48,32},{56,40},{64,48},{72,56},{80,... | collective-permute-start | bytes 1572872 | tf_op jit(solution)/shard_map/ppermute | solution.py:210
  85.1 4.8 %collective-permute-start.5 = (bf16[256,1024]{1,0:T(8,128)(2,1)S(1)}, bf16[256,1024]{1,0:T(8,128)(2,1)S(1)}, u32[]{:S(2)}, u32[]{:S(2)}) collective-permute-start(bf16[256,1024]{1,0:T(8,128)(2,1)S(1)} %get-tuple-element.33), channel_id=1, source_target_pairs={{8,0},{16,8},{24,16},{32,24},{40,32},{48,40},{56,48},{64,56},{72,6... | collective-permute-start | bytes 1572872 | tf_op jit(solution)/shard_map/ppermute | solution.py:210
  90.0 8.8 %collective-permute-done.7 = bf16[256,1024]{1,0:T(8,128)(2,1)S(1)} collective-permute-done((bf16[256,1024]{1,0:T(8,128)(2,1)S(1)}, bf16[256,1024]{1,0:T(8,128)(2,1)S(1)}, u32[]{:S(2)}, u32[]{:S(2)}) %collective-permute-start.7) | collective-permute-done | bytes 524320 | tf_op jit(solution)/shard_map/ppermute | solution.py:210
  98.8 6.2 %collective-permute-done.6 = bf16[256,1024]{1,0:T(8,128)(2,1)S(1)} collective-permute-done((bf16[256,1024]{1,0:T(8,128)(2,1)S(1)}, bf16[256,1024]{1,0:T(8,128)(2,1)S(1)}, u32[]{:S(2)}, u32[]{:S(2)}) %collective-permute-start.6) | collective-permute-done | bytes 524320 | tf_op jit(solution)/shard_map/ppermute | solution.py:210
  105.0 2.5 collective-permute-done.5
  107.5 2.3 add_convert_fusion.2
  109.8 10.5 %collective-permute-start.18 = (bf16[256,1024]{1,0:T(8,128)(2,1)}, bf16[256,1024]{1,0:T(8,128)(2,1)S(1)}, u32[]{:S(2)}, u32[]{:S(2)}) collective-permute-start(bf16[256,1024]{1,0:T(8,128)(2,1)} %add_convert_fusion.2), channel_id=1, source_target_pairs={{0,8},{8,0},{16,24},{24,16},{32,40},{40,32},{48,56},{56,48},{64,72... | collective-permute-start | bytes 1572872 | tf_op jit(solution)/shard_map/ppermute | solution.py:282
  120.3 5.4 %convolution_bitcast_fusion = f32[256,1024]{1,0:T(8,128)} fusion(bf16[256,8,336]{0,2,1:T(8,128)(2,1)S(1)} %collective-permute-done.4, bf16[8,336,1024]{2,1,0:T(8,128)(2,1)} %bitcast.58), kind=kOutput, calls=%fused_computation.14 | convolution fusion | flops 1409286144 | bytes 7929856 | tf_op jit(solution)/shard_map/tfr,frn->tn/dot_general | solution.py:265
  125.8 2.8 convolution_convert_fusion
  129.0 5.3 %reshape_squeeze.7 = bf16[256,16,8,42]{0,3,2,1:T(8,128)(2,1)} reshape(bf16[1,256,5376]{1,2,0:T(8,128)(2,1)} %copy.20) | data formatting | bytes 5505024 | tf_op jit(solution)/shard_map/reshape;squeeze | solution.py:237
  134.4 5.0 %copy.25 = bf16[8,256,16,42]{1,2,3,0:T(8,128)(2,1)} copy(bf16[8,256,16,42]{1,3,0,2:T(8,128)(2,1)} %bitcast.66) | data formatting | bytes 5505024 | tf_op jit(solution)/shard_map/transpose | solution.py:237
  139.4 7.2 %all-to-all-start = ((bf16[8,256,16,42]{1,2,3,0:T(8,128)(2,1)}), bf16[8,256,16,42]{1,2,3,0:T(8,128)(2,1)}, u32[]{:S(2)}, u32[]{:S(2)}) async-start(bf16[8,256,16,42]{1,2,3,0:T(8,128)(2,1)} %copy.25), calls=%async_computation | async-start | bytes 5505024 | tf_op jit(solution)/shard_map/all_to_all | solution.py:239
  146.6 5.0 %add_convert_fusion.1 = bf16[256,1024]{1,0:T(8,128)(2,1)S(1)} fusion(f32[256,1024]{1,0:T(8,128)} %collective-permute-done.9, bf16[8,336,1024]{2,1,0:T(8,128)(2,1)} %bitcast.59, bf16[256,8,2,336]{0,3,2,1:T(8,128)(2,1)} %bitcast.65, s32[]{:T(128)S(6)} %select_n.48), kind=kOutput, calls=%fused_computation.16 | convolution fusion | flops 1409810432 | bytes 8454148 | tf_op jit(solution)/shard_map/tfr,frn->tn/dot_general | solution.py:267
  151.6 4.3 %collective-permute-start.10 = (bf16[256,1024]{1,0:T(8,128)(2,1)S(1)}, bf16[256,1024]{1,0:T(8,128)(2,1)}, u32[]{:S(2)}, u32[]{:S(2)}) collective-permute-start(bf16[256,1024]{1,0:T(8,128)(2,1)S(1)} %add_convert_fusion.1), channel_id=1, source_target_pairs={{0,32},{8,40},{16,48},{24,56},{32,64},{40,72},{48,80},{56,88},{64,... | collective-permute-start | bytes 1572872 | tf_op jit(solution)/shard_map/ppermute | solution.py:210
  159.0 2.7 collective-permute-start.12
  163.6 2.2 maximum_select_fusion
  167.5 4.5 %copy.27 = bf16[1,256,5376]{2,1,0:T(8,128)(2,1)} copy(bf16[1,256,5376]{1,2,0:T(8,128)(2,1)} %bitcast.67) | data formatting | bytes 5505024
  173.9 25.0 %collective-permute-done.11 = bf16[256,1024]{1,0:T(8,128)(2,1)S(1)} collective-permute-done((bf16[256,1024]{1,0:T(8,128)(2,1)S(1)}, bf16[256,1024]{1,0:T(8,128)(2,1)S(1)}, u32[]{:S(2)}, u32[]{:S(2)}) %collective-permute-start.11) | collective-permute-done | bytes 524320 | tf_op jit(solution)/shard_map/ppermute | solution.py:210
  199.7 21.4 %collective-permute-done.12 = bf16[256,1024]{1,0:T(8,128)(2,1)S(1)} collective-permute-done((bf16[256,1024]{1,0:T(8,128)(2,1)S(1)}, bf16[256,1024]{1,0:T(8,128)(2,1)S(1)}, u32[]{:S(2)}, u32[]{:S(2)}) %collective-permute-start.12) | collective-permute-done | bytes 524320 | tf_op jit(solution)/shard_map/ppermute | solution.py:210
  223.6 24.0 %shard_map.102 = (bf16[256,2048]{1,0:T(8,128)(2,1)}, bf16[256,2048]{1,0:T(8,128)(2,1)}, bf16[1280,1024]{1,0:T(8,128)(2,1)}) custom-call(bf16[256,2048]{1,0:T(8,128)(2,1)} %bitcast.73, bf16[1280,1024]{1,0:T(8,128)(2,1)} %slice.36.k_ref, bf16[1280,1024]{1,0:T(8,128)(2,1)} %constant_dynamic-update-slice_fusion.5.v_ref, bf16[256,2048]{1,0:T(8,128)(2,1)} %bitcast.75, ...), custom_call_target="tpu_custom_call" | custom-call | flops 6710886400 | bytes 12058624 | tf_op jit(solution)/shard_map/pallas_call | solution.py:98
  247.6 2.9 fusion.25
  255.1 2.1 collective-permute-start.14
  257.3 7.8 %fusion.7.x_ref = bf16[16,42,1024]{2,1,0:T(8,128)(2,1)} fusion(bf16[8,256,16,42]{1,2,3,0:T(8,128)(2,1)} %all-to-all-done, bf16[8,256,1024]{2,1,0:T(8,128)(2,1)} %bitcast.71), kind=kOutput, calls=%fused_computation.7 | convolution fusion | flops 2819260416 | bytes 8323072 | tf_op jit(solution)/shard_map/ftcr,ftn->crn/dot_general | solution.py:277
  265.0 46.4 %shard_map.103 = f32[42,1024]{1,0:T(8,128)} custom-call(bf16[16,42,1024]{2,1,0:T(8,128)(2,1)} %fusion.7.x_ref), custom_call_target="tpu_custom_call" | custom-call | tf_op jit(solution)/shard_map/pallas_call | solution.py:192
  311.5 2.3 fusion.19
  (73 shorter events, 38.4 us)
Async XLA Ops:
  7.2 1.3 copy-start
  7.2 113.2 %all-gather.5.cloned.1.call-start = ((), (), s32[]{:S(2)}) async-start(), calls=%async_computation.1 | async-start | bytes 6193152 | tf_op jit(solution)/shard_map/all_gather | solution.py:226
  9.4 247.8 %all-gather.7.cloned.1.call-start = ((), (), s32[]{:S(2)}) async-start(), calls=%async_computation.2 | async-start | bytes 4718592 | tf_op jit(solution)/shard_map/all_gather | solution.py:263
  12.2 20.4 %collective-permute-start = (bf16[256,1152]{1,0:T(8,128)(2,1)}, bf16[256,1152]{1,0:T(8,128)(2,1)}, u32[]{:S(2)}, u32[]{:S(2)}) collective-permute-start(bf16[256,1152]{1,0:T(8,128)(2,1)} %pad_maximum_fusion), channel_id=1, source_target_pairs={{0,32},{8,40},{16,48},{24,56},{32,64},{40,72},{48,80},{56,88},{64,... | collective-permute-start | bytes 1769480 | tf_op jit(solution)/shard_map/ppermute | solution.py:210
  16.8 16.8 %collective-permute-start.1 = (bf16[256,1152]{1,0:T(8,128)(2,1)}, bf16[256,1152]{1,0:T(8,128)(2,1)}, u32[]{:S(2)}, u32[]{:S(2)}) collective-permute-start(bf16[256,1152]{1,0:T(8,128)(2,1)} %pad_maximum_fusion), channel_id=1, source_target_pairs={{0,24},{8,32},{16,40},{24,48},{32,56},{40,64},{48,72},{56,80},{64,... | collective-permute-start | bytes 1769480 | tf_op jit(solution)/shard_map/ppermute | solution.py:210
  24.6 7.2 %copy-start.6 = (s32[1,256]{1,0:T(1,128)S(1)}, s32[1,256]{1,0:T(1,128)}, u32[]{:S(2)}) copy-start(s32[1,256]{1,0:T(1,128)} %param.11) | copy-start | bytes 3076
  26.0 29.5 %copy-start.3 = (bf16[1,256,1024]{2,1,0:T(8,128)(2,1)S(1)}, bf16[1,256,1024]{2,1,0:T(8,128)(2,1)}, u32[]{:S(2)}) copy-start(bf16[1,256,1024]{2,1,0:T(8,128)(2,1)} %param.8) | copy-start | bytes 1572868
  26.0 29.6 %collective-permute-start.4 = (bf16[256,8,336]{0,2,1:T(8,128)(2,1)S(1)}, bf16[256,8,336]{0,2,1:T(8,128)(2,1)S(1)}, u32[]{:S(2)}, u32[]{:S(2)}) collective-permute-start(bf16[256,8,336]{0,2,1:T(8,128)(2,1)S(1)} %dynamic-slice_bitcast_fusion), channel_id=1, source_target_pairs={{0,8},{8,0},{16,24},{24,16},{32,40},{40,32},{48,56},{56,48},{64,72... | collective-permute-start | bytes 4128776 | tf_op jit(solution)/shard_map/ppermute | solution.py:232
  26.1 22.5 %collective-permute-start.2 = (bf16[256,1152]{1,0:T(8,128)(2,1)}, bf16[256,1152]{1,0:T(8,128)(2,1)}, u32[]{:S(2)}, u32[]{:S(2)}) collective-permute-start(bf16[256,1152]{1,0:T(8,128)(2,1)} %pad_maximum_fusion), channel_id=1, source_target_pairs={{0,16},{8,24},{16,32},{24,40},{32,48},{40,56},{48,64},{56,72},{64,... | collective-permute-start | bytes 1769480 | tf_op jit(solution)/shard_map/ppermute | solution.py:210
  29.8 24.6 %collective-permute-start.3 = (bf16[256,1152]{1,0:T(8,128)(2,1)}, bf16[256,1152]{1,0:T(8,128)(2,1)}, u32[]{:S(2)}, u32[]{:S(2)}) collective-permute-start(bf16[256,1152]{1,0:T(8,128)(2,1)} %pad_maximum_fusion), channel_id=1, source_target_pairs={{0,8},{8,16},{16,24},{24,32},{32,40},{40,48},{48,56},{56,64},{64,7... | collective-permute-start | bytes 1769480 | tf_op jit(solution)/shard_map/ppermute | solution.py:210
  75.3 14.7 %collective-permute-start.8 = (bf16[256,1024]{1,0:T(8,128)(2,1)S(1)}, bf16[256,1024]{1,0:T(8,128)(2,1)S(1)}, u32[]{:S(2)}, u32[]{:S(2)}) collective-permute-start(bf16[256,1024]{1,0:T(8,128)(2,1)S(1)} %get-tuple-element.34), channel_id=1, source_target_pairs={{32,0},{40,8},{48,16},{56,24},{64,32},{72,40},{80,48},{88,56},{96,... | collective-permute-start | bytes 1572872 | tf_op jit(solution)/shard_map/ppermute | solution.py:210
  76.6 22.2 %collective-permute-start.7 = (bf16[256,1024]{1,0:T(8,128)(2,1)S(1)}, bf16[256,1024]{1,0:T(8,128)(2,1)S(1)}, u32[]{:S(2)}, u32[]{:S(2)}) collective-permute-start(bf16[256,1024]{1,0:T(8,128)(2,1)S(1)} %get-tuple-element.35), channel_id=1, source_target_pairs={{24,0},{32,8},{40,16},{48,24},{56,32},{64,40},{72,48},{80,56},{88,... | collective-permute-start | bytes 1572872 | tf_op jit(solution)/shard_map/ppermute | solution.py:210
  77.9 27.1 %collective-permute-start.6 = (bf16[256,1024]{1,0:T(8,128)(2,1)S(1)}, bf16[256,1024]{1,0:T(8,128)(2,1)S(1)}, u32[]{:S(2)}, u32[]{:S(2)}) collective-permute-start(bf16[256,1024]{1,0:T(8,128)(2,1)S(1)} %get-tuple-element.36), channel_id=1, source_target_pairs={{16,0},{24,8},{32,16},{40,24},{48,32},{56,40},{64,48},{72,56},{80,... | collective-permute-start | bytes 1572872 | tf_op jit(solution)/shard_map/ppermute | solution.py:210
  85.1 22.4 %collective-permute-start.5 = (bf16[256,1024]{1,0:T(8,128)(2,1)S(1)}, bf16[256,1024]{1,0:T(8,128)(2,1)S(1)}, u32[]{:S(2)}, u32[]{:S(2)}) collective-permute-start(bf16[256,1024]{1,0:T(8,128)(2,1)S(1)} %get-tuple-element.33), channel_id=1, source_target_pairs={{8,0},{16,8},{24,16},{32,24},{40,32},{48,40},{56,48},{64,56},{72,6... | collective-permute-start | bytes 1572872 | tf_op jit(solution)/shard_map/ppermute | solution.py:210
  109.8 15.9 %collective-permute-start.18 = (bf16[256,1024]{1,0:T(8,128)(2,1)}, bf16[256,1024]{1,0:T(8,128)(2,1)S(1)}, u32[]{:S(2)}, u32[]{:S(2)}) collective-permute-start(bf16[256,1024]{1,0:T(8,128)(2,1)} %add_convert_fusion.2), channel_id=1, source_target_pairs={{0,8},{8,0},{16,24},{24,16},{32,40},{40,32},{48,56},{56,48},{64,72... | collective-permute-start | bytes 1572872 | tf_op jit(solution)/shard_map/ppermute | solution.py:282
  120.3 5.4 %copy-start.2 = (bf16[2688,1024]{1,0:T(8,128)(2,1)S(1)}, bf16[2688,1024]{1,0:T(8,128)(2,1)}, u32[]{:S(2)}) copy-start(bf16[2688,1024]{1,0:T(8,128)(2,1)} %all-gather.5.cloned.1.call-done) | copy-start | bytes 16515076
  125.7 20.9 %collective-permute-start.9 = (f32[256,1024]{1,0:T(8,128)}, f32[256,1024]{1,0:T(8,128)}, u32[]{:S(2)}, u32[]{:S(2)}) collective-permute-start(f32[256,1024]{1,0:T(8,128)} %convolution_bitcast_fusion), channel_id=1, source_target_pairs={{0,8},{8,0},{16,24},{24,16},{32,40},{40,32},{48,56},{56,48},{64,72... | collective-permute-start | bytes 3145736 | tf_op jit(solution)/shard_map/ppermute | solution.py:268
  128.6 35.0 %collective-permute-start.19 = (bf16[256,8,336]{0,2,1:T(8,128)(2,1)}, bf16[256,8,336]{0,2,1:T(8,128)(2,1)}, u32[]{:S(2)}, u32[]{:S(2)}) collective-permute-start(bf16[256,8,336]{0,2,1:T(8,128)(2,1)} %convolution_convert_fusion), channel_id=1, source_target_pairs={{0,8},{8,0},{16,24},{24,16},{32,40},{40,32},{48,56},{56,48},{64,72... | collective-permute-start | bytes 4128776 | tf_op jit(solution)/shard_map/ppermute | solution.py:283
  139.4 117.9 %all-to-all-start = ((bf16[8,256,16,42]{1,2,3,0:T(8,128)(2,1)}), bf16[8,256,16,42]{1,2,3,0:T(8,128)(2,1)}, u32[]{:S(2)}, u32[]{:S(2)}) async-start(bf16[8,256,16,42]{1,2,3,0:T(8,128)(2,1)} %copy.25), calls=%async_computation | async-start | bytes 5505024 | tf_op jit(solution)/shard_map/all_to_all | solution.py:239
  146.6 10.7 %slice-start = ((s8[5505024]{0:T(1024)(128)(4,1)}), s8[1310720]{0:T(1024)(128)(4,1)S(1)}, s32[]{:S(2)}) async-start(s8[5505024]{0:T(1024)(128)(4,1)} %bitcast.61), calls=%async_computation.3 | async-start | bytes 2621440
  146.6 10.7 %slice-start.1 = ((s8[5505024]{0:T(1024)(128)(4,1)}), s8[4194304]{0:T(1024)(128)(4,1)S(1)}, s32[]{:S(2)}) async-start(s8[5505024]{0:T(1024)(128)(4,1)} %bitcast.61), calls=%async_computation.4 | async-start | bytes 8388608
  146.6 10.7 %copy-start.4 = (bf16[256,1024]{1,0:T(8,128)(2,1)S(1)}, bf16[256,1024]{1,0:T(8,128)(2,1)}, u32[]{:S(2)}) copy-start(bf16[256,1024]{1,0:T(8,128)(2,1)} %add_convert_fusion.2) | copy-start | bytes 1572868
  151.6 20.4 %collective-permute-start.10 = (bf16[256,1024]{1,0:T(8,128)(2,1)S(1)}, bf16[256,1024]{1,0:T(8,128)(2,1)}, u32[]{:S(2)}, u32[]{:S(2)}) collective-permute-start(bf16[256,1024]{1,0:T(8,128)(2,1)S(1)} %add_convert_fusion.1), channel_id=1, source_target_pairs={{0,32},{8,40},{16,48},{24,56},{32,64},{40,72},{48,80},{56,88},{64,... | collective-permute-start | bytes 1572872 | tf_op jit(solution)/shard_map/ppermute | solution.py:210
  156.0 42.9 %collective-permute-start.11 = (bf16[256,1024]{1,0:T(8,128)(2,1)S(1)}, bf16[256,1024]{1,0:T(8,128)(2,1)S(1)}, u32[]{:S(2)}, u32[]{:S(2)}) collective-permute-start(bf16[256,1024]{1,0:T(8,128)(2,1)S(1)} %add_convert_fusion.1), channel_id=1, source_target_pairs={{0,24},{8,32},{16,40},{24,48},{32,56},{40,64},{48,72},{56,80},{64,... | collective-permute-start | bytes 1572872 | tf_op jit(solution)/shard_map/ppermute | solution.py:210
  159.0 62.1 %collective-permute-start.12 = (bf16[256,1024]{1,0:T(8,128)(2,1)S(1)}, bf16[256,1024]{1,0:T(8,128)(2,1)S(1)}, u32[]{:S(2)}, u32[]{:S(2)}) collective-permute-start(bf16[256,1024]{1,0:T(8,128)(2,1)S(1)} %add_convert_fusion.1), channel_id=1, source_target_pairs={{0,16},{8,24},{16,32},{24,40},{32,48},{40,56},{48,64},{56,72},{64,... | collective-permute-start | bytes 1572872 | tf_op jit(solution)/shard_map/ppermute | solution.py:210
  161.7 60.2 %collective-permute-start.13 = (bf16[256,1024]{1,0:T(8,128)(2,1)S(1)}, bf16[256,1024]{1,0:T(8,128)(2,1)S(1)}, u32[]{:S(2)}, u32[]{:S(2)}) collective-permute-start(bf16[256,1024]{1,0:T(8,128)(2,1)S(1)} %add_convert_fusion.1), channel_id=1, source_target_pairs={{0,8},{8,16},{16,24},{24,32},{32,40},{40,48},{48,56},{56,64},{64,7... | collective-permute-start | bytes 1572872 | tf_op jit(solution)/shard_map/ppermute | solution.py:210
  250.5 61.0 %collective-permute-start.17 = (bf16[256,1024]{1,0:T(8,128)(2,1)}, bf16[256,1024]{1,0:T(8,128)(2,1)S(1)}, u32[]{:S(2)}, u32[]{:S(2)}) collective-permute-start(bf16[256,1024]{1,0:T(8,128)(2,1)} %get-tuple-element.30), channel_id=1, source_target_pairs={{32,0},{40,8},{48,16},{56,24},{64,32},{72,40},{80,48},{88,56},{96,... | collective-permute-start | bytes 1572872 | tf_op jit(solution)/shard_map/ppermute | solution.py:210
  251.8 59.7 %collective-permute-start.16 = (bf16[256,1024]{1,0:T(8,128)(2,1)}, bf16[256,1024]{1,0:T(8,128)(2,1)S(1)}, u32[]{:S(2)}, u32[]{:S(2)}) collective-permute-start(bf16[256,1024]{1,0:T(8,128)(2,1)} %get-tuple-element.31), channel_id=1, source_target_pairs={{24,0},{32,8},{40,16},{48,24},{56,32},{64,40},{72,48},{80,56},{88,... | collective-permute-start | bytes 1572872 | tf_op jit(solution)/shard_map/ppermute | solution.py:210
  253.1 58.4 %collective-permute-start.15 = (bf16[256,1024]{1,0:T(8,128)(2,1)}, bf16[256,1024]{1,0:T(8,128)(2,1)S(1)}, u32[]{:S(2)}, u32[]{:S(2)}) collective-permute-start(bf16[256,1024]{1,0:T(8,128)(2,1)} %get-tuple-element.32), channel_id=1, source_target_pairs={{16,0},{24,8},{32,16},{40,24},{48,32},{56,40},{64,48},{72,56},{80,... | collective-permute-start | bytes 1572872 | tf_op jit(solution)/shard_map/ppermute | solution.py:210
  255.1 56.5 %collective-permute-start.14 = (bf16[256,1024]{1,0:T(8,128)(2,1)}, bf16[256,1024]{1,0:T(8,128)(2,1)S(1)}, u32[]{:S(2)}, u32[]{:S(2)}) collective-permute-start(bf16[256,1024]{1,0:T(8,128)(2,1)} %get-tuple-element.29), channel_id=1, source_target_pairs={{8,0},{16,8},{24,16},{32,24},{40,32},{48,40},{56,48},{64,56},{72,6... | collective-permute-start | bytes 1572872 | tf_op jit(solution)/shard_map/ppermute | solution.py:210
  257.2 57.3 %copy-start.1 = (bf16[672,1024]{1,0:T(8,128)(2,1)S(1)}, bf16[672,1024]{1,0:T(8,128)(2,1)}, u32[]{:S(2)}) copy-start(bf16[672,1024]{1,0:T(8,128)(2,1)} %param.9) | copy-start | bytes 4128772
  311.5 2.4 copy-start.5
Sparse Core Ops, SparseCore 0:
  10.9 88.5 all-gather.4
  110.0 115.9 all-gather.6

commit v11 on v8

--- a/solution.py
+++ b/solution.py
@@ -236,11 +236,13 @@
     token_cols = (
         tokens_in.reshape(shard_rows, n_ctx, n_fsdp, out_rows).transpose(2, 0, 1, 3)
     )
-    token_cols = lax.all_to_all(token_cols, "fsdp", 0, 0, tiled=True)
     tag_columns = jnp.broadcast_to(own_segments.astype(jnp.bfloat16)[:, None], (shard_rows, HD))
     parcel = jnp.concatenate([own_keys, tag_columns], 1)
     arrived = [shifted(parcel, "ctx", hop) for hop in range(1, n_hops + 1)]
     window_parcel = jnp.concatenate(arrived[::-1] + [parcel], 0)
+    window_parcel, partner_tokens, token_cols = lax.optimization_barrier(
+        (window_parcel, partner_tokens, token_cols)
+    )
     window_keys = window_parcel[:, :kv_width]
     window_tags = window_parcel[:, kv_width].astype(jnp.int32)
     first_query = lax.axis_index("ctx") * shard_rows
@@ -267,6 +269,8 @@
         + lax.ppermute(partner_part, "ctx", partner)
     ).astype(jnp.bfloat16)
     arrived_values = [shifted(values, "ctx", hop) for hop in range(1, n_hops + 1)]
+    token_cols, _ = lax.optimization_barrier((token_cols, values))
+    token_cols = lax.all_to_all(token_cols, "fsdp", 0, 0, tiled=True)
     window_values = jnp.concatenate(arrived_values[::-1] + [values], 0)
     out_rows_attn, d_query_heads, key_terms = fused_attention(
         queries[0], window_keys, window_values, d_out[0], query_tags, key_tags[None, :]

time: 330 us -> 315 us (0.955)
  Pallas kernels: 86.1 us -> 65.3 us
  waiting for transfers between devices: 95.6 us -> 86.7 us
  starting transfers between devices: 57.3 us -> 64.1 us
  matrix products: 22.6 us -> 27.5 us
    pallas_call x1, Pallas kernels: 46.6 us -> 26.2 us  [peer_sum_scatter(): pl.pallas_call(functools.partial(peer_sum_kernel, axis, n), out_shape=jax...]
    ppermute x1, starting transfers between devices: 0.31 us -> 10.4 us  [shards(): lax.ppermute(partner_part, 'ctx', partner)]
    ppermute x16, waiting for transfers between devices: 91.8 us -> 83.4 us  [shifted(): return lax.ppermute(x, axis, pairs)]
    ppermute x1, starting transfers between devices: 7.18 us -> 0.09 us  [shards(): lax.ppermute(lax.dynamic_index_in_dim(token_halves, 1 - core, axis=2, kee...]
    unnamed x31 -> x23, local copies, waits for them, and re-layouts: 17.7 us -> 22.9 us
    transpose x1 -> x0, local copies, waits for them, and re-layouts: 4.96 us -> none  [shards(): tokens_in.reshape(shard_rows, n_ctx, n_fsdp, out_rows).transpose(2, 0, 1, 3)]
    ppermute x1, waiting for transfers between devices: 3.69 us -> 0.01 us  [shards(): lax.ppermute(lax.dynamic_index_in_dim(token_halves, 1 - core, axis=2, kee...]
    ppermute x16, starting transfers between devices: 42.3 us -> 45.9 us  [shifted(): return lax.ppermute(x, axis, pairs)]
  transfers between devices with their start and end apart: 23 -> 23, of which waited for: 11 -> 10; matrix products, arithmetic and copies ran while one was open for 21% -> 22% of each run, Pallas kernels for 26% -> 13%
where the time goes in v11:
time: 315 us; the launch traced here: 311 us
  waiting for transfers between devices  86.7 us (28%)
  Pallas kernels  65.3 us (21%)
  starting transfers between devices  64.1 us (20%)
  local copies, waits for them, and re-layouts  43.4 us (14%)
  matrix products  27.5 us (9%)
  between operations  14.3 us (5%)
  other arithmetic  9.27 us (3%)
    ppermute x16, waiting for transfers between devices, shifted(): return lax.ppermute(x, axis, pairs)  83.4 us
    ppermute x16, starting transfers between devices, shifted(): return lax.ppermute(x, axis, pairs)  45.9 us
    pallas_call x1, Pallas kernels, peer_sum_scatter(): pl.pallas_call(functools.partial(peer_sum_kernel, axis, n), out_shape=jax...  26.2 us
    pallas_call x1, Pallas kernels, fused_attention(): pl.pallas_call(attention_kernel, grid=(heads,), in_specs=[q_spec, kv_spec...  23.9 us
    unnamed x23, local copies, waits for them, and re-layouts  22.9 us
    pallas_call x1, Pallas kernels, value_grads(): pl.pallas_call(value_grad_kernel, grid=(heads,), in_specs=[q_spec, kv_spe...  15.2 us
    ppermute x1, starting transfers between devices, shards(): lax.ppermute(partner_part, 'ctx', partner)  10.4 us
    dot_general x1, matrix products, shards(): jnp.einsum('ftcr,ftn->crn', token_cols, grads_all, preferred_element_type...  7.73 us
  transfers between devices with their start and end apart: 23, of which 10 were waited for; matrix products, arithmetic and copies ran while one was open for 22% of the time, Pallas kernels for 13%

profile of v11, /device:TPU:28, one launch (start us, length us, event | category | flops | bytes accessed | tf_op | source)
XLA Modules:
  0.0 310.5 jit_solution(13700851317585384134)
XLA Ops:
  12.2 4.6 %collective-permute-start = (bf16[256,1152]{1,0:T(8,128)(2,1)}, bf16[256,1152]{1,0:T(8,128)(2,1)}, u32[]{:S(2)}, u32[]{:S(2)}) collective-permute-start(bf16[256,1152]{1,0:T(8,128)(2,1)} %pad_maximum_fusion), channel_id=1, source_target_pairs={{0,32},{8,40},{16,48},{24,56},{32,64},{40,72},{48,80},{56,88},{64,... | collective-permute-start | bytes 1769480 | tf_op jit(solution)/shard_map/ppermute | solution.py:210
  16.8 3.2 %collective-permute-start.1 = (bf16[256,1152]{1,0:T(8,128)(2,1)}, bf16[256,1152]{1,0:T(8,128)(2,1)}, u32[]{:S(2)}, u32[]{:S(2)}) collective-permute-start(bf16[256,1152]{1,0:T(8,128)(2,1)} %pad_maximum_fusion), channel_id=1, source_target_pairs={{0,24},{8,32},{16,40},{24,48},{32,56},{40,64},{48,72},{56,80},{64,... | collective-permute-start | bytes 1769480 | tf_op jit(solution)/shard_map/ppermute | solution.py:210
  20.0 4.5 %copy.20 = bf16[1,256,5376]{1,2,0:T(8,128)(2,1)} copy(bf16[1,256,5376]{2,1,0:T(8,128)(2,1)} %param.6) | data formatting | bytes 5505024 | tf_op args[0]
  26.1 3.7 %collective-permute-start.2 = (bf16[256,1152]{1,0:T(8,128)(2,1)}, bf16[256,1152]{1,0:T(8,128)(2,1)}, u32[]{:S(2)}, u32[]{:S(2)}) collective-permute-start(bf16[256,1152]{1,0:T(8,128)(2,1)} %pad_maximum_fusion), channel_id=1, source_target_pairs={{0,16},{8,24},{16,32},{24,40},{32,48},{40,56},{48,64},{56,72},{64,... | collective-permute-start | bytes 1769480 | tf_op jit(solution)/shard_map/ppermute | solution.py:210
  31.7 5.3 %reshape_squeeze.7 = bf16[256,16,8,42]{0,3,2,1:T(8,128)(2,1)} reshape(bf16[1,256,5376]{1,2,0:T(8,128)(2,1)} %copy.20) | data formatting | bytes 5505024 | tf_op jit(solution)/shard_map/reshape;squeeze | solution.py:237
  40.1 8.5 %collective-permute-done.2 = bf16[256,1152]{1,0:T(8,128)(2,1)} collective-permute-done((bf16[256,1152]{1,0:T(8,128)(2,1)}, bf16[256,1152]{1,0:T(8,128)(2,1)}, u32[]{:S(2)}, u32[]{:S(2)}) %collective-permute-start.2) | collective-permute-done | bytes 589856 | tf_op jit(solution)/shard_map/ppermute | solution.py:210
  49.7 4.7 %collective-permute-done.3 = bf16[256,1152]{1,0:T(8,128)(2,1)} collective-permute-done((bf16[256,1152]{1,0:T(8,128)(2,1)}, bf16[256,1152]{1,0:T(8,128)(2,1)}, u32[]{:S(2)}, u32[]{:S(2)}) %collective-permute-start.3) | collective-permute-done | bytes 589856 | tf_op jit(solution)/shard_map/ppermute | solution.py:210
  58.3 15.2 %shard_map.101 = bf16[1280,1024]{1,0:T(8,128)(2,1)} custom-call(bf16[256,2048]{1,0:T(8,128)(2,1)} %bitcast.65, bf16[1280,1024]{1,0:T(8,128)(2,1)} %slice.36.k_ref, bf16[256,2048]{1,0:T(8,128)(2,1)} %bitcast.67, s32[256,1]{1,0:T(8,128)} %copy.22.qtag_ref, s32[1,1280]{1,0:T(1,128)} %compare_select_fusion.ktag_ref), custom_call_target="tpu_custom_call" | custom-call | flops 2684354560 | bytes 7340032 | tf_op jit(solution)/shard_map/pallas_call | solution.py:79
  77.8 7.2 %collective-permute-start.6 = (bf16[256,1024]{1,0:T(8,128)(2,1)S(1)}, bf16[256,1024]{1,0:T(8,128)(2,1)S(1)}, u32[]{:S(2)}, u32[]{:S(2)}) collective-permute-start(bf16[256,1024]{1,0:T(8,128)(2,1)S(1)} %get-tuple-element.40), channel_id=1, source_target_pairs={{16,0},{24,8},{32,16},{40,24},{48,32},{56,40},{64,48},{72,56},{80,... | collective-permute-start | bytes 1572872 | tf_op jit(solution)/shard_map/ppermute | solution.py:210
  85.0 4.8 %collective-permute-start.5 = (bf16[256,1024]{1,0:T(8,128)(2,1)S(1)}, bf16[256,1024]{1,0:T(8,128)(2,1)S(1)}, u32[]{:S(2)}, u32[]{:S(2)}) collective-permute-start(bf16[256,1024]{1,0:T(8,128)(2,1)S(1)} %get-tuple-element.37), channel_id=1, source_target_pairs={{8,0},{16,8},{24,16},{32,24},{40,32},{48,40},{56,48},{64,56},{72,6... | collective-permute-start | bytes 1572872 | tf_op jit(solution)/shard_map/ppermute | solution.py:210
  90.0 8.8 %collective-permute-done.7 = bf16[256,1024]{1,0:T(8,128)(2,1)S(1)} collective-permute-done((bf16[256,1024]{1,0:T(8,128)(2,1)S(1)}, bf16[256,1024]{1,0:T(8,128)(2,1)S(1)}, u32[]{:S(2)}, u32[]{:S(2)}) %collective-permute-start.7) | collective-permute-done | bytes 524320 | tf_op jit(solution)/shard_map/ppermute | solution.py:210
  98.7 6.2 %collective-permute-done.6 = bf16[256,1024]{1,0:T(8,128)(2,1)S(1)} collective-permute-done((bf16[256,1024]{1,0:T(8,128)(2,1)S(1)}, bf16[256,1024]{1,0:T(8,128)(2,1)S(1)}, u32[]{:S(2)}, u32[]{:S(2)}) %collective-permute-start.6) | collective-permute-done | bytes 524320 | tf_op jit(solution)/shard_map/ppermute | solution.py:210
  104.9 2.6 collective-permute-done.5
  109.9 5.3 %convolution_bitcast_fusion = f32[256,1024]{1,0:T(8,128)} fusion(bf16[256,8,336]{0,2,1:T(8,128)(2,1)S(1)} %collective-permute-done.4, bf16[8,336,1024]{2,1,0:T(8,128)(2,1)} %bitcast.52), kind=kOutput, calls=%fused_computation.13 | convolution fusion | flops 1409286144 | bytes 7929856 | tf_op jit(solution)/shard_map/tfr,frn->tn/dot_general | solution.py:266
  115.2 10.4 %collective-permute-start.9 = (f32[256,1024]{1,0:T(8,128)}, f32[256,1024]{1,0:T(8,128)S(1)}, u32[]{:S(2)}, u32[]{:S(2)}) collective-permute-start(f32[256,1024]{1,0:T(8,128)} %convolution_bitcast_fusion), channel_id=1, source_target_pairs={{0,8},{8,0},{16,24},{24,16},{32,40},{40,32},{48,56},{56,48},{64,72... | collective-permute-start | bytes 3145736 | tf_op jit(solution)/shard_map/ppermute | solution.py:269
  125.6 3.2 %collective-permute-done.9 = f32[256,1024]{1,0:T(8,128)S(1)} collective-permute-done((f32[256,1024]{1,0:T(8,128)}, f32[256,1024]{1,0:T(8,128)S(1)}, u32[]{:S(2)}, u32[]{:S(2)}) %collective-permute-start.9) | collective-permute-done | bytes 1048608 | tf_op jit(solution)/shard_map/ppermute | solution.py:269
  128.8 5.1 %add_convert_fusion.1 = bf16[256,1024]{1,0:T(8,128)(2,1)S(1)} fusion(f32[256,1024]{1,0:T(8,128)S(1)} %collective-permute-done.9, bf16[8,336,1024]{2,1,0:T(8,128)(2,1)} %bitcast.53, bf16[256,8,2,336]{0,3,2,1:T(8,128)(2,1)} %bitcast.57, s32[]{:T(128)S(6)} %select_n.48), kind=kOutput, calls=%fused_computation.15 | convolution fusion | flops 1409810432 | bytes 8454148 | tf_op jit(solution)/shard_map/tfr,frn->tn/dot_general | solution.py:268
  133.9 4.4 %collective-permute-start.10 = (bf16[256,1024]{1,0:T(8,128)(2,1)S(1)}, bf16[256,1024]{1,0:T(8,128)(2,1)}, u32[]{:S(2)}, u32[]{:S(2)}) collective-permute-start(bf16[256,1024]{1,0:T(8,128)(2,1)S(1)} %add_convert_fusion.1), channel_id=1, source_target_pairs={{0,32},{8,40},{16,48},{24,56},{32,64},{40,72},{48,80},{56,88},{64,... | collective-permute-start | bytes 1572872 | tf_op jit(solution)/shard_map/ppermute | solution.py:210
  140.6 2.8 collective-permute-start.12
  145.4 5.3 %convolution_convert_fusion = bf16[256,8,336]{0,2,1:T(8,128)(2,1)} fusion(bf16[8,336,1024]{2,1,0:T(8,128)(2,1)} %bitcast.54, bf16[256,1024]{1,0:T(8,128)(2,1)S(1)} %collective-permute-done.18), kind=kOutput, calls=%fused_computation.5 | convolution fusion | flops 1409974272 | bytes 7405568 | tf_op jit(solution)/shard_map/tn,frn->tfr/dot_general | solution.py:287
  151.0 3.1 copy.25
  154.1 7.2 %all-to-all-start = ((bf16[8,256,16,42]{1,2,3,0:T(8,128)(2,1)}), bf16[8,256,16,42]{1,2,3,0:T(8,128)(2,1)}, u32[]{:S(2)}, u32[]{:S(2)}) async-start(bf16[8,256,16,42]{1,2,3,0:T(8,128)(2,1)} %copy.25), calls=%async_computation | async-start | bytes 5505024 | tf_op jit(solution)/shard_map/all_to_all | solution.py:273
  165.0 30.4 %collective-permute-done.12 = bf16[256,1024]{1,0:T(8,128)(2,1)} collective-permute-done((bf16[256,1024]{1,0:T(8,128)(2,1)S(1)}, bf16[256,1024]{1,0:T(8,128)(2,1)}, u32[]{:S(2)}, u32[]{:S(2)}) %collective-permute-start.12) | collective-permute-done | bytes 524320 | tf_op jit(solution)/shard_map/ppermute | solution.py:210
  197.3 3.9 %collective-permute-done.13 = bf16[256,1024]{1,0:T(8,128)(2,1)S(1)} collective-permute-done((bf16[256,1024]{1,0:T(8,128)(2,1)S(1)}, bf16[256,1024]{1,0:T(8,128)(2,1)S(1)}, u32[]{:S(2)}, u32[]{:S(2)}) %collective-permute-start.13) | collective-permute-done | bytes 524320 | tf_op jit(solution)/shard_map/ppermute | solution.py:210
  202.9 23.9 %shard_map.102 = (bf16[256,2048]{1,0:T(8,128)(2,1)}, bf16[256,2048]{1,0:T(8,128)(2,1)}, bf16[1280,1024]{1,0:T(8,128)(2,1)}) custom-call(bf16[256,2048]{1,0:T(8,128)(2,1)} %bitcast.66, bf16[1280,1024]{1,0:T(8,128)(2,1)} %slice.36.k_ref, bf16[1280,1024]{1,0:T(8,128)(2,1)} %constant_dynamic-update-slice_fusion.5.v_ref, bf16[256,2048]{1,0:T(8,128)(2,1)} %bitcast.68, ...), custom_call_target="tpu_custom_call" | custom-call | flops 6710886400 | bytes 12058624 | tf_op jit(solution)/shard_map/pallas_call | solution.py:98
  226.8 2.9 fusion.20
  236.1 4.2 %fusion.7 = bf16[256,8,1,336]{0,3,1,2:T(8,128)(2,1)S(1)} fusion(bf16[8,336,1024]{2,1,0:T(8,128)(2,1)} %bitcast.55, bf16[256,1024]{1,0:T(8,128)(2,1)S(1)} %copy-done.4), kind=kOutput, calls=%fused_computation.7 | convolution fusion | flops 1409974272 | bytes 7405568 | tf_op jit(solution)/shard_map/tn,frn->tfr/dot_general | solution.py:284
  242.5 4.5 %copy.27 = bf16[1,256,5376]{2,1,0:T(8,128)(2,1)} copy(bf16[1,256,5376]{1,2,0:T(8,128)(2,1)} %bitcast.59) | data formatting | bytes 5505024
  247.0 18.2 %collective-permute-done.17 = bf16[256,1024]{1,0:T(8,128)(2,1)} collective-permute-done((bf16[256,1024]{1,0:T(8,128)(2,1)}, bf16[256,1024]{1,0:T(8,128)(2,1)}, u32[]{:S(2)}, u32[]{:S(2)}) %collective-permute-start.17) | collective-permute-done | bytes 524320 | tf_op jit(solution)/shard_map/ppermute | solution.py:210
  265.2 2.9 fusion.14
  268.2 7.7 %bitcast_convert_fusion.x_ref = bf16[16,42,1024]{2,1,0:T(8,128)(2,1)} fusion(bf16[8,256,1024]{2,1,0:T(8,128)(2,1)} %bitcast.64, bf16[8,256,16,42]{1,2,3,0:T(8,128)(2,1)} %all-to-all-done), kind=kOutput, calls=%fused_computation.2 | convolution fusion | flops 2819260416 | bytes 8323072 | tf_op jit(solution)/shard_map/ftcr,ftn->crn/dot_general | solution.py:280
  275.9 26.2 %shard_map.103 = f32[42,1024]{1,0:T(8,128)} custom-call(bf16[16,42,1024]{2,1,0:T(8,128)(2,1)} %bitcast_convert_fusion.x_ref), custom_call_target="tpu_custom_call" | custom-call | tf_op jit(solution)/shard_map/pallas_call | solution.py:192
  (66 shorter events, 45.4 us)
Async XLA Ops:
  7.2 1.3 copy-start
  7.2 102.7 %all-gather.5.cloned.1.call-start = ((), (), s32[]{:S(2)}) async-start(), calls=%async_computation.1 | async-start | bytes 6193152 | tf_op jit(solution)/shard_map/all_gather | solution.py:226
  9.4 237.6 %all-gather.7.cloned.1.call-start = ((), (), s32[]{:S(2)}) async-start(), calls=%async_computation.2 | async-start | bytes 4718592 | tf_op jit(solution)/shard_map/all_gather | solution.py:264
  12.2 25.6 %collective-permute-start = (bf16[256,1152]{1,0:T(8,128)(2,1)}, bf16[256,1152]{1,0:T(8,128)(2,1)}, u32[]{:S(2)}, u32[]{:S(2)}) collective-permute-start(bf16[256,1152]{1,0:T(8,128)(2,1)} %pad_maximum_fusion), channel_id=1, source_target_pairs={{0,32},{8,40},{16,48},{24,56},{32,64},{40,72},{48,80},{56,88},{64,... | collective-permute-start | bytes 1769480 | tf_op jit(solution)/shard_map/ppermute | solution.py:210
  16.8 22.1 %collective-permute-start.1 = (bf16[256,1152]{1,0:T(8,128)(2,1)}, bf16[256,1152]{1,0:T(8,128)(2,1)}, u32[]{:S(2)}, u32[]{:S(2)}) collective-permute-start(bf16[256,1152]{1,0:T(8,128)(2,1)} %pad_maximum_fusion), channel_id=1, source_target_pairs={{0,24},{8,32},{16,40},{24,48},{32,56},{40,64},{48,72},{56,80},{64,... | collective-permute-start | bytes 1769480 | tf_op jit(solution)/shard_map/ppermute | solution.py:210
  26.0 11.0 %copy-start.5 = (s32[1,256]{1,0:T(1,128)S(1)}, s32[1,256]{1,0:T(1,128)}, u32[]{:S(2)}) copy-start(s32[1,256]{1,0:T(1,128)} %param.11) | copy-start | bytes 3076
  26.0 29.6 %collective-permute-start.4 = (bf16[256,8,336]{0,2,1:T(8,128)(2,1)S(1)}, bf16[256,8,336]{0,2,1:T(8,128)(2,1)S(1)}, u32[]{:S(2)}, u32[]{:S(2)}) collective-permute-start(bf16[256,8,336]{0,2,1:T(8,128)(2,1)S(1)} %dynamic-slice_bitcast_fusion), channel_id=1, source_target_pairs={{0,8},{8,0},{16,24},{24,16},{32,40},{40,32},{48,56},{56,48},{64,72... | collective-permute-start | bytes 4128776 | tf_op jit(solution)/shard_map/ppermute | solution.py:232
  26.1 22.5 %collective-permute-start.2 = (bf16[256,1152]{1,0:T(8,128)(2,1)}, bf16[256,1152]{1,0:T(8,128)(2,1)}, u32[]{:S(2)}, u32[]{:S(2)}) collective-permute-start(bf16[256,1152]{1,0:T(8,128)(2,1)} %pad_maximum_fusion), channel_id=1, source_target_pairs={{0,16},{8,24},{16,32},{24,40},{32,48},{40,56},{48,64},{56,72},{64,... | collective-permute-start | bytes 1769480 | tf_op jit(solution)/shard_map/ppermute | solution.py:210
  29.8 24.6 %collective-permute-start.3 = (bf16[256,1152]{1,0:T(8,128)(2,1)}, bf16[256,1152]{1,0:T(8,128)(2,1)}, u32[]{:S(2)}, u32[]{:S(2)}) collective-permute-start(bf16[256,1152]{1,0:T(8,128)(2,1)} %pad_maximum_fusion), channel_id=1, source_target_pairs={{0,8},{8,16},{16,24},{24,32},{32,40},{40,48},{48,56},{56,64},{64,7... | collective-permute-start | bytes 1769480 | tf_op jit(solution)/shard_map/ppermute | solution.py:210
  37.0 18.5 %copy-start.3 = (bf16[1,256,1024]{2,1,0:T(8,128)(2,1)S(1)}, bf16[1,256,1024]{2,1,0:T(8,128)(2,1)}, u32[]{:S(2)}) copy-start(bf16[1,256,1024]{2,1,0:T(8,128)(2,1)} %param.8) | copy-start | bytes 1572868
  75.2 14.7 %collective-permute-start.8 = (bf16[256,1024]{1,0:T(8,128)(2,1)S(1)}, bf16[256,1024]{1,0:T(8,128)(2,1)S(1)}, u32[]{:S(2)}, u32[]{:S(2)}) collective-permute-start(bf16[256,1024]{1,0:T(8,128)(2,1)S(1)} %get-tuple-element.38), channel_id=1, source_target_pairs={{32,0},{40,8},{48,16},{56,24},{64,32},{72,40},{80,48},{88,56},{96,... | collective-permute-start | bytes 1572872 | tf_op jit(solution)/shard_map/ppermute | solution.py:210
  76.5 22.2 %collective-permute-start.7 = (bf16[256,1024]{1,0:T(8,128)(2,1)S(1)}, bf16[256,1024]{1,0:T(8,128)(2,1)S(1)}, u32[]{:S(2)}, u32[]{:S(2)}) collective-permute-start(bf16[256,1024]{1,0:T(8,128)(2,1)S(1)} %get-tuple-element.39), channel_id=1, source_target_pairs={{24,0},{32,8},{40,16},{48,24},{56,32},{64,40},{72,48},{80,56},{88,... | collective-permute-start | bytes 1572872 | tf_op jit(solution)/shard_map/ppermute | solution.py:210
  77.8 27.1 %collective-permute-start.6 = (bf16[256,1024]{1,0:T(8,128)(2,1)S(1)}, bf16[256,1024]{1,0:T(8,128)(2,1)S(1)}, u32[]{:S(2)}, u32[]{:S(2)}) collective-permute-start(bf16[256,1024]{1,0:T(8,128)(2,1)S(1)} %get-tuple-element.40), channel_id=1, source_target_pairs={{16,0},{24,8},{32,16},{40,24},{48,32},{56,40},{64,48},{72,56},{80,... | collective-permute-start | bytes 1572872 | tf_op jit(solution)/shard_map/ppermute | solution.py:210
  85.0 22.5 %collective-permute-start.5 = (bf16[256,1024]{1,0:T(8,128)(2,1)S(1)}, bf16[256,1024]{1,0:T(8,128)(2,1)S(1)}, u32[]{:S(2)}, u32[]{:S(2)}) collective-permute-start(bf16[256,1024]{1,0:T(8,128)(2,1)S(1)} %get-tuple-element.37), channel_id=1, source_target_pairs={{8,0},{16,8},{24,16},{32,24},{40,32},{48,40},{56,48},{64,56},{72,6... | collective-permute-start | bytes 1572872 | tf_op jit(solution)/shard_map/ppermute | solution.py:210
  109.9 15.7 %copy-start.4 = (bf16[256,1024]{1,0:T(8,128)(2,1)S(1)}, bf16[256,1024]{1,0:T(8,128)(2,1)}, u32[]{:S(2)}) copy-start(bf16[256,1024]{1,0:T(8,128)(2,1)} %add_convert_fusion.2) | copy-start | bytes 1572868
  115.2 13.6 %collective-permute-start.9 = (f32[256,1024]{1,0:T(8,128)}, f32[256,1024]{1,0:T(8,128)S(1)}, u32[]{:S(2)}, u32[]{:S(2)}) collective-permute-start(f32[256,1024]{1,0:T(8,128)} %convolution_bitcast_fusion), channel_id=1, source_target_pairs={{0,8},{8,0},{16,24},{24,16},{32,40},{40,32},{48,56},{56,48},{64,72... | collective-permute-start | bytes 3145736 | tf_op jit(solution)/shard_map/ppermute | solution.py:269
  125.6 19.8 %collective-permute-start.18 = (bf16[256,1024]{1,0:T(8,128)(2,1)S(1)}, bf16[256,1024]{1,0:T(8,128)(2,1)S(1)}, u32[]{:S(2)}, u32[]{:S(2)}) collective-permute-start(bf16[256,1024]{1,0:T(8,128)(2,1)S(1)} %copy-done.4), channel_id=1, source_target_pairs={{0,8},{8,0},{16,24},{24,16},{32,40},{40,32},{48,56},{56,48},{64,72... | collective-permute-start | bytes 1572872 | tf_op jit(solution)/shard_map/ppermute | solution.py:285
  133.9 27.4 %collective-permute-start.10 = (bf16[256,1024]{1,0:T(8,128)(2,1)S(1)}, bf16[256,1024]{1,0:T(8,128)(2,1)}, u32[]{:S(2)}, u32[]{:S(2)}) collective-permute-start(bf16[256,1024]{1,0:T(8,128)(2,1)S(1)} %add_convert_fusion.1), channel_id=1, source_target_pairs={{0,32},{8,40},{16,48},{24,56},{32,64},{40,72},{48,80},{56,88},{64,... | collective-permute-start | bytes 1572872 | tf_op jit(solution)/shard_map/ppermute | solution.py:210
  138.3 12.8 %copy-start.2 = (bf16[256,16,8,42]{0,3,2,1:T(8,128)(2,1)S(1)}, bf16[256,16,8,42]{0,3,2,1:T(8,128)(2,1)}, u32[]{:S(2)}) copy-start(bf16[256,16,8,42]{0,3,2,1:T(8,128)(2,1)} %reshape_squeeze.7) | copy-start | bytes 8257540
  138.3 24.9 %collective-permute-start.11 = (bf16[256,1024]{1,0:T(8,128)(2,1)S(1)}, bf16[256,1024]{1,0:T(8,128)(2,1)}, u32[]{:S(2)}, u32[]{:S(2)}) collective-permute-start(bf16[256,1024]{1,0:T(8,128)(2,1)S(1)} %add_convert_fusion.1), channel_id=1, source_target_pairs={{0,24},{8,32},{16,40},{24,48},{32,56},{40,64},{48,72},{56,80},{64,... | collective-permute-start | bytes 1572872 | tf_op jit(solution)/shard_map/ppermute | solution.py:210
  140.6 54.8 %collective-permute-start.12 = (bf16[256,1024]{1,0:T(8,128)(2,1)S(1)}, bf16[256,1024]{1,0:T(8,128)(2,1)}, u32[]{:S(2)}, u32[]{:S(2)}) collective-permute-start(bf16[256,1024]{1,0:T(8,128)(2,1)S(1)} %add_convert_fusion.1), channel_id=1, source_target_pairs={{0,16},{8,24},{16,32},{24,40},{32,48},{40,56},{48,64},{56,72},{64,... | collective-permute-start | bytes 1572872 | tf_op jit(solution)/shard_map/ppermute | solution.py:210
  143.4 57.8 %collective-permute-start.13 = (bf16[256,1024]{1,0:T(8,128)(2,1)S(1)}, bf16[256,1024]{1,0:T(8,128)(2,1)S(1)}, u32[]{:S(2)}, u32[]{:S(2)}) collective-permute-start(bf16[256,1024]{1,0:T(8,128)(2,1)S(1)} %add_convert_fusion.1), channel_id=1, source_target_pairs={{0,8},{8,16},{16,24},{24,32},{32,40},{40,48},{48,56},{56,64},{64,7... | collective-permute-start | bytes 1572872 | tf_op jit(solution)/shard_map/ppermute | solution.py:210
  150.7 89.7 %collective-permute-start.19 = (bf16[256,8,336]{0,2,1:T(8,128)(2,1)}, bf16[256,8,336]{0,2,1:T(8,128)(2,1)S(1)}, u32[]{:S(2)}, u32[]{:S(2)}) collective-permute-start(bf16[256,8,336]{0,2,1:T(8,128)(2,1)} %convolution_convert_fusion), channel_id=1, source_target_pairs={{0,8},{8,0},{16,24},{24,16},{32,40},{40,32},{48,56},{56,48},{64,72... | collective-permute-start | bytes 4128776 | tf_op jit(solution)/shard_map/ppermute | solution.py:286
  154.1 114.1 %all-to-all-start = ((bf16[8,256,16,42]{1,2,3,0:T(8,128)(2,1)}), bf16[8,256,16,42]{1,2,3,0:T(8,128)(2,1)}, u32[]{:S(2)}, u32[]{:S(2)}) async-start(bf16[8,256,16,42]{1,2,3,0:T(8,128)(2,1)} %copy.25), calls=%async_computation | async-start | bytes 5505024 | tf_op jit(solution)/shard_map/all_to_all | solution.py:273
  229.7 35.6 %collective-permute-start.17 = (bf16[256,1024]{1,0:T(8,128)(2,1)}, bf16[256,1024]{1,0:T(8,128)(2,1)}, u32[]{:S(2)}, u32[]{:S(2)}) collective-permute-start(bf16[256,1024]{1,0:T(8,128)(2,1)} %get-tuple-element.34), channel_id=1, source_target_pairs={{32,0},{40,8},{48,16},{56,24},{64,32},{72,40},{80,48},{88,56},{96,... | collective-permute-start | bytes 1572872 | tf_op jit(solution)/shard_map/ppermute | solution.py:210
  231.0 34.3 %collective-permute-start.16 = (bf16[256,1024]{1,0:T(8,128)(2,1)}, bf16[256,1024]{1,0:T(8,128)(2,1)}, u32[]{:S(2)}, u32[]{:S(2)}) collective-permute-start(bf16[256,1024]{1,0:T(8,128)(2,1)} %get-tuple-element.35), channel_id=1, source_target_pairs={{24,0},{32,8},{40,16},{48,24},{56,32},{64,40},{72,48},{80,56},{88,... | collective-permute-start | bytes 1572872 | tf_op jit(solution)/shard_map/ppermute | solution.py:210
  232.3 33.0 %collective-permute-start.15 = (bf16[256,1024]{1,0:T(8,128)(2,1)}, bf16[256,1024]{1,0:T(8,128)(2,1)}, u32[]{:S(2)}, u32[]{:S(2)}) collective-permute-start(bf16[256,1024]{1,0:T(8,128)(2,1)} %get-tuple-element.36), channel_id=1, source_target_pairs={{16,0},{24,8},{32,16},{40,24},{48,32},{56,40},{64,48},{72,56},{80,... | collective-permute-start | bytes 1572872 | tf_op jit(solution)/shard_map/ppermute | solution.py:210
  234.2 31.1 %collective-permute-start.14 = (bf16[256,1024]{1,0:T(8,128)(2,1)}, bf16[256,1024]{1,0:T(8,128)(2,1)}, u32[]{:S(2)}, u32[]{:S(2)}) collective-permute-start(bf16[256,1024]{1,0:T(8,128)(2,1)} %get-tuple-element.33), channel_id=1, source_target_pairs={{8,0},{16,8},{24,16},{32,24},{40,32},{48,40},{56,48},{64,56},{72,6... | collective-permute-start | bytes 1572872 | tf_op jit(solution)/shard_map/ppermute | solution.py:210
  268.2 35.5 %copy-start.1 = (bf16[672,1024]{1,0:T(8,128)(2,1)S(1)}, bf16[672,1024]{1,0:T(8,128)(2,1)}, u32[]{:S(2)}) copy-start(bf16[672,1024]{1,0:T(8,128)(2,1)} %param.9) | copy-start | bytes 4128772
Sparse Core Ops, SparseCore 0:
  10.9 88.5 all-gather.4
  110.0 116.7 all-gather.6

commit v12 on v11

--- a/solution.py
+++ b/solution.py
@@ -251,12 +251,21 @@
     query_tags = own_segments.astype(jnp.int32)[:, None]
     own_start = n_hops * shard_rows
 
-    def returned_sum(terms):
-        total = terms[own_start:].astype(jnp.float32)
+    def returned_parts(terms):
+        parts = [terms[own_start:]]
         for hop in range(1, n_hops + 1):
             low_edge = (n_hops - hop) * shard_rows
-            total = total + shifted(terms[low_edge : low_edge + shard_rows], "ctx", -hop).astype(jnp.float32)
+            parts.append(shifted(terms[low_edge : low_edge + shard_rows], "ctx", -hop))
+        return parts
+
+    def added(parts):
+        total = parts[0].astype(jnp.float32)
+        for part in parts[1:]:
+            total = total + part.astype(jnp.float32)
         return total.astype(jnp.bfloat16)
+
+    def returned_sum(terms):
+        return added(returned_parts(terms))
 
     value_terms = value_grads(queries[0], window_keys, d_out[0], query_tags, key_tags[None, :])
     d_values_low = returned_sum(value_terms)
@@ -275,12 +284,14 @@
     out_rows_attn, d_query_heads, key_terms = fused_attention(
         queries[0], window_keys, window_values, d_out[0], query_tags, key_tags[None, :]
     )
-    d_key_rows = returned_sum(key_terms)
+    key_parts = returned_parts(key_terms)
     grads_all, _ = lax.optimization_barrier((grads_all, key_terms))
     weight_part = jnp.einsum(
         "ftcr,ftn->crn", token_cols, grads_all, preferred_element_type=jnp.float32
     )
     d_weight = peer_sum_scatter(weight_part.astype(jnp.bfloat16), "ctx", 3)
+    d_weight, key_parts = lax.optimization_barrier((d_weight, key_parts))
+    d_key_rows = added(key_parts)
     d_mine = jnp.einsum("tn,frn->tfr", d_values_low, w_mine, preferred_element_type=jnp.float32).astype(jnp.bfloat16)
     partner_grads = lax.ppermute(d_values_low, "ctx", partner)
     d_other = lax.ppermute(

time: 315 us -> 326 us (1.035)
  Pallas kernels: 65.3 us -> 88.3 us
  waiting for transfers between devices: 86.7 us -> 81.5 us
    pallas_call x1, Pallas kernels: 26.2 us -> 49.1 us  [peer_sum_scatter(): pl.pallas_call(functools.partial(peer_sum_kernel, axis, n), out_shape=jax...]
    ppermute x1, starting transfers between devices: 0.01 us -> 10.5 us  [shards(): partner_grads = lax.ppermute(d_values_low, 'ctx', partner)]
    ppermute x1, starting transfers between devices: 10.4 us -> 0.05 us  [shards(): lax.ppermute(partner_part, 'ctx', partner)]
    unnamed x23 -> x27, local copies, waits for them, and re-layouts: 22.9 us -> 21 us
  transfers between devices with their start and end apart: 23 -> 23, of which waited for: 10 -> 8; matrix products, arithmetic and copies ran while one was open for 22% -> 22% of each run, Pallas kernels for 13% -> 27%
where the time goes in v12:
time: 326 us; the launch traced here: 324 us
  Pallas kernels  88.3 us (27%)
  waiting for transfers between devices  81.5 us (25%)
  starting transfers between devices  63.4 us (19%)
  local copies, waits for them, and re-layouts  41.4 us (13%)
  matrix products  25.6 us (8%)
  between operations  14.4 us (4%)
  other arithmetic  9.11 us (3%)
    ppermute x16, waiting for transfers between devices, shifted(): return lax.ppermute(x, axis, pairs)  81.5 us
    pallas_call x1, Pallas kernels, peer_sum_scatter(): pl.pallas_call(functools.partial(peer_sum_kernel, axis, n), out_shape=jax...  49.1 us
    ppermute x16, starting transfers between devices, shifted(): return lax.ppermute(x, axis, pairs)  44.7 us
    pallas_call x1, Pallas kernels, fused_attention(): pl.pallas_call(attention_kernel, grid=(heads,), in_specs=[q_spec, kv_spec...  24 us
    unnamed x27, local copies, waits for them, and re-layouts  21 us
    pallas_call x1, Pallas kernels, value_grads(): pl.pallas_call(value_grad_kernel, grid=(heads,), in_specs=[q_spec, kv_spe...  15.2 us
    ppermute x1, starting transfers between devices, shards(): partner_grads = lax.ppermute(d_values_low, 'ctx', partner)  10.5 us
    dot_general x1, matrix products, shards(): jnp.einsum('ftcr,ftn->crn', token_cols, grads_all, preferred_element_type...  7.72 us
  transfers between devices with their start and end apart: 23, of which 8 were waited for; matrix products, arithmetic and copies ran while one was open for 22% of the time, Pallas kernels for 27%

profile of v12, /device:TPU:28, one launch (start us, length us, event | category | flops | bytes accessed | tf_op | source)
XLA Modules:
  0.0 323.7 jit_solution(5987969028152708497)
XLA Ops:
  12.2 4.6 %collective-permute-start = (bf16[256,1152]{1,0:T(8,128)(2,1)}, bf16[256,1152]{1,0:T(8,128)(2,1)}, u32[]{:S(2)}, u32[]{:S(2)}) collective-permute-start(bf16[256,1152]{1,0:T(8,128)(2,1)} %pad_maximum_fusion), channel_id=1, source_target_pairs={{0,32},{8,40},{16,48},{24,56},{32,64},{40,72},{48,80},{56,88},{64,... | collective-permute-start | bytes 1769480 | tf_op jit(solution)/shard_map/ppermute | solution.py:210
  16.8 3.2 collective-permute-start.1
  20.0 4.6 %copy.20 = bf16[1,256,5376]{1,2,0:T(8,128)(2,1)} copy(bf16[1,256,5376]{2,1,0:T(8,128)(2,1)} %param.6) | data formatting | bytes 5505024 | tf_op args[0]
  26.1 3.7 %collective-permute-start.2 = (bf16[256,1152]{1,0:T(8,128)(2,1)}, bf16[256,1152]{1,0:T(8,128)(2,1)}, u32[]{:S(2)}, u32[]{:S(2)}) collective-permute-start(bf16[256,1152]{1,0:T(8,128)(2,1)} %pad_maximum_fusion), channel_id=1, source_target_pairs={{0,16},{8,24},{16,32},{24,40},{32,48},{40,56},{48,64},{56,72},{64,... | collective-permute-start | bytes 1769480 | tf_op jit(solution)/shard_map/ppermute | solution.py:210
  29.8 1.9 collective-permute-start.3
  31.7 5.3 %reshape_squeeze.7 = bf16[256,16,8,42]{0,3,2,1:T(8,128)(2,1)} reshape(bf16[1,256,5376]{1,2,0:T(8,128)(2,1)} %copy.20) | data formatting | bytes 5505024 | tf_op jit(solution)/shard_map/reshape;squeeze | solution.py:237
  40.1 8.5 %collective-permute-done.2 = bf16[256,1152]{1,0:T(8,128)(2,1)} collective-permute-done((bf16[256,1152]{1,0:T(8,128)(2,1)}, bf16[256,1152]{1,0:T(8,128)(2,1)}, u32[]{:S(2)}, u32[]{:S(2)}) %collective-permute-start.2) | collective-permute-done | bytes 589856 | tf_op jit(solution)/shard_map/ppermute | solution.py:210
  49.7 4.7 %collective-permute-done.3 = bf16[256,1152]{1,0:T(8,128)(2,1)} collective-permute-done((bf16[256,1152]{1,0:T(8,128)(2,1)}, bf16[256,1152]{1,0:T(8,128)(2,1)}, u32[]{:S(2)}, u32[]{:S(2)}) %collective-permute-start.3) | collective-permute-done | bytes 589856 | tf_op jit(solution)/shard_map/ppermute | solution.py:210
  58.4 15.2 %shard_map.101 = bf16[1280,1024]{1,0:T(8,128)(2,1)} custom-call(bf16[256,2048]{1,0:T(8,128)(2,1)} %bitcast.65, bf16[1280,1024]{1,0:T(8,128)(2,1)} %slice.36.k_ref, bf16[256,2048]{1,0:T(8,128)(2,1)} %bitcast.67, s32[256,1]{1,0:T(8,128)} %copy.22.qtag_ref, s32[1,1280]{1,0:T(1,128)} %compare_select_fusion.ktag_ref), custom_call_target="tpu_custom_call" | custom-call | flops 2684354560 | bytes 7340032 | tf_op jit(solution)/shard_map/pallas_call | solution.py:79
  77.9 7.2 %collective-permute-start.6 = (bf16[256,1024]{1,0:T(8,128)(2,1)S(1)}, bf16[256,1024]{1,0:T(8,128)(2,1)S(1)}, u32[]{:S(2)}, u32[]{:S(2)}) collective-permute-start(bf16[256,1024]{1,0:T(8,128)(2,1)S(1)} %get-tuple-element.53), channel_id=1, source_target_pairs={{16,0},{24,8},{32,16},{40,24},{48,32},{56,40},{64,48},{72,56},{80,... | collective-permute-start | bytes 1572872 | tf_op jit(solution)/shard_map/ppermute | solution.py:210
  85.1 4.8 %collective-permute-start.5 = (bf16[256,1024]{1,0:T(8,128)(2,1)S(1)}, bf16[256,1024]{1,0:T(8,128)(2,1)S(1)}, u32[]{:S(2)}, u32[]{:S(2)}) collective-permute-start(bf16[256,1024]{1,0:T(8,128)(2,1)S(1)} %get-tuple-element.50), channel_id=1, source_target_pairs={{8,0},{16,8},{24,16},{32,24},{40,32},{48,40},{56,48},{64,56},{72,6... | collective-permute-start | bytes 1572872 | tf_op jit(solution)/shard_map/ppermute | solution.py:210
  90.0 8.8 %collective-permute-done.7 = bf16[256,1024]{1,0:T(8,128)(2,1)S(1)} collective-permute-done((bf16[256,1024]{1,0:T(8,128)(2,1)S(1)}, bf16[256,1024]{1,0:T(8,128)(2,1)S(1)}, u32[]{:S(2)}, u32[]{:S(2)}) %collective-permute-start.7) | collective-permute-done | bytes 524320 | tf_op jit(solution)/shard_map/ppermute | solution.py:210
  98.8 6.2 %collective-permute-done.6 = bf16[256,1024]{1,0:T(8,128)(2,1)S(1)} collective-permute-done((bf16[256,1024]{1,0:T(8,128)(2,1)S(1)}, bf16[256,1024]{1,0:T(8,128)(2,1)S(1)}, u32[]{:S(2)}, u32[]{:S(2)}) %collective-permute-start.6) | collective-permute-done | bytes 524320 | tf_op jit(solution)/shard_map/ppermute | solution.py:210
  104.9 2.6 collective-permute-done.5
  107.5 2.3 add_convert_fusion.2
  109.8 10.5 %collective-permute-start.18 = (bf16[256,1024]{1,0:T(8,128)(2,1)}, bf16[256,1024]{1,0:T(8,128)(2,1)S(1)}, u32[]{:S(2)}, u32[]{:S(2)}) collective-permute-start(bf16[256,1024]{1,0:T(8,128)(2,1)} %add_convert_fusion.2), channel_id=1, source_target_pairs={{0,8},{8,0},{16,24},{24,16},{32,40},{40,32},{48,56},{56,48},{64,72... | collective-permute-start | bytes 1572872 | tf_op jit(solution)/shard_map/ppermute | solution.py:296
  120.3 5.4 %convolution_bitcast_fusion = f32[256,1024]{1,0:T(8,128)} fusion(bf16[256,8,336]{0,2,1:T(8,128)(2,1)S(1)} %collective-permute-done.4, bf16[8,336,1024]{2,1,0:T(8,128)(2,1)} %bitcast.52), kind=kOutput, calls=%fused_computation.13 | convolution fusion | flops 1409286144 | bytes 7929856 | tf_op jit(solution)/shard_map/tfr,frn->tn/dot_general | solution.py:275
  125.7 2.8 convolution_convert_fusion
  129.0 5.5 %add_convert_fusion.1 = bf16[256,1024]{1,0:T(8,128)(2,1)S(1)} fusion(f32[256,1024]{1,0:T(8,128)} %collective-permute-done.9, bf16[8,336,1024]{2,1,0:T(8,128)(2,1)} %bitcast.53, bf16[256,8,2,336]{0,3,2,1:T(8,128)(2,1)} %bitcast.57, s32[]{:T(128)S(6)} %select_n.48), kind=kOutput, calls=%fused_computation.15 | convolution fusion | flops 1409810432 | bytes 8454148 | tf_op jit(solution)/shard_map/tfr,frn->tn/dot_general | solution.py:277
  134.5 3.1 copy.24
  137.6 7.5 %all-to-all-start = ((bf16[8,256,16,42]{1,2,3,0:T(8,128)(2,1)}), bf16[8,256,16,42]{1,2,3,0:T(8,128)(2,1)}, u32[]{:S(2)}, u32[]{:S(2)}) async-start(bf16[8,256,16,42]{1,2,3,0:T(8,128)(2,1)} %copy.24), calls=%async_computation | async-start | bytes 5505024 | tf_op jit(solution)/shard_map/all_to_all | solution.py:282
  145.1 4.3 %collective-permute-start.10 = (bf16[256,1024]{1,0:T(8,128)(2,1)S(1)}, bf16[256,1024]{1,0:T(8,128)(2,1)}, u32[]{:S(2)}, u32[]{:S(2)}) collective-permute-start(bf16[256,1024]{1,0:T(8,128)(2,1)S(1)} %add_convert_fusion.1), channel_id=1, source_target_pairs={{0,32},{8,40},{16,48},{24,56},{32,64},{40,72},{48,80},{56,88},{64,... | collective-permute-start | bytes 1572872 | tf_op jit(solution)/shard_map/ppermute | solution.py:210
  150.7 4.2 %fusion.7 = bf16[256,8,1,336]{0,3,1,2:T(8,128)(2,1)S(1)} fusion(bf16[8,336,1024]{2,1,0:T(8,128)(2,1)} %bitcast.54, bf16[256,1024]{1,0:T(8,128)(2,1)S(1)} %copy-done.5), kind=kOutput, calls=%fused_computation.7 | convolution fusion | flops 1409974272 | bytes 7405568 | tf_op jit(solution)/shard_map/tn,frn->tfr/dot_general | solution.py:295
  154.9 2.7 collective-permute-start.12
  161.8 4.5 %copy.27 = bf16[1,256,5376]{2,1,0:T(8,128)(2,1)} copy(bf16[1,256,5376]{1,2,0:T(8,128)(2,1)} %bitcast.59) | data formatting | bytes 5505024
  168.2 29.3 %collective-permute-done.11 = bf16[256,1024]{1,0:T(8,128)(2,1)S(1)} collective-permute-done((bf16[256,1024]{1,0:T(8,128)(2,1)S(1)}, bf16[256,1024]{1,0:T(8,128)(2,1)S(1)}, u32[]{:S(2)}, u32[]{:S(2)}) %collective-permute-start.11) | collective-permute-done | bytes 524320 | tf_op jit(solution)/shard_map/ppermute | solution.py:210
  198.3 21.4 %collective-permute-done.12 = bf16[256,1024]{1,0:T(8,128)(2,1)} collective-permute-done((bf16[256,1024]{1,0:T(8,128)(2,1)S(1)}, bf16[256,1024]{1,0:T(8,128)(2,1)}, u32[]{:S(2)}, u32[]{:S(2)}) %collective-permute-start.12) | collective-permute-done | bytes 524320 | tf_op jit(solution)/shard_map/ppermute | solution.py:210
  223.2 24.0 %shard_map.102 = (bf16[256,2048]{1,0:T(8,128)(2,1)}, bf16[256,2048]{1,0:T(8,128)(2,1)}, bf16[1280,1024]{1,0:T(8,128)(2,1)}) custom-call(bf16[256,2048]{1,0:T(8,128)(2,1)} %bitcast.66, bf16[1280,1024]{1,0:T(8,128)(2,1)} %slice.36.k_ref, bf16[1280,1024]{1,0:T(8,128)(2,1)} %constant_dynamic-update-slice_fusion.5.v_ref, bf16[256,2048]{1,0:T(8,128)(2,1)} %bitcast.68, ...), custom_call_target="tpu_custom_call" | custom-call | flops 6710886400 | bytes 12058624 | tf_op jit(solution)/shard_map/pallas_call | solution.py:98
  247.2 2.8 fusion.20
  256.5 7.7 %bitcast_convert_fusion.x_ref = bf16[16,42,1024]{2,1,0:T(8,128)(2,1)} fusion(bf16[8,256,1024]{2,1,0:T(8,128)(2,1)} %bitcast.64, bf16[8,256,16,42]{1,2,3,0:T(8,128)(2,1)} %all-to-all-done), kind=kOutput, calls=%fused_computation.2 | convolution fusion | flops 2819260416 | bytes 8323072 | tf_op jit(solution)/shard_map/ftcr,ftn->crn/dot_general | solution.py:289
  264.2 49.1 %shard_map.103 = f32[42,1024]{1,0:T(8,128)} custom-call(bf16[16,42,1024]{2,1,0:T(8,128)(2,1)} %bitcast_convert_fusion.x_ref), custom_call_target="tpu_custom_call" | custom-call | tf_op jit(solution)/shard_map/pallas_call | solution.py:192
  313.3 2.8 fusion.14
  (70 shorter events, 38.3 us)
Async XLA Ops:
  7.2 1.3 copy-start
  7.2 113.1 %all-gather.5.cloned.1.call-start = ((), (), s32[]{:S(2)}) async-start(), calls=%async_computation.1 | async-start | bytes 6193152 | tf_op jit(solution)/shard_map/all_gather | solution.py:226
  9.4 237.8 %all-gather.7.cloned.1.call-start = ((), (), s32[]{:S(2)}) async-start(), calls=%async_computation.2 | async-start | bytes 4718592 | tf_op jit(solution)/shard_map/all_gather | solution.py:273
  12.2 25.6 %collective-permute-start = (bf16[256,1152]{1,0:T(8,128)(2,1)}, bf16[256,1152]{1,0:T(8,128)(2,1)}, u32[]{:S(2)}, u32[]{:S(2)}) collective-permute-start(bf16[256,1152]{1,0:T(8,128)(2,1)} %pad_maximum_fusion), channel_id=1, source_target_pairs={{0,32},{8,40},{16,48},{24,56},{32,64},{40,72},{48,80},{56,88},{64,... | collective-permute-start | bytes 1769480 | tf_op jit(solution)/shard_map/ppermute | solution.py:210
  16.8 22.1 %collective-permute-start.1 = (bf16[256,1152]{1,0:T(8,128)(2,1)}, bf16[256,1152]{1,0:T(8,128)(2,1)}, u32[]{:S(2)}, u32[]{:S(2)}) collective-permute-start(bf16[256,1152]{1,0:T(8,128)(2,1)} %pad_maximum_fusion), channel_id=1, source_target_pairs={{0,24},{8,32},{16,40},{24,48},{32,56},{40,64},{48,72},{56,80},{64,... | collective-permute-start | bytes 1769480 | tf_op jit(solution)/shard_map/ppermute | solution.py:210
  26.0 11.0 %copy-start.7 = (s32[1,256]{1,0:T(1,128)S(1)}, s32[1,256]{1,0:T(1,128)}, u32[]{:S(2)}) copy-start(s32[1,256]{1,0:T(1,128)} %param.11) | copy-start | bytes 3076
  26.0 29.6 %collective-permute-start.4 = (bf16[256,8,336]{0,2,1:T(8,128)(2,1)S(1)}, bf16[256,8,336]{0,2,1:T(8,128)(2,1)S(1)}, u32[]{:S(2)}, u32[]{:S(2)}) collective-permute-start(bf16[256,8,336]{0,2,1:T(8,128)(2,1)S(1)} %dynamic-slice_bitcast_fusion), channel_id=1, source_target_pairs={{0,8},{8,0},{16,24},{24,16},{32,40},{40,32},{48,56},{56,48},{64,72... | collective-permute-start | bytes 4128776 | tf_op jit(solution)/shard_map/ppermute | solution.py:232
  26.1 22.5 %collective-permute-start.2 = (bf16[256,1152]{1,0:T(8,128)(2,1)}, bf16[256,1152]{1,0:T(8,128)(2,1)}, u32[]{:S(2)}, u32[]{:S(2)}) collective-permute-start(bf16[256,1152]{1,0:T(8,128)(2,1)} %pad_maximum_fusion), channel_id=1, source_target_pairs={{0,16},{8,24},{16,32},{24,40},{32,48},{40,56},{48,64},{56,72},{64,... | collective-permute-start | bytes 1769480 | tf_op jit(solution)/shard_map/ppermute | solution.py:210
  29.8 24.6 %collective-permute-start.3 = (bf16[256,1152]{1,0:T(8,128)(2,1)}, bf16[256,1152]{1,0:T(8,128)(2,1)}, u32[]{:S(2)}, u32[]{:S(2)}) collective-permute-start(bf16[256,1152]{1,0:T(8,128)(2,1)} %pad_maximum_fusion), channel_id=1, source_target_pairs={{0,8},{8,16},{16,24},{24,32},{32,40},{40,48},{48,56},{56,64},{64,7... | collective-permute-start | bytes 1769480 | tf_op jit(solution)/shard_map/ppermute | solution.py:210
  37.0 18.6 %copy-start.4 = (bf16[1,256,1024]{2,1,0:T(8,128)(2,1)S(1)}, bf16[1,256,1024]{2,1,0:T(8,128)(2,1)}, u32[]{:S(2)}) copy-start(bf16[1,256,1024]{2,1,0:T(8,128)(2,1)} %param.8) | copy-start | bytes 1572868
  75.3 14.7 %collective-permute-start.8 = (bf16[256,1024]{1,0:T(8,128)(2,1)S(1)}, bf16[256,1024]{1,0:T(8,128)(2,1)S(1)}, u32[]{:S(2)}, u32[]{:S(2)}) collective-permute-start(bf16[256,1024]{1,0:T(8,128)(2,1)S(1)} %get-tuple-element.51), channel_id=1, source_target_pairs={{32,0},{40,8},{48,16},{56,24},{64,32},{72,40},{80,48},{88,56},{96,... | collective-permute-start | bytes 1572872 | tf_op jit(solution)/shard_map/ppermute | solution.py:210
  76.6 22.2 %collective-permute-start.7 = (bf16[256,1024]{1,0:T(8,128)(2,1)S(1)}, bf16[256,1024]{1,0:T(8,128)(2,1)S(1)}, u32[]{:S(2)}, u32[]{:S(2)}) collective-permute-start(bf16[256,1024]{1,0:T(8,128)(2,1)S(1)} %get-tuple-element.52), channel_id=1, source_target_pairs={{24,0},{32,8},{40,16},{48,24},{56,32},{64,40},{72,48},{80,56},{88,... | collective-permute-start | bytes 1572872 | tf_op jit(solution)/shard_map/ppermute | solution.py:210
  77.9 27.1 %collective-permute-start.6 = (bf16[256,1024]{1,0:T(8,128)(2,1)S(1)}, bf16[256,1024]{1,0:T(8,128)(2,1)S(1)}, u32[]{:S(2)}, u32[]{:S(2)}) collective-permute-start(bf16[256,1024]{1,0:T(8,128)(2,1)S(1)} %get-tuple-element.53), channel_id=1, source_target_pairs={{16,0},{24,8},{32,16},{40,24},{48,32},{56,40},{64,48},{72,56},{80,... | collective-permute-start | bytes 1572872 | tf_op jit(solution)/shard_map/ppermute | solution.py:210
  85.1 22.4 %collective-permute-start.5 = (bf16[256,1024]{1,0:T(8,128)(2,1)S(1)}, bf16[256,1024]{1,0:T(8,128)(2,1)S(1)}, u32[]{:S(2)}, u32[]{:S(2)}) collective-permute-start(bf16[256,1024]{1,0:T(8,128)(2,1)S(1)} %get-tuple-element.50), channel_id=1, source_target_pairs={{8,0},{16,8},{24,16},{32,24},{40,32},{48,40},{56,48},{64,56},{72,6... | collective-permute-start | bytes 1572872 | tf_op jit(solution)/shard_map/ppermute | solution.py:210
  109.8 15.9 %collective-permute-start.18 = (bf16[256,1024]{1,0:T(8,128)(2,1)}, bf16[256,1024]{1,0:T(8,128)(2,1)S(1)}, u32[]{:S(2)}, u32[]{:S(2)}) collective-permute-start(bf16[256,1024]{1,0:T(8,128)(2,1)} %add_convert_fusion.2), channel_id=1, source_target_pairs={{0,8},{8,0},{16,24},{24,16},{32,40},{40,32},{48,56},{56,48},{64,72... | collective-permute-start | bytes 1572872 | tf_op jit(solution)/shard_map/ppermute | solution.py:296
  120.3 5.4 %copy-start.2 = (bf16[2688,1024]{1,0:T(8,128)(2,1)S(1)}, bf16[2688,1024]{1,0:T(8,128)(2,1)}, u32[]{:S(2)}) copy-start(bf16[2688,1024]{1,0:T(8,128)(2,1)} %all-gather.5.cloned.1.call-done) | copy-start | bytes 16515076
  125.7 3.3 %collective-permute-start.9 = (f32[256,1024]{1,0:T(8,128)}, f32[256,1024]{1,0:T(8,128)}, u32[]{:S(2)}, u32[]{:S(2)}) collective-permute-start(f32[256,1024]{1,0:T(8,128)} %convolution_bitcast_fusion), channel_id=1, source_target_pairs={{0,8},{8,0},{16,24},{24,16},{32,40},{40,32},{48,56},{56,48},{64,72... | collective-permute-start | bytes 3145736 | tf_op jit(solution)/shard_map/ppermute | solution.py:278
  128.6 31.0 %collective-permute-start.19 = (bf16[256,8,336]{0,2,1:T(8,128)(2,1)}, bf16[256,8,336]{0,2,1:T(8,128)(2,1)S(1)}, u32[]{:S(2)}, u32[]{:S(2)}) collective-permute-start(bf16[256,8,336]{0,2,1:T(8,128)(2,1)} %convolution_convert_fusion), channel_id=1, source_target_pairs={{0,8},{8,0},{16,24},{24,16},{32,40},{40,32},{48,56},{56,48},{64,72... | collective-permute-start | bytes 4128776 | tf_op jit(solution)/shard_map/ppermute | solution.py:297
  129.0 5.5 %copy-start.3 = (bf16[256,16,8,42]{0,3,2,1:T(8,128)(2,1)S(1)}, bf16[256,16,8,42]{0,3,2,1:T(8,128)(2,1)}, u32[]{:S(2)}) copy-start(bf16[256,16,8,42]{0,3,2,1:T(8,128)(2,1)} %reshape_squeeze.7) | copy-start | bytes 8257540
  137.6 13.1 %copy-start.5 = (bf16[256,1024]{1,0:T(8,128)(2,1)S(1)}, bf16[256,1024]{1,0:T(8,128)(2,1)}, u32[]{:S(2)}) copy-start(bf16[256,1024]{1,0:T(8,128)(2,1)} %add_convert_fusion.2) | copy-start | bytes 1572868
  137.6 118.9 %all-to-all-start = ((bf16[8,256,16,42]{1,2,3,0:T(8,128)(2,1)}), bf16[8,256,16,42]{1,2,3,0:T(8,128)(2,1)}, u32[]{:S(2)}, u32[]{:S(2)}) async-start(bf16[8,256,16,42]{1,2,3,0:T(8,128)(2,1)} %copy.24), calls=%async_computation | async-start | bytes 5505024 | tf_op jit(solution)/shard_map/all_to_all | solution.py:282
  145.1 21.2 %collective-permute-start.10 = (bf16[256,1024]{1,0:T(8,128)(2,1)S(1)}, bf16[256,1024]{1,0:T(8,128)(2,1)}, u32[]{:S(2)}, u32[]{:S(2)}) collective-permute-start(bf16[256,1024]{1,0:T(8,128)(2,1)S(1)} %add_convert_fusion.1), channel_id=1, source_target_pairs={{0,32},{8,40},{16,48},{24,56},{32,64},{40,72},{48,80},{56,88},{64,... | collective-permute-start | bytes 1572872 | tf_op jit(solution)/shard_map/ppermute | solution.py:210
  149.4 48.0 %collective-permute-start.11 = (bf16[256,1024]{1,0:T(8,128)(2,1)S(1)}, bf16[256,1024]{1,0:T(8,128)(2,1)S(1)}, u32[]{:S(2)}, u32[]{:S(2)}) collective-permute-start(bf16[256,1024]{1,0:T(8,128)(2,1)S(1)} %add_convert_fusion.1), channel_id=1, source_target_pairs={{0,24},{8,32},{16,40},{24,48},{32,56},{40,64},{48,72},{56,80},{64,... | collective-permute-start | bytes 1572872 | tf_op jit(solution)/shard_map/ppermute | solution.py:210
  154.9 64.7 %collective-permute-start.12 = (bf16[256,1024]{1,0:T(8,128)(2,1)S(1)}, bf16[256,1024]{1,0:T(8,128)(2,1)}, u32[]{:S(2)}, u32[]{:S(2)}) collective-permute-start(bf16[256,1024]{1,0:T(8,128)(2,1)S(1)} %add_convert_fusion.1), channel_id=1, source_target_pairs={{0,16},{8,24},{16,32},{24,40},{32,48},{40,56},{48,64},{56,72},{64,... | collective-permute-start | bytes 1572872 | tf_op jit(solution)/shard_map/ppermute | solution.py:210
  157.7 63.9 %collective-permute-start.13 = (bf16[256,1024]{1,0:T(8,128)(2,1)S(1)}, bf16[256,1024]{1,0:T(8,128)(2,1)S(1)}, u32[]{:S(2)}, u32[]{:S(2)}) collective-permute-start(bf16[256,1024]{1,0:T(8,128)(2,1)S(1)} %add_convert_fusion.1), channel_id=1, source_target_pairs={{0,8},{8,16},{16,24},{24,32},{32,40},{40,48},{48,56},{56,64},{64,7... | collective-permute-start | bytes 1572872 | tf_op jit(solution)/shard_map/ppermute | solution.py:210
  250.0 63.3 %collective-permute-start.14 = (bf16[256,1024]{1,0:T(8,128)(2,1)}, bf16[256,1024]{1,0:T(8,128)(2,1)}, u32[]{:S(2)}, u32[]{:S(2)}) collective-permute-start(bf16[256,1024]{1,0:T(8,128)(2,1)} %get-tuple-element.48), channel_id=1, source_target_pairs={{8,0},{16,8},{24,16},{32,24},{40,32},{48,40},{56,48},{64,56},{72,6... | collective-permute-start | bytes 1572872 | tf_op jit(solution)/shard_map/ppermute | solution.py:210
  251.9 61.4 %collective-permute-start.15 = (bf16[256,1024]{1,0:T(8,128)(2,1)S(1)}, bf16[256,1024]{1,0:T(8,128)(2,1)}, u32[]{:S(2)}, u32[]{:S(2)}) collective-permute-start(bf16[256,1024]{1,0:T(8,128)(2,1)S(1)} %get-tuple-element.47), channel_id=1, source_target_pairs={{16,0},{24,8},{32,16},{40,24},{48,32},{56,40},{64,48},{72,56},{80,... | collective-permute-start | bytes 1572872 | tf_op jit(solution)/shard_map/ppermute | solution.py:210
  253.9 59.5 %collective-permute-start.16 = (bf16[256,1024]{1,0:T(8,128)(2,1)S(1)}, bf16[256,1024]{1,0:T(8,128)(2,1)}, u32[]{:S(2)}, u32[]{:S(2)}) collective-permute-start(bf16[256,1024]{1,0:T(8,128)(2,1)S(1)} %get-tuple-element.46), channel_id=1, source_target_pairs={{24,0},{32,8},{40,16},{48,24},{56,32},{64,40},{72,48},{80,56},{88,... | collective-permute-start | bytes 1572872 | tf_op jit(solution)/shard_map/ppermute | solution.py:210
  255.2 58.2 %collective-permute-start.17 = (bf16[256,1024]{1,0:T(8,128)(2,1)S(1)}, bf16[256,1024]{1,0:T(8,128)(2,1)}, u32[]{:S(2)}, u32[]{:S(2)}) collective-permute-start(bf16[256,1024]{1,0:T(8,128)(2,1)S(1)} %get-tuple-element.45), channel_id=1, source_target_pairs={{32,0},{40,8},{48,16},{56,24},{64,32},{72,40},{80,48},{88,56},{96,... | collective-permute-start | bytes 1572872 | tf_op jit(solution)/shard_map/ppermute | solution.py:210
  256.5 60.4 %copy-start.1 = (bf16[672,1024]{1,0:T(8,128)(2,1)S(1)}, bf16[672,1024]{1,0:T(8,128)(2,1)}, u32[]{:S(2)}) copy-start(bf16[672,1024]{1,0:T(8,128)(2,1)} %param.9) | copy-start | bytes 4128772
  313.3 2.9 copy-start.6
Sparse Core Ops, SparseCore 0:
  10.9 88.5 all-gather.4
  109.9 120.4 all-gather.6

commit v13 on v11

--- a/solution.py
+++ b/solution.py
@@ -266,7 +266,7 @@
     partner_part = jnp.einsum("tfr,frn->tn", partner_tokens, w_mine, preferred_element_type=jnp.float32)
     values = (
         jnp.einsum("tfr,frn->tn", tokens_mine, w_mine, preferred_element_type=jnp.float32)
-        + lax.ppermute(partner_part, "ctx", partner)
+        + lax.ppermute(partner_part.astype(jnp.bfloat16), "ctx", partner).astype(jnp.float32)
     ).astype(jnp.bfloat16)
     arrived_values = [shifted(values, "ctx", hop) for hop in range(1, n_hops + 1)]
     token_cols, _ = lax.optimization_barrier((token_cols, values))

time: 315 us -> 308 us (0.978)
  waiting for transfers between devices: 86.7 us -> 81.4 us
    ppermute x16, waiting for transfers between devices: 83.4 us -> 79.9 us  [shifted(): return lax.ppermute(x, axis, pairs)]
where the time goes in v13:
time: 308 us; the launch traced here: 304 us
  waiting for transfers between devices  81.4 us (26%)
  Pallas kernels  65.3 us (21%)
  starting transfers between devices  64.3 us (21%)
  local copies, waits for them, and re-layouts  43.4 us (14%)
  matrix products  26.2 us (9%)
  between operations  14.3 us (5%)
  other arithmetic  9.27 us (3%)
    ppermute x16, waiting for transfers between devices, shifted(): return lax.ppermute(x, axis, pairs)  79.9 us
    ppermute x16, starting transfers between devices, shifted(): return lax.ppermute(x, axis, pairs)  45.9 us
    pallas_call x1, Pallas kernels, peer_sum_scatter(): pl.pallas_call(functools.partial(peer_sum_kernel, axis, n), out_shape=jax...  26.2 us
    pallas_call x1, Pallas kernels, fused_attention(): pl.pallas_call(attention_kernel, grid=(heads,), in_specs=[q_spec, kv_spec...  23.9 us
    unnamed x23, local copies, waits for them, and re-layouts  22.9 us
    pallas_call x1, Pallas kernels, value_grads(): pl.pallas_call(value_grad_kernel, grid=(heads,), in_specs=[q_spec, kv_spe...  15.2 us
    ppermute x1, starting transfers between devices, shards(): lax.ppermute(partner_part.astype(jnp.bfloat16), 'ctx', partner)  10.5 us
    dot_general x1, matrix products, shards(): jnp.einsum('ftcr,ftn->crn', token_cols, grads_all, preferred_element_type...  7.73 us
  transfers between devices with their start and end apart: 23, of which 10 were waited for; matrix products, arithmetic and copies ran while one was open for 22% of the time, Pallas kernels for 13%

profile of v13, /device:TPU:28, one launch (start us, length us, event | category | flops | bytes accessed | tf_op | source)
XLA Modules:
  0.0 304.2 jit_solution(11149631424835104149)
XLA Ops:
  12.2 4.6 %collective-permute-start = (bf16[256,1152]{1,0:T(8,128)(2,1)}, bf16[256,1152]{1,0:T(8,128)(2,1)}, u32[]{:S(2)}, u32[]{:S(2)}) collective-permute-start(bf16[256,1152]{1,0:T(8,128)(2,1)} %pad_maximum_fusion), channel_id=1, source_target_pairs={{0,32},{8,40},{16,48},{24,56},{32,64},{40,72},{48,80},{56,88},{64,... | collective-permute-start | bytes 1769480 | tf_op jit(solution)/shard_map/ppermute | solution.py:210
  16.8 3.2 %collective-permute-start.1 = (bf16[256,1152]{1,0:T(8,128)(2,1)}, bf16[256,1152]{1,0:T(8,128)(2,1)}, u32[]{:S(2)}, u32[]{:S(2)}) collective-permute-start(bf16[256,1152]{1,0:T(8,128)(2,1)} %pad_maximum_fusion), channel_id=1, source_target_pairs={{0,24},{8,32},{16,40},{24,48},{32,56},{40,64},{48,72},{56,80},{64,... | collective-permute-start | bytes 1769480 | tf_op jit(solution)/shard_map/ppermute | solution.py:210
  20.0 4.5 %copy.20 = bf16[1,256,5376]{1,2,0:T(8,128)(2,1)} copy(bf16[1,256,5376]{2,1,0:T(8,128)(2,1)} %param.6) | data formatting | bytes 5505024 | tf_op args[0]
  26.1 3.7 %collective-permute-start.2 = (bf16[256,1152]{1,0:T(8,128)(2,1)}, bf16[256,1152]{1,0:T(8,128)(2,1)}, u32[]{:S(2)}, u32[]{:S(2)}) collective-permute-start(bf16[256,1152]{1,0:T(8,128)(2,1)} %pad_maximum_fusion), channel_id=1, source_target_pairs={{0,16},{8,24},{16,32},{24,40},{32,48},{40,56},{48,64},{56,72},{64,... | collective-permute-start | bytes 1769480 | tf_op jit(solution)/shard_map/ppermute | solution.py:210
  31.7 5.3 %reshape_squeeze.7 = bf16[256,16,8,42]{0,3,2,1:T(8,128)(2,1)} reshape(bf16[1,256,5376]{1,2,0:T(8,128)(2,1)} %copy.20) | data formatting | bytes 5505024 | tf_op jit(solution)/shard_map/reshape;squeeze | solution.py:237
  40.1 8.5 %collective-permute-done.2 = bf16[256,1152]{1,0:T(8,128)(2,1)} collective-permute-done((bf16[256,1152]{1,0:T(8,128)(2,1)}, bf16[256,1152]{1,0:T(8,128)(2,1)}, u32[]{:S(2)}, u32[]{:S(2)}) %collective-permute-start.2) | collective-permute-done | bytes 589856 | tf_op jit(solution)/shard_map/ppermute | solution.py:210
  49.7 4.7 %collective-permute-done.3 = bf16[256,1152]{1,0:T(8,128)(2,1)} collective-permute-done((bf16[256,1152]{1,0:T(8,128)(2,1)}, bf16[256,1152]{1,0:T(8,128)(2,1)}, u32[]{:S(2)}, u32[]{:S(2)}) %collective-permute-start.3) | collective-permute-done | bytes 589856 | tf_op jit(solution)/shard_map/ppermute | solution.py:210
  58.3 15.2 %shard_map.101 = bf16[1280,1024]{1,0:T(8,128)(2,1)} custom-call(bf16[256,2048]{1,0:T(8,128)(2,1)} %bitcast.67, bf16[1280,1024]{1,0:T(8,128)(2,1)} %slice.36.k_ref, bf16[256,2048]{1,0:T(8,128)(2,1)} %bitcast.69, s32[256,1]{1,0:T(8,128)} %copy.22.qtag_ref, s32[1,1280]{1,0:T(1,128)} %compare_select_fusion.ktag_ref), custom_call_target="tpu_custom_call" | custom-call | flops 2684354560 | bytes 7340032 | tf_op jit(solution)/shard_map/pallas_call | solution.py:79
  77.8 7.2 %collective-permute-start.6 = (bf16[256,1024]{1,0:T(8,128)(2,1)S(1)}, bf16[256,1024]{1,0:T(8,128)(2,1)S(1)}, u32[]{:S(2)}, u32[]{:S(2)}) collective-permute-start(bf16[256,1024]{1,0:T(8,128)(2,1)S(1)} %get-tuple-element.40), channel_id=1, source_target_pairs={{16,0},{24,8},{32,16},{40,24},{48,32},{56,40},{64,48},{72,56},{80,... | collective-permute-start | bytes 1572872 | tf_op jit(solution)/shard_map/ppermute | solution.py:210
  85.0 4.8 %collective-permute-start.5 = (bf16[256,1024]{1,0:T(8,128)(2,1)S(1)}, bf16[256,1024]{1,0:T(8,128)(2,1)S(1)}, u32[]{:S(2)}, u32[]{:S(2)}) collective-permute-start(bf16[256,1024]{1,0:T(8,128)(2,1)S(1)} %get-tuple-element.37), channel_id=1, source_target_pairs={{8,0},{16,8},{24,16},{32,24},{40,32},{48,40},{56,48},{64,56},{72,6... | collective-permute-start | bytes 1572872 | tf_op jit(solution)/shard_map/ppermute | solution.py:210
  90.0 8.8 %collective-permute-done.7 = bf16[256,1024]{1,0:T(8,128)(2,1)S(1)} collective-permute-done((bf16[256,1024]{1,0:T(8,128)(2,1)S(1)}, bf16[256,1024]{1,0:T(8,128)(2,1)S(1)}, u32[]{:S(2)}, u32[]{:S(2)}) %collective-permute-start.7) | collective-permute-done | bytes 524320 | tf_op jit(solution)/shard_map/ppermute | solution.py:210
  98.7 6.2 %collective-permute-done.6 = bf16[256,1024]{1,0:T(8,128)(2,1)S(1)} collective-permute-done((bf16[256,1024]{1,0:T(8,128)(2,1)S(1)}, bf16[256,1024]{1,0:T(8,128)(2,1)S(1)}, u32[]{:S(2)}, u32[]{:S(2)}) %collective-permute-start.6) | collective-permute-done | bytes 524320 | tf_op jit(solution)/shard_map/ppermute | solution.py:210
  104.9 2.6 collective-permute-done.5
  109.9 4.3 %fusion.14 = bf16[256,1024]{1,0:T(8,128)(2,1)S(1)} fusion(bf16[256,8,336]{0,2,1:T(8,128)(2,1)S(1)} %collective-permute-done.4, bf16[8,336,1024]{2,1,0:T(8,128)(2,1)} %bitcast.54), kind=kOutput, calls=%fused_computation.14 | convolution fusion | flops 1409548288 | bytes 7405568 | tf_op jit(solution)/shard_map/tfr,frn->tn/dot_general | solution.py:266
  114.2 10.5 %collective-permute-start.9 = (bf16[256,1024]{1,0:T(8,128)(2,1)S(1)}, bf16[256,1024]{1,0:T(8,128)(2,1)S(1)}, u32[]{:S(2)}, u32[]{:S(2)}) collective-permute-start(bf16[256,1024]{1,0:T(8,128)(2,1)S(1)} %fusion.14), channel_id=1, source_target_pairs={{0,8},{8,0},{16,24},{24,16},{32,40},{40,32},{48,56},{56,48},{64,72... | collective-permute-start | bytes 1572872 | tf_op jit(solution)/shard_map/ppermute | solution.py:269
  126.2 4.7 %add_convert_fusion.1 = bf16[256,1024]{1,0:T(8,128)(2,1)S(1)} fusion(bf16[256,1024]{1,0:T(8,128)(2,1)S(1)} %collective-permute-done.9, bf16[8,336,1024]{2,1,0:T(8,128)(2,1)} %bitcast.55, bf16[256,8,2,336]{0,3,2,1:T(8,128)(2,1)} %bitcast.59, s32[]{:T(128)S(6)} %select_n.48), kind=kOutput, calls=%fused_computation.16 | convolution fusion | flops 1410072576 | bytes 7929860 | tf_op jit(solution)/shard_map/tfr,frn->tn/dot_general | solution.py:268
  130.9 4.3 %collective-permute-start.10 = (bf16[256,1024]{1,0:T(8,128)(2,1)S(1)}, bf16[256,1024]{1,0:T(8,128)(2,1)}, u32[]{:S(2)}, u32[]{:S(2)}) collective-permute-start(bf16[256,1024]{1,0:T(8,128)(2,1)S(1)} %add_convert_fusion.1), channel_id=1, source_target_pairs={{0,32},{8,40},{16,48},{24,56},{32,64},{40,72},{48,80},{56,88},{64,... | collective-permute-start | bytes 1572872 | tf_op jit(solution)/shard_map/ppermute | solution.py:210
  135.2 2.3 collective-permute-start.11
  137.6 2.9 collective-permute-start.12
  142.4 5.3 %convolution_convert_fusion = bf16[256,8,336]{0,2,1:T(8,128)(2,1)} fusion(bf16[8,336,1024]{2,1,0:T(8,128)(2,1)} %bitcast.56, bf16[256,1024]{1,0:T(8,128)(2,1)S(1)} %collective-permute-done.18), kind=kOutput, calls=%fused_computation.5 | convolution fusion | flops 1409974272 | bytes 7405568 | tf_op jit(solution)/shard_map/tn,frn->tfr/dot_general | solution.py:287
  148.1 3.1 %copy.25 = bf16[8,256,16,42]{1,2,3,0:T(8,128)(2,1)} copy(bf16[8,256,16,42]{1,3,0,2:T(8,128)(2,1)S(1)} %bitcast.60) | data formatting | bytes 5505024 | tf_op jit(solution)/shard_map/optimization_barrier | solution.py:272
  151.2 7.2 %all-to-all-start = ((bf16[8,256,16,42]{1,2,3,0:T(8,128)(2,1)}), bf16[8,256,16,42]{1,2,3,0:T(8,128)(2,1)}, u32[]{:S(2)}, u32[]{:S(2)}) async-start(bf16[8,256,16,42]{1,2,3,0:T(8,128)(2,1)} %copy.25), calls=%async_computation | async-start | bytes 5505024 | tf_op jit(solution)/shard_map/all_to_all | solution.py:273
  162.1 12.4 %collective-permute-done.12 = bf16[256,1024]{1,0:T(8,128)(2,1)} collective-permute-done((bf16[256,1024]{1,0:T(8,128)(2,1)S(1)}, bf16[256,1024]{1,0:T(8,128)(2,1)}, u32[]{:S(2)}, u32[]{:S(2)}) %collective-permute-start.12) | collective-permute-done | bytes 524320 | tf_op jit(solution)/shard_map/ppermute | solution.py:210
  176.4 18.3 %collective-permute-done.13 = bf16[256,1024]{1,0:T(8,128)(2,1)S(1)} collective-permute-done((bf16[256,1024]{1,0:T(8,128)(2,1)S(1)}, bf16[256,1024]{1,0:T(8,128)(2,1)S(1)}, u32[]{:S(2)}, u32[]{:S(2)}) %collective-permute-start.13) | collective-permute-done | bytes 524320 | tf_op jit(solution)/shard_map/ppermute | solution.py:210
  196.4 23.9 %shard_map.102 = (bf16[256,2048]{1,0:T(8,128)(2,1)}, bf16[256,2048]{1,0:T(8,128)(2,1)}, bf16[1280,1024]{1,0:T(8,128)(2,1)}) custom-call(bf16[256,2048]{1,0:T(8,128)(2,1)} %bitcast.68, bf16[1280,1024]{1,0:T(8,128)(2,1)} %slice.36.k_ref, bf16[1280,1024]{1,0:T(8,128)(2,1)} %constant_dynamic-update-slice_fusion.5.v_ref, bf16[256,2048]{1,0:T(8,128)(2,1)} %bitcast.70, ...), custom_call_target="tpu_custom_call" | custom-call | flops 6710886400 | bytes 12058624 | tf_op jit(solution)/shard_map/pallas_call | solution.py:98
  220.3 2.9 fusion.21
  229.6 4.2 %fusion.7 = bf16[256,8,1,336]{0,3,1,2:T(8,128)(2,1)S(1)} fusion(bf16[8,336,1024]{2,1,0:T(8,128)(2,1)} %bitcast.57, bf16[256,1024]{1,0:T(8,128)(2,1)S(1)} %copy-done.4), kind=kOutput, calls=%fused_computation.7 | convolution fusion | flops 1409974272 | bytes 7405568 | tf_op jit(solution)/shard_map/tn,frn->tfr/dot_general | solution.py:284
  236.1 4.5 %copy.27 = bf16[1,256,5376]{2,1,0:T(8,128)(2,1)} copy(bf16[1,256,5376]{1,2,0:T(8,128)(2,1)} %bitcast.61) | data formatting | bytes 5505024
  240.6 18.3 %collective-permute-done.17 = bf16[256,1024]{1,0:T(8,128)(2,1)} collective-permute-done((bf16[256,1024]{1,0:T(8,128)(2,1)}, bf16[256,1024]{1,0:T(8,128)(2,1)}, u32[]{:S(2)}, u32[]{:S(2)}) %collective-permute-start.17) | collective-permute-done | bytes 524320 | tf_op jit(solution)/shard_map/ppermute | solution.py:210
  258.9 2.9 fusion.15
  261.8 7.7 %bitcast_convert_fusion.x_ref = bf16[16,42,1024]{2,1,0:T(8,128)(2,1)} fusion(bf16[8,256,1024]{2,1,0:T(8,128)(2,1)} %bitcast.66, bf16[8,256,16,42]{1,2,3,0:T(8,128)(2,1)} %all-to-all-done), kind=kOutput, calls=%fused_computation.2 | convolution fusion | flops 2819260416 | bytes 8323072 | tf_op jit(solution)/shard_map/ftcr,ftn->crn/dot_general | solution.py:280
  269.5 26.2 %shard_map.103 = f32[42,1024]{1,0:T(8,128)} custom-call(bf16[16,42,1024]{2,1,0:T(8,128)(2,1)} %bitcast_convert_fusion.x_ref), custom_call_target="tpu_custom_call" | custom-call | tf_op jit(solution)/shard_map/pallas_call | solution.py:192
  (66 shorter events, 44.6 us)
Async XLA Ops:
  7.2 1.3 copy-start
  7.2 102.7 %all-gather.5.cloned.1.call-start = ((), (), s32[]{:S(2)}) async-start(), calls=%async_computation.1 | async-start | bytes 6193152 | tf_op jit(solution)/shard_map/all_gather | solution.py:226
  9.4 224.4 %all-gather.7.cloned.1.call-start = ((), (), s32[]{:S(2)}) async-start(), calls=%async_computation.2 | async-start | bytes 4718592 | tf_op jit(solution)/shard_map/all_gather | solution.py:264
  12.2 25.6 %collective-permute-start = (bf16[256,1152]{1,0:T(8,128)(2,1)}, bf16[256,1152]{1,0:T(8,128)(2,1)}, u32[]{:S(2)}, u32[]{:S(2)}) collective-permute-start(bf16[256,1152]{1,0:T(8,128)(2,1)} %pad_maximum_fusion), channel_id=1, source_target_pairs={{0,32},{8,40},{16,48},{24,56},{32,64},{40,72},{48,80},{56,88},{64,... | collective-permute-start | bytes 1769480 | tf_op jit(solution)/shard_map/ppermute | solution.py:210
  16.8 22.1 %collective-permute-start.1 = (bf16[256,1152]{1,0:T(8,128)(2,1)}, bf16[256,1152]{1,0:T(8,128)(2,1)}, u32[]{:S(2)}, u32[]{:S(2)}) collective-permute-start(bf16[256,1152]{1,0:T(8,128)(2,1)} %pad_maximum_fusion), channel_id=1, source_target_pairs={{0,24},{8,32},{16,40},{24,48},{32,56},{40,64},{48,72},{56,80},{64,... | collective-permute-start | bytes 1769480 | tf_op jit(solution)/shard_map/ppermute | solution.py:210
  26.0 11.0 %copy-start.5 = (s32[1,256]{1,0:T(1,128)S(1)}, s32[1,256]{1,0:T(1,128)}, u32[]{:S(2)}) copy-start(s32[1,256]{1,0:T(1,128)} %param.11) | copy-start | bytes 3076
  26.0 29.6 %collective-permute-start.4 = (bf16[256,8,336]{0,2,1:T(8,128)(2,1)S(1)}, bf16[256,8,336]{0,2,1:T(8,128)(2,1)S(1)}, u32[]{:S(2)}, u32[]{:S(2)}) collective-permute-start(bf16[256,8,336]{0,2,1:T(8,128)(2,1)S(1)} %dynamic-slice_bitcast_fusion), channel_id=1, source_target_pairs={{0,8},{8,0},{16,24},{24,16},{32,40},{40,32},{48,56},{56,48},{64,72... | collective-permute-start | bytes 4128776 | tf_op jit(solution)/shard_map/ppermute | solution.py:232
  26.1 22.5 %collective-permute-start.2 = (bf16[256,1152]{1,0:T(8,128)(2,1)}, bf16[256,1152]{1,0:T(8,128)(2,1)}, u32[]{:S(2)}, u32[]{:S(2)}) collective-permute-start(bf16[256,1152]{1,0:T(8,128)(2,1)} %pad_maximum_fusion), channel_id=1, source_target_pairs={{0,16},{8,24},{16,32},{24,40},{32,48},{40,56},{48,64},{56,72},{64,... | collective-permute-start | bytes 1769480 | tf_op jit(solution)/shard_map/ppermute | solution.py:210
  29.8 24.6 %collective-permute-start.3 = (bf16[256,1152]{1,0:T(8,128)(2,1)}, bf16[256,1152]{1,0:T(8,128)(2,1)}, u32[]{:S(2)}, u32[]{:S(2)}) collective-permute-start(bf16[256,1152]{1,0:T(8,128)(2,1)} %pad_maximum_fusion), channel_id=1, source_target_pairs={{0,8},{8,16},{16,24},{24,32},{32,40},{40,48},{48,56},{56,64},{64,7... | collective-permute-start | bytes 1769480 | tf_op jit(solution)/shard_map/ppermute | solution.py:210
  37.0 18.5 %copy-start.3 = (bf16[1,256,1024]{2,1,0:T(8,128)(2,1)S(1)}, bf16[1,256,1024]{2,1,0:T(8,128)(2,1)}, u32[]{:S(2)}) copy-start(bf16[1,256,1024]{2,1,0:T(8,128)(2,1)} %param.8) | copy-start | bytes 1572868
  75.2 14.7 %collective-permute-start.8 = (bf16[256,1024]{1,0:T(8,128)(2,1)S(1)}, bf16[256,1024]{1,0:T(8,128)(2,1)S(1)}, u32[]{:S(2)}, u32[]{:S(2)}) collective-permute-start(bf16[256,1024]{1,0:T(8,128)(2,1)S(1)} %get-tuple-element.38), channel_id=1, source_target_pairs={{32,0},{40,8},{48,16},{56,24},{64,32},{72,40},{80,48},{88,56},{96,... | collective-permute-start | bytes 1572872 | tf_op jit(solution)/shard_map/ppermute | solution.py:210
  76.5 22.2 %collective-permute-start.7 = (bf16[256,1024]{1,0:T(8,128)(2,1)S(1)}, bf16[256,1024]{1,0:T(8,128)(2,1)S(1)}, u32[]{:S(2)}, u32[]{:S(2)}) collective-permute-start(bf16[256,1024]{1,0:T(8,128)(2,1)S(1)} %get-tuple-element.39), channel_id=1, source_target_pairs={{24,0},{32,8},{40,16},{48,24},{56,32},{64,40},{72,48},{80,56},{88,... | collective-permute-start | bytes 1572872 | tf_op jit(solution)/shard_map/ppermute | solution.py:210
  77.8 27.1 %collective-permute-start.6 = (bf16[256,1024]{1,0:T(8,128)(2,1)S(1)}, bf16[256,1024]{1,0:T(8,128)(2,1)S(1)}, u32[]{:S(2)}, u32[]{:S(2)}) collective-permute-start(bf16[256,1024]{1,0:T(8,128)(2,1)S(1)} %get-tuple-element.40), channel_id=1, source_target_pairs={{16,0},{24,8},{32,16},{40,24},{48,32},{56,40},{64,48},{72,56},{80,... | collective-permute-start | bytes 1572872 | tf_op jit(solution)/shard_map/ppermute | solution.py:210
  85.0 22.5 %collective-permute-start.5 = (bf16[256,1024]{1,0:T(8,128)(2,1)S(1)}, bf16[256,1024]{1,0:T(8,128)(2,1)S(1)}, u32[]{:S(2)}, u32[]{:S(2)}) collective-permute-start(bf16[256,1024]{1,0:T(8,128)(2,1)S(1)} %get-tuple-element.37), channel_id=1, source_target_pairs={{8,0},{16,8},{24,16},{32,24},{40,32},{48,40},{56,48},{64,56},{72,6... | collective-permute-start | bytes 1572872 | tf_op jit(solution)/shard_map/ppermute | solution.py:210
  109.9 14.8 %copy-start.4 = (bf16[256,1024]{1,0:T(8,128)(2,1)S(1)}, bf16[256,1024]{1,0:T(8,128)(2,1)}, u32[]{:S(2)}) copy-start(bf16[256,1024]{1,0:T(8,128)(2,1)} %add_convert_fusion.2) | copy-start | bytes 1572868
  114.2 12.0 %collective-permute-start.9 = (bf16[256,1024]{1,0:T(8,128)(2,1)S(1)}, bf16[256,1024]{1,0:T(8,128)(2,1)S(1)}, u32[]{:S(2)}, u32[]{:S(2)}) collective-permute-start(bf16[256,1024]{1,0:T(8,128)(2,1)S(1)} %fusion.14), channel_id=1, source_target_pairs={{0,8},{8,0},{16,24},{24,16},{32,40},{40,32},{48,56},{56,48},{64,72... | collective-permute-start | bytes 1572872 | tf_op jit(solution)/shard_map/ppermute | solution.py:269
  124.7 17.7 %collective-permute-start.18 = (bf16[256,1024]{1,0:T(8,128)(2,1)S(1)}, bf16[256,1024]{1,0:T(8,128)(2,1)S(1)}, u32[]{:S(2)}, u32[]{:S(2)}) collective-permute-start(bf16[256,1024]{1,0:T(8,128)(2,1)S(1)} %copy-done.4), channel_id=1, source_target_pairs={{0,8},{8,0},{16,24},{24,16},{32,40},{40,32},{48,56},{56,48},{64,72... | collective-permute-start | bytes 1572872 | tf_op jit(solution)/shard_map/ppermute | solution.py:285
  130.9 27.5 %collective-permute-start.10 = (bf16[256,1024]{1,0:T(8,128)(2,1)S(1)}, bf16[256,1024]{1,0:T(8,128)(2,1)}, u32[]{:S(2)}, u32[]{:S(2)}) collective-permute-start(bf16[256,1024]{1,0:T(8,128)(2,1)S(1)} %add_convert_fusion.1), channel_id=1, source_target_pairs={{0,32},{8,40},{16,48},{24,56},{32,64},{40,72},{48,80},{56,88},{64,... | collective-permute-start | bytes 1572872 | tf_op jit(solution)/shard_map/ppermute | solution.py:210
  135.2 12.9 %copy-start.2 = (bf16[256,16,8,42]{0,3,2,1:T(8,128)(2,1)S(1)}, bf16[256,16,8,42]{0,3,2,1:T(8,128)(2,1)}, u32[]{:S(2)}) copy-start(bf16[256,16,8,42]{0,3,2,1:T(8,128)(2,1)} %reshape_squeeze.7) | copy-start | bytes 8257540
  135.2 25.0 %collective-permute-start.11 = (bf16[256,1024]{1,0:T(8,128)(2,1)S(1)}, bf16[256,1024]{1,0:T(8,128)(2,1)}, u32[]{:S(2)}, u32[]{:S(2)}) collective-permute-start(bf16[256,1024]{1,0:T(8,128)(2,1)S(1)} %add_convert_fusion.1), channel_id=1, source_target_pairs={{0,24},{8,32},{16,40},{24,48},{32,56},{40,64},{48,72},{56,80},{64,... | collective-permute-start | bytes 1572872 | tf_op jit(solution)/shard_map/ppermute | solution.py:210
  137.6 37.0 %collective-permute-start.12 = (bf16[256,1024]{1,0:T(8,128)(2,1)S(1)}, bf16[256,1024]{1,0:T(8,128)(2,1)}, u32[]{:S(2)}, u32[]{:S(2)}) collective-permute-start(bf16[256,1024]{1,0:T(8,128)(2,1)S(1)} %add_convert_fusion.1), channel_id=1, source_target_pairs={{0,16},{8,24},{16,32},{24,40},{32,48},{40,56},{48,64},{56,72},{64,... | collective-permute-start | bytes 1572872 | tf_op jit(solution)/shard_map/ppermute | solution.py:210
  140.5 54.3 %collective-permute-start.13 = (bf16[256,1024]{1,0:T(8,128)(2,1)S(1)}, bf16[256,1024]{1,0:T(8,128)(2,1)S(1)}, u32[]{:S(2)}, u32[]{:S(2)}) collective-permute-start(bf16[256,1024]{1,0:T(8,128)(2,1)S(1)} %add_convert_fusion.1), channel_id=1, source_target_pairs={{0,8},{8,16},{16,24},{24,32},{32,40},{40,48},{48,56},{56,64},{64,7... | collective-permute-start | bytes 1572872 | tf_op jit(solution)/shard_map/ppermute | solution.py:210
  147.7 86.2 %collective-permute-start.19 = (bf16[256,8,336]{0,2,1:T(8,128)(2,1)}, bf16[256,8,336]{0,2,1:T(8,128)(2,1)S(1)}, u32[]{:S(2)}, u32[]{:S(2)}) collective-permute-start(bf16[256,8,336]{0,2,1:T(8,128)(2,1)} %convolution_convert_fusion), channel_id=1, source_target_pairs={{0,8},{8,0},{16,24},{24,16},{32,40},{40,32},{48,56},{56,48},{64,72... | collective-permute-start | bytes 4128776 | tf_op jit(solution)/shard_map/ppermute | solution.py:286
  151.2 110.6 %all-to-all-start = ((bf16[8,256,16,42]{1,2,3,0:T(8,128)(2,1)}), bf16[8,256,16,42]{1,2,3,0:T(8,128)(2,1)}, u32[]{:S(2)}, u32[]{:S(2)}) async-start(bf16[8,256,16,42]{1,2,3,0:T(8,128)(2,1)} %copy.25), calls=%async_computation | async-start | bytes 5505024 | tf_op jit(solution)/shard_map/all_to_all | solution.py:273
  223.2 35.7 %collective-permute-start.17 = (bf16[256,1024]{1,0:T(8,128)(2,1)}, bf16[256,1024]{1,0:T(8,128)(2,1)}, u32[]{:S(2)}, u32[]{:S(2)}) collective-permute-start(bf16[256,1024]{1,0:T(8,128)(2,1)} %get-tuple-element.34), channel_id=1, source_target_pairs={{32,0},{40,8},{48,16},{56,24},{64,32},{72,40},{80,48},{88,56},{96,... | collective-permute-start | bytes 1572872 | tf_op jit(solution)/shard_map/ppermute | solution.py:210
  224.5 34.4 %collective-permute-start.16 = (bf16[256,1024]{1,0:T(8,128)(2,1)}, bf16[256,1024]{1,0:T(8,128)(2,1)}, u32[]{:S(2)}, u32[]{:S(2)}) collective-permute-start(bf16[256,1024]{1,0:T(8,128)(2,1)} %get-tuple-element.35), channel_id=1, source_target_pairs={{24,0},{32,8},{40,16},{48,24},{56,32},{64,40},{72,48},{80,56},{88,... | collective-permute-start | bytes 1572872 | tf_op jit(solution)/shard_map/ppermute | solution.py:210
  225.8 33.1 %collective-permute-start.15 = (bf16[256,1024]{1,0:T(8,128)(2,1)}, bf16[256,1024]{1,0:T(8,128)(2,1)}, u32[]{:S(2)}, u32[]{:S(2)}) collective-permute-start(bf16[256,1024]{1,0:T(8,128)(2,1)} %get-tuple-element.36), channel_id=1, source_target_pairs={{16,0},{24,8},{32,16},{40,24},{48,32},{56,40},{64,48},{72,56},{80,... | collective-permute-start | bytes 1572872 | tf_op jit(solution)/shard_map/ppermute | solution.py:210
  227.7 31.2 %collective-permute-start.14 = (bf16[256,1024]{1,0:T(8,128)(2,1)}, bf16[256,1024]{1,0:T(8,128)(2,1)}, u32[]{:S(2)}, u32[]{:S(2)}) collective-permute-start(bf16[256,1024]{1,0:T(8,128)(2,1)} %get-tuple-element.33), channel_id=1, source_target_pairs={{8,0},{16,8},{24,16},{32,24},{40,32},{48,40},{56,48},{64,56},{72,6... | collective-permute-start | bytes 1572872 | tf_op jit(solution)/shard_map/ppermute | solution.py:210
  261.8 35.5 %copy-start.1 = (bf16[672,1024]{1,0:T(8,128)(2,1)S(1)}, bf16[672,1024]{1,0:T(8,128)(2,1)}, u32[]{:S(2)}) copy-start(bf16[672,1024]{1,0:T(8,128)(2,1)} %param.9) | copy-start | bytes 4128772
Sparse Core Ops, SparseCore 0:
  10.9 88.5 all-gather.4
  110.0 113.7 all-gather.6

commit v14 on v13

--- a/solution.py
+++ b/solution.py
@@ -272,6 +272,13 @@
     token_cols, _ = lax.optimization_barrier((token_cols, values))
     token_cols = lax.all_to_all(token_cols, "fsdp", 0, 0, tiled=True)
     window_values = jnp.concatenate(arrived_values[::-1] + [values], 0)
+    d_mine = jnp.einsum("tn,frn->tfr", d_values_low, w_mine, preferred_element_type=jnp.float32).astype(jnp.bfloat16)
+    partner_grads = lax.ppermute(d_values_low, "ctx", partner)
+    d_for_partner = jnp.einsum(
+        "tn,frn->tfr", partner_grads, w_mine, preferred_element_type=jnp.float32
+    ).astype(jnp.bfloat16)
+    window_values, d_mine, d_for_partner = lax.optimization_barrier((window_values, d_mine, d_for_partner))
+    d_other = lax.ppermute(d_for_partner, "ctx", partner)
     out_rows_attn, d_query_heads, key_terms = fused_attention(
         queries[0], window_keys, window_values, d_out[0], query_tags, key_tags[None, :]
     )
@@ -281,13 +288,6 @@
         "ftcr,ftn->crn", token_cols, grads_all, preferred_element_type=jnp.float32
     )
     d_weight = peer_sum_scatter(weight_part.astype(jnp.bfloat16), "ctx", 3)
-    d_mine = jnp.einsum("tn,frn->tfr", d_values_low, w_mine, preferred_element_type=jnp.float32).astype(jnp.bfloat16)
-    partner_grads = lax.ppermute(d_values_low, "ctx", partner)
-    d_other = lax.ppermute(
-        jnp.einsum("tn,frn->tfr", partner_grads, w_mine, preferred_element_type=jnp.float32).astype(jnp.bfloat16),
-        "ctx",
-        partner,
-    )
     d_tokens = jnp.where(
         core == 0, jnp.stack([d_mine, d_other], 2), jnp.stack([d_other, d_mine], 2)
     ).reshape(shard_rows, model_width)

time: 308 us -> 341 us (1.11)
  waiting for transfers between devices: 81.4 us -> 133 us
  starting transfers between devices: 64.3 us -> 55.6 us
  Pallas kernels: 65.3 us -> 60.3 us
    ppermute x16, waiting for transfers between devices: 79.9 us -> 131 us  [shifted(): return lax.ppermute(x, axis, pairs)]
    ppermute x1, starting transfers between devices: 10.5 us -> 0.01 us  [shards(): lax.ppermute(partner_part.astype(jnp.bfloat16), 'ctx', partner)]
    pallas_call x1, Pallas kernels: 26.2 us -> 21.1 us  [peer_sum_scatter(): pl.pallas_call(functools.partial(peer_sum_kernel, axis, n), out_shape=jax...]
    unnamed x23 -> x31, local copies, waits for them, and re-layouts: 22.9 us -> 21.2 us
  transfers between devices with their start and end apart: 23 -> 23, of which waited for: 10 -> 13; matrix products, arithmetic and copies ran while one was open for 22% -> 18% of each run, Pallas kernels for 13% -> 12%
where the time goes in v14:
time: 341 us; the launch traced here: 336 us
  waiting for transfers between devices  133 us (39%)
  Pallas kernels  60.3 us (18%)
  starting transfers between devices  55.6 us (16%)
  local copies, waits for them, and re-layouts  41.1 us (12%)
  matrix products  22.9 us (7%)
  between operations  14.4 us (4%)
  other arithmetic  9.06 us (3%)
    ppermute x16, waiting for transfers between devices, shifted(): return lax.ppermute(x, axis, pairs)  131 us
    ppermute x16, starting transfers between devices, shifted(): return lax.ppermute(x, axis, pairs)  47.7 us
    pallas_call x1, Pallas kernels, fused_attention(): pl.pallas_call(attention_kernel, grid=(heads,), in_specs=[q_spec, kv_spec...  24 us
    unnamed x31, local copies, waits for them, and re-layouts  21.2 us
    pallas_call x1, Pallas kernels, peer_sum_scatter(): pl.pallas_call(functools.partial(peer_sum_kernel, axis, n), out_shape=jax...  21.1 us
    pallas_call x1, Pallas kernels, value_grads(): pl.pallas_call(value_grad_kernel, grid=(heads,), in_specs=[q_spec, kv_spe...  15.2 us
    dot_general x1, matrix products, shards(): jnp.einsum('ftcr,ftn->crn', token_cols, grads_all, preferred_element_type...  7.7 us
    all_to_all x1, starting transfers between devices, shards(): token_cols = lax.all_to_all(token_cols, 'fsdp', 0, 0, tiled=True)  7.22 us
  transfers between devices with their start and end apart: 23, of which 13 were waited for; matrix products, arithmetic and copies ran while one was open for 18% of the time, Pallas kernels for 12%

profile of v14, /device:TPU:28, one launch (start us, length us, event | category | flops | bytes accessed | tf_op | source)
XLA Modules:
  0.0 336.5 jit_solution(4182440176986348049)
XLA Ops:
  12.2 4.6 %collective-permute-start = (bf16[256,1152]{1,0:T(8,128)(2,1)}, bf16[256,1152]{1,0:T(8,128)(2,1)}, u32[]{:S(2)}, u32[]{:S(2)}) collective-permute-start(bf16[256,1152]{1,0:T(8,128)(2,1)} %pad_maximum_fusion), channel_id=1, source_target_pairs={{0,32},{8,40},{16,48},{24,56},{32,64},{40,72},{48,80},{56,88},{64,... | collective-permute-start | bytes 1769480 | tf_op jit(solution)/shard_map/ppermute | solution.py:210
  16.8 3.2 collective-permute-start.1
  20.0 4.5 %copy.20 = bf16[1,256,5376]{1,2,0:T(8,128)(2,1)} copy(bf16[1,256,5376]{2,1,0:T(8,128)(2,1)} %param.6) | data formatting | bytes 5505024 | tf_op args[0]
  26.1 3.7 %collective-permute-start.2 = (bf16[256,1152]{1,0:T(8,128)(2,1)}, bf16[256,1152]{1,0:T(8,128)(2,1)}, u32[]{:S(2)}, u32[]{:S(2)}) collective-permute-start(bf16[256,1152]{1,0:T(8,128)(2,1)} %pad_maximum_fusion), channel_id=1, source_target_pairs={{0,16},{8,24},{16,32},{24,40},{32,48},{40,56},{48,64},{56,72},{64,... | collective-permute-start | bytes 1769480 | tf_op jit(solution)/shard_map/ppermute | solution.py:210
  31.7 5.3 %reshape_squeeze.7 = bf16[256,16,8,42]{0,3,2,1:T(8,128)(2,1)} reshape(bf16[1,256,5376]{1,2,0:T(8,128)(2,1)} %copy.20) | data formatting | bytes 5505024 | tf_op jit(solution)/shard_map/reshape;squeeze | solution.py:237
  40.1 8.5 %collective-permute-done.2 = bf16[256,1152]{1,0:T(8,128)(2,1)} collective-permute-done((bf16[256,1152]{1,0:T(8,128)(2,1)}, bf16[256,1152]{1,0:T(8,128)(2,1)}, u32[]{:S(2)}, u32[]{:S(2)}) %collective-permute-start.2) | collective-permute-done | bytes 589856 | tf_op jit(solution)/shard_map/ppermute | solution.py:210
  49.7 4.7 %collective-permute-done.3 = bf16[256,1152]{1,0:T(8,128)(2,1)} collective-permute-done((bf16[256,1152]{1,0:T(8,128)(2,1)}, bf16[256,1152]{1,0:T(8,128)(2,1)}, u32[]{:S(2)}, u32[]{:S(2)}) %collective-permute-start.3) | collective-permute-done | bytes 589856 | tf_op jit(solution)/shard_map/ppermute | solution.py:210
  58.3 15.2 %shard_map.101 = bf16[1280,1024]{1,0:T(8,128)(2,1)} custom-call(bf16[256,2048]{1,0:T(8,128)(2,1)} %bitcast.69, bf16[1280,1024]{1,0:T(8,128)(2,1)} %slice.36.k_ref, bf16[256,2048]{1,0:T(8,128)(2,1)} %bitcast.71, s32[256,1]{1,0:T(8,128)} %copy.22.qtag_ref, s32[1,1280]{1,0:T(1,128)} %compare_select_fusion.ktag_ref), custom_call_target="tpu_custom_call" | custom-call | flops 2684354560 | bytes 7340032 | tf_op jit(solution)/shard_map/pallas_call | solution.py:79
  75.2 10.7 %collective-permute-start.5 = (bf16[256,1024]{1,0:T(8,128)(2,1)S(1)}, bf16[256,1024]{1,0:T(8,128)(2,1)S(1)}, u32[]{:S(2)}, u32[]{:S(2)}) collective-permute-start(bf16[256,1024]{1,0:T(8,128)(2,1)S(1)} %get-tuple-element.43), channel_id=1, source_target_pairs={{8,0},{16,8},{24,16},{32,24},{40,32},{48,40},{56,48},{64,56},{72,6... | collective-permute-start | bytes 1572872 | tf_op jit(solution)/shard_map/ppermute | solution.py:210
  90.5 6.4 %collective-permute-done.5 = bf16[256,1024]{1,0:T(8,128)(2,1)S(1)} collective-permute-done((bf16[256,1024]{1,0:T(8,128)(2,1)S(1)}, bf16[256,1024]{1,0:T(8,128)(2,1)S(1)}, u32[]{:S(2)}, u32[]{:S(2)}) %collective-permute-start.5) | collective-permute-done | bytes 524320 | tf_op jit(solution)/shard_map/ppermute | solution.py:210
  96.9 13.6 %collective-permute-done.6 = bf16[256,1024]{1,0:T(8,128)(2,1)S(1)} collective-permute-done((bf16[256,1024]{1,0:T(8,128)(2,1)S(1)}, bf16[256,1024]{1,0:T(8,128)(2,1)S(1)}, u32[]{:S(2)}, u32[]{:S(2)}) %collective-permute-start.6) | collective-permute-done | bytes 524320 | tf_op jit(solution)/shard_map/ppermute | solution.py:210
  112.3 16.7 %collective-permute-done.8 = bf16[256,1024]{1,0:T(8,128)(2,1)S(1)} collective-permute-done((bf16[256,1024]{1,0:T(8,128)(2,1)S(1)}, bf16[256,1024]{1,0:T(8,128)(2,1)S(1)}, u32[]{:S(2)}, u32[]{:S(2)}) %collective-permute-start.8) | collective-permute-done | bytes 524320 | tf_op jit(solution)/shard_map/ppermute | solution.py:210
  131.4 5.1 %fusion.13 = bf16[256,1024]{1,0:T(8,128)(2,1)} fusion(bf16[256,8,336]{0,2,1:T(8,128)(2,1)S(1)} %collective-permute-done.4, bf16[8,336,1024]{2,1,0:T(8,128)(2,1)} %bitcast.53), kind=kOutput, calls=%fused_computation.13 | convolution fusion | flops 1409548288 | bytes 7405568 | tf_op jit(solution)/shard_map/tfr,frn->tn/dot_general | solution.py:266
  138.6 4.7 %add_convert_fusion.1 = bf16[256,1024]{1,0:T(8,128)(2,1)S(1)} fusion(bf16[256,1024]{1,0:T(8,128)(2,1)S(1)} %collective-permute-done.9, bf16[8,336,1024]{2,1,0:T(8,128)(2,1)} %bitcast.54, bf16[256,8,2,336]{0,3,2,1:T(8,128)(2,1)} %bitcast.60, s32[]{:T(128)S(6)} %select_n.48), kind=kOutput, calls=%fused_computation.15 | convolution fusion | flops 1410072576 | bytes 7929860 | tf_op jit(solution)/shard_map/tfr,frn->tn/dot_general | solution.py:268
  143.3 4.6 %collective-permute-start.10 = (bf16[256,1024]{1,0:T(8,128)(2,1)S(1)}, bf16[256,1024]{1,0:T(8,128)(2,1)}, u32[]{:S(2)}, u32[]{:S(2)}) collective-permute-start(bf16[256,1024]{1,0:T(8,128)(2,1)S(1)} %add_convert_fusion.1), channel_id=1, source_target_pairs={{0,32},{8,40},{16,48},{24,56},{32,64},{40,72},{48,80},{56,88},{64,... | collective-permute-start | bytes 1572872 | tf_op jit(solution)/shard_map/ppermute | solution.py:210
  147.9 2.7 convolution_convert_fusion.1
  150.7 2.3 collective-permute-start.11
  153.0 3.5 %collective-permute-start.12 = (bf16[256,1024]{1,0:T(8,128)(2,1)S(1)}, bf16[256,1024]{1,0:T(8,128)(2,1)}, u32[]{:S(2)}, u32[]{:S(2)}) collective-permute-start(bf16[256,1024]{1,0:T(8,128)(2,1)S(1)} %add_convert_fusion.1), channel_id=1, source_target_pairs={{0,16},{8,24},{16,32},{24,40},{32,48},{40,56},{48,64},{56,72},{64,... | collective-permute-start | bytes 1572872 | tf_op jit(solution)/shard_map/ppermute | solution.py:210
  158.6 2.8 convolution_convert_fusion
  161.4 3.1 copy.25
  164.5 7.2 %all-to-all-start = ((bf16[8,256,16,42]{1,2,3,0:T(8,128)(2,1)}), bf16[8,256,16,42]{1,2,3,0:T(8,128)(2,1)}, u32[]{:S(2)}, u32[]{:S(2)}) async-start(bf16[8,256,16,42]{1,2,3,0:T(8,128)(2,1)} %copy.25), calls=%async_computation | async-start | bytes 5505024 | tf_op jit(solution)/shard_map/all_to_all | solution.py:273
  173.9 31.1 %collective-permute-done.12 = bf16[256,1024]{1,0:T(8,128)(2,1)} collective-permute-done((bf16[256,1024]{1,0:T(8,128)(2,1)S(1)}, bf16[256,1024]{1,0:T(8,128)(2,1)}, u32[]{:S(2)}, u32[]{:S(2)}) %collective-permute-start.12) | collective-permute-done | bytes 524320 | tf_op jit(solution)/shard_map/ppermute | solution.py:210
  206.1 9.0 %collective-permute-done.13 = bf16[256,1024]{1,0:T(8,128)(2,1)S(1)} collective-permute-done((bf16[256,1024]{1,0:T(8,128)(2,1)S(1)}, bf16[256,1024]{1,0:T(8,128)(2,1)S(1)}, u32[]{:S(2)}, u32[]{:S(2)}) %collective-permute-start.13) | collective-permute-done | bytes 524320 | tf_op jit(solution)/shard_map/ppermute | solution.py:210
  216.7 24.0 %shard_map.102 = (bf16[256,2048]{1,0:T(8,128)(2,1)}, bf16[256,2048]{1,0:T(8,128)(2,1)}, bf16[1280,1024]{1,0:T(8,128)(2,1)}) custom-call(bf16[256,2048]{1,0:T(8,128)(2,1)} %bitcast.70, bf16[1280,1024]{1,0:T(8,128)(2,1)} %slice.36.k_ref, bf16[1280,1024]{1,0:T(8,128)(2,1)} %copy-done.6, bf16[256,2048]{1,0:T(8,128)(2,1)} %bitcast.72, s32[256,1]{1,0:T(8,128)} %copy.22.qtag_ref, ...), custom_call_target="tpu_custom_call" | custom-call | flops 6710886400 | bytes 12058624 | tf_op jit(solution)/shard_map/pallas_call | solution.py:98
  240.7 3.0 fusion.20
  250.1 6.2 %collective-permute-done.15 = bf16[256,1024]{1,0:T(8,128)(2,1)S(1)} collective-permute-done((bf16[256,1024]{1,0:T(8,128)(2,1)}, bf16[256,1024]{1,0:T(8,128)(2,1)S(1)}, u32[]{:S(2)}, u32[]{:S(2)}) %collective-permute-start.15) | collective-permute-done | bytes 524320 | tf_op jit(solution)/shard_map/ppermute | solution.py:210
  256.4 15.2 %collective-permute-done.16 = bf16[256,1024]{1,0:T(8,128)(2,1)} collective-permute-done((bf16[256,1024]{1,0:T(8,128)(2,1)}, bf16[256,1024]{1,0:T(8,128)(2,1)}, u32[]{:S(2)}, u32[]{:S(2)}) %collective-permute-start.16) | collective-permute-done | bytes 524320 | tf_op jit(solution)/shard_map/ppermute | solution.py:210
  273.0 16.7 %collective-permute-done.18 = bf16[256,1024]{1,0:T(8,128)(2,1)} collective-permute-done((bf16[256,1024]{1,0:T(8,128)(2,1)}, bf16[256,1024]{1,0:T(8,128)(2,1)}, u32[]{:S(2)}, u32[]{:S(2)}) %collective-permute-start.18) | collective-permute-done | bytes 524320 | tf_op jit(solution)/shard_map/ppermute | solution.py:210
  289.7 2.8 fusion.14
  294.7 4.5 %copy.27 = bf16[1,256,5376]{2,1,0:T(8,128)(2,1)} copy(bf16[1,256,5376]{1,2,0:T(8,128)(2,1)} %bitcast.62) | data formatting | bytes 5505024
  299.2 7.7 %bitcast_convert_fusion.x_ref = bf16[16,42,1024]{2,1,0:T(8,128)(2,1)} fusion(bf16[8,256,1024]{2,1,0:T(8,128)(2,1)} %bitcast.68, bf16[8,256,16,42]{1,2,3,0:T(8,128)(2,1)} %all-to-all-done), kind=kOutput, calls=%fused_computation.2 | convolution fusion | flops 2819260416 | bytes 8323072 | tf_op jit(solution)/shard_map/ftcr,ftn->crn/dot_general | solution.py:287
  306.9 21.1 %shard_map.103 = f32[42,1024]{1,0:T(8,128)} custom-call(bf16[16,42,1024]{2,1,0:T(8,128)(2,1)} %bitcast_convert_fusion.x_ref), custom_call_target="tpu_custom_call" | custom-call | tf_op jit(solution)/shard_map/pallas_call | solution.py:192
  (75 shorter events, 47.5 us)
Async XLA Ops:
  7.2 124.2 %all-gather.5.cloned.1.call-start = ((), (), s32[]{:S(2)}) async-start(), calls=%async_computation.1 | async-start | bytes 6193152 | tf_op jit(solution)/shard_map/all_gather | solution.py:226
  9.4 240.7 %all-gather.7.cloned.1.call-start = ((), (), s32[]{:S(2)}) async-start(), calls=%async_computation.2 | async-start | bytes 4718592 | tf_op jit(solution)/shard_map/all_gather | solution.py:264
  12.2 25.6 %collective-permute-start = (bf16[256,1152]{1,0:T(8,128)(2,1)}, bf16[256,1152]{1,0:T(8,128)(2,1)}, u32[]{:S(2)}, u32[]{:S(2)}) collective-permute-start(bf16[256,1152]{1,0:T(8,128)(2,1)} %pad_maximum_fusion), channel_id=1, source_target_pairs={{0,32},{8,40},{16,48},{24,56},{32,64},{40,72},{48,80},{56,88},{64,... | collective-permute-start | bytes 1769480 | tf_op jit(solution)/shard_map/ppermute | solution.py:210
  16.8 22.1 %collective-permute-start.1 = (bf16[256,1152]{1,0:T(8,128)(2,1)}, bf16[256,1152]{1,0:T(8,128)(2,1)}, u32[]{:S(2)}, u32[]{:S(2)}) collective-permute-start(bf16[256,1152]{1,0:T(8,128)(2,1)} %pad_maximum_fusion), channel_id=1, source_target_pairs={{0,24},{8,32},{16,40},{24,48},{32,56},{40,64},{48,72},{56,80},{64,... | collective-permute-start | bytes 1769480 | tf_op jit(solution)/shard_map/ppermute | solution.py:210
  26.0 11.0 %copy-start.7 = (s32[1,256]{1,0:T(1,128)S(1)}, s32[1,256]{1,0:T(1,128)}, u32[]{:S(2)}) copy-start(s32[1,256]{1,0:T(1,128)} %param.11) | copy-start | bytes 3076
  26.0 29.6 %collective-permute-start.4 = (bf16[256,8,336]{0,2,1:T(8,128)(2,1)S(1)}, bf16[256,8,336]{0,2,1:T(8,128)(2,1)S(1)}, u32[]{:S(2)}, u32[]{:S(2)}) collective-permute-start(bf16[256,8,336]{0,2,1:T(8,128)(2,1)S(1)} %dynamic-slice_bitcast_fusion), channel_id=1, source_target_pairs={{0,8},{8,0},{16,24},{24,16},{32,40},{40,32},{48,56},{56,48},{64,72... | collective-permute-start | bytes 4128776 | tf_op jit(solution)/shard_map/ppermute | solution.py:232
  26.1 22.5 %collective-permute-start.2 = (bf16[256,1152]{1,0:T(8,128)(2,1)}, bf16[256,1152]{1,0:T(8,128)(2,1)}, u32[]{:S(2)}, u32[]{:S(2)}) collective-permute-start(bf16[256,1152]{1,0:T(8,128)(2,1)} %pad_maximum_fusion), channel_id=1, source_target_pairs={{0,16},{8,24},{16,32},{24,40},{32,48},{40,56},{48,64},{56,72},{64,... | collective-permute-start | bytes 1769480 | tf_op jit(solution)/shard_map/ppermute | solution.py:210
  29.8 24.6 %collective-permute-start.3 = (bf16[256,1152]{1,0:T(8,128)(2,1)}, bf16[256,1152]{1,0:T(8,128)(2,1)}, u32[]{:S(2)}, u32[]{:S(2)}) collective-permute-start(bf16[256,1152]{1,0:T(8,128)(2,1)} %pad_maximum_fusion), channel_id=1, source_target_pairs={{0,8},{8,16},{16,24},{24,32},{32,40},{40,48},{48,56},{56,64},{64,7... | collective-permute-start | bytes 1769480 | tf_op jit(solution)/shard_map/ppermute | solution.py:210
  37.0 18.6 %copy-start.3 = (bf16[1,256,1024]{2,1,0:T(8,128)(2,1)S(1)}, bf16[1,256,1024]{2,1,0:T(8,128)(2,1)}, u32[]{:S(2)}) copy-start(bf16[1,256,1024]{2,1,0:T(8,128)(2,1)} %param.8) | copy-start | bytes 1572868
  75.2 21.6 %collective-permute-start.5 = (bf16[256,1024]{1,0:T(8,128)(2,1)S(1)}, bf16[256,1024]{1,0:T(8,128)(2,1)S(1)}, u32[]{:S(2)}, u32[]{:S(2)}) collective-permute-start(bf16[256,1024]{1,0:T(8,128)(2,1)S(1)} %get-tuple-element.43), channel_id=1, source_target_pairs={{8,0},{16,8},{24,16},{32,24},{40,32},{48,40},{56,48},{64,56},{72,6... | collective-permute-start | bytes 1572872 | tf_op jit(solution)/shard_map/ppermute | solution.py:210
  86.0 24.5 %collective-permute-start.6 = (bf16[256,1024]{1,0:T(8,128)(2,1)S(1)}, bf16[256,1024]{1,0:T(8,128)(2,1)S(1)}, u32[]{:S(2)}, u32[]{:S(2)}) collective-permute-start(bf16[256,1024]{1,0:T(8,128)(2,1)S(1)} %get-tuple-element.46), channel_id=1, source_target_pairs={{16,0},{24,8},{32,16},{40,24},{48,32},{56,40},{64,48},{72,56},{80,... | collective-permute-start | bytes 1572872 | tf_op jit(solution)/shard_map/ppermute | solution.py:210
  87.9 24.4 %collective-permute-start.7 = (bf16[256,1024]{1,0:T(8,128)(2,1)S(1)}, bf16[256,1024]{1,0:T(8,128)(2,1)S(1)}, u32[]{:S(2)}, u32[]{:S(2)}) collective-permute-start(bf16[256,1024]{1,0:T(8,128)(2,1)S(1)} %get-tuple-element.45), channel_id=1, source_target_pairs={{24,0},{32,8},{40,16},{48,24},{56,32},{64,40},{72,48},{80,56},{88,... | collective-permute-start | bytes 1572872 | tf_op jit(solution)/shard_map/ppermute | solution.py:210
  89.2 39.8 %collective-permute-start.8 = (bf16[256,1024]{1,0:T(8,128)(2,1)S(1)}, bf16[256,1024]{1,0:T(8,128)(2,1)S(1)}, u32[]{:S(2)}, u32[]{:S(2)}) collective-permute-start(bf16[256,1024]{1,0:T(8,128)(2,1)S(1)} %get-tuple-element.44), channel_id=1, source_target_pairs={{32,0},{40,8},{48,16},{56,24},{64,32},{72,40},{80,48},{88,56},{96,... | collective-permute-start | bytes 1572872 | tf_op jit(solution)/shard_map/ppermute | solution.py:210
  131.4 5.1 %copy-start.4 = (bf16[256,1024]{1,0:T(8,128)(2,1)S(1)}, bf16[256,1024]{1,0:T(8,128)(2,1)}, u32[]{:S(2)}) copy-start(bf16[256,1024]{1,0:T(8,128)(2,1)} %add_convert_fusion.2) | copy-start | bytes 1572868
  136.5 2.1 collective-permute-start.9
  136.5 11.4 %slice-start = ((s8[5505024]{0:T(1024)(128)(4,1)}), s8[1310720]{0:T(1024)(128)(4,1)S(1)}, s32[]{:S(2)}) async-start(s8[5505024]{0:T(1024)(128)(4,1)} %bitcast.55), calls=%async_computation.3 | async-start | bytes 2621440
  136.5 11.4 %slice-start.1 = ((s8[5505024]{0:T(1024)(128)(4,1)}), s8[4194304]{0:T(1024)(128)(4,1)S(1)}, s32[]{:S(2)}) async-start(s8[5505024]{0:T(1024)(128)(4,1)} %bitcast.55), calls=%async_computation.4 | async-start | bytes 8388608
  136.5 22.1 %collective-permute-start.14 = (bf16[256,1024]{1,0:T(8,128)(2,1)S(1)}, bf16[256,1024]{1,0:T(8,128)(2,1)S(1)}, u32[]{:S(2)}, u32[]{:S(2)}) collective-permute-start(bf16[256,1024]{1,0:T(8,128)(2,1)S(1)} %copy-done.4), channel_id=1, source_target_pairs={{0,8},{8,0},{16,24},{24,16},{32,40},{40,32},{48,56},{56,48},{64,72... | collective-permute-start | bytes 1572872 | tf_op jit(solution)/shard_map/ppermute | solution.py:276
  143.3 28.4 %collective-permute-start.10 = (bf16[256,1024]{1,0:T(8,128)(2,1)S(1)}, bf16[256,1024]{1,0:T(8,128)(2,1)}, u32[]{:S(2)}, u32[]{:S(2)}) collective-permute-start(bf16[256,1024]{1,0:T(8,128)(2,1)S(1)} %add_convert_fusion.1), channel_id=1, source_target_pairs={{0,32},{8,40},{16,48},{24,56},{32,64},{40,72},{48,80},{56,88},{64,... | collective-permute-start | bytes 1572872 | tf_op jit(solution)/shard_map/ppermute | solution.py:210
  150.7 10.7 %copy-start.2 = (bf16[256,16,8,42]{0,3,2,1:T(8,128)(2,1)S(1)}, bf16[256,16,8,42]{0,3,2,1:T(8,128)(2,1)}, u32[]{:S(2)}) copy-start(bf16[256,16,8,42]{0,3,2,1:T(8,128)(2,1)} %reshape_squeeze.7) | copy-start | bytes 8257540
  150.7 22.2 %collective-permute-start.11 = (bf16[256,1024]{1,0:T(8,128)(2,1)S(1)}, bf16[256,1024]{1,0:T(8,128)(2,1)}, u32[]{:S(2)}, u32[]{:S(2)}) collective-permute-start(bf16[256,1024]{1,0:T(8,128)(2,1)S(1)} %add_convert_fusion.1), channel_id=1, source_target_pairs={{0,24},{8,32},{16,40},{24,48},{32,56},{40,64},{48,72},{56,80},{64,... | collective-permute-start | bytes 1572872 | tf_op jit(solution)/shard_map/ppermute | solution.py:210
  153.0 52.0 %collective-permute-start.12 = (bf16[256,1024]{1,0:T(8,128)(2,1)S(1)}, bf16[256,1024]{1,0:T(8,128)(2,1)}, u32[]{:S(2)}, u32[]{:S(2)}) collective-permute-start(bf16[256,1024]{1,0:T(8,128)(2,1)S(1)} %add_convert_fusion.1), channel_id=1, source_target_pairs={{0,16},{8,24},{16,32},{24,40},{32,48},{40,56},{48,64},{56,72},{64,... | collective-permute-start | bytes 1572872 | tf_op jit(solution)/shard_map/ppermute | solution.py:210
  156.5 58.6 %collective-permute-start.13 = (bf16[256,1024]{1,0:T(8,128)(2,1)S(1)}, bf16[256,1024]{1,0:T(8,128)(2,1)S(1)}, u32[]{:S(2)}, u32[]{:S(2)}) collective-permute-start(bf16[256,1024]{1,0:T(8,128)(2,1)S(1)} %add_convert_fusion.1), channel_id=1, source_target_pairs={{0,8},{8,16},{16,24},{24,32},{32,40},{40,48},{48,56},{56,64},{64,7... | collective-permute-start | bytes 1572872 | tf_op jit(solution)/shard_map/ppermute | solution.py:210
  164.5 134.7 %all-to-all-start = ((bf16[8,256,16,42]{1,2,3,0:T(8,128)(2,1)}), bf16[8,256,16,42]{1,2,3,0:T(8,128)(2,1)}, u32[]{:S(2)}, u32[]{:S(2)}) async-start(bf16[8,256,16,42]{1,2,3,0:T(8,128)(2,1)} %copy.25), calls=%async_computation | async-start | bytes 5505024 | tf_op jit(solution)/shard_map/all_to_all | solution.py:273
  215.2 1.5 copy-start.6
  216.7 75.8 %collective-permute-start.19 = (bf16[256,8,336]{0,2,1:T(8,128)(2,1)}, bf16[256,8,336]{0,2,1:T(8,128)(2,1)S(1)}, u32[]{:S(2)}, u32[]{:S(2)}) collective-permute-start(bf16[256,8,336]{0,2,1:T(8,128)(2,1)} %convolution_convert_fusion), channel_id=1, source_target_pairs={{0,8},{8,0},{16,24},{24,16},{32,40},{40,32},{48,56},{56,48},{64,72... | collective-permute-start | bytes 4128776 | tf_op jit(solution)/shard_map/ppermute | solution.py:281
  240.7 51.8 %copy-start.5 = (bf16[256,8,336]{0,2,1:T(8,128)(2,1)S(1)}, bf16[256,8,336]{0,2,1:T(8,128)(2,1)}, u32[]{:S(2)}) copy-start(bf16[256,8,336]{0,2,1:T(8,128)(2,1)} %convolution_convert_fusion.1) | copy-start | bytes 4128772
  243.7 12.7 %collective-permute-start.15 = (bf16[256,1024]{1,0:T(8,128)(2,1)}, bf16[256,1024]{1,0:T(8,128)(2,1)S(1)}, u32[]{:S(2)}, u32[]{:S(2)}) collective-permute-start(bf16[256,1024]{1,0:T(8,128)(2,1)} %get-tuple-element.39), channel_id=1, source_target_pairs={{8,0},{16,8},{24,16},{32,24},{40,32},{48,40},{56,48},{64,56},{72,6... | collective-permute-start | bytes 1572872 | tf_op jit(solution)/shard_map/ppermute | solution.py:210
  245.6 26.0 %collective-permute-start.16 = (bf16[256,1024]{1,0:T(8,128)(2,1)}, bf16[256,1024]{1,0:T(8,128)(2,1)}, u32[]{:S(2)}, u32[]{:S(2)}) collective-permute-start(bf16[256,1024]{1,0:T(8,128)(2,1)} %get-tuple-element.42), channel_id=1, source_target_pairs={{16,0},{24,8},{32,16},{40,24},{48,32},{56,40},{64,48},{72,56},{80,... | collective-permute-start | bytes 1572872 | tf_op jit(solution)/shard_map/ppermute | solution.py:210
  247.5 25.5 %collective-permute-start.17 = (bf16[256,1024]{1,0:T(8,128)(2,1)}, bf16[256,1024]{1,0:T(8,128)(2,1)}, u32[]{:S(2)}, u32[]{:S(2)}) collective-permute-start(bf16[256,1024]{1,0:T(8,128)(2,1)} %get-tuple-element.41), channel_id=1, source_target_pairs={{24,0},{32,8},{40,16},{48,24},{56,32},{64,40},{72,48},{80,56},{88,... | collective-permute-start | bytes 1572872 | tf_op jit(solution)/shard_map/ppermute | solution.py:210
  248.8 40.9 %collective-permute-start.18 = (bf16[256,1024]{1,0:T(8,128)(2,1)}, bf16[256,1024]{1,0:T(8,128)(2,1)}, u32[]{:S(2)}, u32[]{:S(2)}) collective-permute-start(bf16[256,1024]{1,0:T(8,128)(2,1)} %get-tuple-element.40), channel_id=1, source_target_pairs={{32,0},{40,8},{48,16},{56,24},{64,32},{72,40},{80,48},{88,56},{96,... | collective-permute-start | bytes 1572872 | tf_op jit(solution)/shard_map/ppermute | solution.py:210
  299.2 30.4 %copy-start.1 = (bf16[672,1024]{1,0:T(8,128)(2,1)S(1)}, bf16[672,1024]{1,0:T(8,128)(2,1)}, u32[]{:S(2)}) copy-start(bf16[672,1024]{1,0:T(8,128)(2,1)} %param.9) | copy-start | bytes 4128772
  (1 other events, 1.3 us)
Sparse Core Ops, SparseCore 0:
  10.9 88.0 all-gather.4
  131.5 107.7 all-gather.6

commit v15 on v13

--- a/solution.py
+++ b/solution.py
@@ -276,11 +276,6 @@
         queries[0], window_keys, window_values, d_out[0], query_tags, key_tags[None, :]
     )
     d_key_rows = returned_sum(key_terms)
-    grads_all, _ = lax.optimization_barrier((grads_all, key_terms))
-    weight_part = jnp.einsum(
-        "ftcr,ftn->crn", token_cols, grads_all, preferred_element_type=jnp.float32
-    )
-    d_weight = peer_sum_scatter(weight_part.astype(jnp.bfloat16), "ctx", 3)
     d_mine = jnp.einsum("tn,frn->tfr", d_values_low, w_mine, preferred_element_type=jnp.float32).astype(jnp.bfloat16)
     partner_grads = lax.ppermute(d_values_low, "ctx", partner)
     d_other = lax.ppermute(
@@ -291,6 +286,11 @@
     d_tokens = jnp.where(
         core == 0, jnp.stack([d_mine, d_other], 2), jnp.stack([d_other, d_mine], 2)
     ).reshape(shard_rows, model_width)
+    grads_all, _, d_tokens = lax.optimization_barrier((grads_all, key_terms, d_tokens))
+    weight_part = jnp.einsum(
+        "ftcr,ftn->crn", token_cols, grads_all, preferred_element_type=jnp.float32
+    )
+    d_weight = peer_sum_scatter(weight_part.astype(jnp.bfloat16), "ctx", 3)
     return (
         out_rows_attn[None],
         d_query_heads[None],

time: 308 us -> 322 us (1.045)
  starting transfers between devices: 64.3 us -> 79.4 us
    ppermute x16, starting transfers between devices: 45.9 us -> 66.4 us  [shifted(): return lax.ppermute(x, axis, pairs)]
    ppermute x1, starting transfers between devices: 10.5 us -> 5.51 us  [shards(): lax.ppermute(partner_part.astype(jnp.bfloat16), 'ctx', partner)]
  transfers between devices with their start and end apart: 23 -> 23, of which waited for: 10 -> 7; matrix products, arithmetic and copies ran while one was open for 22% -> 21% of each run, Pallas kernels for 13% -> 12%
where the time goes in v15:
time: 322 us; the launch traced here: 318 us
  starting transfers between devices  79.4 us (25%)
  waiting for transfers between devices  79.1 us (25%)
  Pallas kernels  66.5 us (21%)
  local copies, waits for them, and re-layouts  43.4 us (13%)
  matrix products  26.2 us (8%)
  between operations  14.3 us (4%)
  other arithmetic  9.27 us (3%)
    ppermute x16, waiting for transfers between devices, shifted(): return lax.ppermute(x, axis, pairs)  77.6 us
    ppermute x16, starting transfers between devices, shifted(): return lax.ppermute(x, axis, pairs)  66.4 us
    pallas_call x1, Pallas kernels, peer_sum_scatter(): pl.pallas_call(functools.partial(peer_sum_kernel, axis, n), out_shape=jax...  27.4 us
    pallas_call x1, Pallas kernels, fused_attention(): pl.pallas_call(attention_kernel, grid=(heads,), in_specs=[q_spec, kv_spec...  23.9 us
    unnamed x23, local copies, waits for them, and re-layouts  22.9 us
    pallas_call x1, Pallas kernels, value_grads(): pl.pallas_call(value_grad_kernel, grid=(heads,), in_specs=[q_spec, kv_spe...  15.2 us
    dot_general x1, matrix products, shards(): jnp.einsum('ftcr,ftn->crn', token_cols, grads_all, preferred_element_type...  7.73 us
    all_to_all x1, starting transfers between devices, shards(): token_cols = lax.all_to_all(token_cols, 'fsdp', 0, 0, tiled=True)  7.21 us
  transfers between devices with their start and end apart: 23, of which 7 were waited for; matrix products, arithmetic and copies ran while one was open for 21% of the time, Pallas kernels for 12%

profile of v15, /device:TPU:28, one launch (start us, length us, event | category | flops | bytes accessed | tf_op | source)
XLA Modules:
  0.0 318.2 jit_solution(14721133690229468735)
XLA Ops:
  12.2 4.6 %collective-permute-start = (bf16[256,1152]{1,0:T(8,128)(2,1)}, bf16[256,1152]{1,0:T(8,128)(2,1)}, u32[]{:S(2)}, u32[]{:S(2)}) collective-permute-start(bf16[256,1152]{1,0:T(8,128)(2,1)} %pad_maximum_fusion), channel_id=1, source_target_pairs={{0,32},{8,40},{16,48},{24,56},{32,64},{40,72},{48,80},{56,88},{64,... | collective-permute-start | bytes 1769480 | tf_op jit(solution)/shard_map/ppermute | solution.py:210
  16.8 3.2 collective-permute-start.1
  20.0 4.5 %copy.20 = bf16[1,256,5376]{1,2,0:T(8,128)(2,1)} copy(bf16[1,256,5376]{2,1,0:T(8,128)(2,1)} %param.6) | data formatting | bytes 5505024 | tf_op args[0]
  26.1 3.7 %collective-permute-start.2 = (bf16[256,1152]{1,0:T(8,128)(2,1)}, bf16[256,1152]{1,0:T(8,128)(2,1)}, u32[]{:S(2)}, u32[]{:S(2)}) collective-permute-start(bf16[256,1152]{1,0:T(8,128)(2,1)} %pad_maximum_fusion), channel_id=1, source_target_pairs={{0,16},{8,24},{16,32},{24,40},{32,48},{40,56},{48,64},{56,72},{64,... | collective-permute-start | bytes 1769480 | tf_op jit(solution)/shard_map/ppermute | solution.py:210
  29.8 1.9 collective-permute-start.3
  31.7 5.3 %reshape_squeeze.7 = bf16[256,16,8,42]{0,3,2,1:T(8,128)(2,1)} reshape(bf16[1,256,5376]{1,2,0:T(8,128)(2,1)} %copy.20) | data formatting | bytes 5505024 | tf_op jit(solution)/shard_map/reshape;squeeze | solution.py:237
  40.1 8.5 %collective-permute-done.2 = bf16[256,1152]{1,0:T(8,128)(2,1)} collective-permute-done((bf16[256,1152]{1,0:T(8,128)(2,1)}, bf16[256,1152]{1,0:T(8,128)(2,1)}, u32[]{:S(2)}, u32[]{:S(2)}) %collective-permute-start.2) | collective-permute-done | bytes 589856 | tf_op jit(solution)/shard_map/ppermute | solution.py:210
  49.7 4.7 %collective-permute-done.3 = bf16[256,1152]{1,0:T(8,128)(2,1)} collective-permute-done((bf16[256,1152]{1,0:T(8,128)(2,1)}, bf16[256,1152]{1,0:T(8,128)(2,1)}, u32[]{:S(2)}, u32[]{:S(2)}) %collective-permute-start.3) | collective-permute-done | bytes 589856 | tf_op jit(solution)/shard_map/ppermute | solution.py:210
  58.3 15.2 %shard_map.101 = bf16[1280,1024]{1,0:T(8,128)(2,1)} custom-call(bf16[256,2048]{1,0:T(8,128)(2,1)} %bitcast.68, bf16[1280,1024]{1,0:T(8,128)(2,1)} %slice.36.k_ref, bf16[256,2048]{1,0:T(8,128)(2,1)} %bitcast.70, s32[256,1]{1,0:T(8,128)} %copy.22.qtag_ref, s32[1,1280]{1,0:T(1,128)} %compare_select_fusion.ktag_ref), custom_call_target="tpu_custom_call" | custom-call | flops 2684354560 | bytes 7340032 | tf_op jit(solution)/shard_map/pallas_call | solution.py:79
  75.2 10.7 %collective-permute-start.5 = (bf16[256,1024]{1,0:T(8,128)(2,1)S(1)}, bf16[256,1024]{1,0:T(8,128)(2,1)S(1)}, u32[]{:S(2)}, u32[]{:S(2)}) collective-permute-start(bf16[256,1024]{1,0:T(8,128)(2,1)S(1)} %get-tuple-element.39), channel_id=1, source_target_pairs={{8,0},{16,8},{24,16},{32,24},{40,32},{48,40},{56,48},{64,56},{72,6... | collective-permute-start | bytes 1572872 | tf_op jit(solution)/shard_map/ppermute | solution.py:210
  90.5 7.8 %collective-permute-done.5 = bf16[256,1024]{1,0:T(8,128)(2,1)S(1)} collective-permute-done((bf16[256,1024]{1,0:T(8,128)(2,1)S(1)}, bf16[256,1024]{1,0:T(8,128)(2,1)S(1)}, u32[]{:S(2)}, u32[]{:S(2)}) %collective-permute-start.5) | collective-permute-done | bytes 524320 | tf_op jit(solution)/shard_map/ppermute | solution.py:210
  98.3 19.5 %collective-permute-done.8 = bf16[256,1024]{1,0:T(8,128)(2,1)S(1)} collective-permute-done((bf16[256,1024]{1,0:T(8,128)(2,1)S(1)}, bf16[256,1024]{1,0:T(8,128)(2,1)S(1)}, u32[]{:S(2)}, u32[]{:S(2)}) %collective-permute-start.8) | collective-permute-done | bytes 524320 | tf_op jit(solution)/shard_map/ppermute | solution.py:210
  117.8 2.3 add_convert_fusion.2
  120.2 4.3 %fusion.14 = bf16[256,1024]{1,0:T(8,128)(2,1)S(1)} fusion(bf16[256,8,336]{0,2,1:T(8,128)(2,1)S(1)} %collective-permute-done.4, bf16[8,336,1024]{2,1,0:T(8,128)(2,1)} %bitcast.55), kind=kOutput, calls=%fused_computation.14 | convolution fusion | flops 1409548288 | bytes 7405568 | tf_op jit(solution)/shard_map/tfr,frn->tn/dot_general | solution.py:266
  124.5 5.5 %collective-permute-start.9 = (bf16[256,1024]{1,0:T(8,128)(2,1)S(1)}, bf16[256,1024]{1,0:T(8,128)(2,1)S(1)}, u32[]{:S(2)}, u32[]{:S(2)}) collective-permute-start(bf16[256,1024]{1,0:T(8,128)(2,1)S(1)} %fusion.14), channel_id=1, source_target_pairs={{0,8},{8,0},{16,24},{24,16},{32,40},{40,32},{48,56},{56,48},{64,72... | collective-permute-start | bytes 1572872 | tf_op jit(solution)/shard_map/ppermute | solution.py:269
  131.6 4.7 %add_convert_fusion.1 = bf16[256,1024]{1,0:T(8,128)(2,1)S(1)} fusion(bf16[256,1024]{1,0:T(8,128)(2,1)S(1)} %collective-permute-done.9, bf16[8,336,1024]{2,1,0:T(8,128)(2,1)} %bitcast.56, bf16[256,8,2,336]{0,3,2,1:T(8,128)(2,1)} %bitcast.60, s32[]{:T(128)S(6)} %select_n.42), kind=kOutput, calls=%fused_computation.16 | convolution fusion | flops 1410072576 | bytes 7929860 | tf_op jit(solution)/shard_map/tfr,frn->tn/dot_general | solution.py:268
  136.2 4.6 %collective-permute-start.10 = (bf16[256,1024]{1,0:T(8,128)(2,1)S(1)}, bf16[256,1024]{1,0:T(8,128)(2,1)}, u32[]{:S(2)}, u32[]{:S(2)}) collective-permute-start(bf16[256,1024]{1,0:T(8,128)(2,1)S(1)} %add_convert_fusion.1), channel_id=1, source_target_pairs={{0,32},{8,40},{16,48},{24,56},{32,64},{40,72},{48,80},{56,88},{64,... | collective-permute-start | bytes 1572872 | tf_op jit(solution)/shard_map/ppermute | solution.py:210
  140.9 2.2 collective-permute-start.13
  145.1 4.7 %collective-permute-start.11 = (bf16[256,1024]{1,0:T(8,128)(2,1)S(1)}, bf16[256,1024]{1,0:T(8,128)(2,1)}, u32[]{:S(2)}, u32[]{:S(2)}) collective-permute-start(bf16[256,1024]{1,0:T(8,128)(2,1)S(1)} %add_convert_fusion.1), channel_id=1, source_target_pairs={{0,24},{8,32},{16,40},{24,48},{32,56},{40,64},{48,72},{56,80},{64,... | collective-permute-start | bytes 1572872 | tf_op jit(solution)/shard_map/ppermute | solution.py:210
  149.7 5.3 %convolution_convert_fusion = bf16[256,8,336]{0,2,1:T(8,128)(2,1)} fusion(bf16[8,336,1024]{2,1,0:T(8,128)(2,1)} %bitcast.57, bf16[256,1024]{1,0:T(8,128)(2,1)S(1)} %collective-permute-done.18), kind=kOutput, calls=%fused_computation.5 | convolution fusion | flops 1409974272 | bytes 7405568 | tf_op jit(solution)/shard_map/tn,frn->tfr/dot_general | solution.py:282
  155.0 3.1 copy.25
  158.1 7.2 %all-to-all-start = ((bf16[8,256,16,42]{1,2,3,0:T(8,128)(2,1)}), bf16[8,256,16,42]{1,2,3,0:T(8,128)(2,1)}, u32[]{:S(2)}, u32[]{:S(2)}) async-start(bf16[8,256,16,42]{1,2,3,0:T(8,128)(2,1)} %copy.25), calls=%async_computation | async-start | bytes 5505024 | tf_op jit(solution)/shard_map/all_to_all | solution.py:273
  167.2 15.0 %collective-permute-done.11 = bf16[256,1024]{1,0:T(8,128)(2,1)} collective-permute-done((bf16[256,1024]{1,0:T(8,128)(2,1)S(1)}, bf16[256,1024]{1,0:T(8,128)(2,1)}, u32[]{:S(2)}, u32[]{:S(2)}) %collective-permute-start.11) | collective-permute-done | bytes 524320 | tf_op jit(solution)/shard_map/ppermute | solution.py:210
  187.6 23.9 %shard_map.102 = (bf16[256,2048]{1,0:T(8,128)(2,1)}, bf16[256,2048]{1,0:T(8,128)(2,1)}, bf16[1280,1024]{1,0:T(8,128)(2,1)}) custom-call(bf16[256,2048]{1,0:T(8,128)(2,1)} %bitcast.69, bf16[1280,1024]{1,0:T(8,128)(2,1)} %slice.36.k_ref, bf16[1280,1024]{1,0:T(8,128)(2,1)} %constant_dynamic-update-slice_fusion.5.v_ref, bf16[256,2048]{1,0:T(8,128)(2,1)} %bitcast.71, ...), custom_call_target="tpu_custom_call" | custom-call | flops 6710886400 | bytes 12058624 | tf_op jit(solution)/shard_map/pallas_call | solution.py:98
  211.5 2.9 fusion.21
  218.9 19.8 %collective-permute-start.15 = (bf16[256,1024]{1,0:T(8,128)(2,1)}, bf16[256,1024]{1,0:T(8,128)(2,1)}, u32[]{:S(2)}, u32[]{:S(2)}) collective-permute-start(bf16[256,1024]{1,0:T(8,128)(2,1)} %get-tuple-element.38), channel_id=1, source_target_pairs={{16,0},{24,8},{32,16},{40,24},{48,32},{56,40},{64,48},{72,56},{80,... | collective-permute-start | bytes 1572872 | tf_op jit(solution)/shard_map/ppermute | solution.py:210
  238.7 4.2 %fusion.7 = bf16[256,8,1,336]{0,3,1,2:T(8,128)(2,1)S(1)} fusion(bf16[8,336,1024]{2,1,0:T(8,128)(2,1)} %bitcast.58, bf16[256,1024]{1,0:T(8,128)(2,1)S(1)} %copy-done.4), kind=kOutput, calls=%fused_computation.7 | convolution fusion | flops 1409974272 | bytes 7405568 | tf_op jit(solution)/shard_map/tn,frn->tfr/dot_general | solution.py:279
  245.1 4.5 %copy.27 = bf16[1,256,5376]{2,1,0:T(8,128)(2,1)} copy(bf16[1,256,5376]{1,2,0:T(8,128)(2,1)} %bitcast.62) | data formatting | bytes 5505024
  249.6 22.1 %collective-permute-done.17 = bf16[256,1024]{1,0:T(8,128)(2,1)} collective-permute-done((bf16[256,1024]{1,0:T(8,128)(2,1)}, bf16[256,1024]{1,0:T(8,128)(2,1)}, u32[]{:S(2)}, u32[]{:S(2)}) %collective-permute-start.17) | collective-permute-done | bytes 524320 | tf_op jit(solution)/shard_map/ppermute | solution.py:210
  271.7 2.9 fusion.15
  274.6 7.7 %bitcast_convert_fusion.x_ref = bf16[16,42,1024]{2,1,0:T(8,128)(2,1)} fusion(bf16[8,256,1024]{2,1,0:T(8,128)(2,1)} %bitcast.67, bf16[8,256,16,42]{1,2,3,0:T(8,128)(2,1)} %all-to-all-done), kind=kOutput, calls=%fused_computation.2 | convolution fusion | flops 2819260416 | bytes 8323072 | tf_op jit(solution)/shard_map/ftcr,ftn->crn/dot_general | solution.py:290
  282.4 27.4 %shard_map.103 = f32[42,1024]{1,0:T(8,128)} custom-call(bf16[16,42,1024]{2,1,0:T(8,128)(2,1)} %bitcast_convert_fusion.x_ref), custom_call_target="tpu_custom_call" | custom-call | tf_op jit(solution)/shard_map/pallas_call | solution.py:192
  (66 shorter events, 39.8 us)
Async XLA Ops:
  7.2 1.3 copy-start
  7.2 113.0 %all-gather.5.cloned.1.call-start = ((), (), s32[]{:S(2)}) async-start(), calls=%async_computation.1 | async-start | bytes 6193152 | tf_op jit(solution)/shard_map/all_gather | solution.py:226
  9.4 235.7 %all-gather.7.cloned.1.call-start = ((), (), s32[]{:S(2)}) async-start(), calls=%async_computation.2 | async-start | bytes 4718592 | tf_op jit(solution)/shard_map/all_gather | solution.py:264
  12.2 25.6 %collective-permute-start = (bf16[256,1152]{1,0:T(8,128)(2,1)}, bf16[256,1152]{1,0:T(8,128)(2,1)}, u32[]{:S(2)}, u32[]{:S(2)}) collective-permute-start(bf16[256,1152]{1,0:T(8,128)(2,1)} %pad_maximum_fusion), channel_id=1, source_target_pairs={{0,32},{8,40},{16,48},{24,56},{32,64},{40,72},{48,80},{56,88},{64,... | collective-permute-start | bytes 1769480 | tf_op jit(solution)/shard_map/ppermute | solution.py:210
  16.8 22.1 %collective-permute-start.1 = (bf16[256,1152]{1,0:T(8,128)(2,1)}, bf16[256,1152]{1,0:T(8,128)(2,1)}, u32[]{:S(2)}, u32[]{:S(2)}) collective-permute-start(bf16[256,1152]{1,0:T(8,128)(2,1)} %pad_maximum_fusion), channel_id=1, source_target_pairs={{0,24},{8,32},{16,40},{24,48},{32,56},{40,64},{48,72},{56,80},{64,... | collective-permute-start | bytes 1769480 | tf_op jit(solution)/shard_map/ppermute | solution.py:210
  26.0 11.0 %copy-start.5 = (s32[1,256]{1,0:T(1,128)S(1)}, s32[1,256]{1,0:T(1,128)}, u32[]{:S(2)}) copy-start(s32[1,256]{1,0:T(1,128)} %param.11) | copy-start | bytes 3076
  26.0 29.6 %collective-permute-start.4 = (bf16[256,8,336]{0,2,1:T(8,128)(2,1)S(1)}, bf16[256,8,336]{0,2,1:T(8,128)(2,1)S(1)}, u32[]{:S(2)}, u32[]{:S(2)}) collective-permute-start(bf16[256,8,336]{0,2,1:T(8,128)(2,1)S(1)} %dynamic-slice_bitcast_fusion), channel_id=1, source_target_pairs={{0,8},{8,0},{16,24},{24,16},{32,40},{40,32},{48,56},{56,48},{64,72... | collective-permute-start | bytes 4128776 | tf_op jit(solution)/shard_map/ppermute | solution.py:232
  26.1 22.5 %collective-permute-start.2 = (bf16[256,1152]{1,0:T(8,128)(2,1)}, bf16[256,1152]{1,0:T(8,128)(2,1)}, u32[]{:S(2)}, u32[]{:S(2)}) collective-permute-start(bf16[256,1152]{1,0:T(8,128)(2,1)} %pad_maximum_fusion), channel_id=1, source_target_pairs={{0,16},{8,24},{16,32},{24,40},{32,48},{40,56},{48,64},{56,72},{64,... | collective-permute-start | bytes 1769480 | tf_op jit(solution)/shard_map/ppermute | solution.py:210
  29.8 24.6 %collective-permute-start.3 = (bf16[256,1152]{1,0:T(8,128)(2,1)}, bf16[256,1152]{1,0:T(8,128)(2,1)}, u32[]{:S(2)}, u32[]{:S(2)}) collective-permute-start(bf16[256,1152]{1,0:T(8,128)(2,1)} %pad_maximum_fusion), channel_id=1, source_target_pairs={{0,8},{8,16},{16,24},{24,32},{32,40},{40,48},{48,56},{56,64},{64,7... | collective-permute-start | bytes 1769480 | tf_op jit(solution)/shard_map/ppermute | solution.py:210
  37.0 18.5 %copy-start.3 = (bf16[1,256,1024]{2,1,0:T(8,128)(2,1)S(1)}, bf16[1,256,1024]{2,1,0:T(8,128)(2,1)}, u32[]{:S(2)}) copy-start(bf16[1,256,1024]{2,1,0:T(8,128)(2,1)} %param.8) | copy-start | bytes 1572868
  75.2 23.1 %collective-permute-start.5 = (bf16[256,1024]{1,0:T(8,128)(2,1)S(1)}, bf16[256,1024]{1,0:T(8,128)(2,1)S(1)}, u32[]{:S(2)}, u32[]{:S(2)}) collective-permute-start(bf16[256,1024]{1,0:T(8,128)(2,1)S(1)} %get-tuple-element.39), channel_id=1, source_target_pairs={{8,0},{16,8},{24,16},{32,24},{40,32},{48,40},{56,48},{64,56},{72,6... | collective-permute-start | bytes 1572872 | tf_op jit(solution)/shard_map/ppermute | solution.py:210
  86.0 31.8 %collective-permute-start.8 = (bf16[256,1024]{1,0:T(8,128)(2,1)S(1)}, bf16[256,1024]{1,0:T(8,128)(2,1)S(1)}, u32[]{:S(2)}, u32[]{:S(2)}) collective-permute-start(bf16[256,1024]{1,0:T(8,128)(2,1)S(1)} %get-tuple-element.40), channel_id=1, source_target_pairs={{32,0},{40,8},{48,16},{56,24},{64,32},{72,40},{80,48},{88,56},{96,... | collective-permute-start | bytes 1572872 | tf_op jit(solution)/shard_map/ppermute | solution.py:210
  87.3 30.5 %collective-permute-start.7 = (bf16[256,1024]{1,0:T(8,128)(2,1)S(1)}, bf16[256,1024]{1,0:T(8,128)(2,1)S(1)}, u32[]{:S(2)}, u32[]{:S(2)}) collective-permute-start(bf16[256,1024]{1,0:T(8,128)(2,1)S(1)} %get-tuple-element.41), channel_id=1, source_target_pairs={{24,0},{32,8},{40,16},{48,24},{56,32},{64,40},{72,48},{80,56},{88,... | collective-permute-start | bytes 1572872 | tf_op jit(solution)/shard_map/ppermute | solution.py:210
  88.6 29.2 %collective-permute-start.6 = (bf16[256,1024]{1,0:T(8,128)(2,1)S(1)}, bf16[256,1024]{1,0:T(8,128)(2,1)S(1)}, u32[]{:S(2)}, u32[]{:S(2)}) collective-permute-start(bf16[256,1024]{1,0:T(8,128)(2,1)S(1)} %get-tuple-element.42), channel_id=1, source_target_pairs={{16,0},{24,8},{32,16},{40,24},{48,32},{56,40},{64,48},{72,56},{80,... | collective-permute-start | bytes 1572872 | tf_op jit(solution)/shard_map/ppermute | solution.py:210
  120.2 9.8 %copy-start.4 = (bf16[256,1024]{1,0:T(8,128)(2,1)S(1)}, bf16[256,1024]{1,0:T(8,128)(2,1)}, u32[]{:S(2)}) copy-start(bf16[256,1024]{1,0:T(8,128)(2,1)} %add_convert_fusion.2) | copy-start | bytes 1572868
  124.5 7.1 %collective-permute-start.9 = (bf16[256,1024]{1,0:T(8,128)(2,1)S(1)}, bf16[256,1024]{1,0:T(8,128)(2,1)S(1)}, u32[]{:S(2)}, u32[]{:S(2)}) collective-permute-start(bf16[256,1024]{1,0:T(8,128)(2,1)S(1)} %fusion.14), channel_id=1, source_target_pairs={{0,8},{8,0},{16,24},{24,16},{32,40},{40,32},{48,56},{56,48},{64,72... | collective-permute-start | bytes 1572872 | tf_op jit(solution)/shard_map/ppermute | solution.py:269
  130.0 19.7 %collective-permute-start.18 = (bf16[256,1024]{1,0:T(8,128)(2,1)S(1)}, bf16[256,1024]{1,0:T(8,128)(2,1)S(1)}, u32[]{:S(2)}, u32[]{:S(2)}) collective-permute-start(bf16[256,1024]{1,0:T(8,128)(2,1)S(1)} %copy-done.4), channel_id=1, source_target_pairs={{0,8},{8,0},{16,24},{24,16},{32,40},{40,32},{48,56},{56,48},{64,72... | collective-permute-start | bytes 1572872 | tf_op jit(solution)/shard_map/ppermute | solution.py:280
  136.2 29.0 %collective-permute-start.10 = (bf16[256,1024]{1,0:T(8,128)(2,1)S(1)}, bf16[256,1024]{1,0:T(8,128)(2,1)}, u32[]{:S(2)}, u32[]{:S(2)}) collective-permute-start(bf16[256,1024]{1,0:T(8,128)(2,1)S(1)} %add_convert_fusion.1), channel_id=1, source_target_pairs={{0,32},{8,40},{16,48},{24,56},{32,64},{40,72},{48,80},{56,88},{64,... | collective-permute-start | bytes 1572872 | tf_op jit(solution)/shard_map/ppermute | solution.py:210
  140.9 14.1 %copy-start.2 = (bf16[256,16,8,42]{0,3,2,1:T(8,128)(2,1)S(1)}, bf16[256,16,8,42]{0,3,2,1:T(8,128)(2,1)}, u32[]{:S(2)}) copy-start(bf16[256,16,8,42]{0,3,2,1:T(8,128)(2,1)} %reshape_squeeze.7) | copy-start | bytes 8257540
  140.9 45.1 %collective-permute-start.13 = (bf16[256,1024]{1,0:T(8,128)(2,1)S(1)}, bf16[256,1024]{1,0:T(8,128)(2,1)S(1)}, u32[]{:S(2)}, u32[]{:S(2)}) collective-permute-start(bf16[256,1024]{1,0:T(8,128)(2,1)S(1)} %add_convert_fusion.1), channel_id=1, source_target_pairs={{0,8},{8,16},{16,24},{24,32},{32,40},{40,48},{48,56},{56,64},{64,7... | collective-permute-start | bytes 1572872 | tf_op jit(solution)/shard_map/ppermute | solution.py:210
  143.1 40.9 %collective-permute-start.12 = (bf16[256,1024]{1,0:T(8,128)(2,1)S(1)}, bf16[256,1024]{1,0:T(8,128)(2,1)}, u32[]{:S(2)}, u32[]{:S(2)}) collective-permute-start(bf16[256,1024]{1,0:T(8,128)(2,1)S(1)} %add_convert_fusion.1), channel_id=1, source_target_pairs={{0,16},{8,24},{16,32},{24,40},{32,48},{40,56},{48,64},{56,72},{64,... | collective-permute-start | bytes 1572872 | tf_op jit(solution)/shard_map/ppermute | solution.py:210
  145.1 37.1 %collective-permute-start.11 = (bf16[256,1024]{1,0:T(8,128)(2,1)S(1)}, bf16[256,1024]{1,0:T(8,128)(2,1)}, u32[]{:S(2)}, u32[]{:S(2)}) collective-permute-start(bf16[256,1024]{1,0:T(8,128)(2,1)S(1)} %add_convert_fusion.1), channel_id=1, source_target_pairs={{0,24},{8,32},{16,40},{24,48},{32,56},{40,64},{48,72},{56,80},{64,... | collective-permute-start | bytes 1572872 | tf_op jit(solution)/shard_map/ppermute | solution.py:210
  155.0 87.9 %collective-permute-start.19 = (bf16[256,8,336]{0,2,1:T(8,128)(2,1)}, bf16[256,8,336]{0,2,1:T(8,128)(2,1)S(1)}, u32[]{:S(2)}, u32[]{:S(2)}) collective-permute-start(bf16[256,8,336]{0,2,1:T(8,128)(2,1)} %convolution_convert_fusion), channel_id=1, source_target_pairs={{0,8},{8,0},{16,24},{24,16},{32,40},{40,32},{48,56},{56,48},{64,72... | collective-permute-start | bytes 4128776 | tf_op jit(solution)/shard_map/ppermute | solution.py:281
  158.1 116.6 %all-to-all-start = ((bf16[8,256,16,42]{1,2,3,0:T(8,128)(2,1)}), bf16[8,256,16,42]{1,2,3,0:T(8,128)(2,1)}, u32[]{:S(2)}, u32[]{:S(2)}) async-start(bf16[8,256,16,42]{1,2,3,0:T(8,128)(2,1)} %copy.25), calls=%async_computation | async-start | bytes 5505024 | tf_op jit(solution)/shard_map/all_to_all | solution.py:273
  214.4 35.2 %collective-permute-start.14 = (bf16[256,1024]{1,0:T(8,128)(2,1)}, bf16[256,1024]{1,0:T(8,128)(2,1)}, u32[]{:S(2)}, u32[]{:S(2)}) collective-permute-start(bf16[256,1024]{1,0:T(8,128)(2,1)} %get-tuple-element.35), channel_id=1, source_target_pairs={{8,0},{16,8},{24,16},{32,24},{40,32},{48,40},{56,48},{64,56},{72,6... | collective-permute-start | bytes 1572872 | tf_op jit(solution)/shard_map/ppermute | solution.py:210
  216.3 55.4 %collective-permute-start.17 = (bf16[256,1024]{1,0:T(8,128)(2,1)}, bf16[256,1024]{1,0:T(8,128)(2,1)}, u32[]{:S(2)}, u32[]{:S(2)}) collective-permute-start(bf16[256,1024]{1,0:T(8,128)(2,1)} %get-tuple-element.36), channel_id=1, source_target_pairs={{32,0},{40,8},{48,16},{56,24},{64,32},{72,40},{80,48},{88,56},{96,... | collective-permute-start | bytes 1572872 | tf_op jit(solution)/shard_map/ppermute | solution.py:210
  217.6 54.1 %collective-permute-start.16 = (bf16[256,1024]{1,0:T(8,128)(2,1)}, bf16[256,1024]{1,0:T(8,128)(2,1)}, u32[]{:S(2)}, u32[]{:S(2)}) collective-permute-start(bf16[256,1024]{1,0:T(8,128)(2,1)} %get-tuple-element.37), channel_id=1, source_target_pairs={{24,0},{32,8},{40,16},{48,24},{56,32},{64,40},{72,48},{80,56},{88,... | collective-permute-start | bytes 1572872 | tf_op jit(solution)/shard_map/ppermute | solution.py:210
  218.9 52.8 %collective-permute-start.15 = (bf16[256,1024]{1,0:T(8,128)(2,1)}, bf16[256,1024]{1,0:T(8,128)(2,1)}, u32[]{:S(2)}, u32[]{:S(2)}) collective-permute-start(bf16[256,1024]{1,0:T(8,128)(2,1)} %get-tuple-element.38), channel_id=1, source_target_pairs={{16,0},{24,8},{32,16},{40,24},{48,32},{56,40},{64,48},{72,56},{80,... | collective-permute-start | bytes 1572872 | tf_op jit(solution)/shard_map/ppermute | solution.py:210
  274.6 36.7 %copy-start.1 = (bf16[672,1024]{1,0:T(8,128)(2,1)S(1)}, bf16[672,1024]{1,0:T(8,128)(2,1)}, u32[]{:S(2)}) copy-start(bf16[672,1024]{1,0:T(8,128)(2,1)} %param.9) | copy-start | bytes 4128772
Sparse Core Ops, SparseCore 0:
  10.9 88.0 all-gather.4
  120.3 109.6 all-gather.6
